TPU v7x, 32 devices: a whole 2x2x4 slice. The times are simulated.
32 devices in a mesh: dp: 8 (over z, core), seq: 4 (over y, x).
Axes of the slice: x: 2, y: 2, z: 4, core: 2. Of those that a mesh axis runs over, the one named last changes fastest.
Arguments:
- inputs: bfloat16 [24, 512, 1024], P('dp', 'seq'), may hold values from -6 to 6
- w_query: bfloat16 [1024, 1024], P('dp'), may hold values from -0.1875 to 0.1875
- w_key: bfloat16 [1024, 1024], P('dp'), may hold values from -0.1875 to 0.1875
- w_value: bfloat16 [1024, 1024], P('dp'), may hold values from -0.1875 to 0.1875
- b_query: bfloat16 [1024], P('dp'), may hold values from -4 to 4
- b_value: bfloat16 [1024], P('dp'), may hold values from -0.75 to 0.75
- w_out: bfloat16 [1024, 1024], P('dp'), may hold values from -2.5 to 2.5
- b_out: bfloat16 [1024], P('dp'), may hold values from -4 to 4
- gain_one: bfloat16 [1024], P('dp'), may hold values from 0.5 to 1.5
- shift_one: bfloat16 [1024], P('dp'), may hold values from -4 to 4
- w_up: bfloat16 [1024, 4096], P('dp'), may hold values from -0.1875 to 0.1875
- b_up: bfloat16 [4096], P('dp'), may hold values from -6 to 6
- w_down: bfloat16 [4096, 1024], P('dp'), may hold values from -0.09375 to 0.09375
- b_down: bfloat16 [1024], P('dp'), may hold values from -4 to 4
- gain_two: bfloat16 [1024], P('dp'), may hold values from 0.5 to 1.5
- shift_two: bfloat16 [1024], P('dp'), may hold values from -4 to 4
- cotangent: bfloat16 [24, 512, 1024], P('dp', 'seq'), may hold values from -6 to 6
Outputs:
- output: bfloat16 [24, 512, 1024], P('dp', 'seq')
- grad_inputs: float32 [24, 512, 1024], P('dp', 'seq')
- grad_w_query: float32 [1024, 1024], P('dp')
- grad_w_key: float32 [1024, 1024], P('dp')
- grad_w_value: float32 [1024, 1024], P('dp')
- grad_b_query: float32 [1024], P('dp')
- grad_b_value: float32 [1024], P('dp')
- grad_w_out: float32 [1024, 1024], P('dp')
- grad_b_out: float32 [1024], P('dp')
- grad_gain_one: float32 [1024], P('dp')
- grad_shift_one: float32 [1024], P('dp')
- grad_w_up: float32 [1024, 4096], P('dp')
- grad_b_up: float32 [4096], P('dp')
- grad_w_down: float32 [4096, 1024], P('dp')
- grad_b_down: float32 [1024], P('dp')
- grad_gain_two: float32 [1024], P('dp')
- grad_shift_two: float32 [1024], P('dp')
All inputs are finite; a program needn't handle non-finite values.
Results may differ from a plain program's by a relative error of at most 0.02.
Values may be sent and summed in bfloat16 or wider, within the bound.
No kernel may reach another device: no remote copies, remote signals or barrier semaphores. Data moves between devices by JAX's collectives and lax.ppermute only.
A program may use at most 192 MiB of HBM per device.

v0:
```python
import jax
import jax.numpy as jnp
from jax import lax
from jax.sharding import PartitionSpec as P

HEAD_DIM = 64


EPSILON = 1e-12


def dot_rows(former, latter):
    return jnp.dot(former, latter, preferred_element_type=jnp.float32)


def dot_left(former, latter):
    return lax.dot_general(
        former, latter, (((0,), (0,)), ((), ())), preferred_element_type=jnp.float32
    )


def dot_right(former, latter):
    return lax.dot_general(
        former, latter, (((1,), (1,)), ((), ())), preferred_element_type=jnp.float32
    )


def normalize(hidden, gain_vec, offset):
    center = hidden - jnp.mean(hidden, -1, keepdims=True)
    spread = jnp.mean(center * center, -1, keepdims=True)
    return center * lax.rsqrt(spread + EPSILON) * gain_vec + offset


def normalize_back(hidden, gain_vec, offset, upstream):
    result, pullback = jax.vjp(normalize, hidden, gain_vec, offset)
    return pullback(upstream)


def activation(hidden):
    return jax.nn.gelu(hidden, approximate=False)


def activation_back(hidden, upstream):
    result, pullback = jax.vjp(activation, hidden)
    return pullback(upstream)[0]


def attend(head_query, head_key, head_value):
    groups, length, columns = head_query.shape
    four_dims = (groups, length, columns // HEAD_DIM, HEAD_DIM)
    factor = HEAD_DIM ** (-0.5)
    scores = (
        jnp.einsum(
            "gqhd,gkhd->ghqk",
            head_query.reshape(four_dims),
            head_key.reshape(four_dims),
            preferred_element_type=jnp.float32,
        )
        * factor
    )
    row_max = jnp.max(scores, -1, keepdims=True)
    exponent = jnp.exp(scores - row_max)
    row_total = jnp.sum(exponent, -1, keepdims=True)
    portions_low = (exponent / row_total).astype(jnp.bfloat16)
    context = jnp.einsum(
        "ghqk,gkhd->gqhd",
        portions_low,
        head_value.reshape(four_dims),
        preferred_element_type=jnp.float32,
    )
    return (
        context.astype(jnp.bfloat16).reshape(groups, length, columns),
        row_max + jnp.log(row_total),
    )


def attend_back(head_query, head_key, head_value, log_total, upstream):
    groups, length, columns = head_query.shape
    four_dims = (groups, length, columns // HEAD_DIM, HEAD_DIM)
    factor = HEAD_DIM ** (-0.5)
    query_four = head_query.reshape(four_dims)
    key_four = head_key.reshape(four_dims)
    upstream_four = upstream.reshape(four_dims)
    scores = (
        jnp.einsum("gqhd,gkhd->ghqk", query_four, key_four, preferred_element_type=jnp.float32)
        * factor
    )
    portions = jnp.exp(scores - log_total)
    portions_low = portions.astype(jnp.bfloat16)
    grad_value = jnp.einsum(
        "ghqk,gqhd->gkhd", portions_low, upstream_four, preferred_element_type=jnp.float32
    )
    grad_portions = jnp.einsum(
        "gqhd,gkhd->ghqk",
        upstream_four,
        head_value.reshape(four_dims),
        preferred_element_type=jnp.float32,
    )
    grad_scores = (
        portions * (grad_portions - jnp.sum(portions * grad_portions, -1, keepdims=True))
    ).astype(jnp.bfloat16)
    grad_query = (
        jnp.einsum("ghqk,gkhd->gqhd", grad_scores, key_four, preferred_element_type=jnp.float32)
        * factor
    )
    grad_key = (
        jnp.einsum("ghqk,gqhd->gkhd", grad_scores, query_four, preferred_element_type=jnp.float32)
        * factor
    )
    three_dims = (groups, length, columns)
    return (
        grad_query.astype(jnp.bfloat16).reshape(three_dims),
        grad_key.astype(jnp.bfloat16).reshape(three_dims),
        grad_value.astype(jnp.bfloat16).reshape(three_dims),
    )


def forward(weights, inputs):
    (
        w_query,
        w_key,
        w_value,
        b_query,
        b_value,
        w_out,
        b_out,
        gain_one,
        shift_one,
        w_up,
        b_up,
        w_down,
        b_down,
        gain_two,
        shift_two,
    ) = weights
    groups, local_len, model_width = inputs.shape
    flat_rows = inputs.reshape(groups * local_len, model_width)
    three_dims = (groups, local_len, model_width)
    queries = (
        (dot_rows(flat_rows, w_query) + b_query.astype(jnp.float32))
        .astype(jnp.bfloat16)
        .reshape(three_dims)
    )
    key_rows = dot_rows(flat_rows, w_key).astype(jnp.bfloat16).reshape(three_dims)
    values = (
        (dot_rows(flat_rows, w_value) + b_value.astype(jnp.float32))
        .astype(jnp.bfloat16)
        .reshape(three_dims)
    )
    head_query, head_key, head_value = (
        lax.all_to_all(queries, "seq", split_axis=2, concat_axis=1, tiled=True),
        lax.all_to_all(key_rows, "seq", split_axis=2, concat_axis=1, tiled=True),
        lax.all_to_all(values, "seq", split_axis=2, concat_axis=1, tiled=True),
    )
    head_context, log_total = attend(head_query, head_key, head_value)
    context = lax.all_to_all(head_context, "seq", split_axis=1, concat_axis=2, tiled=True).reshape(
        groups * local_len, model_width
    )
    first_sum = flat_rows.astype(jnp.float32) + (
        dot_rows(context, w_out) + b_out.astype(jnp.float32)
    )
    normed = normalize(first_sum, gain_one.astype(jnp.float32), shift_one.astype(jnp.float32))
    normed_low = normed.astype(jnp.bfloat16)
    pre_active = dot_rows(normed_low, w_up) + b_up.astype(jnp.float32)
    active = activation(pre_active).astype(jnp.bfloat16)
    second_sum = normed + (dot_rows(active, w_down) + b_down.astype(jnp.float32))
    result = normalize(second_sum, gain_two.astype(jnp.float32), shift_two.astype(jnp.float32))
    stored = (
        flat_rows,
        head_query,
        head_key,
        head_value,
        log_total,
        context,
        first_sum,
        normed_low,
        pre_active,
        active,
        second_sum,
    )
    return (result, stored)


def local(
    inputs,
    w_query,
    w_key,
    w_value,
    b_query,
    b_value,
    w_out,
    b_out,
    gain_one,
    shift_one,
    w_up,
    b_up,
    w_down,
    b_down,
    gain_two,
    shift_two,
    cotangent,
):
    gathered = (
        lax.all_gather(w_query, "dp", axis=0, tiled=True),
        lax.all_gather(w_key, "dp", axis=0, tiled=True),
        lax.all_gather(w_value, "dp", axis=0, tiled=True),
        lax.all_gather(b_query, "dp", axis=0, tiled=True),
        lax.all_gather(b_value, "dp", axis=0, tiled=True),
        lax.all_gather(w_out, "dp", axis=0, tiled=True),
        lax.all_gather(b_out, "dp", axis=0, tiled=True),
        lax.all_gather(gain_one, "dp", axis=0, tiled=True),
        lax.all_gather(shift_one, "dp", axis=0, tiled=True),
        lax.all_gather(w_up, "dp", axis=0, tiled=True),
        lax.all_gather(b_up, "dp", axis=0, tiled=True),
        lax.all_gather(w_down, "dp", axis=0, tiled=True),
        lax.all_gather(b_down, "dp", axis=0, tiled=True),
        lax.all_gather(gain_two, "dp", axis=0, tiled=True),
        lax.all_gather(shift_two, "dp", axis=0, tiled=True),
    )
    result, stored = forward(gathered, inputs)
    output = result.astype(jnp.bfloat16).reshape(inputs.shape)
    weights = (
        lax.all_gather(w_query, "dp", axis=0, tiled=True),
        lax.all_gather(w_key, "dp", axis=0, tiled=True),
        lax.all_gather(w_value, "dp", axis=0, tiled=True),
        lax.all_gather(b_query, "dp", axis=0, tiled=True),
        lax.all_gather(b_value, "dp", axis=0, tiled=True),
        lax.all_gather(w_out, "dp", axis=0, tiled=True),
        lax.all_gather(b_out, "dp", axis=0, tiled=True),
        lax.all_gather(gain_one, "dp", axis=0, tiled=True),
        lax.all_gather(shift_one, "dp", axis=0, tiled=True),
        lax.all_gather(w_up, "dp", axis=0, tiled=True),
        lax.all_gather(b_up, "dp", axis=0, tiled=True),
        lax.all_gather(w_down, "dp", axis=0, tiled=True),
        lax.all_gather(b_down, "dp", axis=0, tiled=True),
        lax.all_gather(gain_two, "dp", axis=0, tiled=True),
        lax.all_gather(shift_two, "dp", axis=0, tiled=True),
    )
    unused, stored = forward(weights, inputs)
    (
        full_query,
        full_key,
        full_value,
        full_bq,
        full_bv,
        full_out,
        full_bo,
        full_gain_one,
        full_shift_one,
        full_up,
        full_bup,
        full_down,
        full_bdown,
        full_gain_two,
        full_shift_two,
    ) = weights
    (
        flat_rows,
        head_query,
        head_key,
        head_value,
        log_total,
        context,
        first_sum,
        normed_low,
        pre_active,
        active,
        second_sum,
    ) = stored
    groups, local_len, model_width = inputs.shape
    upstream = cotangent.reshape(groups * local_len, model_width).astype(jnp.float32)
    grad_second, grad_gain_two, grad_shift_two = normalize_back(
        second_sum, full_gain_two.astype(jnp.float32), full_shift_two.astype(jnp.float32), upstream
    )
    grad_branch_two = grad_second.astype(jnp.bfloat16)
    grad_b_down = jnp.sum(grad_branch_two.astype(jnp.float32), 0)
    grad_w_down = dot_left(active, grad_branch_two)
    grad_pre = activation_back(pre_active, dot_right(grad_branch_two, full_down)).astype(
        jnp.bfloat16
    )
    grad_b_up = jnp.sum(grad_pre.astype(jnp.float32), 0)
    grad_w_up = dot_left(normed_low, grad_pre)
    grad_normed = grad_second + dot_right(grad_pre, full_up)
    grad_first, grad_gain_one, grad_shift_one = normalize_back(
        first_sum,
        full_gain_one.astype(jnp.float32),
        full_shift_one.astype(jnp.float32),
        grad_normed,
    )
    grad_branch_one = grad_first.astype(jnp.bfloat16)
    grad_b_out = jnp.sum(grad_branch_one.astype(jnp.float32), 0)
    grad_w_out = dot_left(context, grad_branch_one)
    grad_context = (
        dot_right(grad_branch_one, full_out)
        .astype(jnp.bfloat16)
        .reshape(groups, local_len, model_width)
    )
    head_grad = lax.all_to_all(grad_context, "seq", split_axis=2, concat_axis=1, tiled=True)
    grad_hq, grad_hk, grad_hv = attend_back(head_query, head_key, head_value, log_total, head_grad)
    grad_queries, grad_keys, grad_values = (
        lax.all_to_all(grad_hq, "seq", split_axis=1, concat_axis=2, tiled=True),
        lax.all_to_all(grad_hk, "seq", split_axis=1, concat_axis=2, tiled=True),
        lax.all_to_all(grad_hv, "seq", split_axis=1, concat_axis=2, tiled=True),
    )
    flat_dims = (groups * local_len, model_width)
    grad_queries = grad_queries.reshape(flat_dims)
    grad_keys = grad_keys.reshape(flat_dims)
    grad_values = grad_values.reshape(flat_dims)
    grad_w_query = dot_left(flat_rows, grad_queries)
    grad_w_key = dot_left(flat_rows, grad_keys)
    grad_w_value = dot_left(flat_rows, grad_values)
    grad_b_query = jnp.sum(grad_queries.astype(jnp.float32), 0)
    grad_b_value = jnp.sum(grad_values.astype(jnp.float32), 0)
    grad_inputs = (
        grad_first
        + dot_right(grad_queries, full_query)
        + dot_right(grad_keys, full_key)
        + dot_right(grad_values, full_value)
    )
    owned_grads = (
        lax.psum_scatter(
            grad_w_query.astype(jnp.bfloat16), "dp", scatter_dimension=0, tiled=True
        ).astype(jnp.float32),
        lax.psum_scatter(
            grad_w_key.astype(jnp.bfloat16), "dp", scatter_dimension=0, tiled=True
        ).astype(jnp.float32),
        lax.psum_scatter(
            grad_w_value.astype(jnp.bfloat16), "dp", scatter_dimension=0, tiled=True
        ).astype(jnp.float32),
        lax.psum_scatter(
            grad_b_query.astype(jnp.bfloat16), "dp", scatter_dimension=0, tiled=True
        ).astype(jnp.float32),
        lax.psum_scatter(
            grad_b_value.astype(jnp.bfloat16), "dp", scatter_dimension=0, tiled=True
        ).astype(jnp.float32),
        lax.psum_scatter(
            grad_w_out.astype(jnp.bfloat16), "dp", scatter_dimension=0, tiled=True
        ).astype(jnp.float32),
        lax.psum_scatter(
            grad_b_out.astype(jnp.bfloat16), "dp", scatter_dimension=0, tiled=True
        ).astype(jnp.float32),
        lax.psum_scatter(
            grad_gain_one.astype(jnp.bfloat16), "dp", scatter_dimension=0, tiled=True
        ).astype(jnp.float32),
        lax.psum_scatter(
            grad_shift_one.astype(jnp.bfloat16), "dp", scatter_dimension=0, tiled=True
        ).astype(jnp.float32),
        lax.psum_scatter(
            grad_w_up.astype(jnp.bfloat16), "dp", scatter_dimension=0, tiled=True
        ).astype(jnp.float32),
        lax.psum_scatter(
            grad_b_up.astype(jnp.bfloat16), "dp", scatter_dimension=0, tiled=True
        ).astype(jnp.float32),
        lax.psum_scatter(
            grad_w_down.astype(jnp.bfloat16), "dp", scatter_dimension=0, tiled=True
        ).astype(jnp.float32),
        lax.psum_scatter(
            grad_b_down.astype(jnp.bfloat16), "dp", scatter_dimension=0, tiled=True
        ).astype(jnp.float32),
        lax.psum_scatter(
            grad_gain_two.astype(jnp.bfloat16), "dp", scatter_dimension=0, tiled=True
        ).astype(jnp.float32),
        lax.psum_scatter(
            grad_shift_two.astype(jnp.bfloat16), "dp", scatter_dimension=0, tiled=True
        ).astype(jnp.float32),
    )
    summed = (
        lax.psum(owned_grads[0].astype(jnp.bfloat16), "seq").astype(jnp.float32),
        lax.psum(owned_grads[1].astype(jnp.bfloat16), "seq").astype(jnp.float32),
        lax.psum(owned_grads[2].astype(jnp.bfloat16), "seq").astype(jnp.float32),
        lax.psum(owned_grads[3].astype(jnp.bfloat16), "seq").astype(jnp.float32),
        lax.psum(owned_grads[4].astype(jnp.bfloat16), "seq").astype(jnp.float32),
        lax.psum(owned_grads[5].astype(jnp.bfloat16), "seq").astype(jnp.float32),
        lax.psum(owned_grads[6].astype(jnp.bfloat16), "seq").astype(jnp.float32),
        lax.psum(owned_grads[7].astype(jnp.bfloat16), "seq").astype(jnp.float32),
        lax.psum(owned_grads[8].astype(jnp.bfloat16), "seq").astype(jnp.float32),
        lax.psum(owned_grads[9].astype(jnp.bfloat16), "seq").astype(jnp.float32),
        lax.psum(owned_grads[10].astype(jnp.bfloat16), "seq").astype(jnp.float32),
        lax.psum(owned_grads[11].astype(jnp.bfloat16), "seq").astype(jnp.float32),
        lax.psum(owned_grads[12].astype(jnp.bfloat16), "seq").astype(jnp.float32),
        lax.psum(owned_grads[13].astype(jnp.bfloat16), "seq").astype(jnp.float32),
        lax.psum(owned_grads[14].astype(jnp.bfloat16), "seq").astype(jnp.float32),
    )
    return (output, grad_inputs.reshape(inputs.shape)) + tuple(summed)


def solution(mesh):
    placed = (
        P("dp", "seq", None),
        P("dp", None),
        P("dp", None),
        P("dp", None),
        P("dp"),
        P("dp"),
        P("dp", None),
        P("dp"),
        P("dp"),
        P("dp"),
        P("dp", None),
        P("dp"),
        P("dp", None),
        P("dp"),
        P("dp"),
        P("dp"),
        P("dp", "seq", None),
    )
    return jax.shard_map(
        local,
        mesh=mesh,
        in_specs=placed,
        out_specs=(
            P("dp", "seq", None),
            P("dp", "seq", None),
            P("dp", None),
            P("dp", None),
            P("dp", None),
            P("dp"),
            P("dp"),
            P("dp", None),
            P("dp"),
            P("dp"),
            P("dp"),
            P("dp", None),
            P("dp"),
            P("dp", None),
            P("dp"),
            P("dp"),
            P("dp"),
        ),
        check_vma=False,
    )
```

profile of v0, /device:TPU:0, one launch (start us, length us, event | category | flops | bytes accessed | tf_op | source)
XLA Modules:
  0.0 830.0 jit_solution(2075484790764947876)
XLA Ops:
  11.2 13.5 %all-gather = bf16[8,1,128]{2,1,0:T(2,128)(2,1)S(1)} all-gather(bf16[1,1,128]{2,1,0:T(2,128)(2,1)S(1)} %bitcast.204), channel_id=1, replica_groups=mesh['dp'=8,'seq'=4] {'dp'}, dimensions={0}, use_global_device_ids=true | all-gather | bytes 2304 | tf_op jit(solution)/shard_map/all_gather | solution.py:208
  24.7 16.8 %all-gather.16.cloned.1.call-done = bf16[1024,1024]{1,0:T(8,128)(2,1)} async-done(((bf16[128,1024]{1,0:T(8,128)(2,1)}), bf16[1024,1024]{1,0:T(8,128)(2,1)}) %all-gather.16.cloned.1.call-update) | async-done | bytes 2097168 | tf_op jit(solution)/shard_map/all_gather | solution.py:206
  49.2 10.3 %all-gather.1 = bf16[8,1,128]{2,1,0:T(2,128)(2,1)S(1)} all-gather(bf16[1,1,128]{2,1,0:T(2,128)(2,1)S(1)} %bitcast.205), channel_id=1, replica_groups=mesh['dp'=8,'seq'=4] {'dp'}, dimensions={0}, use_global_device_ids=true | all-gather | bytes 2304 | tf_op jit(solution)/shard_map/all_gather | solution.py:207
  59.5 12.3 %all-gather.18.cloned.1.call-done = bf16[1024,1024]{1,0:T(8,128)(2,1)} async-done(((bf16[128,1024]{1,0:T(8,128)(2,1)}), bf16[1024,1024]{1,0:T(8,128)(2,1)}) %all-gather.18.cloned.1.call-update) | async-done | bytes 2097168 | tf_op jit(solution)/shard_map/all_gather | solution.py:204
  79.4 22.6 %all-gather.20.cloned.1.call-done = bf16[1024,1024]{1,0:T(8,128)(2,1)} async-done(((bf16[128,1024]{1,0:T(8,128)(2,1)}), bf16[1024,1024]{1,0:T(8,128)(2,1)}) %all-gather.20.cloned.1.call-update) | async-done | bytes 2097168 | tf_op jit(solution)/shard_map/all_gather | solution.py:205
  115.1 9.1 %all-to-all-done.2 = bf16[3,128,1024]{1,0,2:T(4,128)(2,1)S(1)} async-done(((bf16[3,128,1024]{1,0,2:T(4,128)(2,1)}), bf16[3,128,1024]{1,0,2:T(4,128)(2,1)S(1)}, u32[]{:S(2)}, u32[]{:S(2)}) %all-to-all-start.2) | async-done | bytes 786464 | tf_op jit(solution)/shard_map/all_to_all | solution.py:152
  139.5 10.5 %all-gather.6 = bf16[8,1,128]{2,1,0:T(2,128)(2,1)S(1)} all-gather(bf16[1,1,128]{2,1,0:T(2,128)(2,1)S(1)} %bitcast.206), channel_id=1, replica_groups=mesh['dp'=8,'seq'=4] {'dp'}, dimensions={0}, use_global_device_ids=true | all-gather | bytes 2304 | tf_op jit(solution)/shard_map/all_gather | solution.py:216
  150.0 12.9 %all-gather.5 = bf16[8,1,512]{2,1,0:T(2,128)(2,1)S(1)} all-gather(bf16[1,1,512]{2,1,0:T(2,128)(2,1)S(1)} %reshape.226), channel_id=1, replica_groups=mesh['dp'=8,'seq'=4] {'dp'}, dimensions={0}, use_global_device_ids=true | all-gather | bytes 9216 | tf_op jit(solution)/shard_map/all_gather | solution.py:214
  163.0 9.6 %all-gather.2 = bf16[8,1,128]{2,1,0:T(2,128)(2,1)S(1)} all-gather(bf16[1,1,128]{2,1,0:T(2,128)(2,1)S(1)} %bitcast.207), channel_id=1, replica_groups=mesh['dp'=8,'seq'=4] {'dp'}, dimensions={0}, use_global_device_ids=true | all-gather | bytes 2304 | tf_op jit(solution)/shard_map/all_gather | solution.py:210
  172.5 11.3 %all-gather.4 = bf16[8,1,128]{2,1,0:T(2,128)(2,1)S(1)} all-gather(bf16[1,1,128]{2,1,0:T(2,128)(2,1)S(1)} %bitcast.208), channel_id=1, replica_groups=mesh['dp'=8,'seq'=4] {'dp'}, dimensions={0}, use_global_device_ids=true | all-gather | bytes 2304 | tf_op jit(solution)/shard_map/all_gather | solution.py:212
  183.8 8.8 %all-gather.3 = bf16[8,1,128]{2,1,0:T(2,128)(2,1)S(1)} all-gather(bf16[1,1,128]{2,1,0:T(2,128)(2,1)S(1)} %bitcast.209), channel_id=1, replica_groups=mesh['dp'=8,'seq'=4] {'dp'}, dimensions={0}, use_global_device_ids=true | all-gather | bytes 2304 | tf_op jit(solution)/shard_map/all_gather | solution.py:211
  192.6 10.0 %all-gather.7 = bf16[8,1,128]{2,1,0:T(2,128)(2,1)S(1)} all-gather(bf16[1,1,128]{2,1,0:T(2,128)(2,1)S(1)} %bitcast.210), channel_id=1, replica_groups=mesh['dp'=8,'seq'=4] {'dp'}, dimensions={0}, use_global_device_ids=true | all-gather | bytes 2304 | tf_op jit(solution)/shard_map/all_gather | solution.py:217
  202.6 10.0 %all-gather.8 = bf16[8,1,128]{2,1,0:T(2,128)(2,1)S(1)} all-gather(bf16[1,1,128]{2,1,0:T(2,128)(2,1)S(1)} %bitcast.211), channel_id=1, replica_groups=mesh['dp'=8,'seq'=4] {'dp'}, dimensions={0}, use_global_device_ids=true | all-gather | bytes 2304 | tf_op jit(solution)/shard_map/all_gather | solution.py:218
  217.1 20.7 %multiply_convert_fusion.1 = (bf16[384,4096]{1,0:T(8,128)(2,1)}, f32[384,4096]{1,0:T(8,128)}, f32[384,4096]{1,0:T(8,128)}) fusion(f32[4096]{0:T(1024)S(1)} %bitcast.187, bf16[1024,4096]{1,0:T(8,128)(2,1)} %all-gather.24.cloned.1.call-done, f32[384,1024]{1,0:T(8,128)S(1)} %get-tuple-element.130, f32[1024]{0:T(1024)S(1)} %bitcast.197, ...), kind=kOutput, calls=%fused_computation.15 | convolution fusion | flops 3327000576 | bytes 25717760 | tf_op jit(solution)/shard_map/dot_general | solution.py:13
  237.8 59.7 %all-gather.26.cloned.1.call-done = bf16[4096,1024]{1,0:T(8,128)(2,1)} async-done(((bf16[512,1024]{1,0:T(8,128)(2,1)}), bf16[4096,1024]{1,0:T(8,128)(2,1)}) %all-gather.26.cloned.1.call-update) | async-done | bytes 8388624 | tf_op jit(solution)/shard_map/all_gather | solution.py:215
  297.5 7.0 fusion.35
  307.3 13.3 %fusion.29 = (bf16[4096]{0:T(1024)(128)(2,1)S(1)}, bf16[384,4096]{1,0:T(8,128)(2,1)S(1)}) fusion(f32[384,4096]{1,0:T(8,128)} %get-tuple-element.125, f32[384,4096]{1,0:T(8,128)} %get-tuple-element.131, bf16[384,1024]{1,0:T(8,128)(2,1)S(1)} %get-tuple-element.115, bf16[4096,1024]{1,0:T(8,128)(2,1)} %all-gather.26.cloned.1.call-done), kind=kOutput, calls=%fused_computation.83 | convolution fusion | flops 3244814336 | bytes 24911872 | tf_op jit(solution)/shard_map/dot_general | solution.py:23
  334.0 14.1 %all-to-all-done.4 = bf16[3,128,1024]{1,0,2:T(4,128)(2,1)S(1)} async-done(((bf16[3,128,1024]{1,0,2:T(4,128)(2,1)}), bf16[3,128,1024]{1,0,2:T(4,128)(2,1)S(1)}, u32[]{:S(2)}, u32[]{:S(2)}) %all-to-all-start.4) | async-done | bytes 786464 | tf_op jit(solution)/shard_map/all_to_all | solution.py:298
  357.9 6.8 multiply_convert_fusion
  369.9 17.6 %all_to_all.140 = bf16[3,512,256]{2,0,1:T(4,128)(2,1)S(1)} all-to-all(bf16[3,512,256]{2,0,1:T(4,128)(2,1)} %copy.88), channel_id=1, replica_groups=mesh['dp'=8,'seq'=4] {'seq'}, dimensions={1} | all-to-all | bytes 1572864 | tf_op jit(solution)/shard_map/all_to_all | solution.py:301
  404.9 16.0 %all_to_all.141 = bf16[3,512,256]{2,0,1:T(4,128)(2,1)S(1)} all-to-all(bf16[3,512,256]{2,0,1:T(4,128)(2,1)} %copy.92), channel_id=1, replica_groups=mesh['dp'=8,'seq'=4] {'seq'}, dimensions={1} | all-to-all | bytes 1572864 | tf_op jit(solution)/shard_map/all_to_all | solution.py:302
  428.5 7.8 fusion.17
  437.9 13.4 %all_to_all.142 = bf16[3,512,256]{2,0,1:T(4,128)(2,1)S(1)} all-to-all(bf16[3,512,256]{2,0,1:T(4,128)(2,1)S(1)} %copy.96), channel_id=1, replica_groups=mesh['dp'=8,'seq'=4] {'seq'}, dimensions={1} | all-to-all | bytes 1572864 | tf_op jit(solution)/shard_map/all_to_all | solution.py:303
  463.9 10.4 %convolution_convert_fusion.1 = bf16[1024,4096]{1,0:T(8,128)(2,1)} fusion(bf16[384,4096]{1,0:T(8,128)(2,1)} %copy-done.38, f32[384,1024]{1,0:T(8,128)} %copy-done.7, f32[1024]{0:T(1024)S(1)} %bitcast.199, f32[1024]{0:T(1024)S(1)} %bitcast.192, f32[384]{0:T(512)S(1)} %fusion.22, f32[384]{0:T(512)S(1)} %broadcast_multiply_fusion.1), kind=kOutput, calls=%fused_computation.10 | convolution fusion | flops 3227385856 | bytes 13118464 | tf_op jit(solution)/shard_map/dot_general | solution.py:17
  475.4 8.7 %convolution_convert_fusion = bf16[4096,1024]{1,0:T(8,128)(2,1)} fusion(bf16[384,4096]{1,0:T(8,128)(2,1)} %get-tuple-element.124, bf16[384,1024]{1,0:T(8,128)(2,1)S(1)} %copy-done.20), kind=kOutput, calls=%fused_computation.9 | convolution fusion | flops 3225419776 | bytes 12320768 | tf_op jit(solution)/shard_map/dot_general | solution.py:17
  487.9 15.7 %reduce-scatter.23.cloned.1.call-done = bf16[128,1024]{1,0:T(8,128)(2,1)} async-done(((bf16[1024,1024]{1,0:T(8,128)(2,1)}), bf16[128,1024]{1,0:T(8,128)(2,1)}) %reduce-scatter.23.cloned.1.call-update) | async-done | bytes 262160
  505.4 35.2 %reduce-scatter.13.cloned.1.call-done = bf16[128,1024]{1,0:T(8,128)(2,1)} async-done(((bf16[1024,1024]{1,0:T(8,128)(2,1)}), bf16[128,1024]{1,0:T(8,128)(2,1)}) %reduce-scatter.13.cloned.1.call-update) | async-done | bytes 262160 | tf_op jit(solution)/shard_map/reduce_scatter | solution.py:336
  540.6 90.6 %reduce-scatter.15.cloned.1.call-done = bf16[128,4096]{1,0:T(8,128)(2,1)} async-done(((bf16[1024,4096]{1,0:T(8,128)(2,1)}), bf16[128,4096]{1,0:T(8,128)(2,1)}) %reduce-scatter.15.cloned.1.call-update) | async-done | bytes 1048592 | tf_op jit(solution)/shard_map/reduce_scatter | solution.py:348
  631.2 90.1 %reduce-scatter.17.cloned.1.call-done = bf16[512,1024]{1,0:T(8,128)(2,1)} async-done(((bf16[4096,1024]{1,0:T(8,128)(2,1)}), bf16[512,1024]{1,0:T(8,128)(2,1)}) %reduce-scatter.17.cloned.1.call-update) | async-done | bytes 1048592 | tf_op jit(solution)/shard_map/reduce_scatter | solution.py:354
  724.8 26.1 %all-reduce.9 = (bf16[1024]{0:T(1024)(128)(2,1)S(1)}, bf16[1024]{0:T(1024)(128)(2,1)S(1)}, bf16[1024]{0:T(1024)(128)(2,1)S(1)}, bf16[1024]{0:T(1024)(128)(2,1)S(...) all-reduce(bf16[1024]{0:T(1024)(128)(2,1)S(1)} %bitcast.195, ...), channel_id=5, replica_groups=mesh['dp'=8,'seq'=4] {'dp'}, use_global_device_ids=true, to_apply=%region_18.0.clone | all-reduce | flops 12288 | bytes 49152
  751.6 10.5 %all-reduce.10 = (bf16[128]{0:T(256)(128)(2,1)S(1)}, bf16[128]{0:T(256)(128)(2,1)S(1)}, bf16[128]{0:T(256)(128)(2,1)S(1)}, bf16[128]{0:T(256)(128)(2,1)S(1)}, bf...) all-reduce(bf16[128]{0:T(256)(128)(2,1)S(1)} %dynamic-slice.1, ...), channel_id=1, replica_groups=mesh['dp'=8,'seq'=4] {'seq'}, use_global_device_ids=true, to_apply=%region_19.0 | all-reduce | flops 1536 | bytes 6144 | tf_op jit(solution)/shard_map/psum | solution.py:371
  774.0 38.3 %all-reduce.14.cloned.1.call-done = (bf16[128,1024]{0,1:T(8,128)(2,1)}, bf16[128,1024]{0,1:T(8,128)(2,1)}, bf16[128,1024]{0,1:T(8,128)(2,1)}, bf16[128,1024]{1,0...) async-done(((bf16[128,1024]{0,1:T(8,128)(2,1)}, bf16[128,1024]{0,1:T(8,128)(2,1)}, bf16[128,1024]{0,1:T(8,128)(2,1)}, bf16[128,1024]{1,0:T(8,128)(2,1)}, ...) | async-done | bytes 3145744 | tf_op jit(solution)/shard_map/psum | solution.py:368
  (230 shorter events, 153.8 us)
Async XLA Ops:
  7.2 34.3 %copy-start.33 = (bf16[3,128,1024]{2,1,0:T(8,128)(2,1)S(1)}, bf16[3,128,1024]{2,1,0:T(8,128)(2,1)}, u32[]{:S(2)}) copy-start(bf16[3,128,1024]{2,1,0:T(8,128)(2,1)} %param.17) | copy-start | bytes 2359300
  7.2 34.3 %all-gather.16.cloned.1.call-start = ((), (), s32[]{:S(2)}) async-start(), calls=%async_computation.14 | async-start | bytes 2359296 | tf_op jit(solution)/shard_map/all_gather | solution.py:206
  7.9 63.8 %all-gather.18.cloned.1.call-start = ((), (), s32[]{:S(2)}) async-start(), calls=%async_computation.15 | async-start | bytes 2359296 | tf_op jit(solution)/shard_map/all_gather | solution.py:204
  8.7 93.3 %all-gather.20.cloned.1.call-start = ((), (), s32[]{:S(2)}) async-start(), calls=%async_computation.16 | async-start | bytes 2359296 | tf_op jit(solution)/shard_map/all_gather | solution.py:205
  9.4 204.1 %all-gather.22.cloned.1.call-start = ((), (), s32[]{:S(2)}) async-start(), calls=%async_computation.17 | async-start | bytes 2359296 | tf_op jit(solution)/shard_map/all_gather | solution.py:209
  10.0 207.1 %all-gather.24.cloned.1.call-start = ((), (), s32[]{:S(2)}) async-start(), calls=%async_computation.18 | async-start | bytes 9437184 | tf_op jit(solution)/shard_map/all_gather | solution.py:213
  10.6 286.9 %all-gather.26.cloned.1.call-start = ((), (), s32[]{:S(2)}) async-start(), calls=%async_computation.19 | async-start | bytes 9437184 | tf_op jit(solution)/shard_map/all_gather | solution.py:215
  45.5 30.2 %all-to-all-start = ((bf16[3,128,1024]{1,0,2:T(4,128)(2,1)}), bf16[3,128,1024]{1,0,2:T(4,128)(2,1)S(1)}, u32[]{:S(2)}, u32[]{:S(2)}) async-start(bf16[3,128,1024]{1,0,2:T(4,128)(2,1)} %copy.75), calls=%async_computation | async-start | bytes 2097152 | tf_op jit(solution)/shard_map/all_to_all | solution.py:153
  75.8 30.5 %all-to-all-start.1 = ((bf16[3,128,1024]{1,0,2:T(4,128)(2,1)}), bf16[3,128,1024]{1,0,2:T(4,128)(2,1)S(1)}, u32[]{:S(2)}, u32[]{:S(2)}) async-start(bf16[3,128,1024]{1,0,2:T(4,128)(2,1)} %copy.77), calls=%async_computation.1 | async-start | bytes 2097152 | tf_op jit(solution)/shard_map/all_to_all | solution.py:151
  106.2 18.0 %all-to-all-start.2 = ((bf16[3,128,1024]{1,0,2:T(4,128)(2,1)}), bf16[3,128,1024]{1,0,2:T(4,128)(2,1)S(1)}, u32[]{:S(2)}, u32[]{:S(2)}) async-start(bf16[3,128,1024]{1,0,2:T(4,128)(2,1)} %copy.79), calls=%async_computation.2 | async-start | bytes 2097152 | tf_op jit(solution)/shard_map/all_to_all | solution.py:152
  134.5 15.5 %copy-start.22 = (bf16[512]{0:T(512)(128)(2,1)S(1)}, bf16[512]{0:T(512)(128)(2,1)}, u32[]{:S(2)}) copy-start(bf16[512]{0:T(512)(128)(2,1)} %param.28) | copy-start | bytes 3076
  134.6 28.4 %copy-start.26 = (bf16[128]{0:T(256)(128)(2,1)S(1)}, bf16[128]{0:T(256)(128)(2,1)}, u32[]{:S(2)}) copy-start(bf16[128]{0:T(256)(128)(2,1)} %param.24) | copy-start | bytes 772
  134.6 38.0 %copy-start.27 = (bf16[128]{0:T(256)(128)(2,1)S(1)}, bf16[128]{0:T(256)(128)(2,1)}, u32[]{:S(2)}) copy-start(bf16[128]{0:T(256)(128)(2,1)} %param.26) | copy-start | bytes 772
  134.6 49.2 %copy-start.28 = (bf16[128]{0:T(256)(128)(2,1)S(1)}, bf16[128]{0:T(256)(128)(2,1)}, u32[]{:S(2)}) copy-start(bf16[128]{0:T(256)(128)(2,1)} %param.25) | copy-start | bytes 772
  134.6 58.0 %copy-start.29 = (bf16[128]{0:T(256)(128)(2,1)S(1)}, bf16[128]{0:T(256)(128)(2,1)}, u32[]{:S(2)}) copy-start(bf16[128]{0:T(256)(128)(2,1)} %param.31) | copy-start | bytes 772
  134.6 68.0 %copy-start.30 = (bf16[128]{0:T(256)(128)(2,1)S(1)}, bf16[128]{0:T(256)(128)(2,1)}, u32[]{:S(2)}) copy-start(bf16[128]{0:T(256)(128)(2,1)} %param.32) | copy-start | bytes 772
  136.0 76.6 %all-to-all-start.3 = ((bf16[3,512,256]{2,0,1:T(4,128)(2,1)}), bf16[3,512,256]{2,0,1:T(4,128)(2,1)S(1)}, u32[]{:S(2)}, u32[]{:S(2)}) async-start(bf16[3,512,256]{2,0,1:T(4,128)(2,1)} %copy.82), calls=%async_computation.3 | async-start | bytes 2097152 | tf_op jit(solution)/shard_map/all_to_all | solution.py:156
  216.7 103.9 %copy-start.7 = (f32[384,1024]{1,0:T(8,128)}, f32[384,1024]{1,0:T(8,128)S(1)}, u32[]{:S(2)}) copy-start(f32[384,1024]{1,0:T(8,128)S(1)} %get-tuple-element.130) | copy-start | bytes 4718596
  330.3 17.8 %all-to-all-start.4 = ((bf16[3,128,1024]{1,0,2:T(4,128)(2,1)}), bf16[3,128,1024]{1,0,2:T(4,128)(2,1)S(1)}, u32[]{:S(2)}, u32[]{:S(2)}) async-start(bf16[3,128,1024]{1,0,2:T(4,128)(2,1)} %copy.85), calls=%async_computation.4 | async-start | bytes 2097152 | tf_op jit(solution)/shard_map/all_to_all | solution.py:298
  333.9 150.3 %reduce-scatter.19.cloned.1.call-start = ((), (), s32[]{:S(2)}) async-start(), calls=%async_computation.23 | async-start | bytes 2359296
  369.9 20.4 %copy-start.34 = (bf16[3,128,1024]{2,1,0:T(8,128)(2,1)S(1)}, bf16[3,128,1024]{2,1,0:T(8,128)(2,1)}, u32[]{:S(2)}) copy-start(bf16[3,128,1024]{2,1,0:T(8,128)(2,1)} %param.17) | copy-start | bytes 2359300
  396.9 89.2 %reduce-scatter.21.cloned.1.call-start = ((), (), s32[]{:S(2)}) async-start(), calls=%async_computation.24 | async-start | bytes 2359296
  404.9 16.9 %copy-start.35 = (bf16[3,128,1024]{2,1,0:T(8,128)(2,1)S(1)}, bf16[3,128,1024]{2,1,0:T(8,128)(2,1)}, u32[]{:S(2)}) copy-start(bf16[3,128,1024]{2,1,0:T(8,128)(2,1)} %param.17) | copy-start | bytes 2359300
  428.4 75.2 %reduce-scatter.23.cloned.1.call-start = ((), (), s32[]{:S(2)}) async-start(), calls=%async_computation.25 | async-start | bytes 2359296
  437.9 15.2 %copy-start.36 = (bf16[3,128,1024]{2,1,0:T(8,128)(2,1)S(1)}, bf16[3,128,1024]{2,1,0:T(8,128)(2,1)}, u32[]{:S(2)}) copy-start(bf16[3,128,1024]{2,1,0:T(8,128)(2,1)} %param.17) | copy-start | bytes 2359300
  459.8 80.9 %reduce-scatter.13.cloned.1.call-start = ((), (), s32[]{:S(2)}) async-start(), calls=%async_computation.20 | async-start | bytes 2359296 | tf_op jit(solution)/shard_map/reduce_scatter | solution.py:336
  463.9 167.3 %reduce-scatter.15.cloned.1.call-start = ((), (), s32[]{:S(2)}) async-start(), calls=%async_computation.21 | async-start | bytes 9437184 | tf_op jit(solution)/shard_map/reduce_scatter | solution.py:348
  474.3 247.0 %reduce-scatter.17.cloned.1.call-start = ((), (), s32[]{:S(2)}) async-start(), calls=%async_computation.22 | async-start | bytes 9437184 | tf_op jit(solution)/shard_map/reduce_scatter | solution.py:354
  484.1 238.5 %copy-start.37 = (u32[32]{0:T(128)S(1)}, u32[32]{0:T(128)}, u32[]{:S(2)}) copy-start(u32[32]{0:T(128)} %constant.93) | copy-start | bytes 388
  484.1 240.4 %copy-start.3 = (bf16[3,512,256]{2,1,0:T(8,128)(2,1)S(1)}, bf16[3,512,256]{2,1,0:T(8,128)(2,1)}, u32[]{:S(2)}) copy-start(bf16[3,512,256]{2,1,0:T(8,128)(2,1)} %copy-done.2) | copy-start | bytes 2359300
  484.1 328.1 %all-reduce.14.cloned.1.call-start = ((), (), s32[]{:S(2)}) async-start(), calls=%async_computation.26 | async-start | bytes 6291456 | tf_op jit(solution)/shard_map/psum | solution.py:368
  724.7 45.1 %copy-start.15 = (bf16[48,8,4,256]{3,1,2,0:T(8,128)(2,1)S(1)}, bf16[48,8,4,256]{3,1,2,0:T(8,128)(2,1)}, u32[]{:S(2)}) copy-start(bf16[48,8,4,256]{3,1,2,0:T(8,128)(2,1)} %copy-done.14) | copy-start | bytes 2359300
  (27 other events, 133.4 us)
Sparse Core Ops, SparseCore 0:
  9.6 31.7 all-gather.15
  43.1 28.6 all-gather.17
  73.3 28.5 all-gather.19
  103.4 28.5 all-gather.21
  133.5 81.7 all-gather.23
  216.7 80.6 all-gather.25
  397.0 32.8 reduce-scatter.18
  432.2 34.4 reduce-scatter.20
  469.0 34.5 reduce-scatter.22
  506.3 34.2 reduce-scatter.12
  542.9 88.2 reduce-scatter.14
  633.4 87.9 reduce-scatter.16
  725.6 86.5 all-reduce.13
where the time goes:
time: 835 us; the launch traced here: 830 us
  waiting for transfers between devices  408 us (49%)
  blocking collectives  180 us (22%)
  matrix products  121 us (14%)
  local copies, waits for them, and re-layouts  59 us (7%)
  other arithmetic  25.5 us (3%)
  starting transfers between devices  19.1 us (2%)
  between operations  16.5 us (2%)
    reduce_scatter x1, waiting for transfers between devices, local(): lax.psum_scatter(grad_w_up.astype(jnp.bfloat16), 'dp', scatter_dimension=...  90.6 us
    reduce_scatter x1, waiting for transfers between devices, local(): lax.psum_scatter(grad_w_down.astype(jnp.bfloat16), 'dp', scatter_dimensio...  90.1 us
    all_gather x1, waiting for transfers between devices, local(): lax.all_gather(w_down, 'dp', axis=0, tiled=True)  59.7 us
    dot_general x6, matrix products, dot_rows(): return jnp.dot(former, latter, preferred_element_type=jnp.float32)  38.9 us
    psum x1, waiting for transfers between devices, local(): lax.psum(owned_grads[0].astype(jnp.bfloat16), 'seq').astype(jnp.float32)  38.3 us
    reduce_scatter x1, waiting for transfers between devices, local(): lax.psum_scatter(grad_w_out.astype(jnp.bfloat16), 'dp', scatter_dimension...  35.2 us
    unnamed x108, local copies, waits for them, and re-layouts  33.4 us
    dot_general x6, matrix products, dot_left(): lax.dot_general(former, latter, (((0,), (0,)), ((), ())), preferred_eleme...  30.7 us
  transfers between devices with their start and end apart: 18, of which 11 were waited for; matrix products, arithmetic and copies ran while one was open for 15% of the time, Pallas kernels for 0%

commit v1 on v0

v1 whole, which is shorter than its diff:
```python
import functools

import jax
import jax.numpy as jnp
import numpy as np
from jax import lax
from jax.experimental import pallas as pl
from jax.experimental.pallas import tpu as pltpu
from jax.sharding import PartitionSpec as P

HEAD_DIM = 64
EPSILON = 1e-12
BOTH = ("dp", "seq")
PAD = 16
F32 = jnp.float32
BF16 = jnp.bfloat16


def dot(former, latter, former_dim=1, latter_dim=0):
    return lax.dot_general(
        former,
        latter,
        (((former_dim,), (latter_dim,)), ((), ())),
        preferred_element_type=F32,
    )


def normalize(hidden, gain_vec, offset):
    center = hidden - jnp.mean(hidden, -1, keepdims=True)
    spread = jnp.mean(center * center, -1, keepdims=True)
    root = lax.rsqrt(spread + EPSILON)
    unit = center * root
    return unit * gain_vec + offset, unit, root


def normalize_back(unit, root, gain_vec, upstream):
    scaled = upstream * gain_vec
    first = jnp.mean(scaled, -1, keepdims=True)
    second = jnp.mean(scaled * unit, -1, keepdims=True)
    return (
        root * (scaled - first - unit * second),
        jnp.sum(upstream * unit, 0),
        jnp.sum(upstream, 0),
    )


class Plan:
    def __init__(self, n_dp, n_seq):
        self.n_dp, self.n_seq, self.n_z = n_dp, n_seq, n_dp // 2
        self.bits = n_seq.bit_length() - 1
        order = [0] + list(range(1, self.n_z, 2))
        order += list(range(2, self.n_z, 2))[::-1]
        self.order = order
        self.place = [order.index(z) for z in range(self.n_z)]
        self.core = self.pairs(lambda z, c, s: (z, 1 - c, s))
        self.ring = self.pairs(lambda z, c, s: (self.behind(z, -1), c, s))
        self.stage = [
            self.pairs(lambda z, c, s, k=k: (z, c, s ^ self.mask(c, 1 << k)))
            for k in range(self.bits)
        ]
        rows = []
        for dp in range(n_dp):
            for s in range(n_seq):
                z, c = dp // 2, dp % 2
                rows.append(
                    [self.behind(z, j) for j in range(self.n_z)]
                    + [s ^ self.mask(c, r) for r in range(n_seq)]
                    + [c, 1 - c]
                    + [s ^ self.mask(1 - c, r) for r in range(n_seq)]
                )
        self.table = np.asarray(rows, np.int32)

    def behind(self, z, j):
        return self.order[(self.place[z] - j) % self.n_z]

    def mask(self, c, r):
        out = 0
        for k in range(self.bits):
            if r >> k & 1:
                out |= 1 << ((k + c) % self.bits)
        return out

    def pairs(self, target):
        out = []
        for dp in range(self.n_dp):
            for s in range(self.n_seq):
                z, c, t = target(dp // 2, dp % 2, s)
                out.append((dp * self.n_seq + s, (2 * z + c) * self.n_seq + t))
        return out

    def row(self):
        here = lax.axis_index("dp") * self.n_seq + lax.axis_index("seq")
        return lax.dynamic_index_in_dim(jnp.asarray(self.table), here, 0, False)

    def swap(self, block):
        return lax.ppermute(block, BOTH, self.core)

    def around(self, block):
        out = [block]
        for _ in range(self.n_z - 1):
            out.append(lax.ppermute(out[-1], BOTH, self.ring))
        return out

    def gather(self, block):
        have = block[None]
        for k in range(self.bits):
            have = jnp.concatenate([have, lax.ppermute(have, BOTH, self.stage[k])], 0)
        return have

    def exchange(self, blocks):
        tail = blocks.shape[1:]
        for k in range(self.bits):
            split = blocks.reshape((-1, 2, 1 << k) + tail)
            come = lax.ppermute(split[:, 1], BOTH, self.stage[k])
            blocks = jnp.stack([split[:, 0], come], 1).reshape((-1,) + tail)
        return blocks

    def scatter(self, blocks):
        for k in reversed(range(self.bits)):
            half = 1 << k
            come = lax.ppermute(blocks[half:], BOTH, self.stage[k])
            blocks = (blocks[:half].astype(F32) + come.astype(F32)).astype(BF16)
        return blocks[0]

    def ring_scatter(self, part):
        moving = part(1 % self.n_z)
        for j in range(2, self.n_z + 1):
            come = lax.ppermute(moving, BOTH, self.ring)
            moving = (part(j % self.n_z).astype(F32) + come.astype(F32)).astype(BF16)
        return moving


def assemble(table, pieces, moves, outs):
    def kernel(table_ref, *refs):
        sources, targets, sems = refs[: len(pieces)], refs[len(pieces) : -1], refs[-1]
        copies = []
        for n, (i, src, o, at) in enumerate(moves):
            copies.append(
                pltpu.make_async_copy(
                    sources[i].at[src], targets[o].at[at(table_ref)], sems.at[n]
                )
            )
        for copy in copies:
            copy.start()
        for copy in copies:
            copy.wait()

    size = sum(int(np.prod(o.shape)) * o.dtype.itemsize for o in outs)
    return pl.pallas_call(
        kernel,
        out_shape=outs,
        in_specs=[pl.BlockSpec(memory_space=pltpu.SMEM)]
        + [pl.BlockSpec(memory_space=pl.ANY)] * len(pieces),
        out_specs=[pl.BlockSpec(memory_space=pltpu.VMEM)] * len(outs),
        scratch_shapes=[pltpu.SemaphoreType.DMA((len(moves),))],
        cost_estimate=pl.CostEstimate(
            flops=0, bytes_accessed=2 * size, transcendentals=0
        ),
    )(table, *pieces)


def at_rows(start, size):
    return pl.ds(pl.multiple_of(start, size), size)


def attend(query, key, value):
    scores = jnp.einsum("ghqd,ghkd->ghqk", query, key, preferred_element_type=F32)
    scores = scores * HEAD_DIM**-0.5
    row_max = jnp.max(scores, -1, keepdims=True)
    exponent = jnp.exp(scores - row_max)
    row_total = jnp.sum(exponent, -1, keepdims=True)
    portions = (exponent / row_total).astype(BF16)
    context = jnp.einsum("ghqk,ghkd->ghqd", portions, value, preferred_element_type=F32)
    return context.astype(BF16), row_max + jnp.log(row_total)


def attend_back(query, key, value, log_total, upstream):
    factor = HEAD_DIM**-0.5
    scores = jnp.einsum("ghqd,ghkd->ghqk", query, key, preferred_element_type=F32)
    portions = jnp.exp(scores * factor - log_total)
    low = portions.astype(BF16)
    grad_value = jnp.einsum("ghqk,ghqd->ghkd", low, upstream, preferred_element_type=F32)
    grad = jnp.einsum("ghqd,ghkd->ghqk", upstream, value, preferred_element_type=F32)
    grad = portions * (grad - jnp.sum(portions * grad, -1, keepdims=True))
    grad = grad.astype(BF16)
    grad_query = jnp.einsum("ghqk,ghkd->ghqd", grad, key, preferred_element_type=F32)
    grad_key = jnp.einsum("ghqk,ghqd->ghkd", grad, query, preferred_element_type=F32)
    return (
        (grad_query * factor).astype(BF16),
        (grad_key * factor).astype(BF16),
        grad_value.astype(BF16),
    )


def local(
    plan,
    inputs,
    w_query,
    w_key,
    w_value,
    b_query,
    b_value,
    w_out,
    b_out,
    gain_one,
    shift_one,
    w_up,
    b_up,
    w_down,
    b_down,
    gain_two,
    shift_two,
    cotangent,
):
    n_dp, n_seq, n_z = plan.n_dp, plan.n_seq, plan.n_z
    seqs, length, width = inputs.shape
    tokens = seqs * length
    own_rows, hidden = w_up.shape
    own_hidden = w_down.shape[0]
    half = hidden // 2
    cols = width // n_seq
    quarter = half // n_seq
    heads = cols // HEAD_DIM
    table = plan.row()
    behind = [table[j] for j in range(n_z)]
    member = [table[n_z + r] for r in range(n_seq)]
    core, other = table[n_z + n_seq], table[n_z + n_seq + 1]
    seq = member[0]
    BEHIND, MEMBER, CORE = 0, n_z, n_z + n_seq
    MEMBERS = (MEMBER, CORE + 2)

    all_inputs = plan.gather(inputs).reshape(n_seq * tokens, width)

    def own_cols(w):
        return lax.dynamic_slice_in_dim(w, seq * cols, cols, 1)

    vectors = jnp.concatenate(
        [b_query, b_value, b_out, gain_one, shift_one, b_down, gain_two, shift_two, b_up]
    )
    vec_rows = -(-vectors.shape[0] // (3 * cols))
    vectors = jnp.pad(vectors, (0, PAD * 3 * cols - vectors.shape[0]))
    first = jnp.concatenate(
        [
            jnp.concatenate([own_cols(w_query), own_cols(w_key), own_cols(w_value)], 1),
            vectors.reshape(PAD, 3 * cols),
        ],
        0,
    )
    mine = jnp.stack(plan.around(first))
    theirs = plan.swap(mine)
    moves = []
    for i in range(2):
        for j in range(n_z):
            moves.append(
                (
                    i,
                    (j, pl.ds(0, own_rows)),
                    0,
                    lambda t, i=i, j=j: (
                        at_rows((t[BEHIND + j] * 2 + t[CORE + i]) * own_rows, own_rows),
                    ),
                )
            )
            moves.append(
                (
                    i,
                    (j, pl.ds(own_rows, PAD)),
                    1,
                    lambda t, i=i, j=j: (
                        at_rows((t[BEHIND + j] * 2 + t[CORE + i]) * PAD, PAD),
                    ),
                )
            )
    w_qkv, vec = assemble(
        table,
        [mine, theirs],
        moves,
        [
            jax.ShapeDtypeStruct((width, 3 * cols), BF16),
            jax.ShapeDtypeStruct((n_dp * PAD, 3 * cols), BF16),
        ],
    )
    vec = vec.reshape(n_dp, PAD, 3 * cols)[:, :vec_rows].reshape(n_dp, -1)
    vec = vec.astype(F32)
    narrow = vec[:, : 8 * own_rows].reshape(n_dp, 8, own_rows)
    narrow = narrow.transpose(1, 0, 2).reshape(8, width)
    full_bq, full_bv, full_bo, full_g1, full_s1, full_bd, full_g2, full_s2 = narrow
    full_bu = vec[:, 8 * own_rows : 8 * own_rows + own_hidden].reshape(n_z, 2, own_hidden)
    half_bu = lax.dynamic_index_in_dim(full_bu, core, 1, False).reshape(half)

    def halves(w):
        parts = w.reshape(own_rows, n_z, 2, own_hidden)
        return [
            lax.dynamic_index_in_dim(parts, c, 2, False).reshape(own_rows, half)
            for c in (core, other)
        ]

    up_mine, up_theirs = halves(w_up)
    across = plan.swap(jnp.concatenate([up_theirs, w_out], 1))
    up_come, out_come = across[:, :half], across[:, half:]
    up_quarter = jnp.concatenate(
        [
            lax.dynamic_slice_in_dim(up_mine, seq * quarter, quarter, 1),
            lax.dynamic_slice_in_dim(up_come, seq * quarter, quarter, 1),
        ],
        0,
    )
    out_cols = own_cols(w_out)
    fold = own_rows // 2
    out_fold = jnp.concatenate([out_cols[:fold], out_cols[fold:]], 1)
    up_ring = plan.around(jnp.concatenate([up_quarter, out_fold], 0))
    up_all = plan.gather(jnp.stack(up_ring[1:]))
    out_all = plan.swap(up_all[:, :, 2 * own_rows :])
    pieces = [up_mine, up_come, up_all]
    moves = []
    whole = pl.ds(0, own_rows)
    for k in range(2):
        moves.append(
            (
                k,
                (whole,),
                0,
                lambda t, k=k: (
                    at_rows((t[BEHIND] * 2 + t[CORE + k]) * own_rows, own_rows),
                ),
            )
        )
        for j in range(1, n_z):
            for r in range(n_seq):
                moves.append(
                    (
                        2,
                        (r, j - 1, pl.ds(k * own_rows, own_rows)),
                        0,
                        lambda t, k=k, j=j, r=r: (
                            at_rows((t[BEHIND + j] * 2 + t[CORE + k]) * own_rows, own_rows),
                            at_rows(t[MEMBER + r] * quarter, quarter),
                        ),
                    )
                )
    (half_up,) = assemble(table, pieces, moves, [jax.ShapeDtypeStruct((width, half), BF16)])
    pieces = [w_out, out_come, up_all, out_all]
    moves = []
    for k in range(2):
        moves.append(
            (
                k,
                (whole,),
                0,
                lambda t, k=k: (
                    at_rows((t[BEHIND] * 2 + t[CORE + k]) * own_rows, own_rows),
                ),
            )
        )
        for j in range(1, n_z):
            for r in range(n_seq):
                for f in range(2):
                    moves.append(
                        (
                            2 + k,
                            (
                                r,
                                j - 1,
                                pl.ds(2 * own_rows * (1 - k), fold),
                                pl.ds(f * cols, cols),
                            ),
                            0,
                            lambda t, k=k, j=j, r=r, f=f: (
                                at_rows(
                                    (t[BEHIND + j] * 2 + t[CORE + k]) * own_rows + f * fold,
                                    fold,
                                ),
                                at_rows(t[MEMBERS[k] + r] * cols, cols),
                            ),
                        )
                    )
    (full_out,) = assemble(table, pieces, moves, [jax.ShapeDtypeStruct((width, width), BF16)])

    slab = own_hidden // n_seq
    down_ring = plan.around(lax.dynamic_slice_in_dim(w_down, seq * slab, slab, 0))
    down_all = plan.gather(jnp.stack(down_ring[1:]))
    moves = [(0, (pl.ds(0, own_hidden),), 0, lambda t: (at_rows(t[BEHIND] * own_hidden, own_hidden),))]
    for j in range(1, n_z):
        for r in range(n_seq):
            moves.append(
                (
                    1,
                    (r, j - 1),
                    0,
                    lambda t, j=j, r=r: (
                        at_rows(t[BEHIND + j] * own_hidden + t[MEMBER + r] * slab, slab),
                    ),
                )
            )
    (half_down,) = assemble(
        table, [w_down, down_all], moves, [jax.ShapeDtypeStruct((half, width), BF16)]
    )

    own_bias = jnp.concatenate(
        [
            lax.dynamic_slice_in_dim(full_bq, seq * cols, cols),
            jnp.zeros((cols,), F32),
            lax.dynamic_slice_in_dim(full_bv, seq * cols, cols),
        ]
    )
    qkv = (dot(all_inputs, w_qkv) + own_bias).astype(BF16)
    qkv = qkv.reshape(n_seq, seqs, length, 3, heads, HEAD_DIM).transpose(3, 1, 4, 0, 2, 5)
    qkv = qkv.reshape(3, seqs, heads, n_seq * length, HEAD_DIM)
    query, key, value = qkv[0], qkv[1], qkv[2]

    def to_rows(v):
        v = v.reshape(seqs, heads, n_seq, length, HEAD_DIM)
        return v.transpose(2, 0, 3, 1, 4).reshape(n_seq, tokens, cols)

    def to_heads(v):
        v = v.reshape(n_seq, seqs, length, heads, HEAD_DIM).transpose(1, 3, 0, 2, 4)
        return v.reshape(seqs, heads, n_seq * length, HEAD_DIM)

    head_context, log_total = attend(query, key, value)
    come = plan.exchange(to_rows(head_context))
    moves = [
        (0, (r,), 0, lambda t, r=r: (pl.ds(0, tokens), at_rows(t[MEMBER + r] * cols, cols)))
        for r in range(n_seq)
    ]
    (context,) = assemble(table, [come], moves, [jax.ShapeDtypeStruct((tokens, width), BF16)])

    flat = inputs.reshape(tokens, width).astype(F32)
    first_sum = flat + (dot(context, full_out) + full_bo)
    normed, unit_one, root_one = normalize(first_sum, full_g1, full_s1)
    normed_low = normed.astype(BF16)
    both_low = jnp.concatenate([normed_low, plan.swap(normed_low)], 0)

    pre_active = dot(both_low, half_up) + half_bu
    phi = jnp.exp(-0.5 * pre_active * pre_active) * (1.0 / np.sqrt(2.0 * np.pi))
    big_phi = 0.5 * (1.0 + lax.erf(pre_active * np.float32(np.sqrt(0.5))))
    active = (pre_active * big_phi).astype(BF16)
    slope = (big_phi + pre_active * phi).astype(BF16)

    def join(partial):
        return partial[:tokens] + plan.swap(partial[tokens:].astype(BF16)).astype(F32)

    second_sum = normed + (join(dot(active, half_down)) + full_bd)
    result, unit_two, root_two = normalize(second_sum, full_g2, full_s2)
    output = result.astype(BF16).reshape(inputs.shape)

    upstream = cotangent.reshape(tokens, width).astype(F32)
    grad_second, grad_g2, grad_s2 = normalize_back(unit_two, root_two, full_g2, upstream)
    branch_two = grad_second.astype(BF16)
    grad_bd = jnp.sum(branch_two.astype(F32), 0)
    both_two = jnp.concatenate([branch_two, plan.swap(branch_two)], 0)
    grad_pre = (dot(both_two, half_down, 1, 1) * slope.astype(F32)).astype(BF16)

    def pick(array, ids, axis):
        return jnp.stack([lax.dynamic_index_in_dim(array, i, axis, False) for i in ids])

    grad_down = dot(active, both_two, 0, 0).astype(BF16)
    grad_down = pick(grad_down.reshape(n_z, n_seq, slab, width), member, 1)
    grad_up = dot(both_low, grad_pre, 0, 0).astype(BF16)
    grad_up = pick(grad_up.reshape(n_z, 2 * own_rows, n_seq, quarter), member, 2)
    grad_down = plan.scatter(grad_down)
    grad_up = plan.scatter(grad_up)
    grad_bu = jnp.sum(grad_pre.astype(F32), 0)

    grad_normed = grad_second + join(dot(grad_pre, half_up, 1, 1))
    grad_first, grad_g1, grad_s1 = normalize_back(unit_one, root_one, full_g1, grad_normed)
    branch_one = grad_first.astype(BF16)
    grad_bo = jnp.sum(branch_one.astype(F32), 0)
    grad_context = dot(branch_one, full_out, 1, 1).astype(BF16)
    head_grad = to_heads(plan.exchange(pick(grad_context.reshape(tokens, n_seq, cols), member, 1)))

    grad_out = dot(context, branch_one, 0, 0).astype(BF16).reshape(n_z, 2, own_rows, width)
    keep = lax.dynamic_index_in_dim(grad_out, core, 1, False)
    come = plan.swap(lax.dynamic_index_in_dim(grad_out, other, 1, False))
    grad_out = (keep.astype(F32) + come.astype(F32)).astype(BF16)
    grad_out = plan.scatter(pick(grad_out.reshape(n_z, own_rows, n_seq, cols), member, 2))
    grad_out = jnp.concatenate([grad_out[:, :fold], grad_out[:, fold:]], 2)

    def rows_of(array):
        return lambda j: lax.dynamic_index_in_dim(array, behind[j], 0, False)

    grad_down = plan.ring_scatter(rows_of(grad_down))
    grad_down = plan.gather(grad_down)
    moves = [
        (0, (r,), 0, lambda t, r=r: (at_rows(t[MEMBER + r] * slab, slab),)) for r in range(n_seq)
    ]
    (grad_down,) = assemble(
        table, [grad_down], moves, [jax.ShapeDtypeStruct((own_hidden, width), BF16)]
    )
    grad_up = plan.ring_scatter(rows_of(jnp.concatenate([grad_up, grad_out], 1)))
    grad_out, grad_up = grad_up[2 * own_rows :], grad_up[: 2 * own_rows]
    grad_up = grad_up.reshape(2, own_rows, quarter)
    come = plan.swap(lax.dynamic_index_in_dim(grad_up, other, 0, False))
    keep = lax.dynamic_index_in_dim(grad_up, core, 0, False)
    grad_up = plan.gather(jnp.concatenate([keep, come, grad_out], 0))
    moves = []
    for r in range(n_seq):
        for k in range(2):
            for part in range(max(1, quarter // own_hidden)):
                moves.append(
                    (
                        0,
                        (r, pl.ds(k * own_rows, own_rows), pl.ds(part * own_hidden, own_hidden)),
                        0,
                        lambda t, r=r, k=k, part=part: (
                            pl.ds(0, own_rows),
                            at_rows(
                                (
                                    (t[MEMBER + r] * (quarter // own_hidden) + part) * 2
                                    + t[CORE + k]
                                )
                                * own_hidden,
                                own_hidden,
                            ),
                        ),
                    )
                )
        for f in range(2):
            moves.append(
                (
                    0,
                    (r, pl.ds(2 * own_rows, fold), pl.ds(f * cols, cols)),
                    1,
                    lambda t, r=r, f=f: (
                        pl.ds(f * fold, fold),
                        at_rows(t[MEMBER + r] * cols, cols),
                    ),
                )
            )
    grad_up, grad_out = assemble(
        table,
        [grad_up],
        moves,
        [
            jax.ShapeDtypeStruct((own_rows, hidden), BF16),
            jax.ShapeDtypeStruct((own_rows, width), BF16),
        ],
    )

    grads = attend_back(query, key, value, log_total, head_grad)
    grad_qkv = jnp.concatenate([to_rows(g) for g in grads], 2).reshape(n_seq * tokens, 3 * cols)
    partial = dot(grad_qkv, w_qkv, 1, 1).astype(BF16).reshape(n_seq, tokens, width)
    grad_inputs = grad_first + plan.scatter(partial).astype(F32)
    grad_w = dot(all_inputs, grad_qkv, 0, 0).astype(BF16)
    grad_b = jnp.sum(grad_qkv.astype(F32), 0)

    def widen(v):
        return lax.dynamic_update_slice_in_dim(jnp.zeros((width,), F32), v, seq * cols, 0)

    narrow = jnp.stack(
        [widen(grad_b[:cols]), widen(grad_b[2 * cols :]), grad_bo, grad_g1, grad_s1]
        + [grad_bd, grad_g2, grad_s2]
    )
    narrow = narrow.reshape(8, n_dp, own_rows).transpose(1, 0, 2).reshape(n_dp, 8 * own_rows)
    wide = jnp.zeros((n_z, 2, own_hidden), F32)
    wide = lax.dynamic_update_slice_in_dim(wide, grad_bu.reshape(n_z, 1, own_hidden), core, 1)
    vec = jnp.concatenate([narrow, wide.reshape(n_dp, own_hidden)], 1).astype(BF16)
    vec = jnp.pad(vec, ((0, 0), (0, PAD * 3 * cols - vec.shape[1])))
    last = jnp.concatenate(
        [
            grad_w.reshape(n_dp, own_rows, 3 * cols),
            vec.reshape(n_dp, PAD, 3 * cols),
        ],
        1,
    ).reshape(n_z, 2, own_rows + PAD, 3 * cols)
    come = plan.swap(lax.dynamic_index_in_dim(last, other, 1, False))
    keep = lax.dynamic_index_in_dim(last, core, 1, False)
    last = (keep.astype(F32) + come.astype(F32)).astype(BF16)
    last = plan.gather(plan.ring_scatter(rows_of(last)))
    moves = []
    for r in range(n_seq):
        for m in range(3):
            moves.append(
                (
                    0,
                    (r, pl.ds(0, own_rows), pl.ds(m * cols, cols)),
                    m,
                    lambda t, r=r: (pl.ds(0, own_rows), at_rows(t[MEMBER + r] * cols, cols)),
                )
            )
    grad_wq, grad_wk, grad_wv = assemble(
        table, [last], moves, [jax.ShapeDtypeStruct((own_rows, width), BF16)] * 3
    )
    vec = jnp.sum(last[:, own_rows : own_rows + vec_rows].astype(F32), 0).reshape(-1)
    small = vec[: 8 * own_rows].reshape(8, own_rows)
    return (
        output,
        grad_inputs.reshape(inputs.shape),
        grad_wq.astype(F32),
        grad_wk.astype(F32),
        grad_wv.astype(F32),
        small[0],
        small[1],
        grad_out.astype(F32),
        small[2],
        small[3],
        small[4],
        grad_up.astype(F32),
        vec[8 * own_rows : 8 * own_rows + own_hidden],
        grad_down.astype(F32),
        small[5],
        small[6],
        small[7],
    )


def solution(mesh):
    plan = Plan(mesh.shape["dp"], mesh.shape["seq"])
    rows, vector, token = P("dp", None), P("dp"), P("dp", "seq", None)
    weights = (rows,) * 3 + (vector,) * 2 + (rows,) + (vector,) * 3
    weights += (rows, vector, rows) + (vector,) * 3
    return jax.shard_map(
        functools.partial(local, plan),
        mesh=mesh,
        in_specs=(token,) + weights + (token,),
        out_specs=(token, token) + weights,
        check_vma=False,
    )
```

time: 835 us -> 566 us (0.68)
  waiting for transfers between devices: 408 us -> 161 us
  blocking collectives: 180 us -> 0 us
  other arithmetic: 25.5 us -> 90.5 us
  local copies, waits for them, and re-layouts: 59 us -> 124 us
  matrix products: 121 us -> 83.7 us
  Pallas kernels: 0 us -> 29.3 us
  starting transfers between devices: 19.1 us -> 43.4 us
    reduce_scatter x3 -> x0, waiting for transfers between devices: 216 us -> none  [the longest x1 90.6 us: local(): lax.psum_scatter(grad_w_up.astype(jnp.bfloat16), 'dp', scatter_dimension=...]
    ppermute x0 -> x52, waiting for transfers between devices: none -> 161 us  [the longest x9 45 us: ring_scatter(): come = lax.ppermute(moving, BOTH, self.ring)]
    all_gather x6 -> x0, waiting for transfers between devices: 111 us -> none  [the longest x1 59.7 us: local(): lax.all_gather(w_down, 'dp', axis=0, tiled=True)]
    all_gather x9 -> x0, blocking collectives: 96.8 us -> none  [the longest x1 13.5 us: local(): lax.all_gather(b_value, 'dp', axis=0, tiled=True)]
    all_to_all x3 -> x0, blocking collectives: 47 us -> none  [the longest x1 17.6 us: local(): lax.all_to_all(grad_hq, 'seq', split_axis=1, concat_axis=2, tiled=True)]
    ppermute x0 -> x52, starting transfers between devices: none -> 43.4 us  [the longest x12 13.8 us: gather(): have = jnp.concatenate([have, lax.ppermute(have, BOTH, self.stage[k])], 0)]
    psum x1 -> x0, waiting for transfers between devices: 38.3 us -> none  [local(): lax.psum(owned_grads[0].astype(jnp.bfloat16), 'seq').astype(jnp.float32)]
    dot_general x24 -> x18, matrix products: 121 us -> 83.7 us  [the longest x12 53.5 us: dot(): lax.dot_general(former, latter, (((former_dim,), (latter_dim,)), ((), ())...]
  transfers between devices with their start and end apart: 18 -> 52, of which waited for: 11 -> 22; matrix products, arithmetic and copies ran while one was open for 15% -> 43% of each run, Pallas kernels for 0% -> 5%
where the time goes in v1:
time: 566 us; the launch traced here: 555 us
  waiting for transfers between devices  161 us (28%)
  local copies, waits for them, and re-layouts  124 us (22%)
  other arithmetic  90.5 us (16%)
  matrix products  83.7 us (15%)
  starting transfers between devices  43.4 us (8%)
  Pallas kernels  29.3 us (5%)
  between operations  23.9 us (4%)
    dot_general x12, matrix products, dot(): lax.dot_general(former, latter, (((former_dim,), (latter_dim,)), ((), ())...  53.5 us
    ppermute x9, waiting for transfers between devices, ring_scatter(): come = lax.ppermute(moving, BOTH, self.ring)  45 us
    ppermute x9, waiting for transfers between devices, around(): out.append(lax.ppermute(out[-1], BOTH, self.ring))  40.1 us
    ppermute x12, waiting for transfers between devices, gather(): have = jnp.concatenate([have, lax.ppermute(have, BOTH, self.stage[k])], 0)  35 us
    pallas_call x8, Pallas kernels, assemble(): pl.pallas_call(kernel, out_shape=outs, in_specs=[pl.BlockSpec(memory_spac...  29.3 us
    unnamed x127, local copies, waits for them, and re-layouts  27.6 us
    ppermute x4, waiting for transfers between devices, exchange(): come = lax.ppermute(split[:, 1], BOTH, self.stage[k])  23.6 us
    concatenate x12, other arithmetic, gather(): have = jnp.concatenate([have, lax.ppermute(have, BOTH, self.stage[k])], 0)  21.8 us
  transfers between devices with their start and end apart: 52, of which 22 were waited for; matrix products, arithmetic and copies ran while one was open for 43% of the time, Pallas kernels for 5%

profile of v1, /device:TPU:0, one launch (start us, length us, event | category | flops | bytes accessed | tf_op | source)
XLA Modules:
  0.0 555.3 jit_solution(3835051411941860060)
XLA Ops:
  20.5 6.5 %dynamic-slice_reduce_fusion.1 = (bf16[128,4,512]{2,1,0:T(4,128)(2,1)S(1)}, bf16[128,4,512]{2,1,0:T(4,128)(2,1)S(1)}) fusion(bf16[128,4,2,512]{3,2,1,0:T(2,128)(2,1)S(1)} %reshape.361, s32[]{:T(128)S(6)} %select_n.93, s32[]{:T(128)S(6)} %select_n.94), kind=kLoop, calls=%fused_computation.107 | loop fusion | bytes 2097160 | tf_op jit(solution)/shard_map/jit(dynamic_index_in_dim)/dynamic_slice | solution.py:294
  38.8 6.2 %collective-permute-done.4 = bf16[144,768]{1,0:T(8,128)(2,1)S(1)} collective-permute-done((bf16[144,768]{1,0:T(8,128)(2,1)S(1)}, bf16[144,768]{1,0:T(8,128)(2,1)S(1)}, u32[]{:S(2)}, u32[]{:S(2)}) %collective-permute-start.4) | collective-permute-done | bytes 221216 | tf_op jit(solution)/shard_map/ppermute | solution.py:101
  59.8 5.6 %collective-permute-done.16 = bf16[128,1024]{1,0:T(8,128)(2,1)S(1)} collective-permute-done((bf16[128,1024]{1,0:T(8,128)(2,1)S(1)}, bf16[128,1024]{1,0:T(8,128)(2,1)S(1)}, u32[]{:S(2)}, u32[]{:S(2)}) %collective-permute-start.16) | collective-permute-done | bytes 262176 | tf_op jit(solution)/shard_map/ppermute | solution.py:101
  65.5 12.1 %collective-permute-done.17 = bf16[128,1024]{1,0:T(8,128)(2,1)} collective-permute-done((bf16[128,1024]{1,0:T(8,128)(2,1)S(1)}, bf16[128,1024]{1,0:T(8,128)(2,1)}, u32[]{:S(2)}, u32[]{:S(2)}) %collective-permute-start.17) | collective-permute-done | bytes 262176 | tf_op jit(solution)/shard_map/ppermute | solution.py:101
  85.3 8.2 %collective-permute-done.11 = bf16[320,512]{1,0:T(8,128)(2,1)} collective-permute-done((bf16[320,512]{1,0:T(8,128)(2,1)S(1)}, bf16[320,512]{1,0:T(8,128)(2,1)}, u32[]{:S(2)}, u32[]{:S(2)}) %collective-permute-start.11) | collective-permute-done | bytes 327712 | tf_op jit(solution)/shard_map/ppermute | solution.py:101
  106.2 4.9 reshape.358
  115.8 6.4 %multiply_reduce_fusion.1 = (f32[3,4,512]{2,1,0:T(4,128)S(1)}, f32[3,4,512,512]{2,3,1,0:T(8,128)}) fusion(bf16[3,4,512,64]{2,3,1,0:T(8,128)(2,1)S(1)} %squeeze.136, bf16[3,4,512,64]{2,3,1,0:T(8,128)(2,1)S(1)} %squeeze.137), kind=kOutput, calls=%fused_computation.6 | convolution fusion | flops 408938496 | bytes 14180352 | tf_op jit(solution)/shard_map/ghqd,ghkd->ghqk/dot_general | solution.py:167
  123.0 7.0 %fusion = f32[3,4,512]{2,1,0:T(4,128)S(1)} fusion(f32[3,4,512,512]{2,3,1,0:T(8,128)} %get-tuple-element.117, f32[3,4,512]{2,1,0:T(4,128)S(1)} %get-tuple-element.116), kind=kLoop, calls=%fused_computation.5 | loop fusion | flops 9431040 | bytes 12632064 | tf_op jit(solution)/shard_map/reduce_sum | solution.py:171
  142.9 28.1 %collective-permute-done.13 = bf16[2,3,320,512]{3,2,1,0:T(8,128)(2,1)} collective-permute-done((bf16[2,3,320,512]{3,2,1,0:T(8,128)(2,1)}, bf16[2,3,320,512]{3,2,1,0:T(8,128)(2,1)}, u32[]{:S(2)}, u32[]{:S(2)}) %collective-permute-start.13) | collective-permute-done | bytes 1966112 | tf_op jit(solution)/shard_map/ppermute | solution.py:107
  196.2 4.9 collective-permute-done.20
  204.5 5.0 shard_map.309
  209.5 5.0 shard_map.308
  214.5 7.8 %multiply_convert_fusion.2 = (bf16[768,2048]{1,0:T(8,128)(2,1)S(1)}, f32[768,2048]{1,0:T(8,128)}) fusion(f32[2048]{0:T(1024)S(1)} %bitcast.390, bf16[1024,2048]{1,0:T(8,128)(2,1)} %shard_map.308, bf16[384,1024]{1,0:T(8,128)(2,1)} %collective-permute-done.15, bf16[384,1024]{1,0:T(8,128)(2,1)} %fusion.29), kind=kOutput, calls=%fused_computation.18 | convolution fusion | flops 3233808384 | bytes 15212544 | tf_op jit(solution)/shard_map/dot_general | solution.py:20
  248.3 8.9 %convert_reduce_fusion = (f32[2048]{0:T(1024)S(1)}, bf16[768,2048]{1,0:T(8,128)(2,1)S(1)}) fusion(f32[768,2048]{1,0:T(8,128)} %get-tuple-element.121, f32[2048]{0:T(1024)S(1)} %bitcast.391, bf16[2048,1024]{1,0:T(8,128)(2,1)} %shard_map.309, bf16[384,1024]{1,0:T(8,128)(2,1)} %collective-permute-done.22, bf16[384,1024]{1,0:T(8,128)(2,1)} %get-tuple-element.40), kind=kOutput, calls=%fused_computation.15 | convolution fusion | flops 3247962112 | bytes 15220736 | tf_op jit(solution)/shard_map/dot_general | solution.py:20
  257.2 5.1 fusion.77
  265.2 5.8 %convolution_convert_fusion.1 = bf16[2048,1024]{1,0:T(8,128)(2,1)S(1)} fusion(bf16[768,2048]{1,0:T(8,128)(2,1)} %copy-done.41, bf16[384,1024]{1,0:T(8,128)(2,1)} %collective-permute-done.22, bf16[384,1024]{1,0:T(8,128)(2,1)} %get-tuple-element.40), kind=kOutput, calls=%fused_computation.28 | convolution fusion | flops 3226468352 | bytes 8912896 | tf_op jit(solution)/shard_map/dot_general | solution.py:20
  275.5 6.9 %convolution_convert_fusion.2 = bf16[1024,2048]{1,0:T(8,128)(2,1)} fusion(bf16[768,2048]{1,0:T(8,128)(2,1)S(1)} %copy-done.43, bf16[384,1024]{1,0:T(8,128)(2,1)} %collective-permute-done.15, bf16[384,1024]{1,0:T(8,128)(2,1)} %fusion.29), kind=kOutput, calls=%fused_computation.29 | convolution fusion | flops 3226468352 | bytes 8912896 | tf_op jit(solution)/shard_map/dot_general | solution.py:20
  282.4 7.8 %reshape.377 = bf16[4,256,4,512]{3,2,1,0:T(4,128)(2,1)} reshape(bf16[1024,2048]{1,0:T(8,128)(2,1)} %convolution_convert_fusion.2) | data formatting | bytes 8388608 | tf_op jit(solution)/shard_map/reshape | solution.py:459
  290.2 4.3 multiply_reduce_fusion.2
  301.6 8.9 %constant_dynamic-slice_fusion.10 = (bf16[4,256,1,512]{3,2,1,0:T(2,128)(2,1)S(1)}, bf16[4,256,1,512]{3,2,1,0:T(2,128)(2,1)S(1)}, bf16[4,256,1,512]{3,2,1,0:T(2,128)(2,1)S(1)}, bf16[4,256,1,512]{3,2,1,0:T(2,128)(2,1)S(1)}) fusion(bf16[4,256,4,512]{3,2,1,0:T(4,128)(2,1)S(1)} %copy-done.4, s32[]{:T(128)S(6)} %select_n.97, s32[]{:T(128)S(6)} %select_n.99, ...), kind=kLoop, calls=%fused_computation.199 | loop fusion | bytes 8388624 | tf_op jit(solution)/shard_map/jit(dynamic_index_in_dim)/dynamic_slice | solution.py:454
  324.1 21.6 %collective-permute-done.25 = bf16[1,2,384,256]{3,2,1,0:T(8,128)(2,1)} collective-permute-done((bf16[1,2,384,256]{3,2,1,0:T(8,128)(2,1)}, bf16[1,2,384,256]{3,2,1,0:T(8,128)(2,1)}, u32[]{:S(2)}, u32[]{:S(2)}) %collective-permute-start.25) | collective-permute-done | bytes 393248 | tf_op jit(solution)/shard_map/ppermute | solution.py:114
  353.7 7.0 %fusion.25 = bf16[3,4,512,64]{2,3,1,0:T(8,128)(2,1)S(1)} fusion(bf16[3,4,512,64]{2,3,1,0:T(8,128)(2,1)S(1)} %reshape.368, f32[3,4,512,512]{2,3,1,0:T(8,128)} %get-tuple-element.117, f32[3,4,512]{2,1,0:T(4,128)S(1)} %log_add_fusion), kind=kOutput, calls=%fused_computation.84 | convolution fusion | flops 412483584 | bytes 14180352 | tf_op jit(solution)/shard_map/ghqk,ghqd->ghkd/dot_general | solution.py:182
  360.7 9.1 %multiply_reduce_fusion = (f32[3,4,512]{2,1,0:T(4,128)S(1)}, f32[3,4,512,512]{2,3,1,0:T(8,128)}) fusion(f32[3,4,512,512]{2,3,1,0:T(8,128)} %get-tuple-element.117, f32[3,4,512]{2,1,0:T(4,128)S(1)} %log_add_fusion, bf16[3,4,512,64]{2,3,1,0:T(8,128)(2,1)S(1)} %reshape.368, bf16[3,4,512,64]{2,3,1,0:T(8,128)(2,1)S(1)} %copy-done.18), kind=kOutput, calls=%fused_computation.1 | convolution fusion | flops 415229952 | bytes 26787840 | tf_op jit(solution)/shard_map/ghqd,ghkd->ghqk/dot_general | solution.py:183
  369.8 7.0 %multiply_convert_fusion = bf16[3,4,512,512]{2,3,1,0:T(8,128)(2,1)S(1)} fusion(f32[3,4,512,512]{2,3,1,0:T(8,128)} %get-tuple-element.123, f32[3,4,512,512]{2,3,1,0:T(8,128)S(1)} %bitcast.334, f32[3,4,512]{2,1,0:T(4,128)S(1)} %get-tuple-element.122, f32[3,4,512]{2,1,0:T(4,128)S(1)} %log_add_fusion), kind=kLoop, calls=%fused_computation | loop fusion | flops 15728640 | bytes 31506432 | tf_op jit(solution)/shard_map/convert_element_type | solution.py:185
  405.8 4.4 convolution_convert_fusion
  444.6 14.4 %collective-permute-done.38 = bf16[1,4,128,256]{3,2,1,0:T(8,128)(2,1)S(1)} collective-permute-done((bf16[1,4,128,256]{3,2,1,0:T(8,128)(2,1)S(1)}, bf16[1,4,128,256]{3,2,1,0:T(8,128)(2,1)S(1)}, u32[]{:S(2)}, u32[]{:S(2)}) %collective-permute-start.38) | collective-permute-done | bytes 262176 | tf_op jit(solution)/shard_map/ppermute | solution.py:121
  459.3 9.0 %collective-permute-done.31 = bf16[144,768]{1,0:T(8,128)(2,1)S(1)} collective-permute-done((bf16[144,768]{1,0:T(8,128)(2,1)S(1)}, bf16[144,768]{1,0:T(8,128)(2,1)S(1)}, u32[]{:S(2)}, u32[]{:S(2)}) %collective-permute-start.31) | collective-permute-done | bytes 221216 | tf_op jit(solution)/shard_map/ppermute | solution.py:128
  474.3 7.9 %collective-permute-done.39 = bf16[320,512]{1,0:T(8,128)(2,1)S(1)} collective-permute-done((bf16[320,512]{1,0:T(8,128)(2,1)S(1)}, bf16[320,512]{1,0:T(8,128)(2,1)S(1)}, u32[]{:S(2)}, u32[]{:S(2)}) %collective-permute-start.39) | collective-permute-done | bytes 327712 | tf_op jit(solution)/shard_map/ppermute | solution.py:128
  489.1 5.8 %collective-permute-done.40 = bf16[320,512]{1,0:T(8,128)(2,1)S(1)} collective-permute-done((bf16[320,512]{1,0:T(8,128)(2,1)S(1)}, bf16[320,512]{1,0:T(8,128)(2,1)S(1)}, u32[]{:S(2)}, u32[]{:S(2)}) %collective-permute-start.40) | collective-permute-done | bytes 327712 | tf_op jit(solution)/shard_map/ppermute | solution.py:128
  496.1 4.4 collective-permute-done.48
  500.6 6.9 %collective-permute-done.41 = bf16[320,512]{1,0:T(8,128)(2,1)S(1)} collective-permute-done((bf16[320,512]{1,0:T(8,128)(2,1)S(1)}, bf16[320,512]{1,0:T(8,128)(2,1)S(1)}, u32[]{:S(2)}, u32[]{:S(2)}) %collective-permute-start.41) | collective-permute-done | bytes 327712 | tf_op jit(solution)/shard_map/ppermute | solution.py:128
  507.7 5.2 collective-permute-done.49
  (399 shorter events, 273.2 us)
Async XLA Ops:
  11.7 16.5 %collective-permute-start.2 = (bf16[144,768]{1,0:T(8,128)(2,1)S(1)}, bf16[144,768]{1,0:T(8,128)(2,1)}, u32[]{:S(2)}, u32[]{:S(2)}) collective-permute-start(bf16[144,768]{1,0:T(8,128)(2,1)S(1)} %get-tuple-element.85), channel_id=1, source_target_pairs={{0,8},{1,9},{2,10},{3,11},{4,12},{5,13},{6,14},{7,15},{8,24},{9,25... | collective-permute-start | bytes 663560 | tf_op jit(solution)/shard_map/ppermute | solution.py:101
  28.1 18.2 %collective-permute-start.8 = (bf16[128,3072]{1,0:T(8,128)(2,1)}, bf16[128,3072]{1,0:T(8,128)(2,1)}, u32[]{:S(2)}, u32[]{:S(2)}) collective-permute-start(bf16[128,3072]{1,0:T(8,128)(2,1)} %pad_maximum_fusion.19), channel_id=1, source_target_pairs={{0,4},{1,5},{2,6},{3,7},{4,0},{5,1},{6,2},{7,3},{8,12},{9,13},{10,... | collective-permute-start | bytes 2359304 | tf_op jit(solution)/shard_map/ppermute | solution.py:96
  30.7 18.5 %collective-permute-start = (bf16[1,3,128,1024]{3,2,1,0:T(8,128)(2,1)S(1)}, bf16[1,3,128,1024]{3,2,1,0:T(8,128)(2,1)S(1)}, u32[]{:S(2)}, u32[]{:S(2)}) collective-permute-start(bf16[1,3,128,1024]{3,2,1,0:T(8,128)(2,1)S(1)} %bitcast.353), channel_id=1, source_target_pairs={{0,1},{1,0},{2,3},{3,2},{4,6},{5,7},{6,4},{7,5},{8,9},{9,8},{10,11... | collective-permute-start | bytes 2359304 | tf_op jit(solution)/shard_map/ppermute | solution.py:107
  46.2 34.4 %collective-permute-start.5 = (bf16[4,144,768]{2,1,0:T(8,128)(2,1)S(1)}, bf16[4,144,768]{2,1,0:T(8,128)(2,1)}, u32[]{:S(2)}, u32[]{:S(2)}) collective-permute-start(bf16[4,144,768]{2,1,0:T(8,128)(2,1)S(1)} %pad_maximum_fusion.16.refs_0_), channel_id=1, source_target_pairs={{0,4},{1,5},{2,6},{3,7},{4,0},{5,1},{6,2},{7,3},{8,12},{9,13},{10,... | collective-permute-start | bytes 2654216 | tf_op jit(solution)/shard_map/ppermute | solution.py:96
  50.5 46.5 %collective-permute-start.1 = (bf16[2,3,128,1024]{3,2,1,0:T(8,128)(2,1)}, bf16[2,3,128,1024]{3,2,1,0:T(8,128)(2,1)}, u32[]{:S(2)}, u32[]{:S(2)}) collective-permute-start(bf16[2,3,128,1024]{3,2,1,0:T(8,128)(2,1)} %pad_maximum_fusion.6), channel_id=1, source_target_pairs={{0,2},{1,3},{2,0},{3,1},{4,5},{5,4},{6,7},{7,6},{8,10},{9,11},{10,... | collective-permute-start | bytes 4718600 | tf_op jit(solution)/shard_map/ppermute | solution.py:107
  59.8 17.7 %collective-permute-start.10 = (bf16[320,512]{1,0:T(8,128)(2,1)S(1)}, bf16[320,512]{1,0:T(8,128)(2,1)S(1)}, u32[]{:S(2)}, u32[]{:S(2)}) collective-permute-start(bf16[320,512]{1,0:T(8,128)(2,1)S(1)} %collective-permute-done.9), channel_id=1, source_target_pairs={{0,8},{1,9},{2,10},{3,11},{4,12},{5,13},{6,14},{7,15},{8,24},{9,25... | collective-permute-start | bytes 983048 | tf_op jit(solution)/shard_map/ppermute | solution.py:101
  77.5 62.7 %collective-permute-start.18 = (bf16[128,1024]{1,0:T(8,128)(2,1)}, bf16[128,1024]{1,0:T(8,128)(2,1)}, u32[]{:S(2)}, u32[]{:S(2)}) collective-permute-start(bf16[128,1024]{1,0:T(8,128)(2,1)} %collective-permute-done.17), channel_id=1, source_target_pairs={{0,8},{1,9},{2,10},{3,11},{4,12},{5,13},{6,14},{7,15},{8,24},{9,25... | collective-permute-start | bytes 786440 | tf_op jit(solution)/shard_map/ppermute | solution.py:101
  77.5 15.9 %collective-permute-start.11 = (bf16[320,512]{1,0:T(8,128)(2,1)S(1)}, bf16[320,512]{1,0:T(8,128)(2,1)}, u32[]{:S(2)}, u32[]{:S(2)}) collective-permute-start(bf16[320,512]{1,0:T(8,128)(2,1)S(1)} %collective-permute-done.10), channel_id=1, source_target_pairs={{0,8},{1,9},{2,10},{3,11},{4,12},{5,13},{6,14},{7,15},{8,24},{9,25... | collective-permute-start | bytes 983048 | tf_op jit(solution)/shard_map/ppermute | solution.py:101
  95.5 34.5 %collective-permute-start.12 = (bf16[1,3,320,512]{3,2,1,0:T(8,128)(2,1)}, bf16[1,3,320,512]{3,2,1,0:T(8,128)(2,1)}, u32[]{:S(2)}, u32[]{:S(2)}) collective-permute-start(bf16[1,3,320,512]{3,2,1,0:T(8,128)(2,1)} %maximum_bitcast_fusion), channel_id=1, source_target_pairs={{0,1},{1,0},{2,3},{3,2},{4,6},{5,7},{6,4},{7,5},{8,9},{9,8},{10,11... | collective-permute-start | bytes 2949128 | tf_op jit(solution)/shard_map/ppermute | solution.py:107
  133.3 37.6 %collective-permute-start.13 = (bf16[2,3,320,512]{3,2,1,0:T(8,128)(2,1)}, bf16[2,3,320,512]{3,2,1,0:T(8,128)(2,1)}, u32[]{:S(2)}, u32[]{:S(2)}) collective-permute-start(bf16[2,3,320,512]{3,2,1,0:T(8,128)(2,1)} %pad_maximum_fusion.5), channel_id=1, source_target_pairs={{0,2},{1,3},{2,0},{3,1},{4,5},{5,4},{6,7},{7,6},{8,10},{9,11},{10,... | collective-permute-start | bytes 5898248 | tf_op jit(solution)/shard_map/ppermute | solution.py:107
  139.6 33.8 %collective-permute-start.6 = (bf16[2,1,384,256]{2,3,0,1:T(8,128)(2,1)S(1)}, bf16[2,1,384,256]{2,3,0,1:T(8,128)(2,1)S(1)}, u32[]{:S(2)}, u32[]{:S(2)}) collective-permute-start(bf16[2,1,384,256]{2,3,0,1:T(8,128)(2,1)S(1)} %get-tuple-element.77), channel_id=1, source_target_pairs={{0,1},{1,0},{2,3},{3,2},{4,6},{5,7},{6,4},{7,5},{8,9},{9,8},{10,11... | collective-permute-start | bytes 1179656 | tf_op jit(solution)/shard_map/ppermute | solution.py:114
  141.3 36.9 %collective-permute-start.19 = (bf16[1,3,128,1024]{3,2,1,0:T(8,128)(2,1)S(1)}, bf16[1,3,128,1024]{3,2,1,0:T(8,128)(2,1)S(1)}, u32[]{:S(2)}, u32[]{:S(2)}) collective-permute-start(bf16[1,3,128,1024]{3,2,1,0:T(8,128)(2,1)S(1)} %maximum_bitcast_fusion.2), channel_id=1, source_target_pairs={{0,1},{1,0},{2,3},{3,2},{4,6},{5,7},{6,4},{7,5},{8,9},{9,8},{10,11... | collective-permute-start | bytes 2359304 | tf_op jit(solution)/shard_map/ppermute | solution.py:107
  180.4 20.7 %collective-permute-start.20 = (bf16[2,3,128,1024]{3,2,1,0:T(8,128)(2,1)}, bf16[2,3,128,1024]{3,2,1,0:T(8,128)(2,1)}, u32[]{:S(2)}, u32[]{:S(2)}) collective-permute-start(bf16[2,3,128,1024]{3,2,1,0:T(8,128)(2,1)} %pad_maximum_fusion.8), channel_id=1, source_target_pairs={{0,2},{1,3},{2,0},{3,1},{4,5},{5,4},{6,7},{7,6},{8,10},{9,11},{10,... | collective-permute-start | bytes 4718600 | tf_op jit(solution)/shard_map/ppermute | solution.py:107
  196.2 18.4 %collective-permute-start.15 = (bf16[384,1024]{1,0:T(8,128)(2,1)}, bf16[384,1024]{1,0:T(8,128)(2,1)}, u32[]{:S(2)}, u32[]{:S(2)}) collective-permute-start(bf16[384,1024]{1,0:T(8,128)(2,1)} %fusion.29), channel_id=1, source_target_pairs={{0,4},{1,5},{2,6},{3,7},{4,0},{5,1},{6,2},{7,3},{8,12},{9,13},{10,... | collective-permute-start | bytes 2359304 | tf_op jit(solution)/shard_map/ppermute | solution.py:96
  231.3 16.9 %collective-permute-start.22 = (bf16[384,1024]{1,0:T(8,128)(2,1)}, bf16[384,1024]{1,0:T(8,128)(2,1)}, u32[]{:S(2)}, u32[]{:S(2)}) collective-permute-start(bf16[384,1024]{1,0:T(8,128)(2,1)} %get-tuple-element.40), channel_id=1, source_target_pairs={{0,4},{1,5},{2,6},{3,7},{4,0},{5,1},{6,2},{7,3},{8,12},{9,13},{10,... | collective-permute-start | bytes 2359304 | tf_op jit(solution)/shard_map/ppermute | solution.py:96
  264.8 25.4 %collective-permute-start.23 = (bf16[384,1024]{1,0:T(8,128)(2,1)}, bf16[384,1024]{1,0:T(8,128)(2,1)}, u32[]{:S(2)}, u32[]{:S(2)}) collective-permute-start(bf16[384,1024]{1,0:T(8,128)(2,1)} %slice.362), channel_id=1, source_target_pairs={{0,4},{1,5},{2,6},{3,7},{4,0},{5,1},{6,2},{7,3},{8,12},{9,13},{10,... | collective-permute-start | bytes 2359304 | tf_op jit(solution)/shard_map/ppermute | solution.py:96
  274.3 154.9 %collective-permute-start.45 = (bf16[2,4,128,1024]{3,2,1,0:T(8,128)(2,1)}, bf16[2,4,128,1024]{3,2,1,0:T(8,128)(2,1)}, u32[]{:S(2)}, u32[]{:S(2)}) collective-permute-start(bf16[2,4,128,1024]{3,2,1,0:T(8,128)(2,1)} %pad_maximum_fusion.4), channel_id=1, source_target_pairs={{0,2},{1,3},{2,0},{3,1},{4,5},{5,4},{6,7},{7,6},{8,10},{9,11},{10,... | collective-permute-start | bytes 6291464 | tf_op jit(solution)/shard_map/ppermute | solution.py:121
  299.7 16.3 %collective-permute-start.24 = (bf16[2,1,384,256]{3,2,0,1:T(8,128)(2,1)S(1)}, bf16[2,1,384,256]{3,2,0,1:T(8,128)(2,1)S(1)}, u32[]{:S(2)}, u32[]{:S(2)}) collective-permute-start(bf16[2,1,384,256]{3,2,0,1:T(8,128)(2,1)S(1)} %get-tuple-element.69), channel_id=1, source_target_pairs={{0,1},{1,0},{2,3},{3,2},{4,6},{5,7},{6,4},{7,5},{8,9},{9,8},{10,11... | collective-permute-start | bytes 1179656 | tf_op jit(solution)/shard_map/ppermute | solution.py:114
  315.1 122.2 %collective-permute-start.34 = (bf16[2,4,256,512]{3,2,1,0:T(8,128)(2,1)}, bf16[2,4,256,512]{3,2,1,0:T(8,128)(2,1)}, u32[]{:S(2)}, u32[]{:S(2)}) collective-permute-start(bf16[2,4,256,512]{3,2,1,0:T(8,128)(2,1)} %pad_maximum_fusion.3), channel_id=1, source_target_pairs={{0,2},{1,3},{2,0},{3,1},{4,5},{5,4},{6,7},{7,6},{8,10},{9,11},{10,... | collective-permute-start | bytes 6291464 | tf_op jit(solution)/shard_map/ppermute | solution.py:121
  316.9 28.8 %collective-permute-start.25 = (bf16[1,2,384,256]{3,2,1,0:T(8,128)(2,1)}, bf16[1,2,384,256]{3,2,1,0:T(8,128)(2,1)}, u32[]{:S(2)}, u32[]{:S(2)}) collective-permute-start(bf16[1,2,384,256]{3,2,1,0:T(8,128)(2,1)} %get-tuple-element.67), channel_id=1, source_target_pairs={{0,2},{1,3},{2,0},{3,1},{4,5},{5,4},{6,7},{7,6},{8,10},{9,11},{10,... | collective-permute-start | bytes 1179656 | tf_op jit(solution)/shard_map/ppermute | solution.py:114
  324.0 87.2 %collective-permute-start.36 = (bf16[4,128,1024]{1,2,0:T(8,128)(2,1)}, bf16[4,128,1024]{1,2,0:T(8,128)(2,1)}, u32[]{:S(2)}, u32[]{:S(2)}) collective-permute-start(bf16[4,128,1024]{1,2,0:T(8,128)(2,1)} %bitcast.367), channel_id=1, source_target_pairs={{0,4},{1,5},{2,6},{3,7},{4,0},{5,1},{6,2},{7,3},{8,12},{9,13},{10,... | collective-permute-start | bytes 3145736 | tf_op jit(solution)/shard_map/ppermute | solution.py:96
  411.2 24.6 %collective-permute-start.28 = (bf16[4,144,768]{2,1,0:T(8,128)(2,1)}, bf16[4,144,768]{2,1,0:T(8,128)(2,1)}, u32[]{:S(2)}, u32[]{:S(2)}) collective-permute-start(bf16[4,144,768]{2,1,0:T(8,128)(2,1)} %fusion.33), channel_id=1, source_target_pairs={{0,4},{1,5},{2,6},{3,7},{4,0},{5,1},{6,2},{7,3},{8,12},{9,13},{10,... | collective-permute-start | bytes 2654216 | tf_op jit(solution)/shard_map/ppermute | solution.py:96
  424.5 57.9 %collective-permute-start.26 = (bf16[2,384,1024]{2,1,0:T(8,128)(2,1)}, bf16[2,384,1024]{2,1,0:T(8,128)(2,1)}, u32[]{:S(2)}, u32[]{:S(2)}) collective-permute-start(bf16[2,384,1024]{2,1,0:T(8,128)(2,1)} %bitcast.61), channel_id=1, source_target_pairs={{0,2},{1,3},{2,0},{3,1},{4,5},{5,4},{6,7},{7,6},{8,10},{9,11},{10,... | collective-permute-start | bytes 4718600 | tf_op jit(solution)/shard_map/ppermute | solution.py:121
  432.5 38.3 %collective-permute-start.46 = (bf16[1,4,128,1024]{3,2,1,0:T(8,128)(2,1)S(1)}, bf16[1,4,128,1024]{3,2,1,0:T(8,128)(2,1)S(1)}, u32[]{:S(2)}, u32[]{:S(2)}) collective-permute-start(bf16[1,4,128,1024]{3,2,1,0:T(8,128)(2,1)S(1)} %slice.334), channel_id=1, source_target_pairs={{0,1},{1,0},{2,3},{3,2},{4,6},{5,7},{6,4},{7,5},{8,9},{9,8},{10,11... | collective-permute-start | bytes 3145736 | tf_op jit(solution)/shard_map/ppermute | solution.py:121
  434.6 24.4 %collective-permute-start.38 = (bf16[1,4,128,256]{3,2,1,0:T(8,128)(2,1)S(1)}, bf16[1,4,128,256]{3,2,1,0:T(8,128)(2,1)S(1)}, u32[]{:S(2)}, u32[]{:S(2)}) collective-permute-start(bf16[1,4,128,256]{3,2,1,0:T(8,128)(2,1)S(1)} %slice.324), channel_id=1, source_target_pairs={{0,1},{1,0},{2,3},{3,2},{4,6},{5,7},{6,4},{7,5},{8,9},{9,8},{10,11... | collective-permute-start | bytes 786440 | tf_op jit(solution)/shard_map/ppermute | solution.py:121
  439.7 30.6 %collective-permute-start.35 = (bf16[1,4,256,512]{3,2,1,0:T(8,128)(2,1)S(1)}, bf16[1,4,256,512]{3,2,1,0:T(8,128)(2,1)S(1)}, u32[]{:S(2)}, u32[]{:S(2)}) collective-permute-start(bf16[1,4,256,512]{3,2,1,0:T(8,128)(2,1)S(1)} %slice.322), channel_id=1, source_target_pairs={{0,1},{1,0},{2,3},{3,2},{4,6},{5,7},{6,4},{7,5},{8,9},{9,8},{10,11... | collective-permute-start | bytes 3145736 | tf_op jit(solution)/shard_map/ppermute | solution.py:121
  444.5 14.6 %collective-permute-start.30 = (bf16[144,768]{1,0:T(8,128)(2,1)S(1)}, bf16[144,768]{1,0:T(8,128)(2,1)S(1)}, u32[]{:S(2)}, u32[]{:S(2)}) collective-permute-start(bf16[144,768]{1,0:T(8,128)(2,1)S(1)} %fusion.43), channel_id=1, source_target_pairs={{0,8},{1,9},{2,10},{3,11},{4,12},{5,13},{6,14},{7,15},{8,24},{9,25... | collective-permute-start | bytes 663560 | tf_op jit(solution)/shard_map/ppermute | solution.py:128
  468.4 26.7 %collective-permute-start.32 = (bf16[1,144,768]{2,1,0:T(8,128)(2,1)S(1)}, bf16[1,144,768]{2,1,0:T(8,128)(2,1)S(1)}, u32[]{:S(2)}, u32[]{:S(2)}) collective-permute-start(bf16[1,144,768]{2,1,0:T(8,128)(2,1)S(1)} %fusion.50), channel_id=1, source_target_pairs={{0,1},{1,0},{2,3},{3,2},{4,6},{5,7},{6,4},{7,5},{8,9},{9,8},{10,11... | collective-permute-start | bytes 663560 | tf_op jit(solution)/shard_map/ppermute | solution.py:107
  471.2 16.6 %collective-permute-start.47 = (bf16[128,1024]{1,0:T(8,128)(2,1)S(1)}, bf16[128,1024]{1,0:T(8,128)(2,1)S(1)}, u32[]{:S(2)}, u32[]{:S(2)}) collective-permute-start(bf16[128,1024]{1,0:T(8,128)(2,1)S(1)} %dynamic-slice_bitcast_fusion.5), channel_id=1, source_target_pairs={{0,8},{1,9},{2,10},{3,11},{4,12},{5,13},{6,14},{7,15},{8,24},{9,25... | collective-permute-start | bytes 786440 | tf_op jit(solution)/shard_map/ppermute | solution.py:128
  485.4 46.7 %collective-permute-start.27 = (bf16[1,384,1024]{2,1,0:T(8,128)(2,1)}, bf16[1,384,1024]{2,1,0:T(8,128)(2,1)}, u32[]{:S(2)}, u32[]{:S(2)}) collective-permute-start(bf16[1,384,1024]{2,1,0:T(8,128)(2,1)} %slice.317), channel_id=1, source_target_pairs={{0,1},{1,0},{2,3},{3,2},{4,6},{5,7},{6,4},{7,5},{8,9},{9,8},{10,11... | collective-permute-start | bytes 2359304 | tf_op jit(solution)/shard_map/ppermute | solution.py:121
  495.1 20.8 %collective-permute-start.33 = (bf16[2,144,768]{2,1,0:T(8,128)(2,1)S(1)}, bf16[2,144,768]{2,1,0:T(8,128)(2,1)S(1)}, u32[]{:S(2)}, u32[]{:S(2)}) collective-permute-start(bf16[2,144,768]{2,1,0:T(8,128)(2,1)S(1)} %pad_maximum_fusion.26), channel_id=1, source_target_pairs={{0,2},{1,3},{2,0},{3,1},{4,5},{5,4},{6,7},{7,6},{8,10},{9,11},{10,... | collective-permute-start | bytes 1327112 | tf_op jit(solution)/shard_map/ppermute | solution.py:107
  514.4 14.1 %collective-permute-start.43 = (bf16[1,320,512]{2,1,0:T(8,128)(2,1)}, bf16[1,320,512]{2,1,0:T(8,128)(2,1)}, u32[]{:S(2)}, u32[]{:S(2)}) collective-permute-start(bf16[1,320,512]{2,1,0:T(8,128)(2,1)} %maximum_bitcast_fusion.3), channel_id=1, source_target_pairs={{0,1},{1,0},{2,3},{3,2},{4,6},{5,7},{6,4},{7,5},{8,9},{9,8},{10,11... | collective-permute-start | bytes 983048 | tf_op jit(solution)/shard_map/ppermute | solution.py:107
  (67 other events, 469.1 us)

commit v2 on v1

v2 whole, which is shorter than its diff:
```python
import functools

import jax
import jax.numpy as jnp
import numpy as np
from jax import lax
from jax.experimental import pallas as pl
from jax.experimental.pallas import tpu as pltpu
from jax.sharding import PartitionSpec as P

HEAD_DIM = 64
PAIR = 2 * HEAD_DIM
EPSILON = 1e-12
BOTH = ("dp", "seq")
PAD = 16
MICROSECOND = 1_100_000_000
F32 = jnp.float32
BF16 = jnp.bfloat16
ANY = pl.BlockSpec(memory_space=pl.ANY)


def dot(former, latter, former_dim=1, latter_dim=0):
    return lax.dot_general(
        former,
        latter,
        (((former_dim,), (latter_dim,)), ((), ())),
        preferred_element_type=F32,
    )


class Plan:
    def __init__(self, n_dp, n_seq):
        self.n_dp, self.n_seq, self.n_z = n_dp, n_seq, n_dp // 2
        self.bits = n_seq.bit_length() - 1
        order = [0] + list(range(1, self.n_z, 2))
        order += list(range(2, self.n_z, 2))[::-1]
        self.order = order
        self.place = [order.index(z) for z in range(self.n_z)]
        self.core = self.pairs(lambda z, c, s: (z, 1 - c, s))
        self.toward = [
            self.pairs(lambda z, c, s, j=j: (self.behind(z, -j), c, s))
            for j in range(self.n_z)
        ]
        self.across = [
            self.pairs(lambda z, c, s, r=r: (z, c, s ^ self.mask(c, r)))
            for r in range(n_seq)
        ]
        self.stage = [
            self.pairs(lambda z, c, s, k=k: (z, c, s ^ self.mask(c, 1 << k)))
            for k in range(self.bits)
        ]
        rows = []
        for dp in range(n_dp):
            for s in range(n_seq):
                z, c = dp // 2, dp % 2
                rows.append(
                    [self.behind(z, j) for j in range(self.n_z)]
                    + [s ^ self.mask(c, r) for r in range(n_seq)]
                    + [c, 1 - c]
                    + [s ^ self.mask(1 - c, r) for r in range(n_seq)]
                )
        self.table = np.asarray(rows, np.int32)
        self.BEHIND, self.MEMBER = 0, self.n_z
        self.CORE = self.n_z + n_seq
        self.MEMBERS = (self.MEMBER, self.CORE + 2)

    def behind(self, z, j):
        return self.order[(self.place[z] - j) % self.n_z]

    def mask(self, c, r):
        out = 0
        for k in range(self.bits):
            if r >> k & 1:
                out |= 1 << ((k + c) % self.bits)
        return out

    def pairs(self, target):
        out = []
        for dp in range(self.n_dp):
            for s in range(self.n_seq):
                z, c, t = target(dp // 2, dp % 2, s)
                out.append((dp * self.n_seq + s, (2 * z + c) * self.n_seq + t))
        return out

    def row(self):
        here = lax.axis_index("dp") * self.n_seq + lax.axis_index("seq")
        return lax.dynamic_index_in_dim(jnp.asarray(self.table), here, 0, False)

    def swap(self, block):
        return lax.ppermute(block, BOTH, self.core)

    def share(self, block):
        return [block] + [lax.ppermute(block, BOTH, way) for way in self.across[1:]]

    def trade(self, blocks):
        return [blocks[0]] + [
            lax.ppermute(block, BOTH, way) for block, way in zip(blocks[1:], self.across[1:])
        ]

    def gather(self, block):
        near = block[None]
        for k in range(self.bits - 1):
            near = self.double(near, k)
        return near, lax.ppermute(near, BOTH, self.stage[self.bits - 1])

    def double(self, near, k):
        return jnp.concatenate([near, lax.ppermute(near, BOTH, self.stage[k])], 0)


def add(former, latter):
    return (former.astype(F32) + latter.astype(F32)).astype(BF16)


def after(value, *others):
    return lax.optimization_barrier((value,) + others)[0]


def shape(dims, dtype=BF16):
    return jax.ShapeDtypeStruct(tuple(dims), dtype)


def aligned(start, size):
    return pl.ds(pl.multiple_of(start, size), size)


def whole_block(dims):
    return pl.BlockSpec(tuple(dims), lambda *_: (0,) * len(dims))


def call(
    kernel, table, operands, in_specs, outs, out_specs, grid, scratch, micros, name, alias=None
):
    size = sum(int(np.prod(o.shape)) * o.dtype.itemsize for o in list(operands) + list(outs))
    return pl.pallas_call(
        kernel,
        out_shape=list(outs),
        grid_spec=pltpu.PrefetchScalarGridSpec(
            num_scalar_prefetch=1,
            grid=grid,
            in_specs=in_specs,
            out_specs=out_specs,
            scratch_shapes=scratch,
        ),
        cost_estimate=pl.CostEstimate(
            flops=micros * MICROSECOND, bytes_accessed=size, transcendentals=0
        ),
        input_output_aliases=alias or {},
        name=name,
    )(table, *operands)


def assemble(table, pieces, moves, outs, name):
    def kernel(table_ref, *refs):
        sources, targets, sems = refs[: len(pieces)], refs[len(pieces) : -1], refs[-1]
        copies = [
            pltpu.make_async_copy(
                sources[i].at[src(table_ref)], targets[o].at[at(table_ref)], sems.at[n]
            )
            for n, (i, src, o, at) in enumerate(moves)
        ]
        for copy in copies:
            copy.start()
        for copy in copies:
            copy.wait()

    return call(
        kernel,
        table,
        pieces,
        [ANY] * len(pieces),
        outs,
        [whole_block(o.shape) for o in outs],
        (1,),
        [pltpu.SemaphoreType.DMA((len(moves),))],
        2,
        name,
    )


def copies_of(moves, sems):
    return [pltpu.make_async_copy(src, at, sems.at[n]) for n, (src, at) in enumerate(moves)]


def lanes_of(half):
    lane = lax.broadcasted_iota(jnp.int32, (1, PAIR), 1)
    return lane < HEAD_DIM if half == 0 else lane >= HEAD_DIM


def only(block, half):
    return jnp.where(lanes_of(half), block, jnp.zeros_like(block))


def statistics(hidden):
    center = hidden - jnp.mean(hidden, -1, keepdims=True)
    spread = jnp.mean(center * center, -1, keepdims=True)
    root = lax.rsqrt(spread + EPSILON)
    return center * root, root


def norm_back(unit, root, gain_vec, upstream):
    scaled = upstream * gain_vec
    first = jnp.mean(scaled, -1, keepdims=True)
    second = jnp.mean(scaled * unit, -1, keepdims=True)
    return root * (scaled - first - unit * second)


def add_rows(target, row, value):
    target[row : row + 1, :] += jnp.sum(value, 0, keepdims=True)


def head_weights(plan, table, mine, theirs):
    n_z, n_dp = plan.n_z, plan.n_dp
    rows, lanes = mine.shape[1:]
    own_rows, cols3 = rows - PAD, lanes // 4 * 3
    width, span = n_dp * own_rows, lanes // 2

    def kernel(t, mine_ref, theirs_ref, w_ref, vec_ref, bias_ref, held, sems):
        moves = []
        for k, source in enumerate((mine_ref, theirs_ref)):
            for j in range(n_z):
                owner = 2 * t[plan.BEHIND + j] + t[plan.CORE + k]
                moves.append((source.at[j, pl.ds(own_rows, PAD)], held.at[owner]))
                moves.append(
                    (
                        source.at[j, pl.ds(0, own_rows), pl.ds(0, cols3)],
                        w_ref.at[aligned(owner * own_rows, own_rows)],
                    )
                )
        copies = copies_of(moves, sems)
        for copy in copies:
            copy.start()
        for copy in copies:
            copy.wait()
        for owner in range(n_dp):
            values = held[owner].astype(F32)
            at = pl.ds(owner * own_rows, own_rows)
            vec_ref[:, at] = values[:8, :own_rows]
            bias_ref[owner] = values[8:9, :span]

    outs = [shape((width, cols3)), shape((8, width), F32), shape((n_dp, 1, span), F32)]
    return call(
        kernel,
        table,
        [mine, theirs],
        [ANY] * 2,
        outs,
        [whole_block(o.shape) for o in outs],
        (1,),
        [pltpu.VMEM((n_dp, PAD, lanes), BF16), pltpu.SemaphoreType.DMA((4 * n_z,))],
        3,
        "head_weights",
    )


def attention_forward(plan, table, g, near, far, weights, vectors, before):
    n = plan.n_seq
    half, seqs, length, width = near.shape
    n_before = len(before)
    cols3 = weights.shape[1]
    cols = cols3 // 3
    total = n * length
    tile = 128
    scale = HEAD_DIM**-0.5

    def kernel(t, near_ref, far_ref, w_ref, vec_ref, *rest):
        qkv_ref, *parts, context = rest[n_before:]
        here = aligned(t[plan.MEMBER] * cols, cols)
        bias = jnp.concatenate(
            [vec_ref[0:1, here], jnp.zeros((1, cols), F32), vec_ref[1:2, here]], 1
        )
        for part, source in enumerate((near_ref, far_ref)):
            rows = source[...].reshape(half * length, width)
            out = dot(rows, w_ref[...]) + bias
            qkv_ref[part * half * length : (part + 1) * half * length, :] = out.astype(BF16)
        def each_pair(pair, carry):
            q_at = aligned(pair * PAIR, PAIR)
            key = qkv_ref[:, aligned(cols + pair * PAIR, PAIR)]
            value = qkv_ref[:, aligned(2 * cols + pair * PAIR, PAIR)]

            def each_tile(i, carry):
                rows = aligned(i * tile, tile)
                query = qkv_ref[rows, q_at] * jnp.asarray(scale, BF16)
                out = None
                for head in range(2):
                    scores = dot(only(query, head), key, 1, 1)
                    exponent = jnp.exp(scores - jnp.max(scores, -1, keepdims=True))
                    inverse = 1.0 / jnp.sum(exponent, -1, keepdims=True)
                    part = dot((exponent * inverse).astype(BF16), value)
                    out = part if head == 0 else jnp.where(lanes_of(0), out, part)
                context[rows, q_at] = out.astype(BF16)
                return carry

            lax.fori_loop(0, total // tile, each_tile, 0)
            return carry

        lax.fori_loop(0, cols // PAIR, each_pair, 0)
        for r in range(n):
            parts[r][0] = context[r * length : (r + 1) * length, :]

    block = pl.BlockSpec((half, 1, length, width), lambda i, t: (0, g, 0, 0))
    return call(
        kernel,
        table,
        [near, far, weights, vectors] + before,
        [block, block, whole_block(weights.shape), whole_block(vectors.shape)]
        + [ANY] * n_before,
        [shape((total, cols3))] + [shape((seqs, length, cols))] * n,
        [whole_block((total, cols3))]
        + [pl.BlockSpec((1, length, cols), lambda i, t: (g, 0, 0))] * n,
        (1,),
        [pltpu.VMEM((total, cols), BF16)],
        11,
        "attention_forward",
        {5 + i: 1 + i for i in range(n_before)},
    )


def attention_backward(plan, table, g, seqs, qkv, upstream, w_qkv, before):
    n = plan.n_seq
    half = n // 2
    width, cols3 = w_qkv.shape
    cols = cols3 // 3
    total = qkv.shape[0]
    length = total // n
    tile = min(256, total)
    scale = HEAD_DIM**-0.5
    n_before = len(before)

    def kernel(t, qkv_ref, w_ref, *rest):
        up_refs, rest = rest[:n], rest[n + n_before :]
        grad_ref, part_keep, part_send = rest[:3]
        up, key_acc, value_acc = rest[3:]
        for r in range(n):
            up[r * length : (r + 1) * length, :] = up_refs[r][0]
        def each_pair(pair, carry):
            q_at = aligned(pair * PAIR, PAIR)
            k_at = aligned(cols + pair * PAIR, PAIR)
            v_at = aligned(2 * cols + pair * PAIR, PAIR)
            value_acc[...] = jnp.zeros_like(value_acc)
            key_acc[...] = jnp.zeros_like(key_acc)

            def each_tile(i, carry):
                rows = aligned(i * tile, tile)
                query = qkv_ref[rows, q_at] * jnp.asarray(scale, BF16)
                above = up[rows, q_at]
                grad_query = None
                for head in range(2):
                    key = only(qkv_ref[:, k_at], head)
                    value = only(qkv_ref[:, v_at], head)
                    scores = dot(key, query, 1, 1)
                    exponent = jnp.exp(scores - jnp.max(scores, 0, keepdims=True))
                    portions = exponent * (1.0 / jnp.sum(exponent, 0, keepdims=True))
                    low = portions.astype(BF16)
                    slope = dot(value, above, 1, 1)
                    total_slope = jnp.sum(portions * slope, 0, keepdims=True)
                    slope = (portions * (slope - total_slope)).astype(BF16)
                    value_acc[...] += dot(low, only(above, head))
                    key_acc[...] += dot(slope, only(query, head))
                    q_part = dot(slope, key, 0, 0)
                    grad_query = q_part if head == 0 else grad_query + q_part
                grad_ref[0, rows, q_at] = (grad_query * scale).astype(BF16)
                return carry

            lax.fori_loop(0, total // tile, each_tile, 0)
            grad_ref[0, :, k_at] = key_acc[...].astype(BF16)
            grad_ref[0, :, v_at] = value_acc[...].astype(BF16)
            return carry

        lax.fori_loop(0, cols // PAIR, each_pair, 0)
        for r in range(n):
            target = part_keep if r < half else part_send
            rows = grad_ref[0, r * length : (r + 1) * length, :]
            target[r % half, 0] = dot(rows, w_ref[...], 1, 1).astype(BF16)

    part = (half, seqs, length, width)
    outs = [shape((seqs, total, cols3)), shape(part), shape(part)]
    block = pl.BlockSpec((half, 1, length, width), lambda i, t: (0, g, 0, 0))
    operands = [qkv, w_qkv] + upstream + before
    first = 1 + len(operands) - n_before
    return call(
        kernel,
        table,
        operands,
        [whole_block(qkv.shape), whole_block(w_qkv.shape)]
        + [pl.BlockSpec((1, length, cols), lambda i, t: (g, 0, 0))] * n
        + [ANY] * n_before,
        outs,
        [pl.BlockSpec((1, total, cols3), lambda i, t: (g, 0, 0)), block, block],
        (1,),
        [
            pltpu.VMEM((total, cols), BF16),
            pltpu.VMEM((total, PAIR), F32),
            pltpu.VMEM((total, PAIR), F32),
        ],
        11,
        "attention_backward",
        {first + i: i for i in range(n_before)},
    )


def head_weights_backward(plan, table, near, far, grad, narrow, wide):
    n, n_z = plan.n_seq, plan.n_z
    half, seqs, length, width = near.shape
    cols3 = grad.shape[2]
    own_rows = width // plan.n_dp
    total = n * length
    span = wide.shape[2]

    def kernel(t, near_ref, far_ref, grad_ref, narrow_ref, wide_ref, *rest):
        w_keep, w_send, w_acc, b_acc = rest
        step_id = pl.program_id(0)

        @pl.when(step_id == 0)
        def _():
            w_acc[...] = jnp.zeros_like(w_acc)
            b_acc[...] = jnp.zeros_like(b_acc)

        for part, source in enumerate((near_ref, far_ref)):
            rows = source[...].reshape(half * length, width)
            these = grad_ref[0, part * half * length : (part + 1) * half * length, :]
            w_acc[...] += dot(rows, these, 0, 0)
        b_acc[0:1, :] += jnp.sum(grad_ref[0].astype(F32), 0, keepdims=True)

        @pl.when(step_id == seqs - 1)
        def _():
            for target, k in ((w_keep, 0), (w_send, 1)):
                for z in range(n_z):
                    row = (2 * z + t[plan.CORE + k]) * own_rows
                    target[z, :own_rows, :] = w_acc[aligned(row, own_rows), :].astype(BF16)
                    here = (t[plan.MEMBER] == z).astype(F32)
                    last = lax.broadcasted_iota(jnp.int32, (8, cols3), 0) == 7
                    rows = jnp.where(
                        last, b_acc[0:1, :] * here, narrow_ref[2 * z + t[plan.CORE + k]]
                    )
                    target[z, own_rows : own_rows + 8, :] = rows.astype(BF16)
                    target[z, own_rows + 8 :, :] = jnp.zeros((PAD - 8, cols3), BF16)
                if k == 0:
                    for r in range(n):
                        rows = wide_ref[r].astype(BF16)
                        target[t[plan.MEMBER + r], own_rows + 8 :, :span] = rows

    block = pl.BlockSpec((half, 1, length, width), lambda g, t: (0, g, 0, 0))
    w_out = (n_z, own_rows + PAD, cols3)
    return call(
        kernel,
        table,
        [near, far, grad, narrow, wide],
        [
            block,
            block,
            pl.BlockSpec((1, total, cols3), lambda g, t: (g, 0, 0)),
            whole_block(narrow.shape),
            whole_block(wide.shape),
        ],
        [shape(w_out), shape(w_out)],
        [whole_block(w_out), whole_block(w_out)],
        (seqs,),
        [pltpu.VMEM((width, cols3), F32), pltpu.VMEM((8, cols3), F32)],
        8,
        "head_weights_backward",
    )


def output_norm(plan, table, pieces, inputs, vectors, w_out, come, near, far, others):
    n, n_z = plan.n_seq, plan.n_z
    half = n // 2
    tokens, width = inputs.shape
    own_rows = w_out.shape[0]
    cols = width // n
    tile = 128
    n_moves = 2 + 2 * (n_z - 1) * n

    def kernel(t, in_ref, vec_ref, w_ref, come_ref, near_ref, far_ref, on_ref, of_ref, *rest):
        refs, rest = rest[:n], rest[n:]
        sum_ref, norm_ref, low_ref, full_ref, sems = rest

        def row(z, k):
            return aligned((z * 2 + t[plan.CORE + k]) * own_rows, own_rows)

        moves = []
        for k, source in enumerate((w_ref, come_ref)):
            at = full_ref.at[row(t[plan.BEHIND], k)]
            lanes = source.shape[1] - width
            moves.append((source.at[pl.ds(0, own_rows), pl.ds(lanes, width)], at))
        for k, (first, second) in enumerate(((near_ref, far_ref), (on_ref, of_ref))):
            for j in range(1, n_z):
                for r in range(n):
                    source = first if r < half else second
                    at = full_ref.at[
                        row(t[plan.BEHIND + j], k),
                        aligned(t[plan.MEMBERS[k] + r] * cols, cols),
                    ]
                    moves.append((source.at[r % half, j - 1], at))
        copies = copies_of(moves, sems)
        for copy in copies:
            copy.start()
        for copy in copies:
            copy.wait()
        for i in range(tokens // tile):
            rows = pl.ds(i * tile, tile)
            total = in_ref[rows, :].astype(F32) + vec_ref[2:3, :]
            for r in range(n):
                weights = full_ref[aligned(t[plan.MEMBER + r] * cols, cols), :]
                total += dot(refs[r][rows, :], weights)
            unit, _ = statistics(total)
            normed = unit * vec_ref[3:4, :] + vec_ref[4:5, :]
            sum_ref[rows, :] = total
            norm_ref[rows, :] = normed
            low_ref[rows, :] = normed.astype(BF16)

    full = (tokens, width)
    return call(
        kernel,
        table,
        [inputs, vectors, w_out, come, near, far, *others, *pieces],
        [whole_block(full), whole_block(vectors.shape)]
        + [ANY] * 6
        + [whole_block(p.shape) for p in pieces],
        [shape(full, F32), shape(full, F32), shape(full), shape((width, width))],
        [whole_block(full)] * 3 + [whole_block((width, width))],
        (1,),
        [pltpu.SemaphoreType.DMA((n_moves,))],
        7,
        "output_norm",
    )


def flatten(remote):
    arrays, found = [], []
    for near, far in remote:
        found += [(len(arrays), i) for i in range(near.shape[1])]
        arrays += [near, far]
    return arrays, found


def gelu_parts(v):
    big = 0.5 + 0.5 * lax.erf(v * np.float32(np.sqrt(0.5)))
    small = jnp.exp(-0.5 * v * v) * np.float32(1.0 / np.sqrt(2.0 * np.pi))
    return v * big, big + v * small


def up_forward(plan, table, low, other_low, w_up, come, remote, bias):
    n, n_z = plan.n_seq, plan.n_z
    half = n // 2
    tokens, width = low.shape
    own_rows, hidden = w_up.shape
    quarter = hidden // 2 // n
    n_moves = 2 + n_z - 1
    tile = 128

    remote, found = flatten(remote)

    def kernel(t, low_ref, other_ref, up_ref, come_ref, bias_ref, *rest):
        remote_refs, rest = rest[: len(remote)], rest[len(remote) :]
        act_ref, slope_ref, w_hbm, w, sems, out_sem = rest
        step_id = pl.program_id(0)

        def moves(r):
            member = t[plan.MEMBER + r]
            z = t[plan.BEHIND]
            at = w.at[r]

            def row(k):
                return aligned((z * 2 + t[plan.CORE + k]) * own_rows, own_rows)

            lanes = aligned((member * 2 + t[plan.CORE]) * quarter, quarter)
            out = [(up_ref.at[:, lanes], at.at[row(0)])]
            lanes = aligned(member * quarter, quarter)
            out.append((come_ref.at[pl.ds(0, own_rows), lanes], at.at[row(1)]))
            for j in range(1, n_z):
                z_j = t[plan.BEHIND + j]
                a, i = found[j - 1]
                source = remote_refs[a + (r >= half)]
                for k in range(2):
                    rows = aligned((z_j * 2 + t[plan.CORE + k]) * own_rows, own_rows)
                    out.append(
                        (
                            source.at[r % half, i, pl.ds(k * own_rows, own_rows)],
                            at.at[rows],
                        )
                    )
            return out

        def copies(r):
            return copies_of(moves(r), sems.at[r])

        @pl.when(step_id == 0)
        def _():
            for r in range(n):
                for copy in copies(r):
                    copy.start()

        for r in range(n):

            @pl.when(step_id == r)
            def _(r=r):
                for copy in copies(r):
                    copy.wait()

        def out_copy(r):
            return pltpu.make_async_copy(w.at[r], w_hbm.at[r], out_sem.at[r])

        for r in range(n):

            @pl.when(step_id == r)
            def _(r=r):
                out_copy(r).start()

        weights = w.at[step_id]
        for part, source in enumerate((low_ref, other_ref)):

            def step(i, carry, part=part, source=source):
                rows = pl.ds(pl.multiple_of(i * tile, tile), tile)
                pre = dot(source[rows, :], weights[...]) + bias_ref[0]
                active, slope = gelu_parts(pre)
                rows = pl.ds(pl.multiple_of(part * tokens + i * tile, tile), tile)
                act_ref[0, rows, :] = active.astype(BF16)
                slope_ref[0, rows, :] = slope.astype(BF16)
                return carry

            lax.fori_loop(0, tokens // tile, step, 0)

        @pl.when(step_id == n - 1)
        def _():
            for r in range(n):
                out_copy(r).wait()

    big = (n, 2 * tokens, quarter)
    block = pl.BlockSpec((1, 2 * tokens, quarter), lambda r, t: (r, 0, 0))
    return call(
        kernel,
        table,
        [low, other_low, w_up, come, bias] + remote,
        [whole_block(low.shape)] * 2
        + [ANY] * 2
        + [
            pl.BlockSpec(
                (1, 1, quarter),
                lambda r, t: (2 * t[plan.MEMBER + r] + t[plan.CORE], 0, 0),
            )
        ]
        + [ANY] * len(remote),
        [shape(big), shape(big), shape((n, width, quarter))],
        [block, block, ANY],
        (n,),
        [
            pltpu.VMEM((n, width, quarter), BF16),
            pltpu.SemaphoreType.DMA((n, 2 + 2 * (n_z - 1))),
            pltpu.SemaphoreType.DMA((n,)),
        ],
        15,
        "up_forward",
    )


def down_forward(plan, table, active, w_down, remote):
    n, n_z = plan.n_seq, plan.n_z
    half = n // 2
    tokens = active.shape[1] // 2
    quarter = active.shape[2]
    own_hidden, width = w_down.shape
    cols = width // n

    remote, found = flatten(remote)

    def kernel(t, act_ref, down_ref, *rest):
        remote_refs, rest = rest[: len(remote)], rest[len(remote) :]
        own_ref, other_ref, w_hbm, w, acc, sems, out_sem = rest
        step_id = pl.program_id(0)
        out_copy = pltpu.make_async_copy(w, w_hbm, out_sem)

        @pl.when(step_id == 0)
        def _():
            moves = [
                (down_ref, w.at[aligned(t[plan.BEHIND] * own_hidden, own_hidden)])
            ]
            for j in range(1, n_z):
                rows = aligned(t[plan.BEHIND + j] * own_hidden, own_hidden)
                a, i = found[j - 1]
                for r in range(n):
                    source = remote_refs[a + (r >= half)]
                    lanes = aligned(t[plan.MEMBER + r] * cols, cols)
                    moves.append((source.at[r % half, i], w.at[rows, lanes]))
            copies = copies_of(moves, sems)
            for copy in copies:
                copy.start()
            acc[...] = jnp.zeros_like(acc)
            for copy in copies:
                copy.wait()
            out_copy.start()

        rows = aligned(t[plan.MEMBER + step_id] * quarter, quarter)
        acc[...] += dot(act_ref[0], w[rows, :])

        @pl.when(step_id == n - 1)
        def _():
            own_ref[...] = acc[:tokens, :]
            other_ref[...] = acc[tokens:, :].astype(BF16)
            out_copy.wait()

    full = (tokens, width)
    return call(
        kernel,
        table,
        [active, w_down] + remote,
        [pl.BlockSpec((1, 2 * tokens, quarter), lambda r, t: (r, 0, 0))]
        + [ANY] * (1 + len(remote)),
        [shape(full, F32), shape(full), shape((n * quarter, width))],
        [whole_block(full), whole_block(full), ANY],
        (n,),
        [
            pltpu.VMEM((n * quarter, width), BF16),
            pltpu.VMEM((2 * tokens, width), F32),
            pltpu.SemaphoreType.DMA((1 + (n_z - 1) * n,)),
            pltpu.SemaphoreType.DMA,
        ],
        10,
        "down_forward",
    )


def norm_two(table, normed, own, come, cotangent, vectors):
    tokens, width = normed.shape
    tile = 128

    def kernel(t, norm_ref, own_ref, come_ref, cot_ref, vec_ref, *rest):
        out_ref, grad_ref, low_ref, sums = rest

        @pl.when(pl.program_id(0) == 0)
        def _():
            sums[...] = jnp.zeros_like(sums)

        second = norm_ref[...] + (own_ref[...] + come_ref[...].astype(F32) + vec_ref[5:6, :])
        unit, root = statistics(second)
        gain = vec_ref[6:7, :]
        out_ref[...] = (unit * gain + vec_ref[7:8, :]).astype(BF16)
        above = cot_ref[...].astype(F32)
        grad = norm_back(unit, root, gain, above)
        low = grad.astype(BF16)
        grad_ref[...] = grad
        low_ref[...] = low
        add_rows(sums, 0, low.astype(F32))
        add_rows(sums, 1, above * unit)
        add_rows(sums, 2, above)

    block = pl.BlockSpec((tile, width), lambda i, t: (i, 0))
    full = (tokens, width)
    return call(
        kernel,
        table,
        [normed, own, come, cotangent, vectors],
        [block] * 4 + [whole_block(vectors.shape)],
        [shape(full), shape(full, F32), shape(full), shape((8, width), F32)],
        [block] * 3 + [whole_block((8, width))],
        (tokens // tile,),
        [],
        6,
        "norm_two",
    )


def ffn_backward(plan, table, low, other_low, w_down, w_up, slope):
    n = plan.n_seq
    tokens, width = low.shape
    quarter = slope.shape[2]

    def kernel(t, low_ref, other_ref, down_ref, up_ref, slope_ref, *rest):
        pre_ref, sum_ref, own_ref, come_ref, acc = rest
        step_id = pl.program_id(0)

        @pl.when(step_id == 0)
        def _():
            acc[...] = jnp.zeros_like(acc)

        sums = jnp.zeros((1, quarter), F32)
        for part, source in enumerate((low_ref, other_ref)):
            rows = pl.ds(part * tokens, tokens)
            grad = dot(source[...], down_ref[...], 1, 1) * slope_ref[0, rows, :].astype(F32)
            grad = grad.astype(BF16)
            pre_ref[0, rows, :] = grad
            sums += jnp.sum(grad.astype(F32), 0, keepdims=True)
            acc[rows, :] += dot(grad, up_ref[0], 1, 1)
        row = lax.broadcasted_iota(jnp.int32, (8, quarter), 0)
        sum_ref[0] = jnp.where(row == 0, sums, 0.0)

        @pl.when(step_id == n - 1)
        def _():
            own_ref[...] = acc[:tokens, :]
            come_ref[...] = acc[tokens:, :].astype(BF16)

    big = pl.BlockSpec((1, 2 * tokens, quarter), lambda r, t: (r, 0, 0))
    full = (tokens, width)
    return call(
        kernel,
        table,
        [low, other_low, w_down, w_up, slope],
        [whole_block(full)] * 2
        + [
            pl.BlockSpec((quarter, width), lambda r, t: (t[plan.MEMBER + r], 0)),
            pl.BlockSpec((1, width, quarter), lambda r, t: (r, 0, 0)),
            big,
        ],
        [shape(slope.shape), shape((n, 8, quarter), F32), shape(full, F32), shape(full)],
        [
            big,
            pl.BlockSpec((1, 8, quarter), lambda r, t: (r, 0, 0)),
            whole_block(full),
            whole_block(full),
        ],
        (n,),
        [pltpu.VMEM((2 * tokens, width), F32)],
        13,
        "ffn_backward",
    )


def down_weights(plan, table, active, low, other_low, base):
    n, n_z = plan.n_seq, plan.n_z
    half = n // 2
    tokens, width = low.shape
    quarter = active.shape[2]
    cols = width // n

    def kernel(t, act_ref, low_ref, other_ref, out_ref, grads):
        @pl.when(pl.program_id(0) == 0)
        def _():
            for r in range(half):
                lanes = aligned(t[plan.MEMBER + base + r] * cols, cols)
                here = pl.ds(r * cols, cols)
                grads[:tokens, here] = low_ref[:, lanes]
                grads[tokens:, here] = other_ref[:, lanes]

        total = dot(act_ref[0], grads[...], 0, 0)
        for r in range(half):
            out_ref[r, 0] = total[:, r * cols : (r + 1) * cols].astype(BF16)

    return call(
        kernel,
        table,
        [active, low, other_low],
        [pl.BlockSpec((1, 2 * tokens, quarter), lambda r, t: (r, 0, 0))]
        + [whole_block((tokens, width))] * 2,
        [shape((half, n_z, quarter, cols))],
        [
            pl.BlockSpec(
                (half, 1, quarter, cols), lambda r, t: (0, t[plan.MEMBER + r], 0, 0)
            )
        ],
        (n,),
        [pltpu.VMEM((2 * tokens, half * cols), BF16)],
        5,
        "down_weights",
    )[0]


def up_weights(plan, table, low, other_low, grad_pre, base):
    n, n_z = plan.n_seq, plan.n_z
    half = n // 2
    tokens, width = low.shape
    quarter = grad_pre.shape[2]
    own_rows = width // plan.n_dp

    def kernel(t, low_ref, other_ref, grad_ref, out_ref):
        for z in range(n_z):
            lanes = pl.ds(2 * z * own_rows, 2 * own_rows)
            total = dot(low_ref[:, lanes], grad_ref[0, :tokens, :], 0, 0)
            total += dot(other_ref[:, lanes], grad_ref[0, tokens:, :], 0, 0)
            total = total.astype(BF16)
            out_ref[0, z, :, :quarter] = total[:own_rows]
            out_ref[0, z, :, quarter:] = total[own_rows:]

    dims = (half, n_z, own_rows, 2 * quarter)
    return call(
        kernel,
        table,
        [low, other_low, grad_pre],
        [whole_block((tokens, width))] * 2
        + [pl.BlockSpec((1, 2 * tokens, quarter), lambda i, t: (base + i, 0, 0))],
        [shape(dims)],
        [pl.BlockSpec((1,) + dims[1:], lambda i, t: (i, 0, 0, 0))],
        (half,),
        [],
        6,
        "up_weights",
    )[0]


def norm_one_back(plan, table, grad_second, own, come, first_sum, vectors, w_out, sums_two):
    n = plan.n_seq
    tokens, width = own.shape
    cols = width // n
    tile = 128

    own_rows = width // plan.n_dp

    def kernel(t, grad_ref, own_ref, come_ref, sum_ref, vec_ref, w_ref, two_ref, *rest):
        first_ref, low_ref, narrow_ref = rest[:3]
        parts, sums = rest[3:-1], rest[-1]
        sums[0:3, :] = jnp.zeros((3, width), F32)
        sums[3:6, :] = two_ref[0:3, :]
        sums[6:8, :] = jnp.zeros((2, width), F32)
        for i in range(tokens // tile):
            rows = pl.ds(i * tile, tile)
            above = grad_ref[rows, :] + (own_ref[rows, :] + come_ref[rows, :].astype(F32))
            unit, root = statistics(sum_ref[rows, :])
            grad = norm_back(unit, root, vec_ref[3:4, :], above)
            low = grad.astype(BF16)
            first_ref[rows, :] = grad
            low_ref[rows, :] = low
            add_rows(sums, 0, low.astype(F32))
            add_rows(sums, 1, above * unit)
            add_rows(sums, 2, above)
            for r in range(n):
                weights = w_ref[aligned(t[plan.MEMBER + r] * cols, cols), :]
                parts[r][rows, :] = dot(low, weights, 1, 1).astype(BF16)
        narrow_ref[...] = jnp.zeros_like(narrow_ref)
        for owner in range(plan.n_dp):
            lanes = pl.ds(owner * own_rows, own_rows)
            narrow_ref[owner, :, 0:own_rows] = sums[:, lanes]

    full = (tokens, width)
    part = (tokens, cols)
    narrow = (plan.n_dp, 8, 3 * cols)
    return call(
        kernel,
        table,
        [grad_second, own, come, first_sum, vectors, w_out, sums_two],
        [whole_block(full)] * 4
        + [whole_block(v.shape) for v in (vectors, w_out, sums_two)],
        [shape(full, F32), shape(full), shape(narrow, F32)] + [shape(part)] * n,
        [whole_block(full)] * 2 + [whole_block(narrow)] + [whole_block(part)] * n,
        (1,),
        [pltpu.VMEM((8, width), F32)],
        8,
        "norm_one_back",
    )


def out_weights(plan, table, pieces, low):
    n, n_z = plan.n_seq, plan.n_z
    tokens, width = low.shape
    cols = width // n
    own_rows = width // plan.n_dp

    def kernel(t, low_ref, *rest):
        refs, (keep_ref, send_ref, both) = rest[:n], rest[n:]
        for r in range(n):
            z = t[plan.MEMBER + r]
            both[...] = dot(refs[r][...], low_ref[...], 0, 0).astype(BF16)
            for target, k in ((send_ref, 1), (keep_ref, 0)):
                rows = aligned(t[plan.CORE + k] * own_rows, own_rows)
                for s in range(n):
                    at = aligned(t[plan.MEMBERS[k] + s] * cols, cols)
                    target[s, z] = both[rows, at]

    dims = (n, n_z, own_rows, cols)
    return call(
        kernel,
        table,
        [low, *pieces],
        [whole_block(low.shape)] + [whole_block(p.shape) for p in pieces],
        [shape(dims), shape(dims)],
        [whole_block(dims)] * 2,
        (1,),
        [pltpu.VMEM((cols, width), BF16)],
        5,
        "out_weights",
    )


def parts_along_z(plan, table, keep, come):
    n_z = plan.n_z
    rows, lanes = keep.shape[1:]

    def kernel(t, keep_ref, come_ref, *outs):
        total = keep_ref[0].astype(F32) + come_ref[0].astype(F32)
        for j in range(n_z):

            @pl.when(pl.program_id(0) == j)
            def _(j=j):
                outs[j][...] = total.astype(BF16)

    def member(i, t):
        return (t[plan.BEHIND + (2 * n_z - 1 - i) % n_z], 0, 0)

    block = pl.BlockSpec((1, rows, lanes), member)
    return call(
        kernel,
        table,
        [keep, come],
        [block, block],
        [shape((rows, lanes))] * n_z,
        [whole_block((rows, lanes))] * n_z,
        (n_z,),
        [],
        2,
        "parts_along_z",
    )


def split_by_core(plan, table, pieces):
    rows, lanes = pieces[0].shape
    lanes //= 2
    n_pieces = len(pieces)

    def kernel(t, *refs):
        for target, k in zip(refs[n_pieces:], range(2)):
            at = aligned(t[plan.CORE + k] * lanes, lanes)
            total = refs[0][:, at].astype(F32)
            for ref in refs[1:n_pieces]:
                total += ref[:, at].astype(F32)
            target[...] = total.astype(BF16)

    return call(
        kernel,
        table,
        pieces,
        [whole_block(p.shape) for p in pieces],
        [shape((rows, lanes))] * 2,
        [whole_block((rows, lanes))] * 2,
        (1,),
        [],
        2,
        "split_by_core",
    )


def place(plan, table, pieces, outs, moves, name):
    n = plan.n_seq

    def kernel(t, *refs):
        sources, targets = refs[:n], refs[n:]
        for r in range(n):
            for src, o, at in moves:
                targets[o][:, at(t, r)] = sources[r][src].astype(F32)

    return call(
        kernel,
        table,
        pieces,
        [whole_block(p.shape) for p in pieces],
        [shape(o, F32) for o in outs],
        [whole_block(o) for o in outs],
        (1,),
        [],
        2,
        name,
    )


def local(
    plan,
    inputs,
    w_query,
    w_key,
    w_value,
    b_query,
    b_value,
    w_out,
    b_out,
    gain_one,
    shift_one,
    w_up,
    b_up,
    w_down,
    b_down,
    gain_two,
    shift_two,
    cotangent,
):
    n_dp, n, n_z = plan.n_dp, plan.n_seq, plan.n_z
    half = n // 2
    seqs, length, width = inputs.shape
    tokens = seqs * length
    own_rows, hidden = w_up.shape
    own_hidden = w_down.shape[0]
    cols = width // n
    cols3 = 3 * cols
    quarter = hidden // 2 // n
    assert n == n_z and quarter == own_hidden
    table = plan.row()
    core = lax.axis_index("dp") % 2

    narrow = jnp.stack(
        [b_query, b_value, b_out, gain_one, shift_one, b_down, gain_two, shift_two]
    )
    vec = jnp.concatenate(
        [
            jnp.pad(narrow, ((0, 0), (0, 4 * cols - own_rows))),
            jnp.pad(b_up[None], ((0, 7), (0, 4 * cols - own_hidden))),
        ],
        0,
    )

    def column_block(t):
        return (pl.ds(0, own_rows), aligned(t[plan.MEMBER] * cols, cols))

    moves = [
        (i, column_block, 0, lambda t, i=i: (pl.ds(0, own_rows), pl.ds(i * cols, cols)))
        for i in range(4)
    ]
    moves.append((4, lambda t: (pl.ds(0, PAD),), 0, lambda t: (pl.ds(own_rows, PAD),)))
    (first,) = assemble(
        table,
        [w_query, w_key, w_value, w_out, vec],
        moves,
        [shape((own_rows + PAD, 4 * cols))],
        "pack_first",
    )

    def straight(block, j):
        return lax.ppermute(block, BOTH, plan.toward[j])

    near_x = inputs[None]
    for k in range(plan.bits - 1):
        near_x = plan.double(near_x, k)
    mine = [first, straight(first, 1)]

    moves = []
    for z in range(n_z):
        moves.append(
            (
                0,
                lambda t, z=z: (
                    pl.ds(0, own_rows),
                    aligned((2 * z + t[plan.CORE + 1]) * quarter, quarter),
                ),
                0,
                lambda t, z=z: (pl.ds(0, own_rows), pl.ds(z * quarter, quarter)),
            )
        )
    moves.append(
        (
            1,
            lambda t: (pl.ds(0, own_rows),),
            0,
            lambda t: (pl.ds(0, own_rows), pl.ds(n * quarter, width)),
        )
    )
    (across,) = assemble(
        table,
        [after(w_up, mine[1]), w_out],
        moves,
        [shape((own_rows, n * quarter + width))],
        "pack_across",
    )
    come = plan.swap(across)

    top = plan.bits - 1

    def final(near, *ready):
        return near, lax.ppermute(after(near, *ready), BOTH, plan.stage[top])

    def begin(block, *ready):
        near = after(block, *ready)[None]
        for k in range(top - 1):
            near = plan.double(near, k)
        return near, lax.ppermute(near, BOTH, plan.stage[top - 1])

    def joined(started, *ready):
        return jnp.concatenate([after(started[0], *ready), started[1]], 0)

    def onward(block, *ready):
        return lax.ppermute(after(block, *ready), BOTH, plan.toward[1])

    ready = (near_x, mine[1])
    far_x = final(near_x, *ready)[1]
    mine += [straight(after(first, *ready), j) for j in range(2, n_z)]

    def rows_at(start, size):
        return lambda t: (pl.ds(start, size), pl.ds(0, quarter))

    moves = [
        (
            0,
            lambda t: (
                pl.ds(0, own_rows),
                aligned((2 * t[plan.MEMBER] + t[plan.CORE]) * quarter, quarter),
            ),
            0,
            rows_at(0, own_rows),
        ),
        (
            1,
            lambda t: (pl.ds(0, own_rows), aligned(t[plan.MEMBER] * quarter, quarter)),
            0,
            rows_at(own_rows, own_rows),
        ),
    ]
    moves.append(
        (
            2,
            lambda t: (pl.ds(0, own_hidden), aligned(t[plan.MEMBER] * cols, cols)),
            1,
            lambda t: (pl.ds(0, own_hidden),),
        )
    )
    second, down = assemble(
        table,
        [w_up, come, w_down],
        moves,
        [shape((2 * own_rows, quarter)), shape((own_hidden, cols))],
        "pack_second",
    )
    ups = [onward(second)]

    ready = (far_x, second) + tuple(mine[1:])
    mine_all = jnp.stack([after(piece, *ready) for piece in mine])
    theirs = plan.swap(mine_all)
    outs = jnp.stack([after(piece, *ready)[:own_rows, cols3:] for piece in mine[1:]])
    outs_started = begin(outs)
    ups.append(onward(ups[0], *ready))
    downs = [onward(down, *ready)]
    w_qkv, vectors, up_bias = head_weights(plan, table, mine_all, theirs)
    qkv = []

    def attend(g, before, *ready):
        out, *parts = attention_forward(
            plan, table, g, near_x, far_x, w_qkv, after(vectors, *ready), before
        )
        qkv.append(out)
        return parts

    parts = attend(0, [])

    near_out = joined(outs_started, parts[0])
    ready = (near_out, parts[0], ups[1], downs[0])
    outs = final(near_out, *ready)
    ups.append(onward(ups[1], *ready))
    downs.append(onward(downs[0], *ready))
    two_started = begin(jnp.stack([after(piece, *ready) for piece in ups[:2]]))
    parts = attend(1, parts, *ready)

    near_two = joined(two_started, parts[0])
    ready = (near_two, outs[1], ups[2], downs[1], parts[0])
    for j in range(3, n_z - 1):
        ups.append(onward(ups[-1]))
        downs.append(onward(downs[-1]))
    others = [plan.swap(after(part, *ready)) for part in outs]
    up_two = final(near_two, *ready)
    downs.append(onward(downs[-1], *ready))
    three_started = begin(jnp.stack([after(piece, *ready) for piece in ups[2:]]))
    for g in range(2, seqs):
        parts = attend(g, parts, *ready)

    pieces = [p.reshape(tokens, cols) for p in plan.trade(parts)]
    near_three = joined(three_started, parts[0])
    ready = (parts[0], up_two[1], near_three, downs[-1]) + tuple(others)
    downs = jnp.stack([after(piece, *ready) for piece in downs])
    ready += (downs,) + tuple(pieces)
    up_three = final(near_three, *ready)
    downs_started = begin(downs, *ready)
    first_sum, normed, low, full_out = output_norm(
        plan,
        table,
        pieces,
        after(inputs.reshape(tokens, width), downs),
        vectors,
        w_out,
        come,
        *outs,
        others,
    )

    other_low = plan.swap(low)
    near_down = joined(downs_started, low)
    ready = (other_low, up_three[1], near_down)
    down_all = final(near_down, *ready)
    active, slope, up_kept = up_forward(
        plan, table, after(low, *ready), other_low, w_up, come, [up_two, up_three], up_bias
    )
    own, away, down_kept = down_forward(plan, table, active, w_down, [down_all])
    output, grad_second, low_two, sums_two = norm_two(
        table, normed, own, plan.swap(away), cotangent.reshape(tokens, width), vectors
    )

    def begun(send, k, *ready):
        return lax.ppermute(after(send, *ready), BOTH, plan.stage[k])

    def summed(keep, come, k, *ready):
        low = (1 << k) // 2
        come = after(come, *ready)
        return add(keep[:low], come[:low]), add(keep[low:], come[low:])

    def middle(keep, come, *ready):
        keep, send = summed(keep, come, top, *ready)
        for k in reversed(range(1, top)):
            keep, send = summed(keep, begun(send, k), k)
        return keep, send

    other_two = plan.swap(low_two)
    down_send = down_weights(plan, table, active, low_two, other_two, half)
    down_come = begun(down_send, top)
    down_keep = down_weights(plan, table, active, after(low_two, down_send), other_two, 0)
    grad_pre, sums_up, own, away = ffn_backward(
        plan, table, after(low_two, down_keep), other_two, down_kept, up_kept, slope
    )
    away = plan.swap(away)
    low = after(low, own)
    up_send = up_weights(plan, table, low, other_low, grad_pre, half)
    up_come = begun(up_send, top)
    down_keep, down_send = middle(down_keep, down_come, up_send)
    down_last = begun(down_send, 0)
    up_keep = up_weights(plan, table, after(low, up_send, down_send), other_low, grad_pre, 0)
    grad_first, low_one, sums, *parts = norm_one_back(
        plan,
        table,
        grad_second,
        after(own, up_keep),
        away,
        first_sum,
        vectors,
        full_out,
        sums_two,
    )
    parts = plan.trade([p.reshape(seqs, length, cols) for p in parts])
    out_keep, out_send = out_weights(plan, table, pieces, low_one)
    out_come = plan.swap(out_send)
    def sent_along_z(keep, come, *ready):
        *away, own = parts_along_z(plan, table, after(keep, *ready), come)
        return [own] + [
            lax.ppermute(part, BOTH, way) for part, way in zip(away, plan.toward[1:])
        ]

    def total(terms, *ready):
        out = after(terms[0], *ready).astype(F32)
        for piece in terms[1:]:
            out += piece.astype(F32)
        return out.astype(BF16)

    def back(g, before, *ready):
        return attention_backward(
            plan, table, g, seqs, after(qkv[g], *ready), parts, w_qkv, before
        )

    ready = (out_keep, out_come, down_last, up_come) + tuple(parts)
    up_keep, up_send = middle(up_keep, up_come, *ready)
    up_last = begun(up_send, 0)
    down_along = sent_along_z(down_keep[0], down_last[0], *ready)
    out_come = after(out_come, *ready)
    out_kept = add(out_keep[:half], out_come[:half])
    out_sent = add(out_keep[half:], out_come[half:])
    out_first = begun(out_sent, top)
    shared = back(0, [], out_sent, up_send, *ready)
    out_kept, out_sent = middle(out_kept, out_first, shared[0])
    out_last = begun(out_sent, 0)
    grad_down = total(down_along, shared[0])
    ready = (grad_down, up_last, out_sent, shared[0])
    up_along = sent_along_z(up_keep[0], up_last[0], *ready)
    grad_down = plan.share(after(grad_down, *ready))
    shared = back(1, list(shared), *ready)
    ready = (out_last, shared[0]) + tuple(grad_down)
    out_along = sent_along_z(out_kept[0], out_last[0], *ready)
    for g in range(2, seqs):
        shared = back(g, list(shared), *ready)
    grad_qkv, part_keep, part_send = shared

    part_come = begun(part_send, top)
    up_along = [after(up_along[0], part_send)] + up_along[1:]
    up_kept, up_sent = split_by_core(plan, table, up_along)
    up_come = plan.swap(up_sent)
    last_keep, last_send = head_weights_backward(
        plan, table, near_x, far_x, after(grad_qkv, up_kept), sums, sums_up
    )
    last_come = plan.swap(last_send)
    ready = (last_keep, last_send)
    grad_up = jnp.concatenate(
        [after(up_kept, *ready), up_come, total(out_along, *ready)], 1
    )
    last_along = sent_along_z(last_keep, last_come)
    part_keep, part_send = middle(part_keep, part_come, last_come)
    part_last = begun(part_send, 0)
    grad_up = plan.share(after(grad_up, part_send))

    def lanes(size):
        return lambda t, r: aligned(t[plan.MEMBER + r] * size, size)

    grad_inputs = grad_first.reshape(inputs.shape) + (
        part_keep[0].astype(F32) + part_last[0].astype(F32)
    )
    (grad_down,) = place(
        plan,
        table,
        [after(v, part_send) for v in grad_down],
        [(own_hidden, width)],
        [((slice(None),), 0, lanes(cols))],
        "place_down",
    )
    grad_up, grad_out = place(
        plan,
        table,
        grad_up,
        [(own_rows, hidden), (own_rows, width)],
        [
            (
                (slice(None), pl.ds(k * quarter, quarter)),
                0,
                lambda t, r, k=k: aligned(
                    (2 * t[plan.MEMBER + r] + t[plan.CORE + k]) * quarter, quarter
                ),
            )
            for k in range(2)
        ]
        + [((slice(None), pl.ds(2 * quarter, cols)), 1, lanes(cols))],
        "place_up",
    )
    grad_last = plan.share(total(last_along, grad_down, grad_inputs))
    grad_wq, grad_wk, grad_wv = place(
        plan,
        table,
        grad_last,
        [(own_rows, width)] * 3,
        [
            ((pl.ds(0, own_rows), pl.ds(m * cols, cols)), m, lanes(cols))
            for m in range(3)
        ],
        "place_heads",
    )
    vec_out = sum(piece[own_rows:].astype(F32) for piece in grad_last)
    biases = vec_out[7].reshape(3, 2, own_rows)
    biases = jnp.where(core == 0, biases[:, 0], biases[:, 1])
    return (
        output.reshape(inputs.shape),
        grad_inputs,
        grad_wq,
        grad_wk,
        grad_wv,
        biases[0],
        biases[2],
        grad_out,
        vec_out[0, :own_rows],
        vec_out[1, :own_rows],
        vec_out[2, :own_rows],
        grad_up,
        vec_out[8, :own_hidden],
        grad_down,
        vec_out[3, :own_rows],
        vec_out[4, :own_rows],
        vec_out[5, :own_rows],
    )


def solution(mesh):
    plan = Plan(mesh.shape["dp"], mesh.shape["seq"])
    rows, vector, token = P("dp", None), P("dp"), P("dp", "seq", None)
    weights = (rows,) * 3 + (vector,) * 2 + (rows,) + (vector,) * 3
    weights += (rows, vector, rows) + (vector,) * 3
    return jax.shard_map(
        functools.partial(local, plan),
        mesh=mesh,
        in_specs=(token,) + weights + (token,),
        out_specs=(token, token) + weights,
        check_vma=False,
    )
```

time: 566 us -> 408 us (0.72)
  Pallas kernels: 29.3 us -> 205 us
  local copies, waits for them, and re-layouts: 124 us -> 11.8 us
  matrix products: 83.7 us -> 0 us
  other arithmetic: 90.5 us -> 16.8 us
  waiting for transfers between devices: 161 us -> 87.3 us
  starting transfers between devices: 43.4 us -> 78.3 us
  between operations: 23.9 us -> 1.74 us
    pallas_call x8 -> x30, Pallas kernels: 29.3 us -> 205 us  [call(): pl.pallas_call(kernel, out_shape=list(outs), grid_spec=pltpu.PrefetchScal...]
    dot_general x18 -> x0, matrix products: 83.7 us -> none  [the longest x12 53.5 us: dot(): lax.dot_general(former, latter, (((former_dim,), (latter_dim,)), ((), ())...]
    ppermute x42 -> x54, waiting for transfers between devices: 159 us -> 82.5 us  [the longest x3 16.2 us: straight(): return lax.ppermute(block, BOTH, plan.toward[j])]
    ppermute x42 -> x54, starting transfers between devices: 42.6 us -> 76.4 us  [the longest x12 20.3 us: sent_along_z(): lax.ppermute(part, BOTH, way)]
    dynamic_slice x19 -> x0, local copies, waits for them, and re-layouts: 30.9 us -> none  [the longest x7 18.6 us: pick(): lax.dynamic_index_in_dim(array, i, axis, False)]
    reshape x17 -> x0, local copies, waits for them, and re-layouts: 30.3 us -> none  [the longest x8 13.5 us: to_rows(): v = v.reshape(seqs, heads, n_seq, length, HEAD_DIM)]
    convert_element_type x22 -> x5, other arithmetic: 33.4 us -> 3.99 us  [the longest x3 2.47 us: total(): return out.astype(BF16)]
    concatenate x17 -> x3, other arithmetic: 22.9 us -> 0.79 us  [the longest x1 0.62 us: local(): jnp.concatenate([jnp.pad(narrow, ((0, 0), (0, 4 * cols - own_rows))), jnp...]
  transfers between devices with their start and end apart: 52 -> 65, of which waited for: 22 -> 21; matrix products, arithmetic and copies ran while one was open for 43% -> 4% of each run, Pallas kernels for 5% -> 43%
where the time goes in v2:
time: 408 us; the launch traced here: 401 us
  Pallas kernels  205 us (50%)
  waiting for transfers between devices  87.3 us (21%)
  starting transfers between devices  78.3 us (19%)
  other arithmetic  16.8 us (4%)
  local copies, waits for them, and re-layouts  11.8 us (3%)
    pallas_call x30, Pallas kernels, call(): pl.pallas_call(kernel, out_shape=list(outs), grid_spec=pltpu.PrefetchScal...  205 us
    ppermute x12, starting transfers between devices, sent_along_z(): lax.ppermute(part, BOTH, way)  20.3 us
    ppermute x3, waiting for transfers between devices, straight(): return lax.ppermute(block, BOTH, plan.toward[j])  16.2 us
    ppermute x6, waiting for transfers between devices, trade(): lax.ppermute(block, BOTH, way)  14.8 us
    ppermute x6, starting transfers between devices, onward(): return lax.ppermute(after(block, *ready), BOTH, plan.toward[1])  13.5 us
    ppermute x12, waiting for transfers between devices, sent_along_z(): lax.ppermute(part, BOTH, way)  13.4 us
    ppermute x8, waiting for transfers between devices, begun(): return lax.ppermute(after(send, *ready), BOTH, plan.stage[k])  12.4 us
    ppermute x5, waiting for transfers between devices, final(): return (near, lax.ppermute(after(near, *ready), BOTH, plan.stage[top]))  10.8 us
  transfers between devices with their start and end apart: 65, of which 21 were waited for; matrix products, arithmetic and copies ran while one was open for 4% of the time, Pallas kernels for 43%

profile of v2, /device:TPU:0, one launch (start us, length us, event | category | flops | bytes accessed | tf_op | source)
XLA Modules:
  0.0 401.3 jit_solution(3701017369360017027)
XLA Ops:
  14.0 5.1 %collective-permute-done = bf16[144,1024]{1,0:T(8,128)(2,1)S(1)} collective-permute-done((bf16[144,1024]{1,0:T(8,128)(2,1)}, bf16[144,1024]{1,0:T(8,128)(2,1)S(1)}, u32[]{:S(2)}, u32[]{:S(2)}) %collective-permute-start) | collective-permute-done | bytes 294944 | tf_op jit(solution)/shard_map/ppermute | solution.py:1112
  32.2 8.0 %collective-permute-done.4 = bf16[144,1024]{1,0:T(8,128)(2,1)S(1)} collective-permute-done((bf16[144,1024]{1,0:T(8,128)(2,1)S(1)}, bf16[144,1024]{1,0:T(8,128)(2,1)S(1)}, u32[]{:S(2)}, u32[]{:S(2)}) %collective-permute-start.4) | collective-permute-done | bytes 294944 | tf_op jit(solution)/shard_map/ppermute | solution.py:1112
  40.5 6.8 %collective-permute-start.8 = (bf16[256,512]{1,0:T(8,128)(2,1)S(1)}, bf16[256,512]{1,0:T(8,128)(2,1)S(1)}, u32[]{:S(2)}, u32[]{:S(2)}) collective-permute-start(bf16[256,512]{1,0:T(8,128)(2,1)S(1)} %copy-done.35), channel_id=1, source_target_pairs={{0,8},{1,9},{2,10},{3,11},{4,12},{5,13},{6,14},{7,15},{8,24},{9,25... | collective-permute-start | bytes 786440 | tf_op jit(solution)/shard_map/ppermute | solution.py:1164
  47.3 7.1 %collective-permute-done.8 = bf16[256,512]{1,0:T(8,128)(2,1)S(1)} collective-permute-done((bf16[256,512]{1,0:T(8,128)(2,1)S(1)}, bf16[256,512]{1,0:T(8,128)(2,1)S(1)}, u32[]{:S(2)}, u32[]{:S(2)}) %collective-permute-start.8) | collective-permute-done | bytes 262176 | tf_op jit(solution)/shard_map/ppermute | solution.py:1164
  62.3 11.1 %attention_forward.3 = (bf16[512,768]{1,0:T(8,128)(2,1)}, bf16[3,128,256]{2,1,0:T(8,128)(2,1)}, bf16[3,128,256]{2,1,0:T(8,128)(2,1)}, bf16[3,128,256]{2,1,0:T(8,128)(2,1)}, bf16[3,128,256]{2,1,0:T(8,128)(2,1)}) custom-call(s32[14]{0:T(128)} %dynamic-slice_bitcast_fusion.table_ref.t, bf16[2,3,128,1024]{3,2,1,0:T(8,128)(2,1)} %copy-done, ...), custom_call_target="tpu_custom_call" | custom-call | flops 12099999744 | bytes 6324224 | tf_op jit(solution)/shard_map/attention_forward/pallas_call | solution.py:134
  77.9 11.1 %attention_forward.4 = (bf16[512,768]{1,0:T(8,128)(2,1)}, bf16[3,128,256]{2,1,0:T(8,128)(2,1)}, bf16[3,128,256]{2,1,0:T(8,128)(2,1)}, bf16[3,128,256]{2,1,0:T(8,128)(2,1)}, bf16[3,128,256]{2,1,0:T(8,128)(2,1)}) custom-call(s32[14]{0:T(128)} %dynamic-slice_bitcast_fusion.table_ref.t, ...), custom_call_target="tpu_custom_call", output_to_operand_aliasing={{1}: (5, {}), {2}: (6, {}), {3}: (7, {}), {4}: (8, {})} | custom-call | flops 12099999744 | bytes 7110656 | tf_op jit(solution)/shard_map/attention_forward/pallas_call | solution.py:134
  93.3 11.3 %attention_forward.5 = (bf16[512,768]{1,0:T(8,128)(2,1)}, bf16[3,128,256]{2,1,0:T(8,128)(2,1)}, bf16[3,128,256]{2,1,0:T(8,128)(2,1)}, bf16[3,128,256]{2,1,0:T(8,128)(2,1)}, bf16[3,128,256]{2,1,0:T(8,128)(2,1)}) custom-call(s32[14]{0:T(128)} %dynamic-slice_bitcast_fusion.table_ref.t, ...), custom_call_target="tpu_custom_call", output_to_operand_aliasing={{1}: (5, {}), {2}: (6, {}), {3}: (7, {}), {4}: (8, {})} | custom-call | flops 12099999744 | bytes 7110656 | tf_op jit(solution)/shard_map/attention_forward/pallas_call | solution.py:134
  119.0 7.0 %output_norm.1 = (f32[384,1024]{1,0:T(8,128)}, f32[384,1024]{1,0:T(8,128)}, bf16[384,1024]{1,0:T(8,128)(2,1)}, bf16[1024,1024]{1,0:T(8,128)(2,1)}) custom-call(s32[14]{0:T(128)} %dynamic-slice_bitcast_fusion.table_ref.t, bf16[384,1024]{1,0:T(8,128)(2,1)} %bitcast.80, f32[8,1024]{1,0:T(8,128)} %get-tuple-element.183.vec_ref, bf16[128,1024]{1,0:T(8,128)(2,1)} %w_ref.1, ...), custom_call_target="tpu_custom_call" | custom-call | flops 7699999744 | bytes 10256384 | tf_op jit(solution)/shard_map/output_norm/pallas_call | solution.py:134
  129.6 5.8 %collective-permute-done.24.rest_3_ = bf16[2,1,256,512]{3,2,1,0:T(8,128)(2,1)S(1)} collective-permute-done((bf16[2,1,256,512]{3,2,1,0:T(8,128)(2,1)}, bf16[2,1,256,512]{3,2,1,0:T(8,128)(2,1)S(1)}, u32[]{:S(2)}, u32[]{:S(2)}) %collective-permute-start.24) | collective-permute-done | bytes 524320 | tf_op jit(solution)/shard_map/ppermute | solution.py:1152
  136.8 15.0 %up_forward.1 = (bf16[4,768,512]{2,1,0:T(8,128)(2,1)}, bf16[4,768,512]{2,1,0:T(8,128)(2,1)}, bf16[4,1024,512]{2,1,0:T(8,128)(2,1)}) custom-call(s32[14]{0:T(128)} %dynamic-slice_bitcast_fusion.table_ref.t, bf16[384,1024]{1,0:T(8,128)(2,1)} %get-tuple-element.224.low_ref, bf16[384,1024]{1,0:T(8,128)(2,1)} %collective-permute-done.23.other_ref, ...), custom_call_target="tpu_custom_call" | custom-call | flops 16499999744 | bytes 17055744 | tf_op jit(solution)/shard_map/up_forward/pallas_call | solution.py:134
  151.8 5.0 %collective-permute-done.26.rest_1_ = bf16[2,3,512,256]{3,2,1,0:T(8,128)(2,1)} collective-permute-done((bf16[2,3,512,256]{3,2,1,0:T(8,128)(2,1)S(1)}, bf16[2,3,512,256]{3,2,1,0:T(8,128)(2,1)}, u32[]{:S(2)}, u32[]{:S(2)}) %collective-permute-start.26) | collective-permute-done | bytes 1572896 | tf_op jit(solution)/shard_map/ppermute | solution.py:1152
  156.8 10.3 %down_forward.1 = (f32[384,1024]{1,0:T(8,128)}, bf16[384,1024]{1,0:T(8,128)(2,1)}, bf16[2048,1024]{1,0:T(8,128)(2,1)}) custom-call(s32[14]{0:T(128)} %dynamic-slice_bitcast_fusion.table_ref.t, bf16[4,768,512]{2,1,0:T(8,128)(2,1)} %get-tuple-element.208.act_ref, bf16[512,1024]{1,0:T(8,128)(2,1)} %down_ref.1, bf16[2,3,512,256]{3,2,1,0:T(8,128)(2,1)} %copy-done.6, ...), custom_call_target="tpu_custom_call" | custom-call | flops 11000000512 | bytes 13893632 | tf_op jit(solution)/shard_map/down_forward/pallas_call | solution.py:134
  170.5 6.1 %norm_two.1 = (bf16[384,1024]{1,0:T(8,128)(2,1)}, f32[384,1024]{1,0:T(8,128)}, bf16[384,1024]{1,0:T(8,128)(2,1)}, f32[8,1024]{1,0:T(8,128)}) custom-call(s32[14]{0:T(128)} %dynamic-slice_bitcast_fusion.table_ref.t, f32[384,1024]{1,0:T(8,128)} %get-tuple-element.201.norm_ref, f32[384,1024]{1,0:T(8,128)} %get-tuple-element.210.own_ref, ...), custom_call_target="tpu_custom_call" | custom-call | flops 6600000000 | bytes 7929856 | tf_op jit(solution)/shard_map/norm_two/pallas_call | solution.py:134
  180.1 6.4 %down_weights.2 = bf16[2,4,512,256]{3,2,1,0:T(8,128)(2,1)} custom-call(s32[14]{0:T(128)} %dynamic-slice_bitcast_fusion.table_ref.t, bf16[4,768,512]{2,1,0:T(8,128)(2,1)} %get-tuple-element.208.act_ref, bf16[384,1024]{1,0:T(8,128)(2,1)} %get-tuple-element.216.low_ref, bf16[384,1024]{1,0:T(8,128)(2,1)} %copy-done.22), custom_call_target="tpu_custom_call" | custom-call | flops 5500000256 | bytes 6815744 | tf_op jit(solution)/shard_map/down_weights/pallas_call | solution.py:134
  187.0 6.4 %down_weights.3 = bf16[2,4,512,256]{3,2,1,0:T(8,128)(2,1)} custom-call(s32[14]{0:T(128)} %dynamic-slice_bitcast_fusion.table_ref.t, bf16[4,768,512]{2,1,0:T(8,128)(2,1)} %get-tuple-element.208.act_ref, bf16[384,1024]{1,0:T(8,128)(2,1)} %get-tuple-element.216.low_ref, bf16[384,1024]{1,0:T(8,128)(2,1)} %copy-done.22), custom_call_target="tpu_custom_call" | custom-call | flops 5500000256 | bytes 6815744 | tf_op jit(solution)/shard_map/down_weights/pallas_call | solution.py:134
  193.5 13.3 %ffn_backward.1 = (bf16[4,768,512]{2,1,0:T(8,128)(2,1)}, f32[4,8,512]{2,1,0:T(8,128)}, f32[384,1024]{1,0:T(8,128)}, bf16[384,1024]{1,0:T(8,128)(2,1)}) custom-call(s32[14]{0:T(128)} %dynamic-slice_bitcast_fusion.table_ref.t, bf16[384,1024]{1,0:T(8,128)(2,1)} %get-tuple-element.216.low_ref, bf16[384,1024]{1,0:T(8,128)(2,1)} %copy-done.22, ...), custom_call_target="tpu_custom_call" | custom-call | flops 14300000256 | bytes 18677760 | tf_op jit(solution)/shard_map/ffn_backward/pallas_call | solution.py:134
  206.8 5.9 %up_weights.2 = bf16[2,4,128,1024]{3,2,1,0:T(8,128)(2,1)} custom-call(s32[14]{0:T(128)} %dynamic-slice_bitcast_fusion.table_ref.t, bf16[384,1024]{1,0:T(8,128)(2,1)} %get-tuple-element.224.low_ref, bf16[384,1024]{1,0:T(8,128)(2,1)} %collective-permute-done.23.other_ref, bf16[4,768,512]{2,1,0:T(8,128)(2,1)} %get-tuple-element.222.grad_ref), custom_call_target="tpu_custom_call" | custom-call | flops 6600000000 | bytes 6815744 | tf_op jit(solution)/shard_map/up_weights/pallas_call | solution.py:134
  218.3 6.0 %up_weights.3 = bf16[2,4,128,1024]{3,2,1,0:T(8,128)(2,1)} custom-call(s32[14]{0:T(128)} %dynamic-slice_bitcast_fusion.table_ref.t, bf16[384,1024]{1,0:T(8,128)(2,1)} %get-tuple-element.224.low_ref, bf16[384,1024]{1,0:T(8,128)(2,1)} %collective-permute-done.23.other_ref, bf16[4,768,512]{2,1,0:T(8,128)(2,1)} %get-tuple-element.222.grad_ref), custom_call_target="tpu_custom_call" | custom-call | flops 6600000000 | bytes 6815744 | tf_op jit(solution)/shard_map/up_weights/pallas_call | solution.py:134
  225.8 8.0 %norm_one_back.1 = (f32[384,1024]{1,0:T(8,128)}, bf16[384,1024]{1,0:T(8,128)(2,1)}, f32[8,8,768]{2,1,0:T(8,128)}, bf16[384,256]{1,0:T(8,128)(2,1)}, bf16[384,256...) custom-call(s32[14]{0:T(128)} %dynamic-slice_bitcast_fusion.table_ref.t, ...), custom_call_target="tpu_custom_call" | custom-call | flops 8800000000 | bytes 11010048 | tf_op jit(solution)/shard_map/norm_one_back/pallas_call | solution.py:134
  233.8 4.9 %out_weights.1 = (bf16[4,4,128,256]{3,2,1,0:T(8,128)(2,1)}, bf16[4,4,128,256]{3,2,1,0:T(8,128)(2,1)}) custom-call(s32[14]{0:T(128)} %dynamic-slice_bitcast_fusion.table_ref.t, bf16[384,1024]{1,0:T(8,128)(2,1)} %get-tuple-element.232.low_ref, bf16[384,256]{1,0:T(8,128)(2,1)} %bitcast.120, bf16[384,256]{1,0:T(8,128)(2,1)} %bitcast.107, ...), custom_call_target="tpu_custom_call" | custom-call | flops 5500000256 | bytes 3670016 | tf_op jit(solution)/shard_map/out_weights/pallas_call | solution.py:134
  240.7 10.1 %collective-permute-done.33 = bf16[2,4,128,1024]{3,2,1,0:T(8,128)(2,1)S(1)} collective-permute-done((bf16[2,4,128,1024]{3,2,1,0:T(8,128)(2,1)}, bf16[2,4,128,1024]{3,2,1,0:T(8,128)(2,1)S(1)}, u32[]{:S(2)}, u32[]{:S(2)}) %collective-permute-start.33) | collective-permute-done | bytes 2097184 | tf_op jit(solution)/shard_map/ppermute | solution.py:1278
  263.6 4.3 %parts_along_z.4 = (bf16[512,256]{1,0:T(8,128)(2,1)}, bf16[512,256]{1,0:T(8,128)(2,1)}, bf16[512,256]{1,0:T(8,128)(2,1)}, bf16[512,256]{1,0:T(8,128)(2,1)}) custom-call(s32[14]{0:T(128)} %dynamic-slice_bitcast_fusion.table_ref.t, bf16[4,512,256]{2,1,0:T(8,128)(2,1)} %get-tuple-element.246.keep_ref, bf16[4,512,256]{2,1,0:T(8,128)(2,1)} %bitcast.40.come_ref), custom_call_target="tpu_custom_call" | custom-call | flops 2200000000 | bytes 3145728 | tf_op jit(solution)/shard_map/parts_along_z/pallas_call | solution.py:134
  273.7 11.4 %attention_backward.3 = (bf16[3,512,768]{2,1,0:T(8,128)(2,1)}, bf16[2,3,128,1024]{3,2,1,0:T(8,128)(2,1)}, bf16[2,3,128,1024]{3,2,1,0:T(8,128)(2,1)}) custom-call(s32[14]{0:T(128)} %dynamic-slice_bitcast_fusion.table_ref.t, bf16[512,768]{1,0:T(8,128)(2,1)} %get-tuple-element.242.qkv_ref, bf16[1024,768]{1,0:T(8,128)(2,1)} %get-tuple-element.168.w_ref, ...), custom_call_target="tpu_custom_call" | custom-call | flops 12099999744 | bytes 8650752 | tf_op jit(solution)/shard_map/attention_backward/pallas_call | solution.py:134
  285.1 4.4 %collective-permute-done.39 = bf16[512,256]{1,0:T(8,128)(2,1)S(1)} collective-permute-done((bf16[512,256]{1,0:T(8,128)(2,1)}, bf16[512,256]{1,0:T(8,128)(2,1)S(1)}, u32[]{:S(2)}, u32[]{:S(2)}) %collective-permute-start.39) | collective-permute-done | bytes 262176 | tf_op jit(solution)/shard_map/ppermute | solution.py:1322
  295.9 4.2 %parts_along_z.5 = (bf16[128,1024]{1,0:T(8,128)(2,1)}, bf16[128,1024]{1,0:T(8,128)(2,1)}, bf16[128,1024]{1,0:T(8,128)(2,1)}, bf16[128,1024]{1,0:T(8,128)(2,1)}) custom-call(s32[14]{0:T(128)} %dynamic-slice_bitcast_fusion.table_ref.t, bf16[4,128,1024]{2,1,0:T(8,128)(2,1)} %get-tuple-element.263.keep_ref, bf16[4,128,1024]{2,1,0:T(8,128)(2,1)} %bitcast.103), custom_call_target="tpu_custom_call" | custom-call | flops 2200000000 | bytes 3145728 | tf_op jit(solution)/shard_map/parts_along_z/pallas_call | solution.py:134
  300.1 4.2 %collective-permute-start.47 = (bf16[128,1024]{1,0:T(8,128)(2,1)}, bf16[128,1024]{1,0:T(8,128)(2,1)S(1)}, u32[]{:S(2)}, u32[]{:S(2)}) collective-permute-start(bf16[128,1024]{1,0:T(8,128)(2,1)} %get-tuple-element.266), channel_id=1, source_target_pairs={{0,8},{1,9},{2,10},{3,11},{4,12},{5,13},{6,14},{7,15},{8,24},{9,25... | collective-permute-start | bytes 786440 | tf_op jit(solution)/shard_map/ppermute | solution.py:1322
  304.3 11.8 %attention_backward.4 = (bf16[3,512,768]{2,1,0:T(8,128)(2,1)}, bf16[2,3,128,1024]{3,2,1,0:T(8,128)(2,1)}, bf16[2,3,128,1024]{3,2,1,0:T(8,128)(2,1)}) custom-call(s32[14]{0:T(128)} %dynamic-slice_bitcast_fusion.table_ref.t, bf16[512,768]{1,0:T(8,128)(2,1)} %get-tuple-element.252.qkv_ref, ...), custom_call_target="tpu_custom_call", output_to_operand_aliasing={{0}: (7, {}), {1}: (8, {}), {2}: (9, {})} | custom-call | flops 12099999744 | bytes 14155776 | tf_op jit(solution)/shard_map/attention_backward/pallas_call | solution.py:134
  317.9 11.4 %attention_backward.5 = (bf16[3,512,768]{2,1,0:T(8,128)(2,1)}, bf16[2,3,128,1024]{3,2,1,0:T(8,128)(2,1)}, bf16[2,3,128,1024]{3,2,1,0:T(8,128)(2,1)}) custom-call(s32[14]{0:T(128)} %dynamic-slice_bitcast_fusion.table_ref.t, bf16[512,768]{1,0:T(8,128)(2,1)} %get-tuple-element.257.qkv_ref, ...), custom_call_target="tpu_custom_call", output_to_operand_aliasing={{0}: (7, {}), {1}: (8, {}), {2}: (9, {})} | custom-call | flops 12099999744 | bytes 14155776 | tf_op jit(solution)/shard_map/attention_backward/pallas_call | solution.py:134
  334.9 7.4 %head_weights_backward.1 = (bf16[4,144,768]{2,1,0:T(8,128)(2,1)}, bf16[4,144,768]{2,1,0:T(8,128)(2,1)}) custom-call(s32[14]{0:T(128)} %dynamic-slice_bitcast_fusion.table_ref.t, bf16[2,3,128,1024]{3,2,1,0:T(8,128)(2,1)} %copy-done, bf16[2,3,128,1024]{3,2,1,0:T(8,128)(2,1)} %collective-permute-done.3.far_ref, ...), custom_call_target="tpu_custom_call" | custom-call | flops 8800000000 | bytes 7536640 | tf_op jit(solution)/shard_map/head_weights_backward/pallas_call | solution.py:134
  345.8 4.5 %collective-permute-start.59 = (bf16[128,256]{1,0:T(8,128)(2,1)}, bf16[128,256]{1,0:T(8,128)(2,1)S(1)}, u32[]{:S(2)}, u32[]{:S(2)}) collective-permute-start(bf16[128,256]{1,0:T(8,128)(2,1)} %get-tuple-element.293), channel_id=1, source_target_pairs={{0,8},{1,9},{2,10},{3,11},{4,12},{5,13},{6,14},{7,15},{8,24},{9,25... | collective-permute-start | bytes 196616 | tf_op jit(solution)/shard_map/ppermute | solution.py:1322
  357.4 4.3 %parts_along_z.6 = (bf16[144,768]{1,0:T(8,128)(2,1)}, bf16[144,768]{1,0:T(8,128)(2,1)}, bf16[144,768]{1,0:T(8,128)(2,1)}, bf16[144,768]{1,0:T(8,128)(2,1)}) custom-call(s32[14]{0:T(128)} %dynamic-slice_bitcast_fusion.table_ref.t, bf16[4,144,768]{2,1,0:T(8,128)(2,1)} %get-tuple-element.275.keep_ref, bf16[4,144,768]{2,1,0:T(8,128)(2,1)} %collective-permute-done.50.come_ref), custom_call_target="tpu_custom_call" | custom-call | flops 2200000000 | bytes 2654208 | tf_op jit(solution)/shard_map/parts_along_z/pallas_call | solution.py:134
  372.1 8.9 %collective-permute-done.52 = bf16[144,768]{1,0:T(8,128)(2,1)} collective-permute-done((bf16[144,768]{1,0:T(8,128)(2,1)}, bf16[144,768]{1,0:T(8,128)(2,1)}, u32[]{:S(2)}, u32[]{:S(2)}) %collective-permute-start.52) | collective-permute-done | bytes 221216 | tf_op jit(solution)/shard_map/ppermute | solution.py:1322
  (253 shorter events, 151.7 us)
Async XLA Ops:
  19.1 21.1 %collective-permute-start.3 = (bf16[2,3,128,1024]{3,2,1,0:T(8,128)(2,1)S(1)}, bf16[2,3,128,1024]{3,2,1,0:T(8,128)(2,1)}, u32[]{:S(2)}, u32[]{:S(2)}) collective-permute-start(bf16[2,3,128,1024]{3,2,1,0:T(8,128)(2,1)S(1)} %pad_maximum_fusion.near_ref), channel_id=1, source_target_pairs={{0,2},{1,3},{2,0},{3,1},{4,5},{5,4},{6,7},{7,6},{8,10},{9,11},{10,... | collective-permute-start | bytes 4718600 | tf_op jit(solution)/shard_map/ppermute | solution.py:1152
  40.4 18.4 %collective-permute-start.7 = (bf16[4,144,1024]{2,1,0:T(8,128)(2,1)S(1)}, bf16[4,144,1024]{2,1,0:T(8,128)(2,1)}, u32[]{:S(2)}, u32[]{:S(2)}) collective-permute-start(bf16[4,144,1024]{2,1,0:T(8,128)(2,1)S(1)} %pad_maximum_fusion.1.mine_ref), channel_id=1, source_target_pairs={{0,4},{1,5},{2,6},{3,7},{4,0},{5,1},{6,2},{7,3},{8,12},{9,13},{10,... | collective-permute-start | bytes 3538952 | tf_op jit(solution)/shard_map/ppermute | solution.py:90
  54.5 18.9 %collective-permute-start.9 = (bf16[1,3,128,256]{3,2,1,0:T(8,128)(2,1)S(1)}, bf16[1,3,128,256]{3,2,1,0:T(8,128)(2,1)S(1)}, u32[]{:S(2)}, u32[]{:S(2)}) collective-permute-start(bf16[1,3,128,256]{3,2,1,0:T(8,128)(2,1)S(1)} %bitcast.77), channel_id=1, source_target_pairs={{0,1},{1,0},{2,3},{3,2},{4,6},{5,7},{6,4},{7,5},{8,9},{9,8},{10,11... | collective-permute-start | bytes 589832 | tf_op jit(solution)/shard_map/ppermute | solution.py:1158
  56.0 17.5 %collective-permute-start.6 = (bf16[512,256]{1,0:T(8,128)(2,1)}, bf16[512,256]{1,0:T(8,128)(2,1)S(1)}, u32[]{:S(2)}, u32[]{:S(2)}) collective-permute-start(bf16[512,256]{1,0:T(8,128)(2,1)} %get-tuple-element.163), channel_id=1, source_target_pairs={{0,8},{1,9},{2,10},{3,11},{4,12},{5,13},{6,14},{7,15},{8,24},{9,25... | collective-permute-start | bytes 786440 | tf_op jit(solution)/shard_map/ppermute | solution.py:1164
  57.6 15.9 %collective-permute-start.10 = (bf16[256,512]{1,0:T(8,128)(2,1)S(1)}, bf16[256,512]{1,0:T(8,128)(2,1)S(1)}, u32[]{:S(2)}, u32[]{:S(2)}) collective-permute-start(bf16[256,512]{1,0:T(8,128)(2,1)S(1)} %collective-permute-done.8), channel_id=1, source_target_pairs={{0,8},{1,9},{2,10},{3,11},{4,12},{5,13},{6,14},{7,15},{8,24},{9,25... | collective-permute-start | bytes 786440 | tf_op jit(solution)/shard_map/ppermute | solution.py:1164
  73.5 15.6 %collective-permute-start.13 = (bf16[256,512]{1,0:T(8,128)(2,1)S(1)}, bf16[256,512]{1,0:T(8,128)(2,1)S(1)}, u32[]{:S(2)}, u32[]{:S(2)}) collective-permute-start(bf16[256,512]{1,0:T(8,128)(2,1)S(1)} %collective-permute-done.10), channel_id=1, source_target_pairs={{0,8},{1,9},{2,10},{3,11},{4,12},{5,13},{6,14},{7,15},{8,24},{9,25... | collective-permute-start | bytes 786440 | tf_op jit(solution)/shard_map/ppermute | solution.py:1164
  89.2 16.2 %collective-permute-start.16 = (bf16[1,1,256,512]{3,2,1,0:T(8,128)(2,1)S(1)}, bf16[1,1,256,512]{3,2,1,0:T(8,128)(2,1)S(1)}, u32[]{:S(2)}, u32[]{:S(2)}) collective-permute-start(bf16[1,1,256,512]{3,2,1,0:T(8,128)(2,1)S(1)} %bitcast.86), channel_id=1, source_target_pairs={{0,1},{1,0},{2,3},{3,2},{4,6},{5,7},{6,4},{7,5},{8,9},{9,8},{10,11... | collective-permute-start | bytes 786440 | tf_op jit(solution)/shard_map/ppermute | solution.py:1158
  92.3 17.2 %collective-permute-start.19 = (bf16[2,3,128,256]{3,2,1,0:T(8,128)(2,1)}, bf16[2,3,128,256]{3,2,1,0:T(8,128)(2,1)}, u32[]{:S(2)}, u32[]{:S(2)}) collective-permute-start(bf16[2,3,128,256]{3,2,1,0:T(8,128)(2,1)} %collective-permute-done.12.far_ref), channel_id=1, source_target_pairs={{0,4},{1,5},{2,6},{3,7},{4,0},{5,1},{6,2},{7,3},{8,12},{9,13},{10,... | collective-permute-start | bytes 1179656 | tf_op jit(solution)/shard_map/ppermute | solution.py:90
  92.8 16.7 %collective-permute-start.15 = (bf16[2,2,256,512]{3,2,1,0:T(8,128)(2,1)S(1)}, bf16[2,2,256,512]{3,2,1,0:T(8,128)(2,1)}, u32[]{:S(2)}, u32[]{:S(2)}) collective-permute-start(bf16[2,2,256,512]{3,2,1,0:T(8,128)(2,1)S(1)} %constant_dynamic-update-slice_fusion.2.rest_0_), channel_id=1, source_target_pairs={{0,2},{1,3},{2,0},{3,1},{4,5},{5,4},{6,7},{7,6},{8,10},{9,11},{10,... | collective-permute-start | bytes 3145736 | tf_op jit(solution)/shard_map/ppermute | solution.py:1152
  136.3 20.5 %collective-permute-start.26 = (bf16[2,3,512,256]{3,2,1,0:T(8,128)(2,1)S(1)}, bf16[2,3,512,256]{3,2,1,0:T(8,128)(2,1)}, u32[]{:S(2)}, u32[]{:S(2)}) collective-permute-start(bf16[2,3,512,256]{3,2,1,0:T(8,128)(2,1)S(1)} %constant_dynamic-update-slice_fusion.6.rest_0_), channel_id=1, source_target_pairs={{0,2},{1,3},{2,0},{3,1},{4,5},{5,4},{6,7},{7,6},{8,10},{9,11},{10,... | collective-permute-start | bytes 4718600 | tf_op jit(solution)/shard_map/ppermute | solution.py:1152
  186.6 27.7 %collective-permute-start.29 = (bf16[2,4,512,256]{3,2,1,0:T(8,128)(2,1)}, bf16[2,4,512,256]{3,2,1,0:T(8,128)(2,1)}, u32[]{:S(2)}, u32[]{:S(2)}) collective-permute-start(bf16[2,4,512,256]{3,2,1,0:T(8,128)(2,1)} %down_weights.2), channel_id=1, source_target_pairs={{0,2},{1,3},{2,0},{3,1},{4,5},{5,4},{6,7},{7,6},{8,10},{9,11},{10,... | collective-permute-start | bytes 6291464 | tf_op jit(solution)/shard_map/ppermute | solution.py:1278
  206.8 18.2 %collective-permute-start.30 = (bf16[384,1024]{1,0:T(8,128)(2,1)}, bf16[384,1024]{1,0:T(8,128)(2,1)S(1)}, u32[]{:S(2)}, u32[]{:S(2)}) collective-permute-start(bf16[384,1024]{1,0:T(8,128)(2,1)} %get-tuple-element.226), channel_id=1, source_target_pairs={{0,4},{1,5},{2,6},{3,7},{4,0},{5,1},{6,2},{7,3},{8,12},{9,13},{10,... | collective-permute-start | bytes 2359304 | tf_op jit(solution)/shard_map/ppermute | solution.py:90
  212.7 38.1 %collective-permute-start.33 = (bf16[2,4,128,1024]{3,2,1,0:T(8,128)(2,1)}, bf16[2,4,128,1024]{3,2,1,0:T(8,128)(2,1)S(1)}, u32[]{:S(2)}, u32[]{:S(2)}) collective-permute-start(bf16[2,4,128,1024]{3,2,1,0:T(8,128)(2,1)} %up_weights.2), channel_id=1, source_target_pairs={{0,2},{1,3},{2,0},{3,1},{4,5},{5,4},{6,7},{7,6},{8,10},{9,11},{10,... | collective-permute-start | bytes 6291464 | tf_op jit(solution)/shard_map/ppermute | solution.py:1278
  224.3 34.8 %collective-permute-start.32 = (bf16[1,4,512,256]{3,2,1,0:T(8,128)(2,1)}, bf16[1,4,512,256]{3,2,1,0:T(8,128)(2,1)}, u32[]{:S(2)}, u32[]{:S(2)}) collective-permute-start(bf16[1,4,512,256]{3,2,1,0:T(8,128)(2,1)} %get-tuple-element.302), channel_id=1, source_target_pairs={{0,1},{1,0},{2,3},{3,2},{4,6},{5,7},{6,4},{7,5},{8,9},{9,8},{10,11... | collective-permute-start | bytes 3145736 | tf_op jit(solution)/shard_map/ppermute | solution.py:1278
  238.8 20.4 %collective-permute-start.31 = (bf16[4,4,128,256]{3,2,1,0:T(8,128)(2,1)}, bf16[4,4,128,256]{3,2,1,0:T(8,128)(2,1)S(1)}, u32[]{:S(2)}, u32[]{:S(2)}) collective-permute-start(bf16[4,4,128,256]{3,2,1,0:T(8,128)(2,1)} %get-tuple-element.234), channel_id=1, source_target_pairs={{0,4},{1,5},{2,6},{3,7},{4,0},{5,1},{6,2},{7,3},{8,12},{9,13},{10,... | collective-permute-start | bytes 3145736 | tf_op jit(solution)/shard_map/ppermute | solution.py:90
  240.2 17.5 %collective-permute-start.35 = (bf16[3,128,256]{2,1,0:T(8,128)(2,1)S(1)}, bf16[3,128,256]{2,1,0:T(8,128)(2,1)S(1)}, u32[]{:S(2)}, u32[]{:S(2)}) collective-permute-start(bf16[3,128,256]{2,1,0:T(8,128)(2,1)S(1)} %bitcast.113), channel_id=1, source_target_pairs={{0,2},{1,3},{2,0},{3,1},{4,5},{5,4},{6,7},{7,6},{8,10},{9,11},{10,... | collective-permute-start | bytes 589832 | tf_op jit(solution)/shard_map/ppermute | solution.py:97
  267.9 21.6 %collective-permute-start.39 = (bf16[512,256]{1,0:T(8,128)(2,1)}, bf16[512,256]{1,0:T(8,128)(2,1)S(1)}, u32[]{:S(2)}, u32[]{:S(2)}) collective-permute-start(bf16[512,256]{1,0:T(8,128)(2,1)} %get-tuple-element.249), channel_id=1, source_target_pairs={{0,8},{1,9},{2,10},{3,11},{4,12},{5,13},{6,14},{7,15},{8,24},{9,25... | collective-permute-start | bytes 786440 | tf_op jit(solution)/shard_map/ppermute | solution.py:1322
  269.1 20.4 %collective-permute-start.40 = (bf16[512,256]{1,0:T(8,128)(2,1)}, bf16[512,256]{1,0:T(8,128)(2,1)}, u32[]{:S(2)}, u32[]{:S(2)}) collective-permute-start(bf16[512,256]{1,0:T(8,128)(2,1)} %get-tuple-element.250), channel_id=1, source_target_pairs={{0,24},{1,25},{2,26},{3,27},{4,28},{5,29},{6,30},{7,31},{8,16},{9,... | collective-permute-start | bytes 786440 | tf_op jit(solution)/shard_map/ppermute | solution.py:1322
  270.7 18.8 %collective-permute-start.41 = (bf16[512,256]{1,0:T(8,128)(2,1)}, bf16[512,256]{1,0:T(8,128)(2,1)}, u32[]{:S(2)}, u32[]{:S(2)}) collective-permute-start(bf16[512,256]{1,0:T(8,128)(2,1)} %get-tuple-element.251), channel_id=1, source_target_pairs={{0,16},{1,17},{2,18},{3,19},{4,20},{5,21},{6,22},{7,23},{8,0},{9,1... | collective-permute-start | bytes 786440 | tf_op jit(solution)/shard_map/ppermute | solution.py:1322
  271.9 18.8 %collective-permute-start.37 = (bf16[2,4,128,256]{3,2,1,0:T(8,128)(2,1)S(1)}, bf16[2,4,128,256]{3,2,1,0:T(8,128)(2,1)S(1)}, u32[]{:S(2)}, u32[]{:S(2)}) collective-permute-start(bf16[2,4,128,256]{3,2,1,0:T(8,128)(2,1)S(1)} %get-tuple-element.303), channel_id=1, source_target_pairs={{0,2},{1,3},{2,0},{3,1},{4,5},{5,4},{6,7},{7,6},{8,10},{9,11},{10,... | collective-permute-start | bytes 1572872 | tf_op jit(solution)/shard_map/ppermute | solution.py:1278
  273.1 19.2 %collective-permute-start.42 = (bf16[1,4,128,1024]{3,2,1,0:T(8,128)(2,1)}, bf16[1,4,128,1024]{3,2,1,0:T(8,128)(2,1)S(1)}, u32[]{:S(2)}, u32[]{:S(2)}) collective-permute-start(bf16[1,4,128,1024]{3,2,1,0:T(8,128)(2,1)} %get-tuple-element.300), channel_id=1, source_target_pairs={{0,1},{1,0},{2,3},{3,2},{4,6},{5,7},{6,4},{7,5},{8,9},{9,8},{10,11... | collective-permute-start | bytes 3145736 | tf_op jit(solution)/shard_map/ppermute | solution.py:1278
  291.6 24.6 %collective-permute-start.38 = (bf16[1,4,128,256]{3,2,1,0:T(8,128)(2,1)S(1)}, bf16[1,4,128,256]{3,2,1,0:T(8,128)(2,1)S(1)}, u32[]{:S(2)}, u32[]{:S(2)}) collective-permute-start(bf16[1,4,128,256]{3,2,1,0:T(8,128)(2,1)S(1)} %get-tuple-element.306), channel_id=1, source_target_pairs={{0,1},{1,0},{2,3},{3,2},{4,6},{5,7},{6,4},{7,5},{8,9},{9,8},{10,11... | collective-permute-start | bytes 786440 | tf_op jit(solution)/shard_map/ppermute | solution.py:1278
  292.4 25.5 %collective-permute-start.45 = (bf16[512,256]{1,0:T(8,128)(2,1)S(1)}, bf16[512,256]{1,0:T(8,128)(2,1)S(1)}, u32[]{:S(2)}, u32[]{:S(2)}) collective-permute-start(bf16[512,256]{1,0:T(8,128)(2,1)S(1)} %add_convert_fusion.9.refs_0_), channel_id=1, source_target_pairs={{0,3},{1,2},{2,1},{3,0},{4,7},{5,6},{6,5},{7,4},{8,11},{9,10},{10,... | collective-permute-start | bytes 786440 | tf_op jit(solution)/shard_map/ppermute | solution.py:93
  293.3 24.6 %collective-permute-start.44 = (bf16[512,256]{1,0:T(8,128)(2,1)S(1)}, bf16[512,256]{1,0:T(8,128)(2,1)S(1)}, u32[]{:S(2)}, u32[]{:S(2)}) collective-permute-start(bf16[512,256]{1,0:T(8,128)(2,1)S(1)} %add_convert_fusion.9.refs_0_), channel_id=1, source_target_pairs={{0,2},{1,3},{2,0},{3,1},{4,5},{5,4},{6,7},{7,6},{8,10},{9,11},{10,... | collective-permute-start | bytes 786440 | tf_op jit(solution)/shard_map/ppermute | solution.py:93
  295.1 22.9 %collective-permute-start.43 = (bf16[512,256]{1,0:T(8,128)(2,1)S(1)}, bf16[512,256]{1,0:T(8,128)(2,1)S(1)}, u32[]{:S(2)}, u32[]{:S(2)}) collective-permute-start(bf16[512,256]{1,0:T(8,128)(2,1)S(1)} %add_convert_fusion.9.refs_0_), channel_id=1, source_target_pairs={{0,1},{1,0},{2,3},{3,2},{4,6},{5,7},{6,4},{7,5},{8,9},{9,8},{10,11... | collective-permute-start | bytes 786440 | tf_op jit(solution)/shard_map/ppermute | solution.py:93
  300.1 29.3 %collective-permute-start.47 = (bf16[128,1024]{1,0:T(8,128)(2,1)}, bf16[128,1024]{1,0:T(8,128)(2,1)S(1)}, u32[]{:S(2)}, u32[]{:S(2)}) collective-permute-start(bf16[128,1024]{1,0:T(8,128)(2,1)} %get-tuple-element.266), channel_id=1, source_target_pairs={{0,8},{1,9},{2,10},{3,11},{4,12},{5,13},{6,14},{7,15},{8,24},{9,25... | collective-permute-start | bytes 786440 | tf_op jit(solution)/shard_map/ppermute | solution.py:1322
  333.6 20.6 %collective-permute-start.46 = (bf16[2,3,128,1024]{3,2,1,0:T(8,128)(2,1)}, bf16[2,3,128,1024]{3,2,1,0:T(8,128)(2,1)S(1)}, u32[]{:S(2)}, u32[]{:S(2)}) collective-permute-start(bf16[2,3,128,1024]{3,2,1,0:T(8,128)(2,1)} %get-tuple-element.261), channel_id=1, source_target_pairs={{0,2},{1,3},{2,0},{3,1},{4,5},{5,4},{6,7},{7,6},{8,10},{9,11},{10,... | collective-permute-start | bytes 4718600 | tf_op jit(solution)/shard_map/ppermute | solution.py:1278
  355.4 26.3 %collective-permute-start.51 = (bf16[1,3,128,1024]{3,2,1,0:T(8,128)(2,1)}, bf16[1,3,128,1024]{3,2,1,0:T(8,128)(2,1)}, u32[]{:S(2)}, u32[]{:S(2)}) collective-permute-start(bf16[1,3,128,1024]{3,2,1,0:T(8,128)(2,1)} %add_convert_fusion.4), channel_id=1, source_target_pairs={{0,1},{1,0},{2,3},{3,2},{4,6},{5,7},{6,4},{7,5},{8,9},{9,8},{10,11... | collective-permute-start | bytes 2359304 | tf_op jit(solution)/shard_map/ppermute | solution.py:1278
  361.8 19.2 %collective-permute-start.52 = (bf16[144,768]{1,0:T(8,128)(2,1)}, bf16[144,768]{1,0:T(8,128)(2,1)}, u32[]{:S(2)}, u32[]{:S(2)}) collective-permute-start(bf16[144,768]{1,0:T(8,128)(2,1)} %get-tuple-element.282), channel_id=1, source_target_pairs={{0,8},{1,9},{2,10},{3,11},{4,12},{5,13},{6,14},{7,15},{8,24},{9,25... | collective-permute-start | bytes 663560 | tf_op jit(solution)/shard_map/ppermute | solution.py:1322
  364.8 20.6 %collective-permute-start.53 = (bf16[144,768]{1,0:T(8,128)(2,1)}, bf16[144,768]{1,0:T(8,128)(2,1)}, u32[]{:S(2)}, u32[]{:S(2)}) collective-permute-start(bf16[144,768]{1,0:T(8,128)(2,1)} %get-tuple-element.283), channel_id=1, source_target_pairs={{0,24},{1,25},{2,26},{3,27},{4,28},{5,29},{6,30},{7,31},{8,16},{9,... | collective-permute-start | bytes 663560 | tf_op jit(solution)/shard_map/ppermute | solution.py:1322
  366.4 19.0 %collective-permute-start.54 = (bf16[144,768]{1,0:T(8,128)(2,1)}, bf16[144,768]{1,0:T(8,128)(2,1)}, u32[]{:S(2)}, u32[]{:S(2)}) collective-permute-start(bf16[144,768]{1,0:T(8,128)(2,1)} %get-tuple-element.284), channel_id=1, source_target_pairs={{0,16},{1,17},{2,18},{3,19},{4,20},{5,21},{6,22},{7,23},{8,0},{9,1... | collective-permute-start | bytes 663560 | tf_op jit(solution)/shard_map/ppermute | solution.py:1322
  366.4 23.2 %collective-permute-start.64 = (bf16[128,1280]{1,0:T(8,128)(2,1)S(1)}, bf16[128,1280]{1,0:T(8,128)(2,1)}, u32[]{:S(2)}, u32[]{:S(2)}) collective-permute-start(bf16[128,1280]{1,0:T(8,128)(2,1)S(1)} %pad_maximum_fusion.4.refs_0_), channel_id=1, source_target_pairs={{0,3},{1,2},{2,1},{3,0},{4,7},{5,6},{6,5},{7,4},{8,11},{9,10},{10,... | collective-permute-start | bytes 983048 | tf_op jit(solution)/shard_map/ppermute | solution.py:93
  (78 other events, 697.3 us)

commit v3 on v2

--- a/solution.py
+++ b/solution.py
@@ -41,6 +41,10 @@
             self.pairs(lambda z, c, s, j=j: (self.behind(z, -j), c, s))
             for j in range(self.n_z)
         ]
+        self.z_bits = self.n_z.bit_length() - 1
+        self.along = [
+            self.pairs(lambda z, c, s, k=k: (z ^ 1 << k, c, s)) for k in range(self.z_bits)
+        ]
         self.across = [
             self.pairs(lambda z, c, s, r=r: (z, c, s ^ self.mask(c, r)))
             for r in range(n_seq)
@@ -49,21 +53,6 @@
             self.pairs(lambda z, c, s, k=k: (z, c, s ^ self.mask(c, 1 << k)))
             for k in range(self.bits)
         ]
-        rows = []
-        for dp in range(n_dp):
-            for s in range(n_seq):
-                z, c = dp // 2, dp % 2
-                rows.append(
-                    [self.behind(z, j) for j in range(self.n_z)]
-                    + [s ^ self.mask(c, r) for r in range(n_seq)]
-                    + [c, 1 - c]
-                    + [s ^ self.mask(1 - c, r) for r in range(n_seq)]
-                )
-        self.table = np.asarray(rows, np.int32)
-        self.BEHIND, self.MEMBER = 0, self.n_z
-        self.CORE = self.n_z + n_seq
-        self.MEMBERS = (self.MEMBER, self.CORE + 2)
-
     def behind(self, z, j):
         return self.order[(self.place[z] - j) % self.n_z]
 
@@ -82,20 +71,26 @@
                 out.append((dp * self.n_seq + s, (2 * z + c) * self.n_seq + t))
         return out
 
-    def row(self):
-        here = lax.axis_index("dp") * self.n_seq + lax.axis_index("seq")
-        return lax.dynamic_index_in_dim(jnp.asarray(self.table), here, 0, False)
-
     def swap(self, block):
         return lax.ppermute(block, BOTH, self.core)
-
-    def share(self, block):
-        return [block] + [lax.ppermute(block, BOTH, way) for way in self.across[1:]]
 
     def trade(self, blocks):
         return [blocks[0]] + [
             lax.ppermute(block, BOTH, way) for block, way in zip(blocks[1:], self.across[1:])
         ]
+
+    def exchange(self, keep, send):
+        held = [(0, keep, 0)]
+        for k in reversed(range(self.bits)):
+            come = lax.ppermute(send, BOTH, self.stage[k])
+            width = 1 << k
+            held = held + [
+                (mask | width, come, i * width) for i, (mask, _, _) in enumerate(held)
+            ]
+            if k:
+                low = width // 2
+                send = jnp.concatenate([a[i + low : i + width] for _, a, i in held], 0)
+        return [(a, i) for _, a, i in sorted(held, key=lambda item: item[0])]
 
     def gather(self, block):
         near = block[None]
@@ -103,6 +98,15 @@
             near = self.double(near, k)
         return near, lax.ppermute(near, BOTH, self.stage[self.bits - 1])
 
+    def halfway(self, block, *ready):
+        near = after(block, *ready)[None]
+        for k in range(self.bits - 1):
+            near = self.double(near, k)
+        return near
+
+    def final(self, near, *ready):
+        return lax.ppermute(after(near, *ready), BOTH, self.stage[self.bits - 1])
+
     def double(self, near, k):
         return jnp.concatenate([near, lax.ppermute(near, BOTH, self.stage[k])], 0)
 
@@ -115,10 +119,46 @@
     return lax.optimization_barrier((value,) + others)[0]
 
 
+class Here:
+    def __init__(self, plan):
+        self.plan = plan
+        dp = lax.axis_index("dp")
+        self.z, self.c, self.s = lax.div(dp, 2), lax.rem(dp, 2), lax.axis_index("seq")
+
+    def core(self, k):
+        return self.c if k == 0 else 1 - self.c
+
+    def behind(self, j):
+        n = self.plan.n_z
+        half = lax.div(self.z, 2)
+        odd = lax.rem(self.z, 2)
+        place = jnp.where(odd == 1, half + 1, lax.rem(n - half, n))
+        at = lax.rem(place - j + n, n)
+        return jnp.where(at <= n // 2, jnp.maximum(2 * at - 1, 0), 2 * (n - at))
+
+    def member(self, r, core):
+        n, bits = self.plan.n_seq, self.plan.bits
+        turned = ((r << 1) & (n - 1)) | (r >> (bits - 1))
+        return self.s ^ (r + core * (turned - r))
+
+
 def shape(dims, dtype=BF16):
     return jax.ShapeDtypeStruct(tuple(dims), dtype)
 
 
+def distinct(found):
+    arrays = []
+    for array, _ in found:
+        if not any(array is other for other in arrays):
+            arrays.append(array)
+    at = [([array is other for other in arrays].index(True), i) for array, i in found]
+    return arrays, at
+
+
+def turned(i, bits):
+    return sum((i >> k & 1) << (bits - 1 - k) for k in range(bits))
+
+
 def aligned(start, size):
     return pl.ds(pl.multiple_of(start, size), size)
 
@@ -128,25 +168,29 @@
 
 
 def call(
-    kernel, table, operands, in_specs, outs, out_specs, grid, scratch, micros, name, alias=None
+    kernel, plan, operands, in_specs, outs, out_specs, grid, scratch, micros, name, alias=None
 ):
     size = sum(int(np.prod(o.shape)) * o.dtype.itemsize for o in list(operands) + list(outs))
+    size = size if micros else 0
+
+    def placed(spec):
+        if spec.index_map is None:
+            return spec
+        return pl.BlockSpec(spec.block_shape, lambda *i: spec.index_map(*i, Here(plan)))
+
     return pl.pallas_call(
-        kernel,
+        lambda *refs: kernel(Here(plan), *refs),
         out_shape=list(outs),
-        grid_spec=pltpu.PrefetchScalarGridSpec(
-            num_scalar_prefetch=1,
-            grid=grid,
-            in_specs=in_specs,
-            out_specs=out_specs,
-            scratch_shapes=scratch,
-        ),
+        grid=grid,
+        in_specs=[placed(spec) for spec in in_specs],
+        out_specs=[placed(spec) for spec in out_specs],
+        scratch_shapes=scratch,
         cost_estimate=pl.CostEstimate(
             flops=micros * MICROSECOND, bytes_accessed=size, transcendentals=0
         ),
         input_output_aliases=alias or {},
         name=name,
-    )(table, *operands)
+    )(*operands)
 
 
 def assemble(table, pieces, moves, outs, name):
@@ -172,7 +216,7 @@
         [whole_block(o.shape) for o in outs],
         (1,),
         [pltpu.SemaphoreType.DMA((len(moves),))],
-        2,
+        0,
         name,
     )
 
@@ -218,7 +262,7 @@
         moves = []
         for k, source in enumerate((mine_ref, theirs_ref)):
             for j in range(n_z):
-                owner = 2 * t[plan.BEHIND + j] + t[plan.CORE + k]
+                owner = 2 * t.behind(j) + t.core(k)
                 moves.append((source.at[j, pl.ds(own_rows, PAD)], held.at[owner]))
                 moves.append(
                     (
@@ -259,12 +303,13 @@
     cols3 = weights.shape[1]
     cols = cols3 // 3
     total = n * length
-    tile = 128
+    tile, chunk = min(512, total), min(256, total)
+    lse = (cols // PAIR, 8, total)
     scale = HEAD_DIM**-0.5
 
     def kernel(t, near_ref, far_ref, w_ref, vec_ref, *rest):
-        qkv_ref, *parts, context = rest[n_before:]
-        here = aligned(t[plan.MEMBER] * cols, cols)
+        qkv_ref, keep_ref, send_ref, lse_ref, context = rest[n_before:]
+        here = aligned(t.s * cols, cols)
         bias = jnp.concatenate(
             [vec_ref[0:1, here], jnp.zeros((1, cols), F32), vec_ref[1:2, here]], 1
         )
@@ -274,20 +319,37 @@
             qkv_ref[part * half * length : (part + 1) * half * length, :] = out.astype(BF16)
         def each_pair(pair, carry):
             q_at = aligned(pair * PAIR, PAIR)
-            key = qkv_ref[:, aligned(cols + pair * PAIR, PAIR)]
+            k_at = aligned(cols + pair * PAIR, PAIR)
             value = qkv_ref[:, aligned(2 * cols + pair * PAIR, PAIR)]
+            value = value.astype(F32).T.astype(BF16)
 
             def each_tile(i, carry):
                 rows = aligned(i * tile, tile)
                 query = qkv_ref[rows, q_at] * jnp.asarray(scale, BF16)
-                out = None
+                out = []
                 for head in range(2):
-                    scores = dot(only(query, head), key, 1, 1)
-                    exponent = jnp.exp(scores - jnp.max(scores, -1, keepdims=True))
-                    inverse = 1.0 / jnp.sum(exponent, -1, keepdims=True)
-                    part = dot((exponent * inverse).astype(BF16), value)
-                    out = part if head == 0 else jnp.where(lanes_of(0), out, part)
-                context[rows, q_at] = out.astype(BF16)
+                    one = only(query, head)
+
+                    def scores(c):
+                        return dot(qkv_ref[pl.ds(c * chunk, chunk), k_at], one, 1, 1)
+
+                    top = None
+                    for c in range(total // chunk):
+                        here = jnp.max(scores(c), 0, keepdims=True)
+                        top = here if c == 0 else jnp.maximum(top, here)
+                    for c in range(total // chunk):
+                        exponent = jnp.exp(scores(c) - top)
+                        here = jnp.sum(exponent, 0, keepdims=True)
+                        these = value[
+                            head * HEAD_DIM : (head + 1) * HEAD_DIM,
+                            c * chunk : (c + 1) * chunk,
+                        ]
+                        part = dot(these, exponent.astype(BF16))
+                        bottom = here if c == 0 else bottom + here
+                        acc = part if c == 0 else acc + part
+                    out.append(acc * (1.0 / bottom))
+                    lse_ref[pair, head : head + 1, rows] = top + jnp.log(bottom)
+                context[rows, q_at] = jnp.concatenate(out, 0).T.astype(BF16)
                 return carry
 
             lax.fori_loop(0, total // tile, each_tile, 0)
@@ -295,7 +357,8 @@
 
         lax.fori_loop(0, cols // PAIR, each_pair, 0)
         for r in range(n):
-            parts[r][0] = context[r * length : (r + 1) * length, :]
+            target = keep_ref if r < half else send_ref
+            target[r % half, 0] = context[r * length : (r + 1) * length, :]
 
     block = pl.BlockSpec((half, 1, length, width), lambda i, t: (0, g, 0, 0))
     return call(
@@ -304,34 +367,41 @@
         [near, far, weights, vectors] + before,
         [block, block, whole_block(weights.shape), whole_block(vectors.shape)]
         + [ANY] * n_before,
-        [shape((total, cols3))] + [shape((seqs, length, cols))] * n,
+        [shape((total, cols3))]
+        + [shape((half, seqs, length, cols))] * 2
+        + [shape(lse, F32)],
         [whole_block((total, cols3))]
-        + [pl.BlockSpec((1, length, cols), lambda i, t: (g, 0, 0))] * n,
+        + [pl.BlockSpec((half, 1, length, cols), lambda i, t: (0, g, 0, 0))] * 2
+        + [whole_block(lse)],
         (1,),
         [pltpu.VMEM((total, cols), BF16)],
-        11,
+        6,
         "attention_forward",
-        {5 + i: 1 + i for i in range(n_before)},
-    )
-
-
-def attention_backward(plan, table, g, seqs, qkv, upstream, w_qkv, before):
+        {4 + i: 1 + i for i in range(n_before)},
+    )
+
+
+def attention_backward(
+    plan, table, g, seqs, qkv, lse, contexts, upstream, where, w_qkv, before
+):
     n = plan.n_seq
     half = n // 2
     width, cols3 = w_qkv.shape
     cols = cols3 // 3
     total = qkv.shape[0]
     length = total // n
-    tile = min(256, total)
+    tile, chunk = min(512, total), min(256, total)
     scale = HEAD_DIM**-0.5
-    n_before = len(before)
-
-    def kernel(t, qkv_ref, w_ref, *rest):
-        up_refs, rest = rest[:n], rest[n + n_before :]
+    n_before, n_up = len(before), len(upstream)
+
+    def kernel(t, qkv_ref, w_ref, lse_ref, near_ref, far_ref, *rest):
+        up_refs, rest = rest[:n_up], rest[n_up + n_before :]
         grad_ref, part_keep, part_send = rest[:3]
-        up, key_acc, value_acc = rest[3:]
-        for r in range(n):
-            up[r * length : (r + 1) * length, :] = up_refs[r][0]
+        up, context, key_acc, value_acc = rest[3:]
+        for r, (a, i) in enumerate(where):
+            rows = pl.ds(r * length, length)
+            up[rows, :] = up_refs[a][i, 0]
+            context[rows, :] = (near_ref if r < half else far_ref)[r % half, 0]
         def each_pair(pair, carry):
             q_at = aligned(pair * PAIR, PAIR)
             k_at = aligned(cols + pair * PAIR, PAIR)
@@ -339,26 +409,31 @@
             value_acc[...] = jnp.zeros_like(value_acc)
             key_acc[...] = jnp.zeros_like(key_acc)
 
+            turned_key = qkv_ref[:, k_at].astype(F32).T.astype(BF16)
+
             def each_tile(i, carry):
                 rows = aligned(i * tile, tile)
                 query = qkv_ref[rows, q_at] * jnp.asarray(scale, BF16)
                 above = up[rows, q_at]
-                grad_query = None
+                both = (above.astype(F32) * context[rows, q_at].astype(F32)).T
+                out = []
                 for head in range(2):
-                    key = only(qkv_ref[:, k_at], head)
-                    value = only(qkv_ref[:, v_at], head)
-                    scores = dot(key, query, 1, 1)
-                    exponent = jnp.exp(scores - jnp.max(scores, 0, keepdims=True))
-                    portions = exponent * (1.0 / jnp.sum(exponent, 0, keepdims=True))
-                    low = portions.astype(BF16)
-                    slope = dot(value, above, 1, 1)
-                    total_slope = jnp.sum(portions * slope, 0, keepdims=True)
-                    slope = (portions * (slope - total_slope)).astype(BF16)
-                    value_acc[...] += dot(low, only(above, head))
-                    key_acc[...] += dot(slope, only(query, head))
-                    q_part = dot(slope, key, 0, 0)
-                    grad_query = q_part if head == 0 else grad_query + q_part
-                grad_ref[0, rows, q_at] = (grad_query * scale).astype(BF16)
+                    lanes = slice(head * HEAD_DIM, (head + 1) * HEAD_DIM)
+                    inner = jnp.sum(both[lanes], 0, keepdims=True)
+                    log_total = lse_ref[pair, head : head + 1, rows]
+                    one, upper = only(query, head), only(above, head)
+                    for c in range(total // chunk):
+                        here = pl.ds(c * chunk, chunk)
+                        portions = jnp.exp(dot(qkv_ref[here, k_at], one, 1, 1) - log_total)
+                        slope = dot(qkv_ref[here, v_at], upper, 1, 1)
+                        slope = (portions * (slope - inner)).astype(BF16)
+                        value_acc[here, :] += dot(portions.astype(BF16), upper)
+                        key_acc[here, :] += dot(slope, one)
+                        these = turned_key[lanes, c * chunk : (c + 1) * chunk]
+                        part = dot(these, slope)
+                        acc = part if c == 0 else acc + part
+                    out.append(acc * scale)
+                grad_ref[0, rows, q_at] = jnp.concatenate(out, 0).T.astype(BF16)
                 return carry
 
             lax.fori_loop(0, total // tile, each_tile, 0)
@@ -375,24 +450,29 @@
     part = (half, seqs, length, width)
     outs = [shape((seqs, total, cols3)), shape(part), shape(part)]
     block = pl.BlockSpec((half, 1, length, width), lambda i, t: (0, g, 0, 0))
-    operands = [qkv, w_qkv] + upstream + before
-    first = 1 + len(operands) - n_before
+    operands = [qkv, w_qkv, lse, *contexts] + upstream + before
+    first = len(operands) - n_before
     return call(
         kernel,
         table,
         operands,
-        [whole_block(qkv.shape), whole_block(w_qkv.shape)]
-        + [pl.BlockSpec((1, length, cols), lambda i, t: (g, 0, 0))] * n
+        [whole_block(v.shape) for v in (qkv, w_qkv, lse)]
+        + [pl.BlockSpec((half, 1, length, cols), lambda i, t: (0, g, 0, 0))] * 2
+        + [
+            pl.BlockSpec((v.shape[0], 1, length, cols), lambda i, t: (0, g, 0, 0))
+            for v in upstream
+        ]
         + [ANY] * n_before,
         outs,
         [pl.BlockSpec((1, total, cols3), lambda i, t: (g, 0, 0)), block, block],
         (1,),
         [
             pltpu.VMEM((total, cols), BF16),
+            pltpu.VMEM((total, cols), BF16),
             pltpu.VMEM((total, PAIR), F32),
             pltpu.VMEM((total, PAIR), F32),
         ],
-        11,
+        8,
         "attention_backward",
         {first + i: i for i in range(n_before)},
     )
@@ -425,19 +505,19 @@
         def _():
             for target, k in ((w_keep, 0), (w_send, 1)):
                 for z in range(n_z):
-                    row = (2 * z + t[plan.CORE + k]) * own_rows
+                    row = (2 * z + t.core(k)) * own_rows
                     target[z, :own_rows, :] = w_acc[aligned(row, own_rows), :].astype(BF16)
-                    here = (t[plan.MEMBER] == z).astype(F32)
+                    here = (t.s == z).astype(F32)
                     last = lax.broadcasted_iota(jnp.int32, (8, cols3), 0) == 7
                     rows = jnp.where(
-                        last, b_acc[0:1, :] * here, narrow_ref[2 * z + t[plan.CORE + k]]
+                        last, b_acc[0:1, :] * here, narrow_ref[2 * z + t.core(k)]
                     )
                     target[z, own_rows : own_rows + 8, :] = rows.astype(BF16)
                     target[z, own_rows + 8 :, :] = jnp.zeros((PAD - 8, cols3), BF16)
                 if k == 0:
                     for r in range(n):
                         rows = wide_ref[r].astype(BF16)
-                        target[t[plan.MEMBER + r], own_rows + 8 :, :span] = rows
+                        target[t.member(r, t.c), own_rows + 8 :, :span] = rows
 
     block = pl.BlockSpec((half, 1, length, width), lambda g, t: (0, g, 0, 0))
     w_out = (n_z, own_rows + PAD, cols3)
@@ -461,7 +541,7 @@
     )
 
 
-def output_norm(plan, table, pieces, inputs, vectors, w_out, come, near, far, others):
+def output_norm(plan, table, pieces, where, inputs, vectors, w_out, come, near, far, others):
     n, n_z = plan.n_seq, plan.n_z
     half = n // 2
     tokens, width = inputs.shape
@@ -471,15 +551,15 @@
     n_moves = 2 + 2 * (n_z - 1) * n
 
     def kernel(t, in_ref, vec_ref, w_ref, come_ref, near_ref, far_ref, on_ref, of_ref, *rest):
-        refs, rest = rest[:n], rest[n:]
+        refs, rest = rest[: len(pieces)], rest[len(pieces) :]
         sum_ref, norm_ref, low_ref, full_ref, sems = rest
 
         def row(z, k):
-            return aligned((z * 2 + t[plan.CORE + k]) * own_rows, own_rows)
+            return aligned((z * 2 + t.core(k)) * own_rows, own_rows)
 
         moves = []
         for k, source in enumerate((w_ref, come_ref)):
-            at = full_ref.at[row(t[plan.BEHIND], k)]
+            at = full_ref.at[row(t.behind(0), k)]
             lanes = source.shape[1] - width
             moves.append((source.at[pl.ds(0, own_rows), pl.ds(lanes, width)], at))
         for k, (first, second) in enumerate(((near_ref, far_ref), (on_ref, of_ref))):
@@ -487,8 +567,8 @@
                 for r in range(n):
                     source = first if r < half else second
                     at = full_ref.at[
-                        row(t[plan.BEHIND + j], k),
-                        aligned(t[plan.MEMBERS[k] + r] * cols, cols),
+                        row(t.behind(j), k),
+                        aligned(t.member(r, t.core(k)) * cols, cols),
                     ]
                     moves.append((source.at[r % half, j - 1], at))
         copies = copies_of(moves, sems)
@@ -499,9 +579,9 @@
         for i in range(tokens // tile):
             rows = pl.ds(i * tile, tile)
             total = in_ref[rows, :].astype(F32) + vec_ref[2:3, :]
-            for r in range(n):
-                weights = full_ref[aligned(t[plan.MEMBER + r] * cols, cols), :]
-                total += dot(refs[r][rows, :], weights)
+            for r, (a, m) in enumerate(where):
+                weights = full_ref[aligned(t.member(r, t.c) * cols, cols), :]
+                total += dot(refs[a][m, rows, :], weights)
             unit, _ = statistics(total)
             normed = unit * vec_ref[3:4, :] + vec_ref[4:5, :]
             sum_ref[rows, :] = total
@@ -556,23 +636,23 @@
         step_id = pl.program_id(0)
 
         def moves(r):
-            member = t[plan.MEMBER + r]
-            z = t[plan.BEHIND]
+            member = t.member(r, t.c)
+            z = t.behind(0)
             at = w.at[r]
 
             def row(k):
-                return aligned((z * 2 + t[plan.CORE + k]) * own_rows, own_rows)
-
-            lanes = aligned((member * 2 + t[plan.CORE]) * quarter, quarter)
+                return aligned((z * 2 + t.core(k)) * own_rows, own_rows)
+
+            lanes = aligned((member * 2 + t.c) * quarter, quarter)
             out = [(up_ref.at[:, lanes], at.at[row(0)])]
             lanes = aligned(member * quarter, quarter)
             out.append((come_ref.at[pl.ds(0, own_rows), lanes], at.at[row(1)]))
             for j in range(1, n_z):
-                z_j = t[plan.BEHIND + j]
+                z_j = t.behind(j)
                 a, i = found[j - 1]
                 source = remote_refs[a + (r >= half)]
                 for k in range(2):
-                    rows = aligned((z_j * 2 + t[plan.CORE + k]) * own_rows, own_rows)
+                    rows = aligned((z_j * 2 + t.core(k)) * own_rows, own_rows)
                     out.append(
                         (
                             source.at[r % half, i, pl.ds(k * own_rows, own_rows)],
@@ -636,7 +716,7 @@
         + [
             pl.BlockSpec(
                 (1, 1, quarter),
-                lambda r, t: (2 * t[plan.MEMBER + r] + t[plan.CORE], 0, 0),
+                lambda r, t: (2 * t.member(r, t.c) + t.c, 0, 0),
             )
         ]
         + [ANY] * len(remote),
@@ -672,14 +752,14 @@
         @pl.when(step_id == 0)
         def _():
             moves = [
-                (down_ref, w.at[aligned(t[plan.BEHIND] * own_hidden, own_hidden)])
+                (down_ref, w.at[aligned(t.behind(0) * own_hidden, own_hidden)])
             ]
             for j in range(1, n_z):
-                rows = aligned(t[plan.BEHIND + j] * own_hidden, own_hidden)
+                rows = aligned(t.behind(j) * own_hidden, own_hidden)
                 a, i = found[j - 1]
                 for r in range(n):
                     source = remote_refs[a + (r >= half)]
-                    lanes = aligned(t[plan.MEMBER + r] * cols, cols)
+                    lanes = aligned(t.member(r, t.c) * cols, cols)
                     moves.append((source.at[r % half, i], w.at[rows, lanes]))
             copies = copies_of(moves, sems)
             for copy in copies:
@@ -689,7 +769,7 @@
                 copy.wait()
             out_copy.start()
 
-        rows = aligned(t[plan.MEMBER + step_id] * quarter, quarter)
+        rows = aligned(t.member(step_id, t.c) * quarter, quarter)
         acc[...] += dot(act_ref[0], w[rows, :])
 
         @pl.when(step_id == n - 1)
@@ -796,7 +876,7 @@
         [low, other_low, w_down, w_up, slope],
         [whole_block(full)] * 2
         + [
-            pl.BlockSpec((quarter, width), lambda r, t: (t[plan.MEMBER + r], 0)),
+            pl.BlockSpec((quarter, width), lambda r, t: (t.member(r, t.c), 0)),
             pl.BlockSpec((1, width, quarter), lambda r, t: (r, 0, 0)),
             big,
         ],
@@ -825,7 +905,7 @@
         @pl.when(pl.program_id(0) == 0)
         def _():
             for r in range(half):
-                lanes = aligned(t[plan.MEMBER + base + r] * cols, cols)
+                lanes = aligned(t.member(base + r, t.c) * cols, cols)
                 here = pl.ds(r * cols, cols)
                 grads[:tokens, here] = low_ref[:, lanes]
                 grads[tokens:, here] = other_ref[:, lanes]
@@ -843,7 +923,7 @@
         [shape((half, n_z, quarter, cols))],
         [
             pl.BlockSpec(
-                (half, 1, quarter, cols), lambda r, t: (0, t[plan.MEMBER + r], 0, 0)
+                (half, 1, quarter, cols), lambda r, t: (0, t.member(r, t.c), 0, 0)
             )
         ],
         (n,),
@@ -895,7 +975,7 @@
 
     def kernel(t, grad_ref, own_ref, come_ref, sum_ref, vec_ref, w_ref, two_ref, *rest):
         first_ref, low_ref, narrow_ref = rest[:3]
-        parts, sums = rest[3:-1], rest[-1]
+        keep_ref, send_ref, sums = rest[3:]
         sums[0:3, :] = jnp.zeros((3, width), F32)
         sums[3:6, :] = two_ref[0:3, :]
         sums[6:8, :] = jnp.zeros((2, width), F32)
@@ -911,15 +991,17 @@
             add_rows(sums, 1, above * unit)
             add_rows(sums, 2, above)
             for r in range(n):
-                weights = w_ref[aligned(t[plan.MEMBER + r] * cols, cols), :]
-                parts[r][rows, :] = dot(low, weights, 1, 1).astype(BF16)
+                weights = w_ref[aligned(t.member(r, t.c) * cols, cols), :]
+                target = keep_ref if r < half else send_ref
+                target[r % half, rows, :] = dot(low, weights, 1, 1).astype(BF16)
         narrow_ref[...] = jnp.zeros_like(narrow_ref)
         for owner in range(plan.n_dp):
             lanes = pl.ds(owner * own_rows, own_rows)
             narrow_ref[owner, :, 0:own_rows] = sums[:, lanes]
 
     full = (tokens, width)
-    part = (tokens, cols)
+    half = n // 2
+    part = (half, tokens, cols)
     narrow = (plan.n_dp, 8, 3 * cols)
     return call(
         kernel,
@@ -927,8 +1009,8 @@
         [grad_second, own, come, first_sum, vectors, w_out, sums_two],
         [whole_block(full)] * 4
         + [whole_block(v.shape) for v in (vectors, w_out, sums_two)],
-        [shape(full, F32), shape(full), shape(narrow, F32)] + [shape(part)] * n,
-        [whole_block(full)] * 2 + [whole_block(narrow)] + [whole_block(part)] * n,
+        [shape(full, F32), shape(full), shape(narrow, F32)] + [shape(part)] * 2,
+        [whole_block(full)] * 2 + [whole_block(narrow)] + [whole_block(part)] * 2,
         (1,),
         [pltpu.VMEM((8, width), F32)],
         8,
@@ -936,21 +1018,21 @@
     )
 
 
-def out_weights(plan, table, pieces, low):
+def out_weights(plan, table, pieces, where, low):
     n, n_z = plan.n_seq, plan.n_z
     tokens, width = low.shape
     cols = width // n
     own_rows = width // plan.n_dp
 
     def kernel(t, low_ref, *rest):
-        refs, (keep_ref, send_ref, both) = rest[:n], rest[n:]
-        for r in range(n):
-            z = t[plan.MEMBER + r]
-            both[...] = dot(refs[r][...], low_ref[...], 0, 0).astype(BF16)
+        refs, (keep_ref, send_ref, both) = rest[: len(pieces)], rest[len(pieces) :]
+        for r, (a, m) in enumerate(where):
+            z = t.member(r, t.c)
+            both[...] = dot(refs[a][m], low_ref[...], 0, 0).astype(BF16)
             for target, k in ((send_ref, 1), (keep_ref, 0)):
-                rows = aligned(t[plan.CORE + k] * own_rows, own_rows)
+                rows = aligned(t.core(k) * own_rows, own_rows)
                 for s in range(n):
-                    at = aligned(t[plan.MEMBERS[k] + s] * cols, cols)
+                    at = aligned(t.member(s, t.core(k)) * cols, cols)
                     target[s, z] = both[rows, at]
 
     dims = (n, n_z, own_rows, cols)
@@ -963,34 +1045,47 @@
         [whole_block(dims)] * 2,
         (1,),
         [pltpu.VMEM((cols, width), BF16)],
-        5,
+        0,
         "out_weights",
     )
 
 
-def parts_along_z(plan, table, keep, come):
+def parts_along_z(plan, table, terms):
     n_z = plan.n_z
-    rows, lanes = keep.shape[1:]
-
-    def kernel(t, keep_ref, come_ref, *outs):
-        total = keep_ref[0].astype(F32) + come_ref[0].astype(F32)
+    rows = terms[0][0].shape[1]
+    operands = [v for group in terms for v in group]
+    lanes = sum(group[0].shape[2] for group in terms)
+
+    def kernel(t, *refs):
+        sources, outs = refs[: len(operands)], refs[len(operands) :]
         for j in range(n_z):
 
             @pl.when(pl.program_id(0) == j)
             def _(j=j):
-                outs[j][...] = total.astype(BF16)
+                left, at = list(sources), 0
+                target = outs[2 * j // n_z]
+                for group in terms:
+                    total = left.pop(0)[0].astype(F32)
+                    for _ in group[1:]:
+                        total += left.pop(0)[0].astype(F32)
+                    end = at + total.shape[1]
+                    target[j % (n_z // 2), :, at:end] = total.astype(BF16)
+                    at = end
 
     def member(i, t):
-        return (t[plan.BEHIND + (2 * n_z - 1 - i) % n_z], 0, 0)
-
-    block = pl.BlockSpec((1, rows, lanes), member)
-    return call(
-        kernel,
-        table,
-        [keep, come],
-        [block, block],
-        [shape((rows, lanes))] * n_z,
-        [whole_block((rows, lanes))] * n_z,
+        here = 0
+        for k in range(plan.z_bits):
+            here = here | ((i >> k) & 1) << (plan.z_bits - 1 - k)
+        return (t.z ^ here, 0, 0)
+
+    out = (n_z // 2, rows, lanes)
+    return call(
+        kernel,
+        table,
+        operands,
+        [pl.BlockSpec((1,) + v.shape[1:], member) for v in operands],
+        [shape(out)] * 2,
+        [whole_block(out)] * 2,
         (n_z,),
         [],
         2,
@@ -998,52 +1093,55 @@
     )
 
 
-def split_by_core(plan, table, pieces):
-    rows, lanes = pieces[0].shape
-    lanes //= 2
+def split_by_core(plan, table, pieces, split):
+    _, rows, lanes = pieces[0].shape
+    half = split // 2
     n_pieces = len(pieces)
 
     def kernel(t, *refs):
-        for target, k in zip(refs[n_pieces:], range(2)):
-            at = aligned(t[plan.CORE + k] * lanes, lanes)
-            total = refs[0][:, at].astype(F32)
+        for k, target in enumerate(refs[n_pieces:]):
+            size = half if k < 2 else lanes - split
+            at = aligned(t.core(k) * half, half) if k < 2 else pl.ds(split, size)
+            total = refs[0][0, :, at].astype(F32)
             for ref in refs[1:n_pieces]:
-                total += ref[:, at].astype(F32)
+                total += ref[0, :, at].astype(F32)
             target[...] = total.astype(BF16)
 
+    outs = [(rows, half), (rows, half), (rows, lanes - split)]
     return call(
         kernel,
         table,
         pieces,
         [whole_block(p.shape) for p in pieces],
-        [shape((rows, lanes))] * 2,
-        [whole_block((rows, lanes))] * 2,
+        [shape(o) for o in outs],
+        [whole_block(o) for o in outs],
         (1,),
         [],
-        2,
+        0,
         "split_by_core",
     )
 
 
-def place(plan, table, pieces, outs, moves, name):
+def place(plan, table, near, far, outs, moves, name):
     n = plan.n_seq
-
-    def kernel(t, *refs):
-        sources, targets = refs[:n], refs[n:]
+    half = n // 2
+
+    def kernel(t, near_ref, far_ref, *targets):
         for r in range(n):
+            source = near_ref if r < half else far_ref
             for src, o, at in moves:
-                targets[o][:, at(t, r)] = sources[r][src].astype(F32)
-
-    return call(
-        kernel,
-        table,
-        pieces,
-        [whole_block(p.shape) for p in pieces],
+                targets[o][:, at(t, r)] = source[(r % half,) + src].astype(F32)
+
+    return call(
+        kernel,
+        table,
+        [near, far],
+        [whole_block(near.shape)] * 2,
         [shape(o, F32) for o in outs],
         [whole_block(o) for o in outs],
         (1,),
         [],
-        2,
+        0,
         name,
     )
 
@@ -1078,7 +1176,7 @@
     cols3 = 3 * cols
     quarter = hidden // 2 // n
     assert n == n_z and quarter == own_hidden
-    table = plan.row()
+    table = plan
     core = lax.axis_index("dp") % 2
 
     narrow = jnp.stack(
@@ -1093,7 +1191,7 @@
     )
 
     def column_block(t):
-        return (pl.ds(0, own_rows), aligned(t[plan.MEMBER] * cols, cols))
+        return (pl.ds(0, own_rows), aligned(t.s * cols, cols))
 
     moves = [
         (i, column_block, 0, lambda t, i=i: (pl.ds(0, own_rows), pl.ds(i * cols, cols)))
@@ -1115,6 +1213,29 @@
     for k in range(plan.bits - 1):
         near_x = plan.double(near_x, k)
     mine = [first, straight(first, 1)]
+
+    top = plan.bits - 1
+
+    def final(near, *ready):
+        return near, lax.ppermute(after(near, *ready), BOTH, plan.stage[top])
+
+    def begin(block, *ready):
+        near = after(block, *ready)[None]
+        for k in range(top - 1):
+            near = plan.double(near, k)
+        return near, lax.ppermute(near, BOTH, plan.stage[top - 1])
+
+    def joined(started, *ready):
+        return jnp.concatenate([after(started[0], *ready), started[1]], 0)
+
+    def onward(block, *ready):
+        return lax.ppermute(after(block, *ready), BOTH, plan.toward[1])
+
+    ready = (near_x, mine[1])
+    far_x = final(near_x, *ready)[1]
+    mine.append(onward(mine[1], *ready))
+    for j in range(3, n_z):
+        mine.append(onward(mine[-1]))
 
     moves = []
     for z in range(n_z):
@@ -1123,7 +1244,7 @@
                 0,
                 lambda t, z=z: (
                     pl.ds(0, own_rows),
-                    aligned((2 * z + t[plan.CORE + 1]) * quarter, quarter),
+                    aligned((2 * z + (1 - t.c)) * quarter, quarter),
                 ),
                 0,
                 lambda t, z=z: (pl.ds(0, own_rows), pl.ds(z * quarter, quarter)),
@@ -1139,33 +1260,13 @@
     )
     (across,) = assemble(
         table,
-        [after(w_up, mine[1]), w_out],
+        [after(w_up, mine[2]), w_out],
         moves,
         [shape((own_rows, n * quarter + width))],
         "pack_across",
     )
     come = plan.swap(across)
 
-    top = plan.bits - 1
-
-    def final(near, *ready):
-        return near, lax.ppermute(after(near, *ready), BOTH, plan.stage[top])
-
-    def begin(block, *ready):
-        near = after(block, *ready)[None]
-        for k in range(top - 1):
-            near = plan.double(near, k)
-        return near, lax.ppermute(near, BOTH, plan.stage[top - 1])
-
-    def joined(started, *ready):
-        return jnp.concatenate([after(started[0], *ready), started[1]], 0)
-
-    def onward(block, *ready):
-        return lax.ppermute(after(block, *ready), BOTH, plan.toward[1])
-
-    ready = (near_x, mine[1])
-    far_x = final(near_x, *ready)[1]
-    mine += [straight(after(first, *ready), j) for j in range(2, n_z)]
 
     def rows_at(start, size):
         return lambda t: (pl.ds(start, size), pl.ds(0, quarter))
@@ -1175,14 +1276,14 @@
             0,
             lambda t: (
                 pl.ds(0, own_rows),
-                aligned((2 * t[plan.MEMBER] + t[plan.CORE]) * quarter, quarter),
+                aligned((2 * t.s + t.c) * quarter, quarter),
             ),
             0,
             rows_at(0, own_rows),
         ),
         (
             1,
-            lambda t: (pl.ds(0, own_rows), aligned(t[plan.MEMBER] * quarter, quarter)),
+            lambda t: (pl.ds(0, own_rows), aligned(t.s * quarter, quarter)),
             0,
             rows_at(own_rows, own_rows),
         ),
@@ -1190,7 +1291,7 @@
     moves.append(
         (
             2,
-            lambda t: (pl.ds(0, own_hidden), aligned(t[plan.MEMBER] * cols, cols)),
+            lambda t: (pl.ds(0, own_hidden), aligned(t.s * cols, cols)),
             1,
             lambda t: (pl.ds(0, own_hidden),),
         )
@@ -1204,7 +1305,7 @@
     )
     ups = [onward(second)]
 
-    ready = (far_x, second) + tuple(mine[1:])
+    ready = (far_x, ups[0]) + tuple(mine[1:])
     mine_all = jnp.stack([after(piece, *ready) for piece in mine])
     theirs = plan.swap(mine_all)
     outs = jnp.stack([after(piece, *ready)[:own_rows, cols3:] for piece in mine[1:]])
@@ -1212,13 +1313,14 @@
     ups.append(onward(ups[0], *ready))
     downs = [onward(down, *ready)]
     w_qkv, vectors, up_bias = head_weights(plan, table, mine_all, theirs)
-    qkv = []
+    qkv, lse = [], []
 
     def attend(g, before, *ready):
-        out, *parts = attention_forward(
+        out, *parts, total = attention_forward(
             plan, table, g, near_x, far_x, w_qkv, after(vectors, *ready), before
         )
         qkv.append(out)
+        lse.append(total)
         return parts
 
     parts = attend(0, [])
@@ -1243,7 +1345,9 @@
     for g in range(2, seqs):
         parts = attend(g, parts, *ready)
 
-    pieces = [p.reshape(tokens, cols) for p in plan.trade(parts)]
+    contexts = parts
+    pieces, where = distinct(plan.exchange(*parts))
+    pieces = [p.reshape(p.shape[0], tokens, cols) for p in pieces]
     near_three = joined(three_started, parts[0])
     ready = (parts[0], up_two[1], near_three, downs[-1]) + tuple(others)
     downs = jnp.stack([after(piece, *ready) for piece in downs])
@@ -1254,6 +1358,7 @@
         plan,
         table,
         pieces,
+        where,
         after(inputs.reshape(tokens, width), downs),
         vectors,
         w_out,
@@ -1313,67 +1418,79 @@
         full_out,
         sums_two,
     )
-    parts = plan.trade([p.reshape(seqs, length, cols) for p in parts])
-    out_keep, out_send = out_weights(plan, table, pieces, low_one)
+    found = plan.exchange(*[p.reshape(half, seqs, length, cols) for p in parts])
+    parts, up_where = distinct(found)
+    out_keep, out_send = out_weights(plan, table, pieces, where, low_one)
     out_come = plan.swap(out_send)
-    def sent_along_z(keep, come, *ready):
-        *away, own = parts_along_z(plan, table, after(keep, *ready), come)
-        return [own] + [
-            lax.ppermute(part, BOTH, way) for part, way in zip(away, plan.toward[1:])
-        ]
-
-    def total(terms, *ready):
-        out = after(terms[0], *ready).astype(F32)
-        for piece in terms[1:]:
-            out += piece.astype(F32)
-        return out.astype(BF16)
+    def sent_along_z(terms, *ready):
+        terms = [[after(group[0], *ready)] + group[1:] for group in terms]
+        keep, send = parts_along_z(plan, table, terms)
+        return keep, lax.ppermute(send, BOTH, plan.along[0])
+
+    def on_along_z(keep, come, *ready):
+        for way in plan.along[1:]:
+            low = keep.shape[0] // 2
+            come = after(come, *ready)
+            sent = add(keep[low:], come[low:])
+            keep = add(keep[:low], come[:low])
+            come = lax.ppermute(sent, BOTH, way)
+        return keep, come
+
+    def total(keep, come, *ready):
+        return add(after(keep, *ready), come)[0]
 
     def back(g, before, *ready):
         return attention_backward(
-            plan, table, g, seqs, after(qkv[g], *ready), parts, w_qkv, before
+            plan,
+            table,
+            g,
+            seqs,
+            after(qkv[g], *ready),
+            lse[g],
+            contexts,
+            parts,
+            up_where,
+            w_qkv,
+            before,
         )
 
     ready = (out_keep, out_come, down_last, up_come) + tuple(parts)
     up_keep, up_send = middle(up_keep, up_come, *ready)
     up_last = begun(up_send, 0)
-    down_along = sent_along_z(down_keep[0], down_last[0], *ready)
-    out_come = after(out_come, *ready)
-    out_kept = add(out_keep[:half], out_come[:half])
-    out_sent = add(out_keep[half:], out_come[half:])
-    out_first = begun(out_sent, top)
-    shared = back(0, [], out_sent, up_send, *ready)
-    out_kept, out_sent = middle(out_kept, out_first, shared[0])
-    out_last = begun(out_sent, 0)
-    grad_down = total(down_along, shared[0])
-    ready = (grad_down, up_last, out_sent, shared[0])
-    up_along = sent_along_z(up_keep[0], up_last[0], *ready)
-    grad_down = plan.share(after(grad_down, *ready))
-    shared = back(1, list(shared), *ready)
-    ready = (out_last, shared[0]) + tuple(grad_down)
-    out_along = sent_along_z(out_kept[0], out_last[0], *ready)
+    out_come = after(out_come, up_send)
+    outs = [add(out_keep[r], out_come[r]) for r in range(n)]
+    down_along = sent_along_z([[down_keep[0], down_last[0]]], up_send)
+    outs = plan.trade([after(v, down_along[0]) for v in outs])
+    shared = back(0, [], down_along[0], up_send, outs[0], *ready)
+    down_along = on_along_z(*down_along, shared[0])
+    up_along = sent_along_z([[up_keep[0], up_last[0]], outs], shared[0])
+    shared = back(1, list(shared), up_along[0], down_along[0])
+    grad_down = total(*down_along, shared[0])
+    up_along = on_along_z(*up_along, shared[0])
+    down_near = plan.halfway(grad_down, up_along[0])
     for g in range(2, seqs):
-        shared = back(g, list(shared), *ready)
+        shared = back(g, list(shared), up_along[0], grad_down)
     grad_qkv, part_keep, part_send = shared
 
     part_come = begun(part_send, top)
-    up_along = [after(up_along[0], part_send)] + up_along[1:]
-    up_kept, up_sent = split_by_core(plan, table, up_along)
+    up_along = (after(up_along[0], grad_qkv), up_along[1])
+    up_kept, up_sent, grad_out = split_by_core(plan, table, up_along, 2 * quarter)
     up_come = plan.swap(up_sent)
+    down_far = plan.final(down_near, up_sent)
     last_keep, last_send = head_weights_backward(
-        plan, table, near_x, far_x, after(grad_qkv, up_kept), sums, sums_up
+        plan, table, near_x, far_x, after(grad_qkv, up_sent), sums, sums_up
     )
     last_come = plan.swap(last_send)
-    ready = (last_keep, last_send)
-    grad_up = jnp.concatenate(
-        [after(up_kept, *ready), up_come, total(out_along, *ready)], 1
-    )
-    last_along = sent_along_z(last_keep, last_come)
-    part_keep, part_send = middle(part_keep, part_come, last_come)
+    last_along = sent_along_z([[last_keep, last_come]])
+    up_kept = after(up_kept, last_along[0])
+    up_near = plan.halfway(jnp.concatenate([up_kept, up_come, grad_out], 1))
+    part_keep, part_send = middle(part_keep, part_come, last_along[0])
     part_last = begun(part_send, 0)
-    grad_up = plan.share(after(grad_up, part_send))
+    last_along = on_along_z(*last_along, part_send)
+    up_far = plan.final(up_near, last_along[0])
 
     def lanes(size):
-        return lambda t, r: aligned(t[plan.MEMBER + r] * size, size)
+        return lambda t, r: aligned(t.member(r, t.c) * size, size)
 
     grad_inputs = grad_first.reshape(inputs.shape) + (
         part_keep[0].astype(F32) + part_last[0].astype(F32)
@@ -1381,22 +1498,29 @@
     (grad_down,) = place(
         plan,
         table,
-        [after(v, part_send) for v in grad_down],
+        after(down_near, last_along[0]),
+        down_far,
         [(own_hidden, width)],
         [((slice(None),), 0, lanes(cols))],
         "place_down",
     )
+    grad_inputs = grad_first.reshape(inputs.shape) + (
+        part_keep[0].astype(F32) + after(part_last[0], grad_down).astype(F32)
+    )
+    last_near = plan.halfway(total(*last_along, grad_inputs))
+    last_far = plan.final(last_near)
     grad_up, grad_out = place(
         plan,
         table,
-        grad_up,
+        after(up_near, last_near),
+        up_far,
         [(own_rows, hidden), (own_rows, width)],
         [
             (
                 (slice(None), pl.ds(k * quarter, quarter)),
                 0,
                 lambda t, r, k=k: aligned(
-                    (2 * t[plan.MEMBER + r] + t[plan.CORE + k]) * quarter, quarter
+                    (2 * t.member(r, t.c) + t.core(k)) * quarter, quarter
                 ),
             )
             for k in range(2)
@@ -1404,11 +1528,11 @@
         + [((slice(None), pl.ds(2 * quarter, cols)), 1, lanes(cols))],
         "place_up",
     )
-    grad_last = plan.share(total(last_along, grad_down, grad_inputs))
     grad_wq, grad_wk, grad_wv = place(
         plan,
         table,
-        grad_last,
+        last_near,
+        last_far,
         [(own_rows, width)] * 3,
         [
             ((pl.ds(0, own_rows), pl.ds(m * cols, cols)), m, lanes(cols))
@@ -1416,7 +1540,8 @@
         ],
         "place_heads",
     )
-    vec_out = sum(piece[own_rows:].astype(F32) for piece in grad_last)
+    vec_out = jnp.sum(last_near[:, own_rows:].astype(F32), 0)
+    vec_out += jnp.sum(last_far[:, own_rows:].astype(F32), 0)
     biases = vec_out[7].reshape(3, 2, own_rows)
     biases = jnp.where(core == 0, biases[:, 0], biases[:, 1])
     return (

time: 408 us -> 393 us (0.963)
  Pallas kernels: 205 us -> 160 us
  waiting for transfers between devices: 87.3 us -> 131 us
  starting transfers between devices: 78.3 us -> 56.1 us
  local copies, waits for them, and re-layouts: 11.8 us -> 16.3 us
    ppermute x21 -> x13, waiting for transfers between devices: 15.5 us -> 61.4 us  [the longest x4 32.2 us: exchange(): come = lax.ppermute(send, BOTH, self.stage[k])]
    pallas_call x30 -> x29, Pallas kernels: 205 us -> 160 us  [call(): pl.pallas_call(lambda *refs: kernel(Here(plan), *refs), out_shape=list(ou...]
    ppermute x6 -> x3, waiting for transfers between devices: 14.8 us -> 0.01 us  [trade(): lax.ppermute(block, BOTH, way)]
    ppermute x6 -> x8, waiting for transfers between devices: 7.08 us -> 21.6 us  [onward(): return lax.ppermute(after(block, *ready), BOTH, plan.toward[1])]
    ppermute x21 -> x13, starting transfers between devices: 31 us -> 16.7 us  [the longest x3 5.29 us: on_along_z(): come = lax.ppermute(sent, BOTH, way)]
    ppermute x3 -> x1, waiting for transfers between devices: 16.2 us -> 3.12 us  [straight(): return lax.ppermute(block, BOTH, plan.toward[j])]
    ppermute x1 -> x4, waiting for transfers between devices: 2.76 us -> 9.38 us  [double(): return jnp.concatenate([near, lax.ppermute(near, BOTH, self.stage[k])], 0)]
    convert_element_type x2 -> x6, other arithmetic: 1.51 us -> 8.03 us  [add(): return (former.astype(F32) + latter.astype(F32)).astype(BF16)]
  transfers between devices with their start and end apart: 65 -> 55, of which waited for: 21 -> 31; matrix products, arithmetic and copies ran while one was open for 4% -> 5% of each run, Pallas kernels for 43% -> 35%
where the time goes in v3:
time: 393 us; the launch traced here: 385 us
  Pallas kernels  160 us (41%)
  waiting for transfers between devices  131 us (33%)
  starting transfers between devices  56.1 us (14%)
  other arithmetic  20.2 us (5%)
  local copies, waits for them, and re-layouts  16.3 us (4%)
    pallas_call x29, Pallas kernels, call(): pl.pallas_call(lambda *refs: kernel(Here(plan), *refs), out_shape=list(ou...  160 us
    ppermute x4, waiting for transfers between devices, exchange(): come = lax.ppermute(send, BOTH, self.stage[k])  32.2 us
    ppermute x8, waiting for transfers between devices, onward(): return lax.ppermute(after(block, *ready), BOTH, plan.toward[1])  21.6 us
    ppermute x3, waiting for transfers between devices, sent_along_z(): return (keep, lax.ppermute(send, BOTH, plan.along[0]))  16 us
    ppermute x8, starting transfers between devices, onward(): return lax.ppermute(after(block, *ready), BOTH, plan.toward[1])  13.9 us
    ppermute x6, waiting for transfers between devices, begun(): return lax.ppermute(after(send, *ready), BOTH, plan.stage[k])  11.1 us
    unnamed x88, local copies, waits for them, and re-layouts  10.6 us
    ppermute x4, waiting for transfers between devices, double(): return jnp.concatenate([near, lax.ppermute(near, BOTH, self.stage[k])], 0)  9.38 us
  transfers between devices with their start and end apart: 55, of which 31 were waited for; matrix products, arithmetic and copies ran while one was open for 5% of the time, Pallas kernels for 35%

profile of v3, /device:TPU:0, one launch (start us, length us, event | category | flops | bytes accessed | tf_op | source)
XLA Modules:
  0.0 385.2 jit_solution(13069121329496634505)
XLA Ops:
  9.1 4.8 %collective-permute-done.1 = bf16[1,3,128,1024]{3,2,1,0:T(8,128)(2,1)S(1)} collective-permute-done((bf16[1,3,128,1024]{3,2,1,0:T(8,128)(2,1)}, bf16[1,3,128,1024]{3,2,1,0:T(8,128)(2,1)S(1)}, u32[]{:S(2)}, u32[]{:S(2)}) %collective-permute-start.1) | collective-permute-done | bytes 786464 | tf_op jit(solution)/shard_map/ppermute | solution.py:111
  18.5 9.6 %collective-permute-done.2 = bf16[144,1024]{1,0:T(8,128)(2,1)S(1)} collective-permute-done((bf16[144,1024]{1,0:T(8,128)(2,1)S(1)}, bf16[144,1024]{1,0:T(8,128)(2,1)S(1)}, u32[]{:S(2)}, u32[]{:S(2)}) %collective-permute-start.2) | collective-permute-done | bytes 294944 | tf_op jit(solution)/shard_map/ppermute | solution.py:1232
  41.2 5.2 %collective-permute-done.5 = bf16[256,512]{1,0:T(8,128)(2,1)S(1)} collective-permute-done((bf16[256,512]{1,0:T(8,128)(2,1)}, bf16[256,512]{1,0:T(8,128)(2,1)S(1)}, u32[]{:S(2)}, u32[]{:S(2)}) %collective-permute-start.5) | collective-permute-done | bytes 262176 | tf_op jit(solution)/shard_map/ppermute | solution.py:1232
  54.1 6.1 %attention_forward.3 = (bf16[512,768]{1,0:T(8,128)(2,1)}, bf16[2,3,128,256]{3,2,1,0:T(8,128)(2,1)}, bf16[2,3,128,256]{3,2,1,0:T(8,128)(2,1)}, f32[2,8,512]{2,1,0:T(8,128)}) custom-call(bf16[2,3,128,1024]{3,2,1,0:T(8,128)(2,1)} %copy-done.3, bf16[2,3,128,1024]{3,2,1,0:T(8,128)(2,1)} %collective-permute-done.4.refs_1_, ...), custom_call_target="tpu_custom_call" | custom-call | flops 6600000000 | bytes 6356992 | tf_op jit(solution)/shard_map/attention_forward/pallas_call | solution.py:181
  67.7 6.1 %attention_forward.4 = (bf16[512,768]{1,0:T(8,128)(2,1)}, bf16[2,3,128,256]{3,2,1,0:T(8,128)(2,1)}, bf16[2,3,128,256]{3,2,1,0:T(8,128)(2,1)}, f32[2,8,512]{2,1,0:T(8,128)}) custom-call(bf16[2,3,128,1024]{3,2,1,0:T(8,128)(2,1)} %copy-done.3, bf16[2,3,128,1024]{3,2,1,0:T(8,128)(2,1)} %collective-permute-done.4.refs_1_, ...), custom_call_target="tpu_custom_call", output_to_operand_aliasing={{1}: (4, {}), {2}: (5, {})} | custom-call | flops 6600000000 | bytes 7143424 | tf_op jit(solution)/shard_map/attention_forward/pallas_call | solution.py:181
  77.0 6.1 %attention_forward.5 = (bf16[512,768]{1,0:T(8,128)(2,1)}, bf16[2,3,128,256]{3,2,1,0:T(8,128)(2,1)}, bf16[2,3,128,256]{3,2,1,0:T(8,128)(2,1)}, f32[2,8,512]{2,1,0:T(8,128)}) custom-call(bf16[2,3,128,1024]{3,2,1,0:T(8,128)(2,1)} %copy-done.3, bf16[2,3,128,1024]{3,2,1,0:T(8,128)(2,1)} %collective-permute-done.4.refs_1_, ...), custom_call_target="tpu_custom_call", output_to_operand_aliasing={{1}: (4, {}), {2}: (5, {})} | custom-call | flops 6600000000 | bytes 7143424 | tf_op jit(solution)/shard_map/attention_forward/pallas_call | solution.py:181
  86.5 11.4 %collective-permute-done.20 = bf16[2,3,128,256]{3,2,1,0:T(8,128)(2,1)S(1)} collective-permute-done((bf16[2,3,128,256]{3,2,1,0:T(8,128)(2,1)}, bf16[2,3,128,256]{3,2,1,0:T(8,128)(2,1)S(1)}, u32[]{:S(2)}, u32[]{:S(2)}) %collective-permute-start.20) | collective-permute-done | bytes 393248 | tf_op jit(solution)/shard_map/ppermute | solution.py:85
  109.8 6.2 %output_norm.1 = (f32[384,1024]{1,0:T(8,128)}, f32[384,1024]{1,0:T(8,128)}, bf16[384,1024]{1,0:T(8,128)(2,1)}, bf16[1024,1024]{1,0:T(8,128)(2,1)}) custom-call(bf16[384,1024]{1,0:T(8,128)(2,1)} %bitcast.105, f32[8,1024]{1,0:T(8,128)} %get-tuple-element.172.refs_3_.refs_1_.refs_4_, bf16[128,1024]{1,0:T(8,128)(2,1)} %refs_2_.6, bf16[128,3072]{1,0:T(8,128)(2,1)} %copy-done.12, ...), custom_call_target="tpu_custom_call" | custom-call | flops 7699999744 | bytes 10649600 | tf_op jit(solution)/shard_map/output_norm/pallas_call | solution.py:181
  116.7 5.4 %collective-permute-done.24 = bf16[1,3,512,256]{3,2,1,0:T(8,128)(2,1)S(1)} collective-permute-done((bf16[1,3,512,256]{3,2,1,0:T(8,128)(2,1)S(1)}, bf16[1,3,512,256]{3,2,1,0:T(8,128)(2,1)S(1)}, u32[]{:S(2)}, u32[]{:S(2)}) %collective-permute-start.24) | collective-permute-done | bytes 786464 | tf_op jit(solution)/shard_map/ppermute | solution.py:1226
  126.8 14.4 %up_forward.1 = (bf16[4,768,512]{2,1,0:T(8,128)(2,1)}, bf16[4,768,512]{2,1,0:T(8,128)(2,1)}, bf16[4,1024,512]{2,1,0:T(8,128)(2,1)}) custom-call(bf16[384,1024]{1,0:T(8,128)(2,1)} %get-tuple-element.209.refs_0_, bf16[384,1024]{1,0:T(8,128)(2,1)} %collective-permute-done.22.refs_1_, bf16[128,4096]{1,0:T(8,128)(2,1)} %refs_2_.7, bf16[128,3072]{1,0:T(8,128)(2,1)} %copy-done.12, ...), custom_call_target="tpu_custom_call" | custom-call | flops 16499999744 | bytes 17055744 | tf_op jit(solution)/shard_map/up_forward/pallas_call | solution.py:181
  141.2 5.6 %collective-permute-done.25.refs_3_ = bf16[2,3,512,256]{3,2,1,0:T(8,128)(2,1)S(1)} collective-permute-done((bf16[2,3,512,256]{3,2,1,0:T(8,128)(2,1)S(1)}, bf16[2,3,512,256]{3,2,1,0:T(8,128)(2,1)S(1)}, u32[]{:S(2)}, u32[]{:S(2)}) %collective-permute-start.25) | collective-permute-done | bytes 1572896 | tf_op jit(solution)/shard_map/ppermute | solution.py:1220
  148.0 9.6 %down_forward.1 = (f32[384,1024]{1,0:T(8,128)}, bf16[384,1024]{1,0:T(8,128)(2,1)}, bf16[2048,1024]{1,0:T(8,128)(2,1)}) custom-call(bf16[4,768,512]{2,1,0:T(8,128)(2,1)} %get-tuple-element.193.refs_0_, bf16[512,1024]{1,0:T(8,128)(2,1)} %refs_1_.5, bf16[2,3,512,256]{3,2,1,0:T(8,128)(2,1)} %copy-done.21, bf16[2,3,512,256]{3,2,1,0:T(8,128)(2,1)} %copy-done.31), custom_call_target="tpu_custom_call" | custom-call | flops 11000000512 | bytes 13893632 | tf_op jit(solution)/shard_map/down_forward/pallas_call | solution.py:181
  161.1 5.4 %norm_two.1 = (bf16[384,1024]{1,0:T(8,128)(2,1)}, f32[384,1024]{1,0:T(8,128)}, bf16[384,1024]{1,0:T(8,128)(2,1)}, f32[8,1024]{1,0:T(8,128)}) custom-call(f32[384,1024]{1,0:T(8,128)} %get-tuple-element.186.refs_0_, f32[384,1024]{1,0:T(8,128)} %get-tuple-element.195.refs_1_, bf16[384,1024]{1,0:T(8,128)(2,1)} %copy-done.34, bf16[384,1024]{1,0:T(8,128)(2,1)} %bitcast.132, ...), custom_call_target="tpu_custom_call" | custom-call | flops 6600000000 | bytes 7929856 | tf_op jit(solution)/shard_map/norm_two/pallas_call | solution.py:181
  170.0 5.8 %down_weights.2 = bf16[2,4,512,256]{3,2,1,0:T(8,128)(2,1)} custom-call(bf16[4,768,512]{2,1,0:T(8,128)(2,1)} %get-tuple-element.193.refs_0_, bf16[384,1024]{1,0:T(8,128)(2,1)} %get-tuple-element.201.refs_1_.refs_0_, bf16[384,1024]{1,0:T(8,128)(2,1)} %copy-done.33), custom_call_target="tpu_custom_call" | custom-call | flops 5500000256 | bytes 6815744 | tf_op jit(solution)/shard_map/down_weights/pallas_call | solution.py:181
  176.2 5.8 %down_weights.3 = bf16[2,4,512,256]{3,2,1,0:T(8,128)(2,1)} custom-call(bf16[4,768,512]{2,1,0:T(8,128)(2,1)} %get-tuple-element.193.refs_0_, bf16[384,1024]{1,0:T(8,128)(2,1)} %get-tuple-element.201.refs_1_.refs_0_, bf16[384,1024]{1,0:T(8,128)(2,1)} %copy-done.33), custom_call_target="tpu_custom_call" | custom-call | flops 5500000256 | bytes 6815744 | tf_op jit(solution)/shard_map/down_weights/pallas_call | solution.py:181
  182.0 12.7 %ffn_backward.1 = (bf16[4,768,512]{2,1,0:T(8,128)(2,1)}, f32[4,8,512]{2,1,0:T(8,128)}, f32[384,1024]{1,0:T(8,128)}, bf16[384,1024]{1,0:T(8,128)(2,1)}) custom-call(bf16[384,1024]{1,0:T(8,128)(2,1)} %get-tuple-element.201.refs_1_.refs_0_, bf16[384,1024]{1,0:T(8,128)(2,1)} %copy-done.33, bf16[2048,1024]{1,0:T(8,128)(2,1)} %get-tuple-element.202.refs_2_, ...), custom_call_target="tpu_custom_call" | custom-call | flops 14300000256 | bytes 18677760 | tf_op jit(solution)/shard_map/ffn_backward/pallas_call | solution.py:181
  195.1 5.2 %up_weights.2 = bf16[2,4,128,1024]{3,2,1,0:T(8,128)(2,1)} custom-call(bf16[384,1024]{1,0:T(8,128)(2,1)} %get-tuple-element.209.refs_0_, bf16[384,1024]{1,0:T(8,128)(2,1)} %collective-permute-done.22.refs_1_, bf16[4,768,512]{2,1,0:T(8,128)(2,1)} %get-tuple-element.207.refs_2_), custom_call_target="tpu_custom_call" | custom-call | flops 6600000000 | bytes 6815744 | tf_op jit(solution)/shard_map/up_weights/pallas_call | solution.py:181
  205.8 5.3 %up_weights.3 = bf16[2,4,128,1024]{3,2,1,0:T(8,128)(2,1)} custom-call(bf16[384,1024]{1,0:T(8,128)(2,1)} %get-tuple-element.209.refs_0_, bf16[384,1024]{1,0:T(8,128)(2,1)} %collective-permute-done.22.refs_1_, bf16[4,768,512]{2,1,0:T(8,128)(2,1)} %get-tuple-element.207.refs_2_), custom_call_target="tpu_custom_call" | custom-call | flops 6600000000 | bytes 6815744 | tf_op jit(solution)/shard_map/up_weights/pallas_call | solution.py:181
  211.2 7.4 %norm_one_back.1 = (f32[384,1024]{1,0:T(8,128)}, bf16[384,1024]{1,0:T(8,128)(2,1)}, f32[8,8,768]{2,1,0:T(8,128)}, bf16[2,384,256]{2,1,0:T(8,128)(2,1)}, bf16[2,384,256]{2,1,0:T(8,128)(2,1)}) custom-call(f32[384,1024]{1,0:T(8,128)} %get-tuple-element.198.refs_0_, f32[384,1024]{1,0:T(8,128)} %get-tuple-element.210.refs_1_, ...), custom_call_target="tpu_custom_call" | custom-call | flops 8800000000 | bytes 11010048 | tf_op jit(solution)/shard_map/norm_one_back/pallas_call | solution.py:181
  218.5 4.3 %out_weights.1 = (bf16[4,4,128,256]{3,2,1,0:T(8,128)(2,1)}, bf16[4,4,128,256]{3,2,1,0:T(8,128)(2,1)}) custom-call(bf16[384,1024]{1,0:T(8,128)(2,1)} %get-tuple-element.217.refs_0_, bf16[2,384,256]{2,1,0:T(8,128)(2,1)} %bitcast.100, bf16[2,384,256]{2,1,0:T(8,128)(2,1)} %bitcast.111, bf16[2,384,256]{2,1,0:T(8,128)(2,1)} %bitcast.98), custom_call_target="tpu_custom_call" | custom-call | tf_op jit(solution)/shard_map/out_weights/pallas_call | solution.py:181
  224.6 11.5 %collective-permute-done.33.refs_7_ = bf16[2,3,128,256]{3,2,1,0:T(8,128)(2,1)S(1)} collective-permute-done((bf16[2,3,128,256]{3,2,1,0:T(8,128)(2,1)}, bf16[2,3,128,256]{3,2,1,0:T(8,128)(2,1)S(1)}, u32[]{:S(2)}, u32[]{:S(2)}) %collective-permute-start.33) | collective-permute-done | bytes 393248 | tf_op jit(solution)/shard_map/ppermute | solution.py:85
  238.0 7.9 %collective-permute-done.34.refs_6_ = bf16[2,3,128,256]{3,2,1,0:T(8,128)(2,1)S(1)} collective-permute-done((bf16[2,3,128,256]{3,2,1,0:T(8,128)(2,1)S(1)}, bf16[2,3,128,256]{3,2,1,0:T(8,128)(2,1)S(1)}, u32[]{:S(2)}, u32[]{:S(2)}) %collective-permute-start.34) | collective-permute-done | bytes 393248 | tf_op jit(solution)/shard_map/ppermute | solution.py:85
  245.9 4.0 %add_convert_fusion = (bf16[1,4,128,1024]{3,2,1,0:T(8,128)(2,1)S(1)}, bf16[4,128,1024]{2,1,0:T(8,128)(2,1)}) fusion(bf16[2,4,128,1024]{3,2,1,0:T(8,128)(2,1)} %up_weights.3, bf16[2,4,128,1024]{3,2,1,0:T(8,128)(2,1)S(1)} %collective-permute-done.30), kind=kLoop, calls=%fused_computation | loop fusion | flops 4194304 | bytes 6291456 | tf_op jit(solution)/shard_map/convert_element_type | solution.py:115
  260.4 7.9 %attention_backward.3 = (bf16[3,512,768]{2,1,0:T(8,128)(2,1)}, bf16[2,3,128,1024]{3,2,1,0:T(8,128)(2,1)}, bf16[2,3,128,1024]{3,2,1,0:T(8,128)(2,1)}) custom-call(bf16[512,768]{1,0:T(8,128)(2,1)} %get-tuple-element.228.refs_0_, bf16[1024,768]{1,0:T(8,128)(2,1)} %get-tuple-element.159.refs_2_.refs_1_, f32[2,8,512]{2,1,0:T(8,128)} %get-tuple-element.229.refs_2_, ...), custom_call_target="tpu_custom_call" | custom-call | flops 8800000000 | bytes 9863168 | tf_op jit(solution)/shard_map/attention_backward/pallas_call | solution.py:181
  270.9 10.5 %collective-permute-done.35 = bf16[1,4,128,1024]{3,2,1,0:T(8,128)(2,1)} collective-permute-done((bf16[1,4,128,1024]{3,2,1,0:T(8,128)(2,1)S(1)}, bf16[1,4,128,1024]{3,2,1,0:T(8,128)(2,1)}, u32[]{:S(2)}, u32[]{:S(2)}) %collective-permute-start.35) | collective-permute-done | bytes 1048608 | tf_op jit(solution)/shard_map/ppermute | solution.py:1383
  286.0 8.2 %attention_backward.4 = (bf16[3,512,768]{2,1,0:T(8,128)(2,1)}, bf16[2,3,128,1024]{3,2,1,0:T(8,128)(2,1)}, bf16[2,3,128,1024]{3,2,1,0:T(8,128)(2,1)}) custom-call(bf16[512,768]{1,0:T(8,128)(2,1)} %get-tuple-element.241.refs_0_, bf16[1024,768]{1,0:T(8,128)(2,1)} %get-tuple-element.159.refs_2_.refs_1_, ...), custom_call_target="tpu_custom_call", output_to_operand_aliasing={{0}: (8, {}), {1}: (9, {}), {2}: (10, {})} | custom-call | flops 8800000000 | bytes 15368192 | tf_op jit(solution)/shard_map/attention_backward/pallas_call | solution.py:181
  295.1 7.7 %collective-permute-done.39 = bf16[2,128,1280]{2,1,0:T(8,128)(2,1)S(1)} collective-permute-done((bf16[2,128,1280]{2,1,0:T(8,128)(2,1)}, bf16[2,128,1280]{2,1,0:T(8,128)(2,1)S(1)}, u32[]{:S(2)}, u32[]{:S(2)}) %collective-permute-start.39) | collective-permute-done | bytes 655392 | tf_op jit(solution)/shard_map/ppermute | solution.py:1428
  305.5 7.8 %attention_backward.5 = (bf16[3,512,768]{2,1,0:T(8,128)(2,1)}, bf16[2,3,128,1024]{3,2,1,0:T(8,128)(2,1)}, bf16[2,3,128,1024]{3,2,1,0:T(8,128)(2,1)}) custom-call(bf16[512,768]{1,0:T(8,128)(2,1)} %get-tuple-element.248.refs_0_, bf16[1024,768]{1,0:T(8,128)(2,1)} %get-tuple-element.159.refs_2_.refs_1_, ...), custom_call_target="tpu_custom_call", output_to_operand_aliasing={{0}: (8, {}), {1}: (9, {}), {2}: (10, {})} | custom-call | flops 8800000000 | bytes 15368192 | tf_op jit(solution)/shard_map/attention_backward/pallas_call | solution.py:181
  314.5 6.1 %collective-permute-done.43.refs_1_ = bf16[1,128,1280]{2,1,0:T(8,128)(2,1)S(1)} collective-permute-done((bf16[1,128,1280]{2,1,0:T(8,128)(2,1)S(1)}, bf16[1,128,1280]{2,1,0:T(8,128)(2,1)S(1)}, u32[]{:S(2)}, u32[]{:S(2)}) %collective-permute-start.43) | collective-permute-done | bytes 327712 | tf_op jit(solution)/shard_map/ppermute | solution.py:1436
  323.1 6.7 %head_weights_backward.1 = (bf16[4,144,768]{2,1,0:T(8,128)(2,1)}, bf16[4,144,768]{2,1,0:T(8,128)(2,1)}) custom-call(bf16[2,3,128,1024]{3,2,1,0:T(8,128)(2,1)} %copy-done.3, bf16[2,3,128,1024]{3,2,1,0:T(8,128)(2,1)} %collective-permute-done.4.refs_1_, bf16[3,512,768]{2,1,0:T(8,128)(2,1)} %get-tuple-element.257.refs_2_, ...), custom_call_target="tpu_custom_call" | custom-call | flops 8800000000 | bytes 7536640 | tf_op jit(solution)/shard_map/head_weights_backward/pallas_call | solution.py:181
  342.1 8.0 %collective-permute-done.47 = bf16[2,144,768]{2,1,0:T(8,128)(2,1)S(1)} collective-permute-done((bf16[2,144,768]{2,1,0:T(8,128)(2,1)S(1)}, bf16[2,144,768]{2,1,0:T(8,128)(2,1)S(1)}, u32[]{:S(2)}, u32[]{:S(2)}) %collective-permute-start.47) | collective-permute-done | bytes 442400 | tf_op jit(solution)/shard_map/ppermute | solution.py:1428
  367.2 4.6 %collective-permute-done.50 = bf16[1,144,768]{2,1,0:T(8,128)(2,1)S(1)} collective-permute-done((bf16[1,144,768]{2,1,0:T(8,128)(2,1)S(1)}, bf16[1,144,768]{2,1,0:T(8,128)(2,1)S(1)}, u32[]{:S(2)}, u32[]{:S(2)}) %collective-permute-start.50) | collective-permute-done | bytes 221216 | tf_op jit(solution)/shard_map/ppermute | solution.py:111
  (237 shorter events, 150.4 us)
Async XLA Ops:
  0.7 13.2 %collective-permute-start.1 = (bf16[1,3,128,1024]{3,2,1,0:T(8,128)(2,1)}, bf16[1,3,128,1024]{3,2,1,0:T(8,128)(2,1)S(1)}, u32[]{:S(2)}, u32[]{:S(2)}) collective-permute-start(bf16[1,3,128,1024]{3,2,1,0:T(8,128)(2,1)} %bitcast.104), channel_id=1, source_target_pairs={{0,1},{1,0},{2,3},{3,2},{4,6},{5,7},{6,4},{7,5},{8,9},{9,8},{10,11... | collective-permute-start | bytes 2359304 | tf_op jit(solution)/shard_map/ppermute | solution.py:111
  17.1 29.2 %collective-permute-start.4 = (bf16[2,3,128,1024]{3,2,1,0:T(8,128)(2,1)S(1)}, bf16[2,3,128,1024]{3,2,1,0:T(8,128)(2,1)}, u32[]{:S(2)}, u32[]{:S(2)}) collective-permute-start(bf16[2,3,128,1024]{3,2,1,0:T(8,128)(2,1)S(1)} %pad_maximum_fusion.refs_0_), channel_id=1, source_target_pairs={{0,2},{1,3},{2,0},{3,1},{4,5},{5,4},{6,7},{7,6},{8,10},{9,11},{10,... | collective-permute-start | bytes 4718600 | tf_op jit(solution)/shard_map/ppermute | solution.py:1220
  46.7 14.2 %collective-permute-start.9 = (bf16[1,3,128,256]{3,2,1,0:T(8,128)(2,1)S(1)}, bf16[1,3,128,256]{3,2,1,0:T(8,128)(2,1)S(1)}, u32[]{:S(2)}, u32[]{:S(2)}) collective-permute-start(bf16[1,3,128,256]{3,2,1,0:T(8,128)(2,1)S(1)} %bitcast.101), channel_id=1, source_target_pairs={{0,1},{1,0},{2,3},{3,2},{4,6},{5,7},{6,4},{7,5},{8,9},{9,8},{10,11... | collective-permute-start | bytes 589832 | tf_op jit(solution)/shard_map/ppermute | solution.py:1226
  47.3 14.3 %collective-permute-start.7 = (bf16[512,256]{1,0:T(8,128)(2,1)S(1)}, bf16[512,256]{1,0:T(8,128)(2,1)S(1)}, u32[]{:S(2)}, u32[]{:S(2)}) collective-permute-start(bf16[512,256]{1,0:T(8,128)(2,1)S(1)} %copy-done.40), channel_id=1, source_target_pairs={{0,8},{1,9},{2,10},{3,11},{4,12},{5,13},{6,14},{7,15},{8,24},{9,25... | collective-permute-start | bytes 786440 | tf_op jit(solution)/shard_map/ppermute | solution.py:1232
  47.9 14.1 %collective-permute-start.10 = (bf16[256,512]{1,0:T(8,128)(2,1)S(1)}, bf16[256,512]{1,0:T(8,128)(2,1)S(1)}, u32[]{:S(2)}, u32[]{:S(2)}) collective-permute-start(bf16[256,512]{1,0:T(8,128)(2,1)S(1)} %collective-permute-done.5), channel_id=1, source_target_pairs={{0,8},{1,9},{2,10},{3,11},{4,12},{5,13},{6,14},{7,15},{8,24},{9,25... | collective-permute-start | bytes 786440 | tf_op jit(solution)/shard_map/ppermute | solution.py:1232
  62.1 13.7 %collective-permute-start.13 = (bf16[256,512]{1,0:T(8,128)(2,1)S(1)}, bf16[256,512]{1,0:T(8,128)(2,1)S(1)}, u32[]{:S(2)}, u32[]{:S(2)}) collective-permute-start(bf16[256,512]{1,0:T(8,128)(2,1)S(1)} %collective-permute-done.10), channel_id=1, source_target_pairs={{0,8},{1,9},{2,10},{3,11},{4,12},{5,13},{6,14},{7,15},{8,24},{9,25... | collective-permute-start | bytes 786440 | tf_op jit(solution)/shard_map/ppermute | solution.py:1232
  62.6 13.0 %collective-permute-start.11 = (bf16[1,2,256,512]{3,2,1,0:T(8,128)(2,1)S(1)}, bf16[1,2,256,512]{3,2,1,0:T(8,128)(2,1)S(1)}, u32[]{:S(2)}, u32[]{:S(2)}) collective-permute-start(bf16[1,2,256,512]{3,2,1,0:T(8,128)(2,1)S(1)} %bitcast.86), channel_id=1, source_target_pairs={{0,1},{1,0},{2,3},{3,2},{4,6},{5,7},{6,4},{7,5},{8,9},{9,8},{10,11... | collective-permute-start | bytes 1572872 | tf_op jit(solution)/shard_map/ppermute | solution.py:1226
  63.3 12.7 %collective-permute-start.12 = (bf16[2,3,128,256]{3,2,1,0:T(8,128)(2,1)}, bf16[2,3,128,256]{3,2,1,0:T(8,128)(2,1)}, u32[]{:S(2)}, u32[]{:S(2)}) collective-permute-start(bf16[2,3,128,256]{3,2,1,0:T(8,128)(2,1)} %constant_dynamic-update-slice_fusion.refs_4_), channel_id=1, source_target_pairs={{0,2},{1,3},{2,0},{3,1},{4,5},{5,4},{6,7},{7,6},{8,10},{9,11},{10,... | collective-permute-start | bytes 1179656 | tf_op jit(solution)/shard_map/ppermute | solution.py:1220
  76.0 29.5 %collective-permute-start.15 = (bf16[2,2,256,512]{3,2,1,0:T(8,128)(2,1)S(1)}, bf16[2,2,256,512]{3,2,1,0:T(8,128)(2,1)}, u32[]{:S(2)}, u32[]{:S(2)}) collective-permute-start(bf16[2,2,256,512]{3,2,1,0:T(8,128)(2,1)S(1)} %constant_dynamic-update-slice_fusion.2.refs_5_), channel_id=1, source_target_pairs={{0,2},{1,3},{2,0},{3,1},{4,5},{5,4},{6,7},{7,6},{8,10},{9,11},{10,... | collective-permute-start | bytes 3145736 | tf_op jit(solution)/shard_map/ppermute | solution.py:1220
  83.1 14.8 %collective-permute-start.20 = (bf16[2,3,128,256]{3,2,1,0:T(8,128)(2,1)}, bf16[2,3,128,256]{3,2,1,0:T(8,128)(2,1)S(1)}, u32[]{:S(2)}, u32[]{:S(2)}) collective-permute-start(bf16[2,3,128,256]{3,2,1,0:T(8,128)(2,1)} %get-tuple-element.185.refs_4_), channel_id=1, source_target_pairs={{0,2},{1,3},{2,0},{3,1},{4,5},{5,4},{6,7},{7,6},{8,10},{9,11},{10,... | collective-permute-start | bytes 1179656 | tf_op jit(solution)/shard_map/ppermute | solution.py:85
  84.2 16.7 %collective-permute-start.16 = (bf16[1,1,256,512]{3,2,1,0:T(8,128)(2,1)S(1)}, bf16[1,1,256,512]{3,2,1,0:T(8,128)(2,1)S(1)}, u32[]{:S(2)}, u32[]{:S(2)}) collective-permute-start(bf16[1,1,256,512]{3,2,1,0:T(8,128)(2,1)S(1)} %bitcast.112), channel_id=1, source_target_pairs={{0,1},{1,0},{2,3},{3,2},{4,6},{5,7},{6,4},{7,5},{8,9},{9,8},{10,11... | collective-permute-start | bytes 786440 | tf_op jit(solution)/shard_map/ppermute | solution.py:1226
  85.0 20.5 %collective-permute-start.18 = (bf16[2,3,128,256]{3,2,1,0:T(8,128)(2,1)}, bf16[2,3,128,256]{3,2,1,0:T(8,128)(2,1)S(1)}, u32[]{:S(2)}, u32[]{:S(2)}) collective-permute-start(bf16[2,3,128,256]{3,2,1,0:T(8,128)(2,1)} %constant_dynamic-update-slice_fusion.refs_4_), channel_id=1, source_target_pairs={{0,4},{1,5},{2,6},{3,7},{4,0},{5,1},{6,2},{7,3},{8,12},{9,13},{10,... | collective-permute-start | bytes 1179656 | tf_op jit(solution)/shard_map/ppermute | solution.py:75
  85.0 20.5 %collective-permute-start.19 = (bf16[2,3,128,256]{3,2,1,0:T(8,128)(2,1)}, bf16[2,3,128,256]{3,2,1,0:T(8,128)(2,1)S(1)}, u32[]{:S(2)}, u32[]{:S(2)}) collective-permute-start(bf16[2,3,128,256]{3,2,1,0:T(8,128)(2,1)} %collective-permute-done.12.refs_5_), channel_id=1, source_target_pairs={{0,4},{1,5},{2,6},{3,7},{4,0},{5,1},{6,2},{7,3},{8,12},{9,13},{10,... | collective-permute-start | bytes 1179656 | tf_op jit(solution)/shard_map/ppermute | solution.py:75
  108.8 13.3 %collective-permute-start.24 = (bf16[1,3,512,256]{3,2,1,0:T(8,128)(2,1)S(1)}, bf16[1,3,512,256]{3,2,1,0:T(8,128)(2,1)S(1)}, u32[]{:S(2)}, u32[]{:S(2)}) collective-permute-start(bf16[1,3,512,256]{3,2,1,0:T(8,128)(2,1)S(1)} %bitcast.84), channel_id=1, source_target_pairs={{0,1},{1,0},{2,3},{3,2},{4,6},{5,7},{6,4},{7,5},{8,9},{9,8},{10,11... | collective-permute-start | bytes 2359304 | tf_op jit(solution)/shard_map/ppermute | solution.py:1226
  126.3 20.4 %collective-permute-start.25 = (bf16[2,3,512,256]{3,2,1,0:T(8,128)(2,1)S(1)}, bf16[2,3,512,256]{3,2,1,0:T(8,128)(2,1)S(1)}, u32[]{:S(2)}, u32[]{:S(2)}) collective-permute-start(bf16[2,3,512,256]{3,2,1,0:T(8,128)(2,1)S(1)} %constant_dynamic-update-slice_fusion.6.refs_2_), channel_id=1, source_target_pairs={{0,2},{1,3},{2,0},{3,1},{4,5},{5,4},{6,7},{7,6},{8,10},{9,11},{10,... | collective-permute-start | bytes 4718600 | tf_op jit(solution)/shard_map/ppermute | solution.py:1220
  175.8 26.4 %collective-permute-start.28 = (bf16[2,4,512,256]{3,2,1,0:T(8,128)(2,1)}, bf16[2,4,512,256]{3,2,1,0:T(8,128)(2,1)}, u32[]{:S(2)}, u32[]{:S(2)}) collective-permute-start(bf16[2,4,512,256]{3,2,1,0:T(8,128)(2,1)} %down_weights.2), channel_id=1, source_target_pairs={{0,2},{1,3},{2,0},{3,1},{4,5},{5,4},{6,7},{7,6},{8,10},{9,11},{10,... | collective-permute-start | bytes 6291464 | tf_op jit(solution)/shard_map/ppermute | solution.py:1383
  194.7 16.5 %collective-permute-start.29 = (bf16[384,1024]{1,0:T(8,128)(2,1)}, bf16[384,1024]{1,0:T(8,128)(2,1)}, u32[]{:S(2)}, u32[]{:S(2)}) collective-permute-start(bf16[384,1024]{1,0:T(8,128)(2,1)} %get-tuple-element.211), channel_id=1, source_target_pairs={{0,4},{1,5},{2,6},{3,7},{4,0},{5,1},{6,2},{7,3},{8,12},{9,13},{10,... | collective-permute-start | bytes 2359304 | tf_op jit(solution)/shard_map/ppermute | solution.py:75
  200.3 37.7 %collective-permute-start.30 = (bf16[2,4,128,1024]{3,2,1,0:T(8,128)(2,1)}, bf16[2,4,128,1024]{3,2,1,0:T(8,128)(2,1)S(1)}, u32[]{:S(2)}, u32[]{:S(2)}) collective-permute-start(bf16[2,4,128,1024]{3,2,1,0:T(8,128)(2,1)} %up_weights.2), channel_id=1, source_target_pairs={{0,2},{1,3},{2,0},{3,1},{4,5},{5,4},{6,7},{7,6},{8,10},{9,11},{10,... | collective-permute-start | bytes 6291464 | tf_op jit(solution)/shard_map/ppermute | solution.py:1383
  222.8 23.1 %collective-permute-start.31 = (bf16[4,4,128,256]{3,2,1,0:T(8,128)(2,1)}, bf16[4,4,128,256]{3,2,1,0:T(8,128)(2,1)S(1)}, u32[]{:S(2)}, u32[]{:S(2)}) collective-permute-start(bf16[4,4,128,256]{3,2,1,0:T(8,128)(2,1)} %get-tuple-element.219), channel_id=1, source_target_pairs={{0,4},{1,5},{2,6},{3,7},{4,0},{5,1},{6,2},{7,3},{8,12},{9,13},{10,... | collective-permute-start | bytes 3145736 | tf_op jit(solution)/shard_map/ppermute | solution.py:75
  222.8 23.1 %collective-permute-start.32 = (bf16[1,4,512,256]{3,2,1,0:T(8,128)(2,1)S(1)}, bf16[1,4,512,256]{3,2,1,0:T(8,128)(2,1)S(1)}, u32[]{:S(2)}, u32[]{:S(2)}) collective-permute-start(bf16[1,4,512,256]{3,2,1,0:T(8,128)(2,1)S(1)} %get-tuple-element.284), channel_id=1, source_target_pairs={{0,1},{1,0},{2,3},{3,2},{4,6},{5,7},{6,4},{7,5},{8,9},{9,8},{10,11... | collective-permute-start | bytes 3145736 | tf_op jit(solution)/shard_map/ppermute | solution.py:1383
  254.4 14.2 %collective-permute-start.40 = (bf16[2,512,256]{2,1,0:T(8,128)(2,1)}, bf16[2,512,256]{2,1,0:T(8,128)(2,1)S(1)}, u32[]{:S(2)}, u32[]{:S(2)}) collective-permute-start(bf16[2,512,256]{2,1,0:T(8,128)(2,1)} %get-tuple-element.239), channel_id=1, source_target_pairs={{0,8},{1,9},{2,10},{3,11},{4,12},{5,13},{6,14},{7,15},{8,0},{9,1},... | collective-permute-start | bytes 1572872 | tf_op jit(solution)/shard_map/ppermute | solution.py:1428
  256.0 14.9 %collective-permute-start.38 = (bf16[4,128,256]{2,1,0:T(8,128)(2,1)S(1)}, bf16[4,128,256]{2,1,0:T(8,128)(2,1)}, u32[]{:S(2)}, u32[]{:S(2)}) collective-permute-start(bf16[4,128,256]{2,1,0:T(8,128)(2,1)S(1)} %get-tuple-element.235), channel_id=1, source_target_pairs={{0,3},{1,2},{2,1},{3,0},{4,7},{5,6},{6,5},{7,4},{8,11},{9,10},{10,... | collective-permute-start | bytes 786440 | tf_op jit(solution)/shard_map/ppermute | solution.py:79
  257.4 13.5 %collective-permute-start.37 = (bf16[4,128,256]{2,1,0:T(8,128)(2,1)S(1)}, bf16[4,128,256]{2,1,0:T(8,128)(2,1)}, u32[]{:S(2)}, u32[]{:S(2)}) collective-permute-start(bf16[4,128,256]{2,1,0:T(8,128)(2,1)S(1)} %get-tuple-element.234), channel_id=1, source_target_pairs={{0,2},{1,3},{2,0},{3,1},{4,5},{5,4},{6,7},{7,6},{8,10},{9,11},{10,... | collective-permute-start | bytes 786440 | tf_op jit(solution)/shard_map/ppermute | solution.py:79
  258.4 12.6 %collective-permute-start.36 = (bf16[4,128,256]{2,1,0:T(8,128)(2,1)S(1)}, bf16[4,128,256]{2,1,0:T(8,128)(2,1)}, u32[]{:S(2)}, u32[]{:S(2)}) collective-permute-start(bf16[4,128,256]{2,1,0:T(8,128)(2,1)S(1)} %get-tuple-element.233), channel_id=1, source_target_pairs={{0,1},{1,0},{2,3},{3,2},{4,6},{5,7},{6,4},{7,5},{8,9},{9,8},{10,11... | collective-permute-start | bytes 786440 | tf_op jit(solution)/shard_map/ppermute | solution.py:79
  259.5 21.9 %collective-permute-start.35 = (bf16[1,4,128,1024]{3,2,1,0:T(8,128)(2,1)S(1)}, bf16[1,4,128,1024]{3,2,1,0:T(8,128)(2,1)}, u32[]{:S(2)}, u32[]{:S(2)}) collective-permute-start(bf16[1,4,128,1024]{3,2,1,0:T(8,128)(2,1)S(1)} %get-tuple-element.281), channel_id=1, source_target_pairs={{0,1},{1,0},{2,3},{3,2},{4,6},{5,7},{6,4},{7,5},{8,9},{9,8},{10,11... | collective-permute-start | bytes 3145736 | tf_op jit(solution)/shard_map/ppermute | solution.py:1383
  268.7 25.4 %collective-permute-start.41 = (bf16[1,512,256]{2,1,0:T(8,128)(2,1)S(1)}, bf16[1,512,256]{2,1,0:T(8,128)(2,1)}, u32[]{:S(2)}, u32[]{:S(2)}) collective-permute-start(bf16[1,512,256]{2,1,0:T(8,128)(2,1)S(1)} %get-tuple-element.291), channel_id=1, source_target_pairs={{0,16},{1,17},{2,18},{3,19},{4,20},{5,21},{6,22},{7,23},{8,24},{9,... | collective-permute-start | bytes 786440 | tf_op jit(solution)/shard_map/ppermute | solution.py:1436
  285.2 17.7 %collective-permute-start.39 = (bf16[2,128,1280]{2,1,0:T(8,128)(2,1)}, bf16[2,128,1280]{2,1,0:T(8,128)(2,1)S(1)}, u32[]{:S(2)}, u32[]{:S(2)}) collective-permute-start(bf16[2,128,1280]{2,1,0:T(8,128)(2,1)} %get-tuple-element.237), channel_id=1, source_target_pairs={{0,8},{1,9},{2,10},{3,11},{4,12},{5,13},{6,14},{7,15},{8,0},{9,1},... | collective-permute-start | bytes 1966088 | tf_op jit(solution)/shard_map/ppermute | solution.py:1428
  303.8 16.8 %collective-permute-start.43 = (bf16[1,128,1280]{2,1,0:T(8,128)(2,1)S(1)}, bf16[1,128,1280]{2,1,0:T(8,128)(2,1)S(1)}, u32[]{:S(2)}, u32[]{:S(2)}) collective-permute-start(bf16[1,128,1280]{2,1,0:T(8,128)(2,1)S(1)} %get-tuple-element.289), channel_id=1, source_target_pairs={{0,16},{1,17},{2,18},{3,19},{4,20},{5,21},{6,22},{7,23},{8,24},{9,... | collective-permute-start | bytes 983048 | tf_op jit(solution)/shard_map/ppermute | solution.py:1436
  313.3 22.7 %collective-permute-start.42 = (bf16[2,3,128,1024]{3,2,1,0:T(8,128)(2,1)}, bf16[2,3,128,1024]{3,2,1,0:T(8,128)(2,1)S(1)}, u32[]{:S(2)}, u32[]{:S(2)}) collective-permute-start(bf16[2,3,128,1024]{3,2,1,0:T(8,128)(2,1)} %get-tuple-element.253), channel_id=1, source_target_pairs={{0,2},{1,3},{2,0},{3,1},{4,5},{5,4},{6,7},{7,6},{8,10},{9,11},{10,... | collective-permute-start | bytes 4718600 | tf_op jit(solution)/shard_map/ppermute | solution.py:1383
  337.3 21.0 %collective-permute-start.45 = (bf16[1,3,128,1024]{3,2,1,0:T(8,128)(2,1)}, bf16[1,3,128,1024]{3,2,1,0:T(8,128)(2,1)}, u32[]{:S(2)}, u32[]{:S(2)}) collective-permute-start(bf16[1,3,128,1024]{3,2,1,0:T(8,128)(2,1)} %add_convert_fusion.4), channel_id=1, source_target_pairs={{0,1},{1,0},{2,3},{3,2},{4,6},{5,7},{6,4},{7,5},{8,9},{9,8},{10,11... | collective-permute-start | bytes 2359304 | tf_op jit(solution)/shard_map/ppermute | solution.py:1383
  339.9 14.9 %collective-permute-start.48 = (bf16[2,512,256]{2,1,0:T(8,128)(2,1)S(1)}, bf16[2,512,256]{2,1,0:T(8,128)(2,1)S(1)}, u32[]{:S(2)}, u32[]{:S(2)}) collective-permute-start(bf16[2,512,256]{2,1,0:T(8,128)(2,1)S(1)} %pad_maximum_fusion.5.refs_0_), channel_id=1, source_target_pairs={{0,2},{1,3},{2,0},{3,1},{4,5},{5,4},{6,7},{7,6},{8,10},{9,11},{10,... | collective-permute-start | bytes 1572872 | tf_op jit(solution)/shard_map/ppermute | solution.py:108
  341.0 24.1 %collective-permute-start.53 = (bf16[1,128,1280]{2,1,0:T(8,128)(2,1)S(1)}, bf16[1,128,1280]{2,1,0:T(8,128)(2,1)S(1)}, u32[]{:S(2)}, u32[]{:S(2)}) collective-permute-start(bf16[1,128,1280]{2,1,0:T(8,128)(2,1)S(1)} %bitcast.92), channel_id=1, source_target_pairs={{0,1},{1,0},{2,3},{3,2},{4,6},{5,7},{6,4},{7,5},{8,9},{9,8},{10,11... | collective-permute-start | bytes 983048 | tf_op jit(solution)/shard_map/ppermute | solution.py:111
  (65 other events, 478.2 us)

commit v4 on v3

--- a/solution.py
+++ b/solution.py
@@ -79,11 +79,11 @@
             lax.ppermute(block, BOTH, way) for block, way in zip(blocks[1:], self.across[1:])
         ]
 
-    def exchange(self, keep, send):
+    def exchange(self, keep, send, *ready):
         held = [(0, keep, 0)]
         for k in reversed(range(self.bits)):
-            come = lax.ppermute(send, BOTH, self.stage[k])
-            width = 1 << k
+            come = after(lax.ppermute(send, BOTH, self.stage[k]), *ready)
+            width, ready = 1 << k, ()
             held = held + [
                 (mask | width, come, i * width) for i, (mask, _, _) in enumerate(held)
             ]
@@ -442,10 +442,14 @@
             return carry
 
         lax.fori_loop(0, cols // PAIR, each_pair, 0)
-        for r in range(n):
-            target = part_keep if r < half else part_send
-            rows = grad_ref[0, r * length : (r + 1) * length, :]
-            target[r % half, 0] = dot(rows, w_ref[...], 1, 1).astype(BF16)
+        for target, base in ((part_send, half), (part_keep, 0)):
+
+            def each_part(r, carry, target=target, base=base):
+                rows = grad_ref[0, aligned((base + r) * length, length), :]
+                target[r, 0] = dot(rows, w_ref[...], 1, 1).astype(BF16)
+                return carry
+
+            lax.fori_loop(0, half, each_part, 0)
 
     part = (half, seqs, length, width)
     outs = [shape((seqs, total, cols3)), shape(part), shape(part)]
@@ -576,8 +580,9 @@
             copy.start()
         for copy in copies:
             copy.wait()
-        for i in range(tokens // tile):
-            rows = pl.ds(i * tile, tile)
+
+        def each_tile(i, carry):
+            rows = aligned(i * tile, tile)
             total = in_ref[rows, :].astype(F32) + vec_ref[2:3, :]
             for r, (a, m) in enumerate(where):
                 weights = full_ref[aligned(t.member(r, t.c) * cols, cols), :]
@@ -587,6 +592,9 @@
             sum_ref[rows, :] = total
             norm_ref[rows, :] = normed
             low_ref[rows, :] = normed.astype(BF16)
+            return carry
+
+        lax.fori_loop(0, tokens // tile, each_tile, 0)
 
     full = (tokens, width)
     return call(
@@ -979,8 +987,9 @@
         sums[0:3, :] = jnp.zeros((3, width), F32)
         sums[3:6, :] = two_ref[0:3, :]
         sums[6:8, :] = jnp.zeros((2, width), F32)
-        for i in range(tokens // tile):
-            rows = pl.ds(i * tile, tile)
+
+        def each_tile(i, carry):
+            rows = aligned(i * tile, tile)
             above = grad_ref[rows, :] + (own_ref[rows, :] + come_ref[rows, :].astype(F32))
             unit, root = statistics(sum_ref[rows, :])
             grad = norm_back(unit, root, vec_ref[3:4, :], above)
@@ -994,6 +1003,9 @@
                 weights = w_ref[aligned(t.member(r, t.c) * cols, cols), :]
                 target = keep_ref if r < half else send_ref
                 target[r % half, rows, :] = dot(low, weights, 1, 1).astype(BF16)
+            return carry
+
+        lax.fori_loop(0, tokens // tile, each_tile, 0)
         narrow_ref[...] = jnp.zeros_like(narrow_ref)
         for owner in range(plan.n_dp):
             lanes = pl.ds(owner * own_rows, own_rows)
@@ -1346,14 +1358,13 @@
         parts = attend(g, parts, *ready)
 
     contexts = parts
-    pieces, where = distinct(plan.exchange(*parts))
+    send = after(parts[1], up_two[1], three_started[1], *others)
+    near_three = joined(three_started, send)
+    up_three = final(near_three)
+    pieces, where = distinct(plan.exchange(parts[0], send))
     pieces = [p.reshape(p.shape[0], tokens, cols) for p in pieces]
-    near_three = joined(three_started, parts[0])
-    ready = (parts[0], up_two[1], near_three, downs[-1]) + tuple(others)
-    downs = jnp.stack([after(piece, *ready) for piece in downs])
-    ready += (downs,) + tuple(pieces)
-    up_three = final(near_three, *ready)
-    downs_started = begin(downs, *ready)
+    downs = jnp.stack([after(piece, near_three) for piece in downs])
+    downs_started = begin(downs, *pieces)
     first_sum, normed, low, full_out = output_norm(
         plan,
         table,
@@ -1367,7 +1378,7 @@
         others,
     )
 
-    other_low = plan.swap(low)
+    other_low = plan.swap(after(low, up_three[1]))
     near_down = joined(downs_started, low)
     ready = (other_low, up_three[1], near_down)
     down_all = final(near_down, *ready)
@@ -1403,25 +1414,29 @@
     away = plan.swap(away)
     low = after(low, own)
     up_send = up_weights(plan, table, low, other_low, grad_pre, half)
-    up_come = begun(up_send, top)
     down_keep, down_send = middle(down_keep, down_come, up_send)
     down_last = begun(down_send, 0)
-    up_keep = up_weights(plan, table, after(low, up_send, down_send), other_low, grad_pre, 0)
     grad_first, low_one, sums, *parts = norm_one_back(
         plan,
         table,
         grad_second,
-        after(own, up_keep),
+        after(own, down_send),
         away,
         first_sum,
         vectors,
         full_out,
         sums_two,
     )
-    found = plan.exchange(*[p.reshape(half, seqs, length, cols) for p in parts])
+    up_keep = up_weights(plan, table, after(low, low_one), other_low, grad_pre, 0)
+    parts = [p.reshape(half, seqs, length, cols) for p in parts]
+    found = plan.exchange(parts[0], after(parts[1], down_last), up_keep)
+    out_keep, out_send = out_weights(
+        plan, table, pieces, where, after(low_one, found[half][0])
+    )
     parts, up_where = distinct(found)
-    out_keep, out_send = out_weights(plan, table, pieces, where, low_one)
-    out_come = plan.swap(out_send)
+    parts = [after(part, out_keep) for part in parts]
+    out_come = plan.swap(after(out_send, *parts))
+
     def sent_along_z(terms, *ready):
         terms = [[after(group[0], *ready)] + group[1:] for group in terms]
         keep, send = parts_along_z(plan, table, terms)
@@ -1454,40 +1469,39 @@
             before,
         )
 
-    ready = (out_keep, out_come, down_last, up_come) + tuple(parts)
-    up_keep, up_send = middle(up_keep, up_come, *ready)
+    ready = (out_keep, out_come) + tuple(parts)
+    up_come = begun(up_send, top, *ready)
+    out_come = after(out_come, *ready)
+    out_sent = add(out_keep[half:], out_come[half:])
+    out_first = begun(out_sent, top)
+    out_kept = add(out_keep[:half], out_come[:half])
+    shared = back(0, [], out_sent, out_kept, *ready)
+    down_along = sent_along_z([[down_keep[0], down_last[0]]], shared[0])
+    shared = back(1, list(shared), down_along[0])
+    up_keep, up_send = middle(up_keep, up_come, shared[0])
     up_last = begun(up_send, 0)
-    out_come = after(out_come, up_send)
-    outs = [add(out_keep[r], out_come[r]) for r in range(n)]
-    down_along = sent_along_z([[down_keep[0], down_last[0]]], up_send)
-    outs = plan.trade([after(v, down_along[0]) for v in outs])
-    shared = back(0, [], down_along[0], up_send, outs[0], *ready)
-    down_along = on_along_z(*down_along, shared[0])
-    up_along = sent_along_z([[up_keep[0], up_last[0]], outs], shared[0])
-    shared = back(1, list(shared), up_along[0], down_along[0])
-    grad_down = total(*down_along, shared[0])
-    up_along = on_along_z(*up_along, shared[0])
-    down_near = plan.halfway(grad_down, up_along[0])
+    down_along = on_along_z(*down_along, up_send)
+    out_kept, out_sent = middle(out_kept, out_first, up_send)
+    out_last = begun(out_sent, 0)
     for g in range(2, seqs):
-        shared = back(g, list(shared), up_along[0], grad_down)
+        shared = back(g, list(shared), up_send, out_sent, down_along[0])
     grad_qkv, part_keep, part_send = shared
-
-    part_come = begun(part_send, top)
-    up_along = (after(up_along[0], grad_qkv), up_along[1])
-    up_kept, up_sent, grad_out = split_by_core(plan, table, up_along, 2 * quarter)
-    up_come = plan.swap(up_sent)
-    down_far = plan.final(down_near, up_sent)
+    up_along = sent_along_z(
+        [[up_keep[0], up_last[0]], [out_kept[0], out_last[0]]], grad_qkv
+    )
+
+    part_come = begun(part_send, top, up_along[0])
+    down_started = begin(total(*down_along, up_along[0]))
     last_keep, last_send = head_weights_backward(
-        plan, table, near_x, far_x, after(grad_qkv, up_sent), sums, sums_up
-    )
+        plan, table, near_x, far_x, after(grad_qkv, up_along[0], down_started[0]), sums, sums_up
+    )
+    down_near = joined(down_started, last_keep)
+    down_far = plan.final(down_near)
+    up_along = on_along_z(*up_along, last_keep)
     last_come = plan.swap(last_send)
-    last_along = sent_along_z([[last_keep, last_come]])
-    up_kept = after(up_kept, last_along[0])
-    up_near = plan.halfway(jnp.concatenate([up_kept, up_come, grad_out], 1))
+    last_along = sent_along_z([[last_keep, last_come]], up_along[0])
     part_keep, part_send = middle(part_keep, part_come, last_along[0])
     part_last = begun(part_send, 0)
-    last_along = on_along_z(*last_along, part_send)
-    up_far = plan.final(up_near, last_along[0])
 
     def lanes(size):
         return lambda t, r: aligned(t.member(r, t.c) * size, size)
@@ -1498,14 +1512,20 @@
     (grad_down,) = place(
         plan,
         table,
-        after(down_near, last_along[0]),
+        after(down_near, part_send),
         down_far,
         [(own_hidden, width)],
         [((slice(None),), 0, lanes(cols))],
         "place_down",
     )
+    last_along = on_along_z(*last_along, part_last, grad_down)
+    up_along = (after(up_along[0], last_along[0]), up_along[1])
+    up_kept, up_sent, grad_out = split_by_core(plan, table, up_along, 2 * quarter)
+    up_come = plan.swap(up_sent)
+    up_near = plan.halfway(jnp.concatenate([up_kept, up_come, grad_out], 1))
+    up_far = plan.final(up_near)
     grad_inputs = grad_first.reshape(inputs.shape) + (
-        part_keep[0].astype(F32) + after(part_last[0], grad_down).astype(F32)
+        part_keep[0].astype(F32) + after(part_last[0], up_near).astype(F32)
     )
     last_near = plan.halfway(total(*last_along, grad_inputs))
     last_far = plan.final(last_near)

time: 393 us -> 383 us (0.975); the launches traced: 385 us -> 382 us
  starting transfers between devices: 56.1 us -> 50.9 us
    ppermute x7 -> x4, waiting for transfers between devices: 32.2 us -> 16.9 us  [exchange(): come = after(lax.ppermute(send, BOTH, self.stage[k]), *ready)]
    ppermute x3, waiting for transfers between devices: 16 us -> 6.27 us  [sent_along_z(): return (keep, lax.ppermute(send, BOTH, plan.along[0]))]
    ppermute x6 -> x8, waiting for transfers between devices: 11.1 us -> 19 us  [begun(): return lax.ppermute(after(send, *ready), BOTH, plan.stage[k])]
    ppermute x3, waiting for transfers between devices: 5.91 us -> 13.6 us  [final(): return lax.ppermute(after(near, *ready), BOTH, self.stage[self.bits - 1])]
    ppermute x4 -> x3, waiting for transfers between devices: 9.38 us -> 16.2 us  [double(): return jnp.concatenate([near, lax.ppermute(near, BOTH, self.stage[k])], 0)]
    squeeze x1 -> x3, other arithmetic: 3.64 us -> 8.69 us  [the longest x1 3.82 us: local(): up_keep[0]]
    ppermute x7 -> x4, starting transfers between devices: 7.61 us -> 2.77 us  [exchange(): come = after(lax.ppermute(send, BOTH, self.stage[k]), *ready)]
    convert_element_type x6 -> x5, other arithmetic: 8.03 us -> 4.93 us  [add(): return (former.astype(F32) + latter.astype(F32)).astype(BF16)]
  transfers between devices with their start and end apart: 55 -> 54, of which waited for: 31 -> 34; matrix products, arithmetic and copies ran while one was open for 5% -> 6% of each run, Pallas kernels for 35% -> 36%
where the time goes in v4:
time: 383 us; the launch traced here: 382 us
  Pallas kernels  163 us (43%)
  waiting for transfers between devices  131 us (34%)
  starting transfers between devices  50.9 us (13%)
  other arithmetic  19.5 us (5%)
  local copies, waits for them, and re-layouts  16.4 us (4%)
    pallas_call x29, Pallas kernels, call(): pl.pallas_call(lambda *refs: kernel(Here(plan), *refs), out_shape=list(ou...  163 us
    ppermute x8, waiting for transfers between devices, onward(): return lax.ppermute(after(block, *ready), BOTH, plan.toward[1])  21.7 us
    ppermute x8, waiting for transfers between devices, begun(): return lax.ppermute(after(send, *ready), BOTH, plan.stage[k])  19 us
    ppermute x4, waiting for transfers between devices, exchange(): come = after(lax.ppermute(send, BOTH, self.stage[k]), *ready)  16.9 us
    ppermute x3, waiting for transfers between devices, double(): return jnp.concatenate([near, lax.ppermute(near, BOTH, self.stage[k])], 0)  16.2 us
    ppermute x8, starting transfers between devices, onward(): return lax.ppermute(after(block, *ready), BOTH, plan.toward[1])  13.6 us
    ppermute x3, waiting for transfers between devices, final(): return lax.ppermute(after(near, *ready), BOTH, self.stage[self.bits - 1])  13.6 us
    ppermute x5, waiting for transfers between devices, final(): return (near, lax.ppermute(after(near, *ready), BOTH, plan.stage[top]))  12.4 us
  transfers between devices with their start and end apart: 54, of which 34 were waited for; matrix products, arithmetic and copies ran while one was open for 6% of the time, Pallas kernels for 36%

profile of v4, /device:TPU:0, one launch (start us, length us, event | category | flops | bytes accessed | tf_op | source)
XLA Modules:
  0.0 381.9 jit_solution(16442043264850564833)
XLA Ops:
  9.1 4.8 %collective-permute-done.1 = bf16[1,3,128,1024]{3,2,1,0:T(8,128)(2,1)S(1)} collective-permute-done((bf16[1,3,128,1024]{3,2,1,0:T(8,128)(2,1)}, bf16[1,3,128,1024]{3,2,1,0:T(8,128)(2,1)S(1)}, u32[]{:S(2)}, u32[]{:S(2)}) %collective-permute-start.1) | collective-permute-done | bytes 786464 | tf_op jit(solution)/shard_map/ppermute | solution.py:111
  18.5 9.6 %collective-permute-done.2 = bf16[144,1024]{1,0:T(8,128)(2,1)S(1)} collective-permute-done((bf16[144,1024]{1,0:T(8,128)(2,1)S(1)}, bf16[144,1024]{1,0:T(8,128)(2,1)S(1)}, u32[]{:S(2)}, u32[]{:S(2)}) %collective-permute-start.2) | collective-permute-done | bytes 294944 | tf_op jit(solution)/shard_map/ppermute | solution.py:1244
  37.2 3.9 %collective-permute-done.6 = bf16[144,1024]{1,0:T(8,128)(2,1)S(1)} collective-permute-done((bf16[144,1024]{1,0:T(8,128)(2,1)S(1)}, bf16[144,1024]{1,0:T(8,128)(2,1)S(1)}, u32[]{:S(2)}, u32[]{:S(2)}) %collective-permute-start.6) | collective-permute-done | bytes 294944 | tf_op jit(solution)/shard_map/ppermute | solution.py:1244
  41.2 5.2 %collective-permute-done.5 = bf16[256,512]{1,0:T(8,128)(2,1)S(1)} collective-permute-done((bf16[256,512]{1,0:T(8,128)(2,1)}, bf16[256,512]{1,0:T(8,128)(2,1)S(1)}, u32[]{:S(2)}, u32[]{:S(2)}) %collective-permute-start.5) | collective-permute-done | bytes 262176 | tf_op jit(solution)/shard_map/ppermute | solution.py:1244
  53.8 6.1 %attention_forward.3 = (bf16[512,768]{1,0:T(8,128)(2,1)}, bf16[2,3,128,256]{3,2,1,0:T(8,128)(2,1)}, bf16[2,3,128,256]{3,2,1,0:T(8,128)(2,1)}, f32[2,8,512]{2,1,0:T(8,128)}) custom-call(bf16[2,3,128,1024]{3,2,1,0:T(8,128)(2,1)} %copy-done.3, bf16[2,3,128,1024]{3,2,1,0:T(8,128)(2,1)} %collective-permute-done.4.refs_1_, ...), custom_call_target="tpu_custom_call" | custom-call | flops 6600000000 | bytes 6356992 | tf_op jit(solution)/shard_map/attention_forward/pallas_call | solution.py:181
  67.9 6.1 %attention_forward.4 = (bf16[512,768]{1,0:T(8,128)(2,1)}, bf16[2,3,128,256]{3,2,1,0:T(8,128)(2,1)}, bf16[2,3,128,256]{3,2,1,0:T(8,128)(2,1)}, f32[2,8,512]{2,1,0:T(8,128)}) custom-call(bf16[2,3,128,1024]{3,2,1,0:T(8,128)(2,1)} %copy-done.3, bf16[2,3,128,1024]{3,2,1,0:T(8,128)(2,1)} %collective-permute-done.4.refs_1_, ...), custom_call_target="tpu_custom_call", output_to_operand_aliasing={{1}: (4, {}), {2}: (5, {})} | custom-call | flops 6600000000 | bytes 7143424 | tf_op jit(solution)/shard_map/attention_forward/pallas_call | solution.py:181
  78.9 6.1 %attention_forward.5 = (bf16[512,768]{1,0:T(8,128)(2,1)}, bf16[2,3,128,256]{3,2,1,0:T(8,128)(2,1)}, bf16[2,3,128,256]{3,2,1,0:T(8,128)(2,1)}, f32[2,8,512]{2,1,0:T(8,128)}) custom-call(bf16[2,3,128,1024]{3,2,1,0:T(8,128)(2,1)} %copy-done.3, bf16[2,3,128,1024]{3,2,1,0:T(8,128)(2,1)} %collective-permute-done.4.refs_1_, ...), custom_call_target="tpu_custom_call", output_to_operand_aliasing={{1}: (4, {}), {2}: (5, {})} | custom-call | flops 6600000000 | bytes 7143424 | tf_op jit(solution)/shard_map/attention_forward/pallas_call | solution.py:181
  87.0 7.1 %collective-permute-done.15.refs_6_ = bf16[2,2,256,512]{3,2,1,0:T(8,128)(2,1)} collective-permute-done((bf16[2,2,256,512]{3,2,1,0:T(8,128)(2,1)S(1)}, bf16[2,2,256,512]{3,2,1,0:T(8,128)(2,1)}, u32[]{:S(2)}, u32[]{:S(2)}) %collective-permute-start.15) | collective-permute-done | bytes 1048608 | tf_op jit(solution)/shard_map/ppermute | solution.py:1232
  105.8 8.5 %collective-permute-done.21 = bf16[2,3,128,256]{3,2,1,0:T(8,128)(2,1)S(1)} collective-permute-done((bf16[2,3,128,256]{3,2,1,0:T(8,128)(2,1)S(1)}, bf16[2,3,128,256]{3,2,1,0:T(8,128)(2,1)S(1)}, u32[]{:S(2)}, u32[]{:S(2)}) %collective-permute-start.21) | collective-permute-done | bytes 393248 | tf_op jit(solution)/shard_map/ppermute | solution.py:85
  115.0 7.5 %output_norm.1 = (f32[384,1024]{1,0:T(8,128)}, f32[384,1024]{1,0:T(8,128)}, bf16[384,1024]{1,0:T(8,128)(2,1)}, bf16[1024,1024]{1,0:T(8,128)(2,1)}) custom-call(bf16[384,1024]{1,0:T(8,128)(2,1)} %bitcast.100, f32[8,1024]{1,0:T(8,128)} %get-tuple-element.178.refs_3_.refs_1_.refs_4_, bf16[128,1024]{1,0:T(8,128)(2,1)} %refs_2_.6, bf16[128,3072]{1,0:T(8,128)(2,1)} %copy-done.12, ...), custom_call_target="tpu_custom_call" | custom-call | flops 7699999744 | bytes 10649600 | tf_op jit(solution)/shard_map/output_norm/pallas_call | solution.py:181
  127.1 14.4 %up_forward.1 = (bf16[4,768,512]{2,1,0:T(8,128)(2,1)}, bf16[4,768,512]{2,1,0:T(8,128)(2,1)}, bf16[4,1024,512]{2,1,0:T(8,128)(2,1)}) custom-call(bf16[384,1024]{1,0:T(8,128)(2,1)} %get-tuple-element.223.refs_0_, bf16[384,1024]{1,0:T(8,128)(2,1)} %collective-permute-done.23.refs_1_, bf16[128,4096]{1,0:T(8,128)(2,1)} %refs_2_.7, bf16[128,3072]{1,0:T(8,128)(2,1)} %copy-done.12, ...), custom_call_target="tpu_custom_call" | custom-call | flops 16499999744 | bytes 17055744 | tf_op jit(solution)/shard_map/up_forward/pallas_call | solution.py:181
  141.5 5.3 %collective-permute-done.25.refs_3_ = bf16[2,3,512,256]{3,2,1,0:T(8,128)(2,1)S(1)} collective-permute-done((bf16[2,3,512,256]{3,2,1,0:T(8,128)(2,1)S(1)}, bf16[2,3,512,256]{3,2,1,0:T(8,128)(2,1)S(1)}, u32[]{:S(2)}, u32[]{:S(2)}) %collective-permute-start.25) | collective-permute-done | bytes 1572896 | tf_op jit(solution)/shard_map/ppermute | solution.py:1232
  148.0 9.6 %down_forward.1 = (f32[384,1024]{1,0:T(8,128)}, bf16[384,1024]{1,0:T(8,128)(2,1)}, bf16[2048,1024]{1,0:T(8,128)(2,1)}) custom-call(bf16[4,768,512]{2,1,0:T(8,128)(2,1)} %get-tuple-element.199.refs_0_, bf16[512,1024]{1,0:T(8,128)(2,1)} %refs_1_.5, bf16[2,3,512,256]{3,2,1,0:T(8,128)(2,1)} %copy-done.21, bf16[2,3,512,256]{3,2,1,0:T(8,128)(2,1)} %copy-done.29), custom_call_target="tpu_custom_call" | custom-call | flops 11000000512 | bytes 13893632 | tf_op jit(solution)/shard_map/down_forward/pallas_call | solution.py:181
  161.1 5.4 %norm_two.1 = (bf16[384,1024]{1,0:T(8,128)(2,1)}, f32[384,1024]{1,0:T(8,128)}, bf16[384,1024]{1,0:T(8,128)(2,1)}, f32[8,1024]{1,0:T(8,128)}) custom-call(f32[384,1024]{1,0:T(8,128)} %get-tuple-element.192.refs_0_, f32[384,1024]{1,0:T(8,128)} %get-tuple-element.201.refs_1_, bf16[384,1024]{1,0:T(8,128)(2,1)} %copy-done.33, bf16[384,1024]{1,0:T(8,128)(2,1)} %bitcast.129, ...), custom_call_target="tpu_custom_call" | custom-call | flops 6600000000 | bytes 7929856 | tf_op jit(solution)/shard_map/norm_two/pallas_call | solution.py:181
  170.0 5.8 %down_weights.2 = bf16[2,4,512,256]{3,2,1,0:T(8,128)(2,1)} custom-call(bf16[4,768,512]{2,1,0:T(8,128)(2,1)} %get-tuple-element.199.refs_0_, bf16[384,1024]{1,0:T(8,128)(2,1)} %get-tuple-element.207.refs_1_.refs_0_, bf16[384,1024]{1,0:T(8,128)(2,1)} %copy-done.32), custom_call_target="tpu_custom_call" | custom-call | flops 5500000256 | bytes 6815744 | tf_op jit(solution)/shard_map/down_weights/pallas_call | solution.py:181
  176.5 5.8 %down_weights.3 = bf16[2,4,512,256]{3,2,1,0:T(8,128)(2,1)} custom-call(bf16[4,768,512]{2,1,0:T(8,128)(2,1)} %get-tuple-element.199.refs_0_, bf16[384,1024]{1,0:T(8,128)(2,1)} %get-tuple-element.207.refs_1_.refs_0_, bf16[384,1024]{1,0:T(8,128)(2,1)} %copy-done.32), custom_call_target="tpu_custom_call" | custom-call | flops 5500000256 | bytes 6815744 | tf_op jit(solution)/shard_map/down_weights/pallas_call | solution.py:181
  182.2 12.7 %ffn_backward.1 = (bf16[4,768,512]{2,1,0:T(8,128)(2,1)}, f32[4,8,512]{2,1,0:T(8,128)}, f32[384,1024]{1,0:T(8,128)}, bf16[384,1024]{1,0:T(8,128)(2,1)}) custom-call(bf16[384,1024]{1,0:T(8,128)(2,1)} %get-tuple-element.207.refs_1_.refs_0_, bf16[384,1024]{1,0:T(8,128)(2,1)} %copy-done.32, bf16[2048,1024]{1,0:T(8,128)(2,1)} %get-tuple-element.208.refs_2_, ...), custom_call_target="tpu_custom_call" | custom-call | flops 14300000256 | bytes 18677760 | tf_op jit(solution)/shard_map/ffn_backward/pallas_call | solution.py:181
  195.0 5.2 %up_weights.2 = bf16[2,4,128,1024]{3,2,1,0:T(8,128)(2,1)} custom-call(bf16[384,1024]{1,0:T(8,128)(2,1)} %get-tuple-element.223.refs_0_, bf16[384,1024]{1,0:T(8,128)(2,1)} %collective-permute-done.23.refs_1_, bf16[4,768,512]{2,1,0:T(8,128)(2,1)} %get-tuple-element.213.refs_2_), custom_call_target="tpu_custom_call" | custom-call | flops 6600000000 | bytes 6815744 | tf_op jit(solution)/shard_map/up_weights/pallas_call | solution.py:181
  205.8 7.9 %norm_one_back.1 = (f32[384,1024]{1,0:T(8,128)}, bf16[384,1024]{1,0:T(8,128)(2,1)}, f32[8,8,768]{2,1,0:T(8,128)}, bf16[2,384,256]{2,1,0:T(8,128)(2,1)}, bf16[2,384,256]{2,1,0:T(8,128)(2,1)}) custom-call(f32[384,1024]{1,0:T(8,128)} %get-tuple-element.204.refs_0_, f32[384,1024]{1,0:T(8,128)} %get-tuple-element.215.refs_1_, ...), custom_call_target="tpu_custom_call" | custom-call | flops 8800000000 | bytes 11010048 | tf_op jit(solution)/shard_map/norm_one_back/pallas_call | solution.py:181
  214.7 5.1 %collective-permute-done.30 = bf16[1,4,512,256]{3,2,1,0:T(8,128)(2,1)S(1)} collective-permute-done((bf16[1,4,512,256]{3,2,1,0:T(8,128)(2,1)S(1)}, bf16[1,4,512,256]{3,2,1,0:T(8,128)(2,1)S(1)}, u32[]{:S(2)}, u32[]{:S(2)}) %collective-permute-start.30) | collective-permute-done | bytes 1048608 | tf_op jit(solution)/shard_map/ppermute | solution.py:1394
  220.5 5.2 %up_weights.3 = bf16[2,4,128,1024]{3,2,1,0:T(8,128)(2,1)} custom-call(bf16[384,1024]{1,0:T(8,128)(2,1)} %get-tuple-element.223.refs_0_, bf16[384,1024]{1,0:T(8,128)(2,1)} %collective-permute-done.23.refs_1_, bf16[4,768,512]{2,1,0:T(8,128)(2,1)} %get-tuple-element.213.refs_2_), custom_call_target="tpu_custom_call" | custom-call | flops 6600000000 | bytes 6815744 | tf_op jit(solution)/shard_map/up_weights/pallas_call | solution.py:181
  228.7 4.2 %out_weights.1 = (bf16[4,4,128,256]{3,2,1,0:T(8,128)(2,1)}, bf16[4,4,128,256]{3,2,1,0:T(8,128)(2,1)}) custom-call(bf16[384,1024]{1,0:T(8,128)(2,1)} %get-tuple-element.227.refs_0_, bf16[2,384,256]{2,1,0:T(8,128)(2,1)} %bitcast.95, bf16[2,384,256]{2,1,0:T(8,128)(2,1)} %bitcast.106, bf16[2,384,256]{2,1,0:T(8,128)(2,1)} %bitcast.93), custom_call_target="tpu_custom_call" | custom-call | tf_op jit(solution)/shard_map/out_weights/pallas_call | solution.py:181
  241.6 8.5 %attention_backward.3 = (bf16[3,512,768]{2,1,0:T(8,128)(2,1)}, bf16[2,3,128,1024]{3,2,1,0:T(8,128)(2,1)}, bf16[2,3,128,1024]{3,2,1,0:T(8,128)(2,1)}) custom-call(bf16[512,768]{1,0:T(8,128)(2,1)} %get-tuple-element.239.refs_0_, bf16[1024,768]{1,0:T(8,128)(2,1)} %get-tuple-element.165.refs_2_.refs_1_, f32[2,8,512]{2,1,0:T(8,128)} %get-tuple-element.240.refs_2_, ...), custom_call_target="tpu_custom_call" | custom-call | flops 8800000000 | bytes 9863168 | tf_op jit(solution)/shard_map/attention_backward/pallas_call | solution.py:181
  257.3 8.6 %attention_backward.4 = (bf16[3,512,768]{2,1,0:T(8,128)(2,1)}, bf16[2,3,128,1024]{3,2,1,0:T(8,128)(2,1)}, bf16[2,3,128,1024]{3,2,1,0:T(8,128)(2,1)}) custom-call(bf16[512,768]{1,0:T(8,128)(2,1)} %get-tuple-element.244.refs_0_, bf16[1024,768]{1,0:T(8,128)(2,1)} %get-tuple-element.165.refs_2_.refs_1_, ...), custom_call_target="tpu_custom_call", output_to_operand_aliasing={{0}: (8, {}), {1}: (9, {}), {2}: (10, {})} | custom-call | flops 8800000000 | bytes 15368192 | tf_op jit(solution)/shard_map/attention_backward/pallas_call | solution.py:181
  275.9 8.5 %attention_backward.5 = (bf16[3,512,768]{2,1,0:T(8,128)(2,1)}, bf16[2,3,128,1024]{3,2,1,0:T(8,128)(2,1)}, bf16[2,3,128,1024]{3,2,1,0:T(8,128)(2,1)}) custom-call(bf16[512,768]{1,0:T(8,128)(2,1)} %get-tuple-element.253.refs_0_, bf16[1024,768]{1,0:T(8,128)(2,1)} %get-tuple-element.165.refs_2_.refs_1_, ...), custom_call_target="tpu_custom_call", output_to_operand_aliasing={{0}: (8, {}), {1}: (9, {}), {2}: (10, {})} | custom-call | flops 8800000000 | bytes 15368192 | tf_op jit(solution)/shard_map/attention_backward/pallas_call | solution.py:181
  284.3 5.9 %collective-permute-done.38 = bf16[1,4,128,256]{3,2,1,0:T(8,128)(2,1)S(1)} collective-permute-done((bf16[1,4,128,256]{3,2,1,0:T(8,128)(2,1)S(1)}, bf16[1,4,128,256]{3,2,1,0:T(8,128)(2,1)S(1)}, u32[]{:S(2)}, u32[]{:S(2)}) %collective-permute-start.38) | collective-permute-done | bytes 262176 | tf_op jit(solution)/shard_map/ppermute | solution.py:1394
  298.3 6.8 %head_weights_backward.1 = (bf16[4,144,768]{2,1,0:T(8,128)(2,1)}, bf16[4,144,768]{2,1,0:T(8,128)(2,1)}) custom-call(bf16[2,3,128,1024]{3,2,1,0:T(8,128)(2,1)} %copy-done.3, bf16[2,3,128,1024]{3,2,1,0:T(8,128)(2,1)} %collective-permute-done.4.refs_1_, bf16[3,512,768]{2,1,0:T(8,128)(2,1)} %get-tuple-element.265.refs_2_, ...), custom_call_target="tpu_custom_call" | custom-call | flops 8800000000 | bytes 7536640 | tf_op jit(solution)/shard_map/head_weights_backward/pallas_call | solution.py:181
  305.9 5.1 %collective-permute-done.41 = bf16[2,128,1280]{2,1,0:T(8,128)(2,1)S(1)} collective-permute-done((bf16[2,128,1280]{2,1,0:T(8,128)(2,1)}, bf16[2,128,1280]{2,1,0:T(8,128)(2,1)S(1)}, u32[]{:S(2)}, u32[]{:S(2)}) %collective-permute-start.41) | collective-permute-done | bytes 655392 | tf_op jit(solution)/shard_map/ppermute | solution.py:1443
  315.6 5.3 %collective-permute-done.39 = bf16[2,3,128,1024]{3,2,1,0:T(8,128)(2,1)S(1)} collective-permute-done((bf16[2,3,128,1024]{3,2,1,0:T(8,128)(2,1)}, bf16[2,3,128,1024]{3,2,1,0:T(8,128)(2,1)S(1)}, u32[]{:S(2)}, u32[]{:S(2)}) %collective-permute-start.39) | collective-permute-done | bytes 1572896 | tf_op jit(solution)/shard_map/ppermute | solution.py:1394
  327.2 9.3 %collective-permute-done.46.refs_1_ = bf16[2,512,256]{2,1,0:T(8,128)(2,1)S(1)} collective-permute-done((bf16[2,512,256]{2,1,0:T(8,128)(2,1)S(1)}, bf16[2,512,256]{2,1,0:T(8,128)(2,1)S(1)}, u32[]{:S(2)}, u32[]{:S(2)}) %collective-permute-start.46) | collective-permute-done | bytes 524320 | tf_op jit(solution)/shard_map/ppermute | solution.py:108
  348.7 4.7 %collective-permute-done.49 = bf16[1,128,1280]{2,1,0:T(8,128)(2,1)S(1)} collective-permute-done((bf16[1,128,1280]{2,1,0:T(8,128)(2,1)S(1)}, bf16[1,128,1280]{2,1,0:T(8,128)(2,1)S(1)}, u32[]{:S(2)}, u32[]{:S(2)}) %collective-permute-start.49) | collective-permute-done | bytes 327712 | tf_op jit(solution)/shard_map/ppermute | solution.py:111
  362.6 6.7 %collective-permute-done.51 = bf16[1,144,768]{2,1,0:T(8,128)(2,1)S(1)} collective-permute-done((bf16[1,144,768]{2,1,0:T(8,128)(2,1)S(1)}, bf16[1,144,768]{2,1,0:T(8,128)(2,1)S(1)}, u32[]{:S(2)}, u32[]{:S(2)}) %collective-permute-start.51) | collective-permute-done | bytes 221216 | tf_op jit(solution)/shard_map/ppermute | solution.py:111
  (231 shorter events, 160.0 us)
Async XLA Ops:
  0.7 13.2 %collective-permute-start.1 = (bf16[1,3,128,1024]{3,2,1,0:T(8,128)(2,1)}, bf16[1,3,128,1024]{3,2,1,0:T(8,128)(2,1)S(1)}, u32[]{:S(2)}, u32[]{:S(2)}) collective-permute-start(bf16[1,3,128,1024]{3,2,1,0:T(8,128)(2,1)} %bitcast.99), channel_id=1, source_target_pairs={{0,1},{1,0},{2,3},{3,2},{4,6},{5,7},{6,4},{7,5},{8,9},{9,8},{10,11... | collective-permute-start | bytes 2359304 | tf_op jit(solution)/shard_map/ppermute | solution.py:111
  17.1 29.2 %collective-permute-start.4 = (bf16[2,3,128,1024]{3,2,1,0:T(8,128)(2,1)S(1)}, bf16[2,3,128,1024]{3,2,1,0:T(8,128)(2,1)}, u32[]{:S(2)}, u32[]{:S(2)}) collective-permute-start(bf16[2,3,128,1024]{3,2,1,0:T(8,128)(2,1)S(1)} %pad_maximum_fusion.refs_0_), channel_id=1, source_target_pairs={{0,2},{1,3},{2,0},{3,1},{4,5},{5,4},{6,7},{7,6},{8,10},{9,11},{10,... | collective-permute-start | bytes 4718600 | tf_op jit(solution)/shard_map/ppermute | solution.py:1232
  46.7 13.3 %collective-permute-start.10 = (bf16[1,3,128,256]{3,2,1,0:T(8,128)(2,1)S(1)}, bf16[1,3,128,256]{3,2,1,0:T(8,128)(2,1)S(1)}, u32[]{:S(2)}, u32[]{:S(2)}) collective-permute-start(bf16[1,3,128,256]{3,2,1,0:T(8,128)(2,1)S(1)} %bitcast.96), channel_id=1, source_target_pairs={{0,1},{1,0},{2,3},{3,2},{4,6},{5,7},{6,4},{7,5},{8,9},{9,8},{10,11... | collective-permute-start | bytes 589832 | tf_op jit(solution)/shard_map/ppermute | solution.py:1238
  47.0 13.0 %collective-permute-start.7 = (bf16[512,256]{1,0:T(8,128)(2,1)}, bf16[512,256]{1,0:T(8,128)(2,1)S(1)}, u32[]{:S(2)}, u32[]{:S(2)}) collective-permute-start(bf16[512,256]{1,0:T(8,128)(2,1)} %get-tuple-element.159), channel_id=1, source_target_pairs={{0,8},{1,9},{2,10},{3,11},{4,12},{5,13},{6,14},{7,15},{8,24},{9,25... | collective-permute-start | bytes 786440 | tf_op jit(solution)/shard_map/ppermute | solution.py:1244
  47.7 14.6 %collective-permute-start.8 = (bf16[256,512]{1,0:T(8,128)(2,1)S(1)}, bf16[256,512]{1,0:T(8,128)(2,1)S(1)}, u32[]{:S(2)}, u32[]{:S(2)}) collective-permute-start(bf16[256,512]{1,0:T(8,128)(2,1)S(1)} %collective-permute-done.5), channel_id=1, source_target_pairs={{0,8},{1,9},{2,10},{3,11},{4,12},{5,13},{6,14},{7,15},{8,24},{9,25... | collective-permute-start | bytes 786440 | tf_op jit(solution)/shard_map/ppermute | solution.py:1244
  62.3 13.5 %collective-permute-start.11 = (bf16[256,512]{1,0:T(8,128)(2,1)S(1)}, bf16[256,512]{1,0:T(8,128)(2,1)S(1)}, u32[]{:S(2)}, u32[]{:S(2)}) collective-permute-start(bf16[256,512]{1,0:T(8,128)(2,1)S(1)} %collective-permute-done.8), channel_id=1, source_target_pairs={{0,8},{1,9},{2,10},{3,11},{4,12},{5,13},{6,14},{7,15},{8,24},{9,25... | collective-permute-start | bytes 786440 | tf_op jit(solution)/shard_map/ppermute | solution.py:1244
  62.8 12.8 %collective-permute-start.12 = (bf16[1,2,256,512]{3,2,1,0:T(8,128)(2,1)S(1)}, bf16[1,2,256,512]{3,2,1,0:T(8,128)(2,1)S(1)}, u32[]{:S(2)}, u32[]{:S(2)}) collective-permute-start(bf16[1,2,256,512]{3,2,1,0:T(8,128)(2,1)S(1)} %bitcast.81), channel_id=1, source_target_pairs={{0,1},{1,0},{2,3},{3,2},{4,6},{5,7},{6,4},{7,5},{8,9},{9,8},{10,11... | collective-permute-start | bytes 1572872 | tf_op jit(solution)/shard_map/ppermute | solution.py:1238
  63.2 13.2 %collective-permute-start.13 = (bf16[2,3,128,256]{3,2,1,0:T(8,128)(2,1)S(1)}, bf16[2,3,128,256]{3,2,1,0:T(8,128)(2,1)}, u32[]{:S(2)}, u32[]{:S(2)}) collective-permute-start(bf16[2,3,128,256]{3,2,1,0:T(8,128)(2,1)S(1)} %constant_dynamic-update-slice_fusion.refs_4_), channel_id=1, source_target_pairs={{0,2},{1,3},{2,0},{3,1},{4,5},{5,4},{6,7},{7,6},{8,10},{9,11},{10,... | collective-permute-start | bytes 1179656 | tf_op jit(solution)/shard_map/ppermute | solution.py:1232
  64.5 11.9 %collective-permute-start.14 = (bf16[512,256]{1,0:T(8,128)(2,1)S(1)}, bf16[512,256]{1,0:T(8,128)(2,1)S(1)}, u32[]{:S(2)}, u32[]{:S(2)}) collective-permute-start(bf16[512,256]{1,0:T(8,128)(2,1)S(1)} %collective-permute-done.7), channel_id=1, source_target_pairs={{0,8},{1,9},{2,10},{3,11},{4,12},{5,13},{6,14},{7,15},{8,24},{9,25... | collective-permute-start | bytes 786440 | tf_op jit(solution)/shard_map/ppermute | solution.py:1244
  76.4 17.7 %collective-permute-start.15 = (bf16[2,2,256,512]{3,2,1,0:T(8,128)(2,1)S(1)}, bf16[2,2,256,512]{3,2,1,0:T(8,128)(2,1)}, u32[]{:S(2)}, u32[]{:S(2)}) collective-permute-start(bf16[2,2,256,512]{3,2,1,0:T(8,128)(2,1)S(1)} %constant_dynamic-update-slice_fusion.2.refs_5_), channel_id=1, source_target_pairs={{0,2},{1,3},{2,0},{3,1},{4,5},{5,4},{6,7},{7,6},{8,10},{9,11},{10,... | collective-permute-start | bytes 3145736 | tf_op jit(solution)/shard_map/ppermute | solution.py:1232
  102.2 12.1 %collective-permute-start.21 = (bf16[2,3,128,256]{3,2,1,0:T(8,128)(2,1)S(1)}, bf16[2,3,128,256]{3,2,1,0:T(8,128)(2,1)S(1)}, u32[]{:S(2)}, u32[]{:S(2)}) collective-permute-start(bf16[2,3,128,256]{3,2,1,0:T(8,128)(2,1)S(1)} %pad_maximum_fusion.6), channel_id=1, source_target_pairs={{0,1},{1,0},{2,3},{3,2},{4,6},{5,7},{6,4},{7,5},{8,9},{9,8},{10,11... | collective-permute-start | bytes 1179656 | tf_op jit(solution)/shard_map/ppermute | solution.py:85
  104.1 18.4 %collective-permute-start.22 = (bf16[2,1,256,512]{3,2,1,0:T(8,128)(2,1)}, bf16[2,1,256,512]{3,2,1,0:T(8,128)(2,1)S(1)}, u32[]{:S(2)}, u32[]{:S(2)}) collective-permute-start(bf16[2,1,256,512]{3,2,1,0:T(8,128)(2,1)} %constant_dynamic-update-slice_fusion.4.refs_7_), channel_id=1, source_target_pairs={{0,2},{1,3},{2,0},{3,1},{4,5},{5,4},{6,7},{7,6},{8,10},{9,11},{10,... | collective-permute-start | bytes 1572872 | tf_op jit(solution)/shard_map/ppermute | solution.py:1232
  114.3 12.0 %collective-permute-start.24 = (bf16[1,3,512,256]{3,2,1,0:T(8,128)(2,1)S(1)}, bf16[1,3,512,256]{3,2,1,0:T(8,128)(2,1)S(1)}, u32[]{:S(2)}, u32[]{:S(2)}) collective-permute-start(bf16[1,3,512,256]{3,2,1,0:T(8,128)(2,1)S(1)} %bitcast.79), channel_id=1, source_target_pairs={{0,1},{1,0},{2,3},{3,2},{4,6},{5,7},{6,4},{7,5},{8,9},{9,8},{10,11... | collective-permute-start | bytes 2359304 | tf_op jit(solution)/shard_map/ppermute | solution.py:1238
  126.3 20.5 %collective-permute-start.25 = (bf16[2,3,512,256]{3,2,1,0:T(8,128)(2,1)S(1)}, bf16[2,3,512,256]{3,2,1,0:T(8,128)(2,1)S(1)}, u32[]{:S(2)}, u32[]{:S(2)}) collective-permute-start(bf16[2,3,512,256]{3,2,1,0:T(8,128)(2,1)S(1)} %constant_dynamic-update-slice_fusion.6.refs_2_), channel_id=1, source_target_pairs={{0,2},{1,3},{2,0},{3,1},{4,5},{5,4},{6,7},{7,6},{8,10},{9,11},{10,... | collective-permute-start | bytes 4718600 | tf_op jit(solution)/shard_map/ppermute | solution.py:1232
  175.7 26.2 %collective-permute-start.28 = (bf16[2,4,512,256]{3,2,1,0:T(8,128)(2,1)}, bf16[2,4,512,256]{3,2,1,0:T(8,128)(2,1)S(1)}, u32[]{:S(2)}, u32[]{:S(2)}) collective-permute-start(bf16[2,4,512,256]{3,2,1,0:T(8,128)(2,1)} %down_weights.2), channel_id=1, source_target_pairs={{0,2},{1,3},{2,0},{3,1},{4,5},{5,4},{6,7},{7,6},{8,10},{9,11},{10,... | collective-permute-start | bytes 6291464 | tf_op jit(solution)/shard_map/ppermute | solution.py:1394
  194.9 10.9 %collective-permute-start.29 = (bf16[384,1024]{1,0:T(8,128)(2,1)}, bf16[384,1024]{1,0:T(8,128)(2,1)}, u32[]{:S(2)}, u32[]{:S(2)}) collective-permute-start(bf16[384,1024]{1,0:T(8,128)(2,1)} %get-tuple-element.216), channel_id=1, source_target_pairs={{0,4},{1,5},{2,6},{3,7},{4,0},{5,1},{6,2},{7,3},{8,12},{9,13},{10,... | collective-permute-start | bytes 2359304 | tf_op jit(solution)/shard_map/ppermute | solution.py:75
  205.0 14.8 %collective-permute-start.30 = (bf16[1,4,512,256]{3,2,1,0:T(8,128)(2,1)S(1)}, bf16[1,4,512,256]{3,2,1,0:T(8,128)(2,1)S(1)}, u32[]{:S(2)}, u32[]{:S(2)}) collective-permute-start(bf16[1,4,512,256]{3,2,1,0:T(8,128)(2,1)S(1)} %get-tuple-element.294), channel_id=1, source_target_pairs={{0,1},{1,0},{2,3},{3,2},{4,6},{5,7},{6,4},{7,5},{8,9},{9,8},{10,11... | collective-permute-start | bytes 3145736 | tf_op jit(solution)/shard_map/ppermute | solution.py:1394
  238.6 27.3 %collective-permute-start.34 = (bf16[2,4,128,1024]{3,2,1,0:T(8,128)(2,1)}, bf16[2,4,128,1024]{3,2,1,0:T(8,128)(2,1)}, u32[]{:S(2)}, u32[]{:S(2)}) collective-permute-start(bf16[2,4,128,1024]{3,2,1,0:T(8,128)(2,1)} %up_weights.2), channel_id=1, source_target_pairs={{0,2},{1,3},{2,0},{3,1},{4,5},{5,4},{6,7},{7,6},{8,10},{9,11},{10,... | collective-permute-start | bytes 6291464 | tf_op jit(solution)/shard_map/ppermute | solution.py:1394
  253.5 16.2 %collective-permute-start.36 = (bf16[2,512,256]{2,1,0:T(8,128)(2,1)}, bf16[2,512,256]{2,1,0:T(8,128)(2,1)S(1)}, u32[]{:S(2)}, u32[]{:S(2)}) collective-permute-start(bf16[2,512,256]{2,1,0:T(8,128)(2,1)} %get-tuple-element.251), channel_id=1, source_target_pairs={{0,8},{1,9},{2,10},{3,11},{4,12},{5,13},{6,14},{7,15},{8,0},{9,1},... | collective-permute-start | bytes 1572872 | tf_op jit(solution)/shard_map/ppermute | solution.py:1443
  256.1 14.5 %collective-permute-start.35 = (bf16[2,4,128,256]{3,2,1,0:T(8,128)(2,1)}, bf16[2,4,128,256]{3,2,1,0:T(8,128)(2,1)}, u32[]{:S(2)}, u32[]{:S(2)}) collective-permute-start(bf16[2,4,128,256]{3,2,1,0:T(8,128)(2,1)} %get-tuple-element.296), channel_id=1, source_target_pairs={{0,2},{1,3},{2,0},{3,1},{4,5},{5,4},{6,7},{7,6},{8,10},{9,11},{10,... | collective-permute-start | bytes 1572872 | tf_op jit(solution)/shard_map/ppermute | solution.py:1394
  272.4 17.8 %collective-permute-start.37 = (bf16[1,4,128,1024]{3,2,1,0:T(8,128)(2,1)}, bf16[1,4,128,1024]{3,2,1,0:T(8,128)(2,1)S(1)}, u32[]{:S(2)}, u32[]{:S(2)}) collective-permute-start(bf16[1,4,128,1024]{3,2,1,0:T(8,128)(2,1)} %get-tuple-element.292), channel_id=1, source_target_pairs={{0,1},{1,0},{2,3},{3,2},{4,6},{5,7},{6,4},{7,5},{8,9},{9,8},{10,11... | collective-permute-start | bytes 3145736 | tf_op jit(solution)/shard_map/ppermute | solution.py:1394
  273.3 16.9 %collective-permute-start.38 = (bf16[1,4,128,256]{3,2,1,0:T(8,128)(2,1)S(1)}, bf16[1,4,128,256]{3,2,1,0:T(8,128)(2,1)S(1)}, u32[]{:S(2)}, u32[]{:S(2)}) collective-permute-start(bf16[1,4,128,256]{3,2,1,0:T(8,128)(2,1)S(1)} %get-tuple-element.302), channel_id=1, source_target_pairs={{0,1},{1,0},{2,3},{3,2},{4,6},{5,7},{6,4},{7,5},{8,9},{9,8},{10,11... | collective-permute-start | bytes 786440 | tf_op jit(solution)/shard_map/ppermute | solution.py:1394
  274.6 20.3 %collective-permute-start.40 = (bf16[1,512,256]{2,1,0:T(8,128)(2,1)S(1)}, bf16[1,512,256]{2,1,0:T(8,128)(2,1)S(1)}, u32[]{:S(2)}, u32[]{:S(2)}) collective-permute-start(bf16[1,512,256]{2,1,0:T(8,128)(2,1)S(1)} %get-tuple-element.299), channel_id=1, source_target_pairs={{0,16},{1,17},{2,18},{3,19},{4,20},{5,21},{6,22},{7,23},{8,24},{9,... | collective-permute-start | bytes 786440 | tf_op jit(solution)/shard_map/ppermute | solution.py:1451
  294.9 16.1 %collective-permute-start.41 = (bf16[2,128,1280]{2,1,0:T(8,128)(2,1)}, bf16[2,128,1280]{2,1,0:T(8,128)(2,1)S(1)}, u32[]{:S(2)}, u32[]{:S(2)}) collective-permute-start(bf16[2,128,1280]{2,1,0:T(8,128)(2,1)} %get-tuple-element.269), channel_id=1, source_target_pairs={{0,8},{1,9},{2,10},{3,11},{4,12},{5,13},{6,14},{7,15},{8,0},{9,1},... | collective-permute-start | bytes 1966088 | tf_op jit(solution)/shard_map/ppermute | solution.py:1443
  297.5 23.4 %collective-permute-start.39 = (bf16[2,3,128,1024]{3,2,1,0:T(8,128)(2,1)}, bf16[2,3,128,1024]{3,2,1,0:T(8,128)(2,1)S(1)}, u32[]{:S(2)}, u32[]{:S(2)}) collective-permute-start(bf16[2,3,128,1024]{3,2,1,0:T(8,128)(2,1)} %get-tuple-element.263), channel_id=1, source_target_pairs={{0,2},{1,3},{2,0},{3,1},{4,5},{5,4},{6,7},{7,6},{8,10},{9,11},{10,... | collective-permute-start | bytes 4718600 | tf_op jit(solution)/shard_map/ppermute | solution.py:1394
  305.1 18.5 %collective-permute-start.45 = (bf16[1,512,256]{2,1,0:T(8,128)(2,1)S(1)}, bf16[1,512,256]{2,1,0:T(8,128)(2,1)}, u32[]{:S(2)}, u32[]{:S(2)}) collective-permute-start(bf16[1,512,256]{2,1,0:T(8,128)(2,1)S(1)} %bitcast.90), channel_id=1, source_target_pairs={{0,1},{1,0},{2,3},{3,2},{4,6},{5,7},{6,4},{7,5},{8,9},{9,8},{10,11... | collective-permute-start | bytes 786440 | tf_op jit(solution)/shard_map/ppermute | solution.py:1238
  322.3 18.8 %collective-permute-start.43 = (bf16[1,3,128,1024]{3,2,1,0:T(8,128)(2,1)}, bf16[1,3,128,1024]{3,2,1,0:T(8,128)(2,1)}, u32[]{:S(2)}, u32[]{:S(2)}) collective-permute-start(bf16[1,3,128,1024]{3,2,1,0:T(8,128)(2,1)} %add_convert_fusion.4), channel_id=1, source_target_pairs={{0,1},{1,0},{2,3},{3,2},{4,6},{5,7},{6,4},{7,5},{8,9},{9,8},{10,11... | collective-permute-start | bytes 2359304 | tf_op jit(solution)/shard_map/ppermute | solution.py:1394
  324.6 11.9 %collective-permute-start.46 = (bf16[2,512,256]{2,1,0:T(8,128)(2,1)S(1)}, bf16[2,512,256]{2,1,0:T(8,128)(2,1)S(1)}, u32[]{:S(2)}, u32[]{:S(2)}) collective-permute-start(bf16[2,512,256]{2,1,0:T(8,128)(2,1)S(1)} %constant_dynamic-update-slice_fusion.8.refs_0_), channel_id=1, source_target_pairs={{0,2},{1,3},{2,0},{3,1},{4,5},{5,4},{6,7},{7,6},{8,10},{9,11},{10,... | collective-permute-start | bytes 1572872 | tf_op jit(solution)/shard_map/ppermute | solution.py:108
  325.1 16.0 %collective-permute-start.44 = (bf16[2,144,768]{2,1,0:T(8,128)(2,1)}, bf16[2,144,768]{2,1,0:T(8,128)(2,1)S(1)}, u32[]{:S(2)}, u32[]{:S(2)}) collective-permute-start(bf16[2,144,768]{2,1,0:T(8,128)(2,1)} %get-tuple-element.275), channel_id=1, source_target_pairs={{0,8},{1,9},{2,10},{3,11},{4,12},{5,13},{6,14},{7,15},{8,0},{9,1},... | collective-permute-start | bytes 1327112 | tf_op jit(solution)/shard_map/ppermute | solution.py:1443
  325.1 16.1 %collective-permute-start.47 = (bf16[1,128,1280]{2,1,0:T(8,128)(2,1)}, bf16[1,128,1280]{2,1,0:T(8,128)(2,1)S(1)}, u32[]{:S(2)}, u32[]{:S(2)}) collective-permute-start(bf16[1,128,1280]{2,1,0:T(8,128)(2,1)} %get-tuple-element.297), channel_id=1, source_target_pairs={{0,16},{1,17},{2,18},{3,19},{4,20},{5,21},{6,22},{7,23},{8,24},{9,... | collective-permute-start | bytes 983048 | tf_op jit(solution)/shard_map/ppermute | solution.py:1451
  347.6 13.3 %collective-permute-start.50 = (bf16[1,144,768]{2,1,0:T(8,128)(2,1)S(1)}, bf16[1,144,768]{2,1,0:T(8,128)(2,1)S(1)}, u32[]{:S(2)}, u32[]{:S(2)}) collective-permute-start(bf16[1,144,768]{2,1,0:T(8,128)(2,1)S(1)} %get-tuple-element.303), channel_id=1, source_target_pairs={{0,16},{1,17},{2,18},{3,19},{4,20},{5,21},{6,22},{7,23},{8,24},{9,... | collective-permute-start | bytes 663560 | tf_op jit(solution)/shard_map/ppermute | solution.py:1451
  361.8 11.0 %collective-permute-start.53 = (bf16[2,128,1280]{2,1,0:T(8,128)(2,1)S(1)}, bf16[2,128,1280]{2,1,0:T(8,128)(2,1)S(1)}, u32[]{:S(2)}, u32[]{:S(2)}) collective-permute-start(bf16[2,128,1280]{2,1,0:T(8,128)(2,1)S(1)} %pad_maximum_fusion.3.refs_0_), channel_id=1, source_target_pairs={{0,2},{1,3},{2,0},{3,1},{4,5},{5,4},{6,7},{7,6},{8,10},{9,11},{10,... | collective-permute-start | bytes 1966088 | tf_op jit(solution)/shard_map/ppermute | solution.py:108
  (61 other events, 445.4 us)

commit v5 on v4

--- a/solution.py
+++ b/solution.py
@@ -13,7 +13,7 @@
 EPSILON = 1e-12
 BOTH = ("dp", "seq")
 PAD = 16
-MICROSECOND = 1_100_000_000
+MICROSECOND = 600_000_000
 F32 = jnp.float32
 BF16 = jnp.bfloat16
 ANY = pl.BlockSpec(memory_space=pl.ANY)
@@ -1317,7 +1317,7 @@
     )
     ups = [onward(second)]
 
-    ready = (far_x, ups[0]) + tuple(mine[1:])
+    ready = (far_x, second) + tuple(mine[1:])
     mine_all = jnp.stack([after(piece, *ready) for piece in mine])
     theirs = plan.swap(mine_all)
     outs = jnp.stack([after(piece, *ready)[:own_rows, cols3:] for piece in mine[1:]])

time: 383 us -> 379 us (0.990)
  waiting for transfers between devices: 131 us -> 127 us
    ppermute x8, waiting for transfers between devices: 21.7 us -> 26.8 us  [onward(): return lax.ppermute(after(block, *ready), BOTH, plan.toward[1])]
    unnamed x83 -> x79, local copies, waits for them, and re-layouts: 9.47 us -> 8.33 us
  transfers between devices with their start and end apart: 54 -> 54, of which waited for: 34 -> 36; matrix products, arithmetic and copies ran while one was open for 6% -> 6% of each run, Pallas kernels for 36% -> 37%
where the time goes in v5:
time: 379 us; the launch traced here: 377 us
  Pallas kernels  163 us (43%)
  waiting for transfers between devices  127 us (34%)
  starting transfers between devices  51.1 us (13%)
  other arithmetic  19.4 us (5%)
  local copies, waits for them, and re-layouts  15.3 us (4%)
    pallas_call x29, Pallas kernels, call(): pl.pallas_call(lambda *refs: kernel(Here(plan), *refs), out_shape=list(ou...  163 us
    ppermute x8, waiting for transfers between devices, onward(): return lax.ppermute(after(block, *ready), BOTH, plan.toward[1])  26.8 us
    ppermute x4, waiting for transfers between devices, exchange(): come = after(lax.ppermute(send, BOTH, self.stage[k]), *ready)  16.7 us
    ppermute x8, waiting for transfers between devices, begun(): return lax.ppermute(after(send, *ready), BOTH, plan.stage[k])  16.3 us
    ppermute x3, waiting for transfers between devices, double(): return jnp.concatenate([near, lax.ppermute(near, BOTH, self.stage[k])], 0)  13.7 us
    ppermute x11, waiting for transfers between devices, swap(): return lax.ppermute(block, BOTH, self.core)  11.2 us
    ppermute x5, waiting for transfers between devices, final(): return (near, lax.ppermute(after(near, *ready), BOTH, plan.stage[top]))  10.8 us
    ppermute x8, starting transfers between devices, onward(): return lax.ppermute(after(block, *ready), BOTH, plan.toward[1])  10.7 us
  transfers between devices with their start and end apart: 54, of which 36 were waited for; matrix products, arithmetic and copies ran while one was open for 6% of the time, Pallas kernels for 37%

profile of v5, /device:TPU:0, one launch (start us, length us, event | category | flops | bytes accessed | tf_op | source)
XLA Modules:
  0.0 377.1 jit_solution(18215367993417367945)
XLA Ops:
  9.1 4.8 %collective-permute-done.1 = bf16[1,3,128,1024]{3,2,1,0:T(8,128)(2,1)S(1)} collective-permute-done((bf16[1,3,128,1024]{3,2,1,0:T(8,128)(2,1)}, bf16[1,3,128,1024]{3,2,1,0:T(8,128)(2,1)S(1)}, u32[]{:S(2)}, u32[]{:S(2)}) %collective-permute-start.1) | collective-permute-done | bytes 786464 | tf_op jit(solution)/shard_map/ppermute | solution.py:111
  18.5 9.6 %collective-permute-done.2 = bf16[144,1024]{1,0:T(8,128)(2,1)S(1)} collective-permute-done((bf16[144,1024]{1,0:T(8,128)(2,1)S(1)}, bf16[144,1024]{1,0:T(8,128)(2,1)S(1)}, u32[]{:S(2)}, u32[]{:S(2)}) %collective-permute-start.2) | collective-permute-done | bytes 294944 | tf_op jit(solution)/shard_map/ppermute | solution.py:1244
  35.7 5.0 %collective-permute-done.5 = bf16[144,1024]{1,0:T(8,128)(2,1)S(1)} collective-permute-done((bf16[144,1024]{1,0:T(8,128)(2,1)S(1)}, bf16[144,1024]{1,0:T(8,128)(2,1)S(1)}, u32[]{:S(2)}, u32[]{:S(2)}) %collective-permute-start.5) | collective-permute-done | bytes 294944 | tf_op jit(solution)/shard_map/ppermute | solution.py:1244
  42.0 8.6 %collective-permute-done.7 = bf16[256,512]{1,0:T(8,128)(2,1)S(1)} collective-permute-done((bf16[256,512]{1,0:T(8,128)(2,1)S(1)}, bf16[256,512]{1,0:T(8,128)(2,1)S(1)}, u32[]{:S(2)}, u32[]{:S(2)}) %collective-permute-start.7) | collective-permute-done | bytes 262176 | tf_op jit(solution)/shard_map/ppermute | solution.py:1244
  57.4 6.1 %attention_forward.3 = (bf16[512,768]{1,0:T(8,128)(2,1)}, bf16[2,3,128,256]{3,2,1,0:T(8,128)(2,1)}, bf16[2,3,128,256]{3,2,1,0:T(8,128)(2,1)}, f32[2,8,512]{2,1,0:T(8,128)}) custom-call(bf16[2,3,128,1024]{3,2,1,0:T(8,128)(2,1)} %copy-done.3, bf16[2,3,128,1024]{3,2,1,0:T(8,128)(2,1)} %collective-permute-done.4.refs_1_, ...), custom_call_target="tpu_custom_call" | custom-call | flops 3600000000 | bytes 6356992 | tf_op jit(solution)/shard_map/attention_forward/pallas_call | solution.py:181
  69.4 6.1 %attention_forward.4 = (bf16[512,768]{1,0:T(8,128)(2,1)}, bf16[2,3,128,256]{3,2,1,0:T(8,128)(2,1)}, bf16[2,3,128,256]{3,2,1,0:T(8,128)(2,1)}, f32[2,8,512]{2,1,0:T(8,128)}) custom-call(bf16[2,3,128,1024]{3,2,1,0:T(8,128)(2,1)} %copy-done.3, bf16[2,3,128,1024]{3,2,1,0:T(8,128)(2,1)} %collective-permute-done.4.refs_1_, ...), custom_call_target="tpu_custom_call", output_to_operand_aliasing={{1}: (4, {}), {2}: (5, {})} | custom-call | flops 3600000000 | bytes 7143424 | tf_op jit(solution)/shard_map/attention_forward/pallas_call | solution.py:181
  81.1 6.1 %attention_forward.5 = (bf16[512,768]{1,0:T(8,128)(2,1)}, bf16[2,3,128,256]{3,2,1,0:T(8,128)(2,1)}, bf16[2,3,128,256]{3,2,1,0:T(8,128)(2,1)}, f32[2,8,512]{2,1,0:T(8,128)}) custom-call(bf16[2,3,128,1024]{3,2,1,0:T(8,128)(2,1)} %copy-done.3, bf16[2,3,128,1024]{3,2,1,0:T(8,128)(2,1)} %collective-permute-done.4.refs_1_, ...), custom_call_target="tpu_custom_call", output_to_operand_aliasing={{1}: (4, {}), {2}: (5, {})} | custom-call | flops 3600000000 | bytes 7143424 | tf_op jit(solution)/shard_map/attention_forward/pallas_call | solution.py:181
  90.1 6.3 %collective-permute-done.15.refs_6_ = bf16[2,2,256,512]{3,2,1,0:T(8,128)(2,1)} collective-permute-done((bf16[2,2,256,512]{3,2,1,0:T(8,128)(2,1)S(1)}, bf16[2,2,256,512]{3,2,1,0:T(8,128)(2,1)}, u32[]{:S(2)}, u32[]{:S(2)}) %collective-permute-start.15) | collective-permute-done | bytes 1048608 | tf_op jit(solution)/shard_map/ppermute | solution.py:1232
  99.6 4.7 %collective-permute-done.20 = bf16[2,3,128,256]{3,2,1,0:T(8,128)(2,1)S(1)} collective-permute-done((bf16[2,3,128,256]{3,2,1,0:T(8,128)(2,1)}, bf16[2,3,128,256]{3,2,1,0:T(8,128)(2,1)S(1)}, u32[]{:S(2)}, u32[]{:S(2)}) %collective-permute-start.20) | collective-permute-done | bytes 393248 | tf_op jit(solution)/shard_map/ppermute | solution.py:85
  108.0 8.5 %collective-permute-done.21 = bf16[2,3,128,256]{3,2,1,0:T(8,128)(2,1)S(1)} collective-permute-done((bf16[2,3,128,256]{3,2,1,0:T(8,128)(2,1)S(1)}, bf16[2,3,128,256]{3,2,1,0:T(8,128)(2,1)S(1)}, u32[]{:S(2)}, u32[]{:S(2)}) %collective-permute-start.21) | collective-permute-done | bytes 393248 | tf_op jit(solution)/shard_map/ppermute | solution.py:85
  117.2 7.4 %output_norm.1 = (f32[384,1024]{1,0:T(8,128)}, f32[384,1024]{1,0:T(8,128)}, bf16[384,1024]{1,0:T(8,128)(2,1)}, bf16[1024,1024]{1,0:T(8,128)(2,1)}) custom-call(bf16[384,1024]{1,0:T(8,128)(2,1)} %bitcast.100, f32[8,1024]{1,0:T(8,128)} %get-tuple-element.178.refs_3_.refs_1_.refs_4_, bf16[128,1024]{1,0:T(8,128)(2,1)} %refs_2_.6, bf16[128,3072]{1,0:T(8,128)(2,1)} %copy-done.12, ...), custom_call_target="tpu_custom_call" | custom-call | flops 4200000000 | bytes 10649600 | tf_op jit(solution)/shard_map/output_norm/pallas_call | solution.py:181
  130.1 14.4 %up_forward.1 = (bf16[4,768,512]{2,1,0:T(8,128)(2,1)}, bf16[4,768,512]{2,1,0:T(8,128)(2,1)}, bf16[4,1024,512]{2,1,0:T(8,128)(2,1)}) custom-call(bf16[384,1024]{1,0:T(8,128)(2,1)} %get-tuple-element.223.refs_0_, bf16[384,1024]{1,0:T(8,128)(2,1)} %collective-permute-done.23.refs_1_, bf16[128,4096]{1,0:T(8,128)(2,1)} %refs_2_.7, bf16[128,3072]{1,0:T(8,128)(2,1)} %copy-done.12, ...), custom_call_target="tpu_custom_call" | custom-call | flops 8999999488 | bytes 17055744 | tf_op jit(solution)/shard_map/up_forward/pallas_call | solution.py:181
  144.5 4.5 %collective-permute-done.25.refs_3_ = bf16[2,3,512,256]{3,2,1,0:T(8,128)(2,1)S(1)} collective-permute-done((bf16[2,3,512,256]{3,2,1,0:T(8,128)(2,1)S(1)}, bf16[2,3,512,256]{3,2,1,0:T(8,128)(2,1)S(1)}, u32[]{:S(2)}, u32[]{:S(2)}) %collective-permute-start.25) | collective-permute-done | bytes 1572896 | tf_op jit(solution)/shard_map/ppermute | solution.py:1232
  150.2 9.6 %down_forward.1 = (f32[384,1024]{1,0:T(8,128)}, bf16[384,1024]{1,0:T(8,128)(2,1)}, bf16[2048,1024]{1,0:T(8,128)(2,1)}) custom-call(bf16[4,768,512]{2,1,0:T(8,128)(2,1)} %get-tuple-element.199.refs_0_, bf16[512,1024]{1,0:T(8,128)(2,1)} %refs_1_.5, bf16[2,3,512,256]{3,2,1,0:T(8,128)(2,1)} %copy-done.21, bf16[2,3,512,256]{3,2,1,0:T(8,128)(2,1)} %copy-done.27), custom_call_target="tpu_custom_call" | custom-call | flops 6000000000 | bytes 13893632 | tf_op jit(solution)/shard_map/down_forward/pallas_call | solution.py:181
  163.3 5.4 %norm_two.1 = (bf16[384,1024]{1,0:T(8,128)(2,1)}, f32[384,1024]{1,0:T(8,128)}, bf16[384,1024]{1,0:T(8,128)(2,1)}, f32[8,1024]{1,0:T(8,128)}) custom-call(f32[384,1024]{1,0:T(8,128)} %get-tuple-element.192.refs_0_, f32[384,1024]{1,0:T(8,128)} %get-tuple-element.201.refs_1_, bf16[384,1024]{1,0:T(8,128)(2,1)} %copy-done.30, bf16[384,1024]{1,0:T(8,128)(2,1)} %bitcast.128, ...), custom_call_target="tpu_custom_call" | custom-call | flops 3600000000 | bytes 7929856 | tf_op jit(solution)/shard_map/norm_two/pallas_call | solution.py:181
  172.2 5.8 %down_weights.2 = bf16[2,4,512,256]{3,2,1,0:T(8,128)(2,1)} custom-call(bf16[4,768,512]{2,1,0:T(8,128)(2,1)} %get-tuple-element.199.refs_0_, bf16[384,1024]{1,0:T(8,128)(2,1)} %get-tuple-element.207.refs_1_.refs_0_, bf16[384,1024]{1,0:T(8,128)(2,1)} %copy-done.29), custom_call_target="tpu_custom_call" | custom-call | flops 3000000000 | bytes 6815744 | tf_op jit(solution)/shard_map/down_weights/pallas_call | solution.py:181
  179.5 5.8 %down_weights.3 = bf16[2,4,512,256]{3,2,1,0:T(8,128)(2,1)} custom-call(bf16[4,768,512]{2,1,0:T(8,128)(2,1)} %get-tuple-element.199.refs_0_, bf16[384,1024]{1,0:T(8,128)(2,1)} %get-tuple-element.207.refs_1_.refs_0_, bf16[384,1024]{1,0:T(8,128)(2,1)} %copy-done.29), custom_call_target="tpu_custom_call" | custom-call | flops 3000000000 | bytes 6815744 | tf_op jit(solution)/shard_map/down_weights/pallas_call | solution.py:181
  185.3 12.6 %ffn_backward.1 = (bf16[4,768,512]{2,1,0:T(8,128)(2,1)}, f32[4,8,512]{2,1,0:T(8,128)}, f32[384,1024]{1,0:T(8,128)}, bf16[384,1024]{1,0:T(8,128)(2,1)}) custom-call(bf16[384,1024]{1,0:T(8,128)(2,1)} %get-tuple-element.207.refs_1_.refs_0_, bf16[384,1024]{1,0:T(8,128)(2,1)} %copy-done.29, bf16[2048,1024]{1,0:T(8,128)(2,1)} %get-tuple-element.208.refs_2_, ...), custom_call_target="tpu_custom_call" | custom-call | flops 7800000000 | bytes 18677760 | tf_op jit(solution)/shard_map/ffn_backward/pallas_call | solution.py:181
  198.0 5.2 %up_weights.2 = bf16[2,4,128,1024]{3,2,1,0:T(8,128)(2,1)} custom-call(bf16[384,1024]{1,0:T(8,128)(2,1)} %get-tuple-element.223.refs_0_, bf16[384,1024]{1,0:T(8,128)(2,1)} %collective-permute-done.23.refs_1_, bf16[4,768,512]{2,1,0:T(8,128)(2,1)} %get-tuple-element.213.refs_2_), custom_call_target="tpu_custom_call" | custom-call | flops 3600000000 | bytes 6815744 | tf_op jit(solution)/shard_map/up_weights/pallas_call | solution.py:181
  207.5 7.9 %norm_one_back.1 = (f32[384,1024]{1,0:T(8,128)}, bf16[384,1024]{1,0:T(8,128)(2,1)}, f32[8,8,768]{2,1,0:T(8,128)}, bf16[2,384,256]{2,1,0:T(8,128)(2,1)}, bf16[2,384,256]{2,1,0:T(8,128)(2,1)}) custom-call(f32[384,1024]{1,0:T(8,128)} %get-tuple-element.204.refs_0_, f32[384,1024]{1,0:T(8,128)} %get-tuple-element.215.refs_1_, ...), custom_call_target="tpu_custom_call" | custom-call | flops 4800000000 | bytes 11010048 | tf_op jit(solution)/shard_map/norm_one_back/pallas_call | solution.py:181
  215.4 6.6 %collective-permute-done.30 = bf16[1,4,512,256]{3,2,1,0:T(8,128)(2,1)S(1)} collective-permute-done((bf16[1,4,512,256]{3,2,1,0:T(8,128)(2,1)S(1)}, bf16[1,4,512,256]{3,2,1,0:T(8,128)(2,1)S(1)}, u32[]{:S(2)}, u32[]{:S(2)}) %collective-permute-start.30) | collective-permute-done | bytes 1048608 | tf_op jit(solution)/shard_map/ppermute | solution.py:1394
  224.5 5.2 %up_weights.3 = bf16[2,4,128,1024]{3,2,1,0:T(8,128)(2,1)} custom-call(bf16[384,1024]{1,0:T(8,128)(2,1)} %get-tuple-element.223.refs_0_, bf16[384,1024]{1,0:T(8,128)(2,1)} %collective-permute-done.23.refs_1_, bf16[4,768,512]{2,1,0:T(8,128)(2,1)} %get-tuple-element.213.refs_2_), custom_call_target="tpu_custom_call" | custom-call | flops 3600000000 | bytes 6815744 | tf_op jit(solution)/shard_map/up_weights/pallas_call | solution.py:181
  230.4 4.2 %out_weights.1 = (bf16[4,4,128,256]{3,2,1,0:T(8,128)(2,1)}, bf16[4,4,128,256]{3,2,1,0:T(8,128)(2,1)}) custom-call(bf16[384,1024]{1,0:T(8,128)(2,1)} %get-tuple-element.227.refs_0_, bf16[2,384,256]{2,1,0:T(8,128)(2,1)} %bitcast.95, bf16[2,384,256]{2,1,0:T(8,128)(2,1)} %bitcast.106, bf16[2,384,256]{2,1,0:T(8,128)(2,1)} %bitcast.93), custom_call_target="tpu_custom_call" | custom-call | tf_op jit(solution)/shard_map/out_weights/pallas_call | solution.py:181
  244.6 8.5 %attention_backward.3 = (bf16[3,512,768]{2,1,0:T(8,128)(2,1)}, bf16[2,3,128,1024]{3,2,1,0:T(8,128)(2,1)}, bf16[2,3,128,1024]{3,2,1,0:T(8,128)(2,1)}) custom-call(bf16[512,768]{1,0:T(8,128)(2,1)} %get-tuple-element.239.refs_0_, bf16[1024,768]{1,0:T(8,128)(2,1)} %get-tuple-element.165.refs_2_.refs_1_, f32[2,8,512]{2,1,0:T(8,128)} %get-tuple-element.240.refs_2_, ...), custom_call_target="tpu_custom_call" | custom-call | flops 4800000000 | bytes 9863168 | tf_op jit(solution)/shard_map/attention_backward/pallas_call | solution.py:181
  257.5 8.6 %attention_backward.4 = (bf16[3,512,768]{2,1,0:T(8,128)(2,1)}, bf16[2,3,128,1024]{3,2,1,0:T(8,128)(2,1)}, bf16[2,3,128,1024]{3,2,1,0:T(8,128)(2,1)}) custom-call(bf16[512,768]{1,0:T(8,128)(2,1)} %get-tuple-element.244.refs_0_, bf16[1024,768]{1,0:T(8,128)(2,1)} %get-tuple-element.165.refs_2_.refs_1_, ...), custom_call_target="tpu_custom_call", output_to_operand_aliasing={{0}: (8, {}), {1}: (9, {}), {2}: (10, {})} | custom-call | flops 4800000000 | bytes 15368192 | tf_op jit(solution)/shard_map/attention_backward/pallas_call | solution.py:181
  267.1 3.8 %fusion.2 = (bf16[4,128,1024]{2,1,0:T(8,128)(2,1)}, bf16[1,4,128,1024]{3,2,1,0:T(8,128)(2,1)}) fusion(bf16[2,4,128,1024]{3,2,1,0:T(8,128)(2,1)S(1)} %copy-done.1, bf16[2,4,128,1024]{3,2,1,0:T(8,128)(2,1)} %collective-permute-done.34), kind=kLoop, calls=%fused_computation.11 | loop fusion | flops 4194304 | bytes 6291456 | tf_op jit(solution)/shard_map/squeeze | solution.py:1490
  277.4 8.5 %attention_backward.5 = (bf16[3,512,768]{2,1,0:T(8,128)(2,1)}, bf16[2,3,128,1024]{3,2,1,0:T(8,128)(2,1)}, bf16[2,3,128,1024]{3,2,1,0:T(8,128)(2,1)}) custom-call(bf16[512,768]{1,0:T(8,128)(2,1)} %get-tuple-element.253.refs_0_, bf16[1024,768]{1,0:T(8,128)(2,1)} %get-tuple-element.165.refs_2_.refs_1_, ...), custom_call_target="tpu_custom_call", output_to_operand_aliasing={{0}: (8, {}), {1}: (9, {}), {2}: (10, {})} | custom-call | flops 4800000000 | bytes 15368192 | tf_op jit(solution)/shard_map/attention_backward/pallas_call | solution.py:181
  295.4 6.8 %head_weights_backward.1 = (bf16[4,144,768]{2,1,0:T(8,128)(2,1)}, bf16[4,144,768]{2,1,0:T(8,128)(2,1)}) custom-call(bf16[2,3,128,1024]{3,2,1,0:T(8,128)(2,1)} %copy-done.3, bf16[2,3,128,1024]{3,2,1,0:T(8,128)(2,1)} %collective-permute-done.4.refs_1_, bf16[3,512,768]{2,1,0:T(8,128)(2,1)} %get-tuple-element.265.refs_2_, ...), custom_call_target="tpu_custom_call" | custom-call | flops 4800000000 | bytes 7536640 | tf_op jit(solution)/shard_map/head_weights_backward/pallas_call | solution.py:181
  302.5 6.0 %collective-permute-done.41 = bf16[2,128,1280]{2,1,0:T(8,128)(2,1)S(1)} collective-permute-done((bf16[2,128,1280]{2,1,0:T(8,128)(2,1)}, bf16[2,128,1280]{2,1,0:T(8,128)(2,1)S(1)}, u32[]{:S(2)}, u32[]{:S(2)}) %collective-permute-start.41) | collective-permute-done | bytes 655392 | tf_op jit(solution)/shard_map/ppermute | solution.py:1443
  324.9 7.4 %collective-permute-done.46.refs_1_ = bf16[2,512,256]{2,1,0:T(8,128)(2,1)S(1)} collective-permute-done((bf16[2,512,256]{2,1,0:T(8,128)(2,1)S(1)}, bf16[2,512,256]{2,1,0:T(8,128)(2,1)S(1)}, u32[]{:S(2)}, u32[]{:S(2)}) %collective-permute-start.46) | collective-permute-done | bytes 524320 | tf_op jit(solution)/shard_map/ppermute | solution.py:108
  345.8 3.8 %collective-permute-done.49 = bf16[1,128,1280]{2,1,0:T(8,128)(2,1)S(1)} collective-permute-done((bf16[1,128,1280]{2,1,0:T(8,128)(2,1)S(1)}, bf16[1,128,1280]{2,1,0:T(8,128)(2,1)S(1)}, u32[]{:S(2)}, u32[]{:S(2)}) %collective-permute-start.49) | collective-permute-done | bytes 327712 | tf_op jit(solution)/shard_map/ppermute | solution.py:111
  359.0 5.1 %collective-permute-done.51 = bf16[1,144,768]{2,1,0:T(8,128)(2,1)S(1)} collective-permute-done((bf16[1,144,768]{2,1,0:T(8,128)(2,1)S(1)}, bf16[1,144,768]{2,1,0:T(8,128)(2,1)S(1)}, u32[]{:S(2)}, u32[]{:S(2)}) %collective-permute-start.51) | collective-permute-done | bytes 221216 | tf_op jit(solution)/shard_map/ppermute | solution.py:111
  (227 shorter events, 157.2 us)
Async XLA Ops:
  0.7 13.2 %collective-permute-start.1 = (bf16[1,3,128,1024]{3,2,1,0:T(8,128)(2,1)}, bf16[1,3,128,1024]{3,2,1,0:T(8,128)(2,1)S(1)}, u32[]{:S(2)}, u32[]{:S(2)}) collective-permute-start(bf16[1,3,128,1024]{3,2,1,0:T(8,128)(2,1)} %bitcast.99), channel_id=1, source_target_pairs={{0,1},{1,0},{2,3},{3,2},{4,6},{5,7},{6,4},{7,5},{8,9},{9,8},{10,11... | collective-permute-start | bytes 2359304 | tf_op jit(solution)/shard_map/ppermute | solution.py:111
  17.1 23.6 %collective-permute-start.4 = (bf16[2,3,128,1024]{3,2,1,0:T(8,128)(2,1)S(1)}, bf16[2,3,128,1024]{3,2,1,0:T(8,128)(2,1)}, u32[]{:S(2)}, u32[]{:S(2)}) collective-permute-start(bf16[2,3,128,1024]{3,2,1,0:T(8,128)(2,1)S(1)} %pad_maximum_fusion.refs_0_), channel_id=1, source_target_pairs={{0,2},{1,3},{2,0},{3,1},{4,5},{5,4},{6,7},{7,6},{8,10},{9,11},{10,... | collective-permute-start | bytes 4718600 | tf_op jit(solution)/shard_map/ppermute | solution.py:1232
  40.9 13.6 %collective-permute-start.9 = (bf16[4,144,1024]{2,1,0:T(8,128)(2,1)S(1)}, bf16[4,144,1024]{2,1,0:T(8,128)(2,1)}, u32[]{:S(2)}, u32[]{:S(2)}) collective-permute-start(bf16[4,144,1024]{2,1,0:T(8,128)(2,1)S(1)} %pad_maximum_fusion.1.refs_0_), channel_id=1, source_target_pairs={{0,4},{1,5},{2,6},{3,7},{4,0},{5,1},{6,2},{7,3},{8,12},{9,13},{10,... | collective-permute-start | bytes 3538952 | tf_op jit(solution)/shard_map/ppermute | solution.py:75
  41.7 21.8 %collective-permute-start.10 = (bf16[1,3,128,256]{3,2,1,0:T(8,128)(2,1)S(1)}, bf16[1,3,128,256]{3,2,1,0:T(8,128)(2,1)S(1)}, u32[]{:S(2)}, u32[]{:S(2)}) collective-permute-start(bf16[1,3,128,256]{3,2,1,0:T(8,128)(2,1)S(1)} %bitcast.96), channel_id=1, source_target_pairs={{0,1},{1,0},{2,3},{3,2},{4,6},{5,7},{6,4},{7,5},{8,9},{9,8},{10,11... | collective-permute-start | bytes 589832 | tf_op jit(solution)/shard_map/ppermute | solution.py:1238
  50.6 12.9 %collective-permute-start.8 = (bf16[256,512]{1,0:T(8,128)(2,1)S(1)}, bf16[256,512]{1,0:T(8,128)(2,1)S(1)}, u32[]{:S(2)}, u32[]{:S(2)}) collective-permute-start(bf16[256,512]{1,0:T(8,128)(2,1)S(1)} %collective-permute-done.7), channel_id=1, source_target_pairs={{0,8},{1,9},{2,10},{3,11},{4,12},{5,13},{6,14},{7,15},{8,24},{9,25... | collective-permute-start | bytes 786440 | tf_op jit(solution)/shard_map/ppermute | solution.py:1244
  51.1 13.8 %collective-permute-start.6 = (bf16[512,256]{1,0:T(8,128)(2,1)S(1)}, bf16[512,256]{1,0:T(8,128)(2,1)S(1)}, u32[]{:S(2)}, u32[]{:S(2)}) collective-permute-start(bf16[512,256]{1,0:T(8,128)(2,1)S(1)} %copy-done.34), channel_id=1, source_target_pairs={{0,8},{1,9},{2,10},{3,11},{4,12},{5,13},{6,14},{7,15},{8,24},{9,25... | collective-permute-start | bytes 786440 | tf_op jit(solution)/shard_map/ppermute | solution.py:1244
  65.0 11.6 %collective-permute-start.12 = (bf16[1,2,256,512]{3,2,1,0:T(8,128)(2,1)S(1)}, bf16[1,2,256,512]{3,2,1,0:T(8,128)(2,1)S(1)}, u32[]{:S(2)}, u32[]{:S(2)}) collective-permute-start(bf16[1,2,256,512]{3,2,1,0:T(8,128)(2,1)S(1)} %bitcast.81), channel_id=1, source_target_pairs={{0,1},{1,0},{2,3},{3,2},{4,6},{5,7},{6,4},{7,5},{8,9},{9,8},{10,11... | collective-permute-start | bytes 1572872 | tf_op jit(solution)/shard_map/ppermute | solution.py:1238
  65.4 11.3 %collective-permute-start.11 = (bf16[256,512]{1,0:T(8,128)(2,1)S(1)}, bf16[256,512]{1,0:T(8,128)(2,1)S(1)}, u32[]{:S(2)}, u32[]{:S(2)}) collective-permute-start(bf16[256,512]{1,0:T(8,128)(2,1)S(1)} %collective-permute-done.8), channel_id=1, source_target_pairs={{0,8},{1,9},{2,10},{3,11},{4,12},{5,13},{6,14},{7,15},{8,24},{9,25... | collective-permute-start | bytes 786440 | tf_op jit(solution)/shard_map/ppermute | solution.py:1244
  65.9 12.7 %collective-permute-start.13 = (bf16[2,3,128,256]{3,2,1,0:T(8,128)(2,1)S(1)}, bf16[2,3,128,256]{3,2,1,0:T(8,128)(2,1)}, u32[]{:S(2)}, u32[]{:S(2)}) collective-permute-start(bf16[2,3,128,256]{3,2,1,0:T(8,128)(2,1)S(1)} %constant_dynamic-update-slice_fusion.refs_4_), channel_id=1, source_target_pairs={{0,2},{1,3},{2,0},{3,1},{4,5},{5,4},{6,7},{7,6},{8,10},{9,11},{10,... | collective-permute-start | bytes 1179656 | tf_op jit(solution)/shard_map/ppermute | solution.py:1232
  66.0 12.6 %collective-permute-start.14 = (bf16[512,256]{1,0:T(8,128)(2,1)S(1)}, bf16[512,256]{1,0:T(8,128)(2,1)S(1)}, u32[]{:S(2)}, u32[]{:S(2)}) collective-permute-start(bf16[512,256]{1,0:T(8,128)(2,1)S(1)} %collective-permute-done.6), channel_id=1, source_target_pairs={{0,8},{1,9},{2,10},{3,11},{4,12},{5,13},{6,14},{7,15},{8,24},{9,25... | collective-permute-start | bytes 786440 | tf_op jit(solution)/shard_map/ppermute | solution.py:1244
  78.6 17.7 %collective-permute-start.15 = (bf16[2,2,256,512]{3,2,1,0:T(8,128)(2,1)S(1)}, bf16[2,2,256,512]{3,2,1,0:T(8,128)(2,1)}, u32[]{:S(2)}, u32[]{:S(2)}) collective-permute-start(bf16[2,2,256,512]{3,2,1,0:T(8,128)(2,1)S(1)} %constant_dynamic-update-slice_fusion.2.refs_5_), channel_id=1, source_target_pairs={{0,2},{1,3},{2,0},{3,1},{4,5},{5,4},{6,7},{7,6},{8,10},{9,11},{10,... | collective-permute-start | bytes 3145736 | tf_op jit(solution)/shard_map/ppermute | solution.py:1232
  104.4 12.1 %collective-permute-start.21 = (bf16[2,3,128,256]{3,2,1,0:T(8,128)(2,1)S(1)}, bf16[2,3,128,256]{3,2,1,0:T(8,128)(2,1)S(1)}, u32[]{:S(2)}, u32[]{:S(2)}) collective-permute-start(bf16[2,3,128,256]{3,2,1,0:T(8,128)(2,1)S(1)} %pad_maximum_fusion.6), channel_id=1, source_target_pairs={{0,1},{1,0},{2,3},{3,2},{4,6},{5,7},{6,4},{7,5},{8,9},{9,8},{10,11... | collective-permute-start | bytes 1179656 | tf_op jit(solution)/shard_map/ppermute | solution.py:85
  106.4 18.3 %collective-permute-start.22 = (bf16[2,1,256,512]{3,2,1,0:T(8,128)(2,1)}, bf16[2,1,256,512]{3,2,1,0:T(8,128)(2,1)}, u32[]{:S(2)}, u32[]{:S(2)}) collective-permute-start(bf16[2,1,256,512]{3,2,1,0:T(8,128)(2,1)} %constant_dynamic-update-slice_fusion.4.refs_7_), channel_id=1, source_target_pairs={{0,2},{1,3},{2,0},{3,1},{4,5},{5,4},{6,7},{7,6},{8,10},{9,11},{10,... | collective-permute-start | bytes 1572872 | tf_op jit(solution)/shard_map/ppermute | solution.py:1232
  116.5 12.0 %collective-permute-start.24 = (bf16[1,3,512,256]{3,2,1,0:T(8,128)(2,1)S(1)}, bf16[1,3,512,256]{3,2,1,0:T(8,128)(2,1)S(1)}, u32[]{:S(2)}, u32[]{:S(2)}) collective-permute-start(bf16[1,3,512,256]{3,2,1,0:T(8,128)(2,1)S(1)} %bitcast.79), channel_id=1, source_target_pairs={{0,1},{1,0},{2,3},{3,2},{4,6},{5,7},{6,4},{7,5},{8,9},{9,8},{10,11... | collective-permute-start | bytes 2359304 | tf_op jit(solution)/shard_map/ppermute | solution.py:1238
  128.5 20.5 %collective-permute-start.25 = (bf16[2,3,512,256]{3,2,1,0:T(8,128)(2,1)S(1)}, bf16[2,3,512,256]{3,2,1,0:T(8,128)(2,1)S(1)}, u32[]{:S(2)}, u32[]{:S(2)}) collective-permute-start(bf16[2,3,512,256]{3,2,1,0:T(8,128)(2,1)S(1)} %constant_dynamic-update-slice_fusion.6.refs_2_), channel_id=1, source_target_pairs={{0,2},{1,3},{2,0},{3,1},{4,5},{5,4},{6,7},{7,6},{8,10},{9,11},{10,... | collective-permute-start | bytes 4718600 | tf_op jit(solution)/shard_map/ppermute | solution.py:1232
  177.9 26.2 %collective-permute-start.28 = (bf16[2,4,512,256]{3,2,1,0:T(8,128)(2,1)}, bf16[2,4,512,256]{3,2,1,0:T(8,128)(2,1)S(1)}, u32[]{:S(2)}, u32[]{:S(2)}) collective-permute-start(bf16[2,4,512,256]{3,2,1,0:T(8,128)(2,1)} %down_weights.2), channel_id=1, source_target_pairs={{0,2},{1,3},{2,0},{3,1},{4,5},{5,4},{6,7},{7,6},{8,10},{9,11},{10,... | collective-permute-start | bytes 6291464 | tf_op jit(solution)/shard_map/ppermute | solution.py:1394
  207.2 14.8 %collective-permute-start.30 = (bf16[1,4,512,256]{3,2,1,0:T(8,128)(2,1)S(1)}, bf16[1,4,512,256]{3,2,1,0:T(8,128)(2,1)S(1)}, u32[]{:S(2)}, u32[]{:S(2)}) collective-permute-start(bf16[1,4,512,256]{3,2,1,0:T(8,128)(2,1)S(1)} %get-tuple-element.294), channel_id=1, source_target_pairs={{0,1},{1,0},{2,3},{3,2},{4,6},{5,7},{6,4},{7,5},{8,9},{9,8},{10,11... | collective-permute-start | bytes 3145736 | tf_op jit(solution)/shard_map/ppermute | solution.py:1394
  240.8 26.4 %collective-permute-start.34 = (bf16[2,4,128,1024]{3,2,1,0:T(8,128)(2,1)}, bf16[2,4,128,1024]{3,2,1,0:T(8,128)(2,1)}, u32[]{:S(2)}, u32[]{:S(2)}) collective-permute-start(bf16[2,4,128,1024]{3,2,1,0:T(8,128)(2,1)} %up_weights.2), channel_id=1, source_target_pairs={{0,2},{1,3},{2,0},{3,1},{4,5},{5,4},{6,7},{7,6},{8,10},{9,11},{10,... | collective-permute-start | bytes 6291464 | tf_op jit(solution)/shard_map/ppermute | solution.py:1394
  256.5 14.7 %collective-permute-start.36 = (bf16[2,512,256]{2,1,0:T(8,128)(2,1)}, bf16[2,512,256]{2,1,0:T(8,128)(2,1)S(1)}, u32[]{:S(2)}, u32[]{:S(2)}) collective-permute-start(bf16[2,512,256]{2,1,0:T(8,128)(2,1)} %get-tuple-element.251), channel_id=1, source_target_pairs={{0,8},{1,9},{2,10},{3,11},{4,12},{5,13},{6,14},{7,15},{8,0},{9,1},... | collective-permute-start | bytes 1572872 | tf_op jit(solution)/shard_map/ppermute | solution.py:1443
  257.2 15.6 %collective-permute-start.35 = (bf16[2,4,128,256]{3,2,1,0:T(8,128)(2,1)}, bf16[2,4,128,256]{3,2,1,0:T(8,128)(2,1)}, u32[]{:S(2)}, u32[]{:S(2)}) collective-permute-start(bf16[2,4,128,256]{3,2,1,0:T(8,128)(2,1)} %get-tuple-element.296), channel_id=1, source_target_pairs={{0,2},{1,3},{2,0},{3,1},{4,5},{5,4},{6,7},{7,6},{8,10},{9,11},{10,... | collective-permute-start | bytes 1572872 | tf_op jit(solution)/shard_map/ppermute | solution.py:1394
  270.9 17.8 %collective-permute-start.37 = (bf16[1,4,128,1024]{3,2,1,0:T(8,128)(2,1)}, bf16[1,4,128,1024]{3,2,1,0:T(8,128)(2,1)}, u32[]{:S(2)}, u32[]{:S(2)}) collective-permute-start(bf16[1,4,128,1024]{3,2,1,0:T(8,128)(2,1)} %get-tuple-element.292), channel_id=1, source_target_pairs={{0,1},{1,0},{2,3},{3,2},{4,6},{5,7},{6,4},{7,5},{8,9},{9,8},{10,11... | collective-permute-start | bytes 3145736 | tf_op jit(solution)/shard_map/ppermute | solution.py:1394
  274.7 14.0 %collective-permute-start.38 = (bf16[1,4,128,256]{3,2,1,0:T(8,128)(2,1)S(1)}, bf16[1,4,128,256]{3,2,1,0:T(8,128)(2,1)S(1)}, u32[]{:S(2)}, u32[]{:S(2)}) collective-permute-start(bf16[1,4,128,256]{3,2,1,0:T(8,128)(2,1)S(1)} %get-tuple-element.302), channel_id=1, source_target_pairs={{0,1},{1,0},{2,3},{3,2},{4,6},{5,7},{6,4},{7,5},{8,9},{9,8},{10,11... | collective-permute-start | bytes 786440 | tf_op jit(solution)/shard_map/ppermute | solution.py:1394
  275.1 19.5 %collective-permute-start.40 = (bf16[1,512,256]{2,1,0:T(8,128)(2,1)S(1)}, bf16[1,512,256]{2,1,0:T(8,128)(2,1)S(1)}, u32[]{:S(2)}, u32[]{:S(2)}) collective-permute-start(bf16[1,512,256]{2,1,0:T(8,128)(2,1)S(1)} %get-tuple-element.299), channel_id=1, source_target_pairs={{0,16},{1,17},{2,18},{3,19},{4,20},{5,21},{6,22},{7,23},{8,24},{9,... | collective-permute-start | bytes 786440 | tf_op jit(solution)/shard_map/ppermute | solution.py:1451
  293.1 23.4 %collective-permute-start.39 = (bf16[2,3,128,1024]{3,2,1,0:T(8,128)(2,1)}, bf16[2,3,128,1024]{3,2,1,0:T(8,128)(2,1)S(1)}, u32[]{:S(2)}, u32[]{:S(2)}) collective-permute-start(bf16[2,3,128,1024]{3,2,1,0:T(8,128)(2,1)} %get-tuple-element.263), channel_id=1, source_target_pairs={{0,2},{1,3},{2,0},{3,1},{4,5},{5,4},{6,7},{7,6},{8,10},{9,11},{10,... | collective-permute-start | bytes 4718600 | tf_op jit(solution)/shard_map/ppermute | solution.py:1394
  294.7 13.8 %collective-permute-start.41 = (bf16[2,128,1280]{2,1,0:T(8,128)(2,1)}, bf16[2,128,1280]{2,1,0:T(8,128)(2,1)S(1)}, u32[]{:S(2)}, u32[]{:S(2)}) collective-permute-start(bf16[2,128,1280]{2,1,0:T(8,128)(2,1)} %get-tuple-element.269), channel_id=1, source_target_pairs={{0,8},{1,9},{2,10},{3,11},{4,12},{5,13},{6,14},{7,15},{8,0},{9,1},... | collective-permute-start | bytes 1966088 | tf_op jit(solution)/shard_map/ppermute | solution.py:1443
  302.2 16.1 %collective-permute-start.45 = (bf16[1,512,256]{2,1,0:T(8,128)(2,1)S(1)}, bf16[1,512,256]{2,1,0:T(8,128)(2,1)}, u32[]{:S(2)}, u32[]{:S(2)}) collective-permute-start(bf16[1,512,256]{2,1,0:T(8,128)(2,1)S(1)} %bitcast.90), channel_id=1, source_target_pairs={{0,1},{1,0},{2,3},{3,2},{4,6},{5,7},{6,4},{7,5},{8,9},{9,8},{10,11... | collective-permute-start | bytes 786440 | tf_op jit(solution)/shard_map/ppermute | solution.py:1238
  317.9 19.3 %collective-permute-start.43 = (bf16[1,3,128,1024]{3,2,1,0:T(8,128)(2,1)}, bf16[1,3,128,1024]{3,2,1,0:T(8,128)(2,1)}, u32[]{:S(2)}, u32[]{:S(2)}) collective-permute-start(bf16[1,3,128,1024]{3,2,1,0:T(8,128)(2,1)} %add_convert_fusion.4), channel_id=1, source_target_pairs={{0,1},{1,0},{2,3},{3,2},{4,6},{5,7},{6,4},{7,5},{8,9},{9,8},{10,11... | collective-permute-start | bytes 2359304 | tf_op jit(solution)/shard_map/ppermute | solution.py:1394
  319.2 13.1 %collective-permute-start.46 = (bf16[2,512,256]{2,1,0:T(8,128)(2,1)S(1)}, bf16[2,512,256]{2,1,0:T(8,128)(2,1)S(1)}, u32[]{:S(2)}, u32[]{:S(2)}) collective-permute-start(bf16[2,512,256]{2,1,0:T(8,128)(2,1)S(1)} %constant_dynamic-update-slice_fusion.8.refs_0_), channel_id=1, source_target_pairs={{0,2},{1,3},{2,0},{3,1},{4,5},{5,4},{6,7},{7,6},{8,10},{9,11},{10,... | collective-permute-start | bytes 1572872 | tf_op jit(solution)/shard_map/ppermute | solution.py:108
  320.6 16.6 %collective-permute-start.44 = (bf16[2,144,768]{2,1,0:T(8,128)(2,1)}, bf16[2,144,768]{2,1,0:T(8,128)(2,1)S(1)}, u32[]{:S(2)}, u32[]{:S(2)}) collective-permute-start(bf16[2,144,768]{2,1,0:T(8,128)(2,1)} %get-tuple-element.275), channel_id=1, source_target_pairs={{0,8},{1,9},{2,10},{3,11},{4,12},{5,13},{6,14},{7,15},{8,0},{9,1},... | collective-permute-start | bytes 1327112 | tf_op jit(solution)/shard_map/ppermute | solution.py:1443
  321.5 15.8 %collective-permute-start.47 = (bf16[1,128,1280]{2,1,0:T(8,128)(2,1)}, bf16[1,128,1280]{2,1,0:T(8,128)(2,1)S(1)}, u32[]{:S(2)}, u32[]{:S(2)}) collective-permute-start(bf16[1,128,1280]{2,1,0:T(8,128)(2,1)} %get-tuple-element.297), channel_id=1, source_target_pairs={{0,16},{1,17},{2,18},{3,19},{4,20},{5,21},{6,22},{7,23},{8,24},{9,... | collective-permute-start | bytes 983048 | tf_op jit(solution)/shard_map/ppermute | solution.py:1451
  344.2 11.6 %collective-permute-start.50 = (bf16[1,144,768]{2,1,0:T(8,128)(2,1)S(1)}, bf16[1,144,768]{2,1,0:T(8,128)(2,1)S(1)}, u32[]{:S(2)}, u32[]{:S(2)}) collective-permute-start(bf16[1,144,768]{2,1,0:T(8,128)(2,1)S(1)} %get-tuple-element.303), channel_id=1, source_target_pairs={{0,16},{1,17},{2,18},{3,19},{4,20},{5,21},{6,22},{7,23},{8,24},{9,... | collective-permute-start | bytes 663560 | tf_op jit(solution)/shard_map/ppermute | solution.py:1451
  357.6 10.6 %collective-permute-start.53 = (bf16[2,128,1280]{2,1,0:T(8,128)(2,1)S(1)}, bf16[2,128,1280]{2,1,0:T(8,128)(2,1)S(1)}, u32[]{:S(2)}, u32[]{:S(2)}) collective-permute-start(bf16[2,128,1280]{2,1,0:T(8,128)(2,1)S(1)} %pad_maximum_fusion.3.refs_0_), channel_id=1, source_target_pairs={{0,2},{1,3},{2,0},{3,1},{4,5},{5,4},{6,7},{7,6},{8,10},{9,11},{10,... | collective-permute-start | bytes 1966088 | tf_op jit(solution)/shard_map/ppermute | solution.py:108
  (59 other events, 456.7 us)

commit v6 on v5

--- a/solution.py
+++ b/solution.py
@@ -13,7 +13,7 @@
 EPSILON = 1e-12
 BOTH = ("dp", "seq")
 PAD = 16
-MICROSECOND = 600_000_000
+MICROSECOND = 500_000_000
 F32 = jnp.float32
 BF16 = jnp.bfloat16
 ANY = pl.BlockSpec(memory_space=pl.ANY)

time: 379 us -> 379 us (level)
  transfers between devices with their start and end apart: 54 -> 54, of which waited for: 36 -> 35; matrix products, arithmetic and copies ran while one was open for 6% -> 6% of each run, Pallas kernels for 37% -> 37%
where the time goes in v6:
time: 379 us; the launch traced here: 377 us
  Pallas kernels  163 us (43%)
  waiting for transfers between devices  127 us (34%)
  starting transfers between devices  50.9 us (13%)
  other arithmetic  19.4 us (5%)
  local copies, waits for them, and re-layouts  15.3 us (4%)
    pallas_call x29, Pallas kernels, call(): pl.pallas_call(lambda *refs: kernel(Here(plan), *refs), out_shape=list(ou...  163 us
    ppermute x8, waiting for transfers between devices, onward(): return lax.ppermute(after(block, *ready), BOTH, plan.toward[1])  26.7 us
    ppermute x4, waiting for transfers between devices, exchange(): come = after(lax.ppermute(send, BOTH, self.stage[k]), *ready)  16.6 us
    ppermute x8, waiting for transfers between devices, begun(): return lax.ppermute(after(send, *ready), BOTH, plan.stage[k])  16.3 us
    ppermute x3, waiting for transfers between devices, double(): return jnp.concatenate([near, lax.ppermute(near, BOTH, self.stage[k])], 0)  14.1 us
    ppermute x11, waiting for transfers between devices, swap(): return lax.ppermute(block, BOTH, self.core)  11.2 us
    ppermute x3, waiting for transfers between devices, final(): return lax.ppermute(after(near, *ready), BOTH, self.stage[self.bits - 1])  10.8 us
    ppermute x8, starting transfers between devices, onward(): return lax.ppermute(after(block, *ready), BOTH, plan.toward[1])  10.7 us
  transfers between devices with their start and end apart: 54, of which 35 were waited for; matrix products, arithmetic and copies ran while one was open for 6% of the time, Pallas kernels for 37%

profile of v6, /device:TPU:0, one launch (start us, length us, event | category | flops | bytes accessed | tf_op | source)
XLA Modules:
  0.0 377.1 jit_solution(1905440682681622410)
XLA Ops:
  9.1 4.8 %collective-permute-done.1 = bf16[1,3,128,1024]{3,2,1,0:T(8,128)(2,1)S(1)} collective-permute-done((bf16[1,3,128,1024]{3,2,1,0:T(8,128)(2,1)}, bf16[1,3,128,1024]{3,2,1,0:T(8,128)(2,1)S(1)}, u32[]{:S(2)}, u32[]{:S(2)}) %collective-permute-start.1) | collective-permute-done | bytes 786464 | tf_op jit(solution)/shard_map/ppermute | solution.py:111
  18.5 9.6 %collective-permute-done.2 = bf16[144,1024]{1,0:T(8,128)(2,1)S(1)} collective-permute-done((bf16[144,1024]{1,0:T(8,128)(2,1)S(1)}, bf16[144,1024]{1,0:T(8,128)(2,1)S(1)}, u32[]{:S(2)}, u32[]{:S(2)}) %collective-permute-start.2) | collective-permute-done | bytes 294944 | tf_op jit(solution)/shard_map/ppermute | solution.py:1244
  35.7 5.0 %collective-permute-done.5 = bf16[144,1024]{1,0:T(8,128)(2,1)S(1)} collective-permute-done((bf16[144,1024]{1,0:T(8,128)(2,1)S(1)}, bf16[144,1024]{1,0:T(8,128)(2,1)S(1)}, u32[]{:S(2)}, u32[]{:S(2)}) %collective-permute-start.5) | collective-permute-done | bytes 294944 | tf_op jit(solution)/shard_map/ppermute | solution.py:1244
  42.0 8.6 %collective-permute-done.7 = bf16[256,512]{1,0:T(8,128)(2,1)S(1)} collective-permute-done((bf16[256,512]{1,0:T(8,128)(2,1)S(1)}, bf16[256,512]{1,0:T(8,128)(2,1)S(1)}, u32[]{:S(2)}, u32[]{:S(2)}) %collective-permute-start.7) | collective-permute-done | bytes 262176 | tf_op jit(solution)/shard_map/ppermute | solution.py:1244
  57.4 6.1 %attention_forward.3 = (bf16[512,768]{1,0:T(8,128)(2,1)}, bf16[2,3,128,256]{3,2,1,0:T(8,128)(2,1)}, bf16[2,3,128,256]{3,2,1,0:T(8,128)(2,1)}, f32[2,8,512]{2,1,0:T(8,128)}) custom-call(bf16[2,3,128,1024]{3,2,1,0:T(8,128)(2,1)} %copy-done.3, bf16[2,3,128,1024]{3,2,1,0:T(8,128)(2,1)} %collective-permute-done.4.refs_1_, ...), custom_call_target="tpu_custom_call" | custom-call | flops 3000000000 | bytes 6356992 | tf_op jit(solution)/shard_map/attention_forward/pallas_call | solution.py:181
  69.4 6.1 %attention_forward.4 = (bf16[512,768]{1,0:T(8,128)(2,1)}, bf16[2,3,128,256]{3,2,1,0:T(8,128)(2,1)}, bf16[2,3,128,256]{3,2,1,0:T(8,128)(2,1)}, f32[2,8,512]{2,1,0:T(8,128)}) custom-call(bf16[2,3,128,1024]{3,2,1,0:T(8,128)(2,1)} %copy-done.3, bf16[2,3,128,1024]{3,2,1,0:T(8,128)(2,1)} %collective-permute-done.4.refs_1_, ...), custom_call_target="tpu_custom_call", output_to_operand_aliasing={{1}: (4, {}), {2}: (5, {})} | custom-call | flops 3000000000 | bytes 7143424 | tf_op jit(solution)/shard_map/attention_forward/pallas_call | solution.py:181
  81.1 6.1 %attention_forward.5 = (bf16[512,768]{1,0:T(8,128)(2,1)}, bf16[2,3,128,256]{3,2,1,0:T(8,128)(2,1)}, bf16[2,3,128,256]{3,2,1,0:T(8,128)(2,1)}, f32[2,8,512]{2,1,0:T(8,128)}) custom-call(bf16[2,3,128,1024]{3,2,1,0:T(8,128)(2,1)} %copy-done.3, bf16[2,3,128,1024]{3,2,1,0:T(8,128)(2,1)} %collective-permute-done.4.refs_1_, ...), custom_call_target="tpu_custom_call", output_to_operand_aliasing={{1}: (4, {}), {2}: (5, {})} | custom-call | flops 3000000000 | bytes 7143424 | tf_op jit(solution)/shard_map/attention_forward/pallas_call | solution.py:181
  90.1 6.3 %collective-permute-done.15.refs_6_ = bf16[2,2,256,512]{3,2,1,0:T(8,128)(2,1)} collective-permute-done((bf16[2,2,256,512]{3,2,1,0:T(8,128)(2,1)S(1)}, bf16[2,2,256,512]{3,2,1,0:T(8,128)(2,1)}, u32[]{:S(2)}, u32[]{:S(2)}) %collective-permute-start.15) | collective-permute-done | bytes 1048608 | tf_op jit(solution)/shard_map/ppermute | solution.py:1232
  99.6 4.7 %collective-permute-done.20 = bf16[2,3,128,256]{3,2,1,0:T(8,128)(2,1)S(1)} collective-permute-done((bf16[2,3,128,256]{3,2,1,0:T(8,128)(2,1)}, bf16[2,3,128,256]{3,2,1,0:T(8,128)(2,1)S(1)}, u32[]{:S(2)}, u32[]{:S(2)}) %collective-permute-start.20) | collective-permute-done | bytes 393248 | tf_op jit(solution)/shard_map/ppermute | solution.py:85
  108.0 8.5 %collective-permute-done.21 = bf16[2,3,128,256]{3,2,1,0:T(8,128)(2,1)S(1)} collective-permute-done((bf16[2,3,128,256]{3,2,1,0:T(8,128)(2,1)S(1)}, bf16[2,3,128,256]{3,2,1,0:T(8,128)(2,1)S(1)}, u32[]{:S(2)}, u32[]{:S(2)}) %collective-permute-start.21) | collective-permute-done | bytes 393248 | tf_op jit(solution)/shard_map/ppermute | solution.py:85
  117.2 7.4 %output_norm.1 = (f32[384,1024]{1,0:T(8,128)}, f32[384,1024]{1,0:T(8,128)}, bf16[384,1024]{1,0:T(8,128)(2,1)}, bf16[1024,1024]{1,0:T(8,128)(2,1)}) custom-call(bf16[384,1024]{1,0:T(8,128)(2,1)} %bitcast.100, f32[8,1024]{1,0:T(8,128)} %get-tuple-element.178.refs_3_.refs_1_.refs_4_, bf16[128,1024]{1,0:T(8,128)(2,1)} %refs_2_.6, bf16[128,3072]{1,0:T(8,128)(2,1)} %copy-done.12, ...), custom_call_target="tpu_custom_call" | custom-call | flops 3500000000 | bytes 10649600 | tf_op jit(solution)/shard_map/output_norm/pallas_call | solution.py:181
  130.2 14.4 %up_forward.1 = (bf16[4,768,512]{2,1,0:T(8,128)(2,1)}, bf16[4,768,512]{2,1,0:T(8,128)(2,1)}, bf16[4,1024,512]{2,1,0:T(8,128)(2,1)}) custom-call(bf16[384,1024]{1,0:T(8,128)(2,1)} %get-tuple-element.223.refs_0_, bf16[384,1024]{1,0:T(8,128)(2,1)} %collective-permute-done.23.refs_1_, bf16[128,4096]{1,0:T(8,128)(2,1)} %refs_2_.7, bf16[128,3072]{1,0:T(8,128)(2,1)} %copy-done.12, ...), custom_call_target="tpu_custom_call" | custom-call | flops 7500000256 | bytes 17055744 | tf_op jit(solution)/shard_map/up_forward/pallas_call | solution.py:181
  144.6 4.4 %collective-permute-done.25.refs_3_ = bf16[2,3,512,256]{3,2,1,0:T(8,128)(2,1)S(1)} collective-permute-done((bf16[2,3,512,256]{3,2,1,0:T(8,128)(2,1)S(1)}, bf16[2,3,512,256]{3,2,1,0:T(8,128)(2,1)S(1)}, u32[]{:S(2)}, u32[]{:S(2)}) %collective-permute-start.25) | collective-permute-done | bytes 1572896 | tf_op jit(solution)/shard_map/ppermute | solution.py:1232
  150.2 9.6 %down_forward.1 = (f32[384,1024]{1,0:T(8,128)}, bf16[384,1024]{1,0:T(8,128)(2,1)}, bf16[2048,1024]{1,0:T(8,128)(2,1)}) custom-call(bf16[4,768,512]{2,1,0:T(8,128)(2,1)} %get-tuple-element.199.refs_0_, bf16[512,1024]{1,0:T(8,128)(2,1)} %refs_1_.5, bf16[2,3,512,256]{3,2,1,0:T(8,128)(2,1)} %copy-done.21, bf16[2,3,512,256]{3,2,1,0:T(8,128)(2,1)} %copy-done.27), custom_call_target="tpu_custom_call" | custom-call | flops 5000000000 | bytes 13893632 | tf_op jit(solution)/shard_map/down_forward/pallas_call | solution.py:181
  163.3 5.4 %norm_two.1 = (bf16[384,1024]{1,0:T(8,128)(2,1)}, f32[384,1024]{1,0:T(8,128)}, bf16[384,1024]{1,0:T(8,128)(2,1)}, f32[8,1024]{1,0:T(8,128)}) custom-call(f32[384,1024]{1,0:T(8,128)} %get-tuple-element.192.refs_0_, f32[384,1024]{1,0:T(8,128)} %get-tuple-element.201.refs_1_, bf16[384,1024]{1,0:T(8,128)(2,1)} %copy-done.30, bf16[384,1024]{1,0:T(8,128)(2,1)} %bitcast.128, ...), custom_call_target="tpu_custom_call" | custom-call | flops 3000000000 | bytes 7929856 | tf_op jit(solution)/shard_map/norm_two/pallas_call | solution.py:181
  172.2 5.8 %down_weights.2 = bf16[2,4,512,256]{3,2,1,0:T(8,128)(2,1)} custom-call(bf16[4,768,512]{2,1,0:T(8,128)(2,1)} %get-tuple-element.199.refs_0_, bf16[384,1024]{1,0:T(8,128)(2,1)} %get-tuple-element.207.refs_1_.refs_0_, bf16[384,1024]{1,0:T(8,128)(2,1)} %copy-done.29), custom_call_target="tpu_custom_call" | custom-call | flops 2500000000 | bytes 6815744 | tf_op jit(solution)/shard_map/down_weights/pallas_call | solution.py:181
  179.6 5.8 %down_weights.3 = bf16[2,4,512,256]{3,2,1,0:T(8,128)(2,1)} custom-call(bf16[4,768,512]{2,1,0:T(8,128)(2,1)} %get-tuple-element.199.refs_0_, bf16[384,1024]{1,0:T(8,128)(2,1)} %get-tuple-element.207.refs_1_.refs_0_, bf16[384,1024]{1,0:T(8,128)(2,1)} %copy-done.29), custom_call_target="tpu_custom_call" | custom-call | flops 2500000000 | bytes 6815744 | tf_op jit(solution)/shard_map/down_weights/pallas_call | solution.py:181
  185.3 12.6 %ffn_backward.1 = (bf16[4,768,512]{2,1,0:T(8,128)(2,1)}, f32[4,8,512]{2,1,0:T(8,128)}, f32[384,1024]{1,0:T(8,128)}, bf16[384,1024]{1,0:T(8,128)(2,1)}) custom-call(bf16[384,1024]{1,0:T(8,128)(2,1)} %get-tuple-element.207.refs_1_.refs_0_, bf16[384,1024]{1,0:T(8,128)(2,1)} %copy-done.29, bf16[2048,1024]{1,0:T(8,128)(2,1)} %get-tuple-element.208.refs_2_, ...), custom_call_target="tpu_custom_call" | custom-call | flops 6499999744 | bytes 18677760 | tf_op jit(solution)/shard_map/ffn_backward/pallas_call | solution.py:181
  198.1 5.2 %up_weights.2 = bf16[2,4,128,1024]{3,2,1,0:T(8,128)(2,1)} custom-call(bf16[384,1024]{1,0:T(8,128)(2,1)} %get-tuple-element.223.refs_0_, bf16[384,1024]{1,0:T(8,128)(2,1)} %collective-permute-done.23.refs_1_, bf16[4,768,512]{2,1,0:T(8,128)(2,1)} %get-tuple-element.213.refs_2_), custom_call_target="tpu_custom_call" | custom-call | flops 3000000000 | bytes 6815744 | tf_op jit(solution)/shard_map/up_weights/pallas_call | solution.py:181
  207.5 7.9 %norm_one_back.1 = (f32[384,1024]{1,0:T(8,128)}, bf16[384,1024]{1,0:T(8,128)(2,1)}, f32[8,8,768]{2,1,0:T(8,128)}, bf16[2,384,256]{2,1,0:T(8,128)(2,1)}, bf16[2,384,256]{2,1,0:T(8,128)(2,1)}) custom-call(f32[384,1024]{1,0:T(8,128)} %get-tuple-element.204.refs_0_, f32[384,1024]{1,0:T(8,128)} %get-tuple-element.215.refs_1_, ...), custom_call_target="tpu_custom_call" | custom-call | flops 4000000000 | bytes 11010048 | tf_op jit(solution)/shard_map/norm_one_back/pallas_call | solution.py:181
  215.4 6.6 %collective-permute-done.30 = bf16[1,4,512,256]{3,2,1,0:T(8,128)(2,1)S(1)} collective-permute-done((bf16[1,4,512,256]{3,2,1,0:T(8,128)(2,1)S(1)}, bf16[1,4,512,256]{3,2,1,0:T(8,128)(2,1)S(1)}, u32[]{:S(2)}, u32[]{:S(2)}) %collective-permute-start.30) | collective-permute-done | bytes 1048608 | tf_op jit(solution)/shard_map/ppermute | solution.py:1394
  224.6 5.2 %up_weights.3 = bf16[2,4,128,1024]{3,2,1,0:T(8,128)(2,1)} custom-call(bf16[384,1024]{1,0:T(8,128)(2,1)} %get-tuple-element.223.refs_0_, bf16[384,1024]{1,0:T(8,128)(2,1)} %collective-permute-done.23.refs_1_, bf16[4,768,512]{2,1,0:T(8,128)(2,1)} %get-tuple-element.213.refs_2_), custom_call_target="tpu_custom_call" | custom-call | flops 3000000000 | bytes 6815744 | tf_op jit(solution)/shard_map/up_weights/pallas_call | solution.py:181
  230.4 4.2 %out_weights.1 = (bf16[4,4,128,256]{3,2,1,0:T(8,128)(2,1)}, bf16[4,4,128,256]{3,2,1,0:T(8,128)(2,1)}) custom-call(bf16[384,1024]{1,0:T(8,128)(2,1)} %get-tuple-element.227.refs_0_, bf16[2,384,256]{2,1,0:T(8,128)(2,1)} %bitcast.95, bf16[2,384,256]{2,1,0:T(8,128)(2,1)} %bitcast.106, bf16[2,384,256]{2,1,0:T(8,128)(2,1)} %bitcast.93), custom_call_target="tpu_custom_call" | custom-call | tf_op jit(solution)/shard_map/out_weights/pallas_call | solution.py:181
  244.7 8.5 %attention_backward.3 = (bf16[3,512,768]{2,1,0:T(8,128)(2,1)}, bf16[2,3,128,1024]{3,2,1,0:T(8,128)(2,1)}, bf16[2,3,128,1024]{3,2,1,0:T(8,128)(2,1)}) custom-call(bf16[512,768]{1,0:T(8,128)(2,1)} %get-tuple-element.239.refs_0_, bf16[1024,768]{1,0:T(8,128)(2,1)} %get-tuple-element.165.refs_2_.refs_1_, f32[2,8,512]{2,1,0:T(8,128)} %get-tuple-element.240.refs_2_, ...), custom_call_target="tpu_custom_call" | custom-call | flops 4000000000 | bytes 9863168 | tf_op jit(solution)/shard_map/attention_backward/pallas_call | solution.py:181
  257.5 8.6 %attention_backward.4 = (bf16[3,512,768]{2,1,0:T(8,128)(2,1)}, bf16[2,3,128,1024]{3,2,1,0:T(8,128)(2,1)}, bf16[2,3,128,1024]{3,2,1,0:T(8,128)(2,1)}) custom-call(bf16[512,768]{1,0:T(8,128)(2,1)} %get-tuple-element.244.refs_0_, bf16[1024,768]{1,0:T(8,128)(2,1)} %get-tuple-element.165.refs_2_.refs_1_, ...), custom_call_target="tpu_custom_call", output_to_operand_aliasing={{0}: (8, {}), {1}: (9, {}), {2}: (10, {})} | custom-call | flops 4000000000 | bytes 15368192 | tf_op jit(solution)/shard_map/attention_backward/pallas_call | solution.py:181
  267.1 3.8 %fusion.2 = (bf16[4,128,1024]{2,1,0:T(8,128)(2,1)}, bf16[1,4,128,1024]{3,2,1,0:T(8,128)(2,1)}) fusion(bf16[2,4,128,1024]{3,2,1,0:T(8,128)(2,1)S(1)} %copy-done.1, bf16[2,4,128,1024]{3,2,1,0:T(8,128)(2,1)} %collective-permute-done.34), kind=kLoop, calls=%fused_computation.11 | loop fusion | flops 4194304 | bytes 6291456 | tf_op jit(solution)/shard_map/squeeze | solution.py:1490
  277.5 8.5 %attention_backward.5 = (bf16[3,512,768]{2,1,0:T(8,128)(2,1)}, bf16[2,3,128,1024]{3,2,1,0:T(8,128)(2,1)}, bf16[2,3,128,1024]{3,2,1,0:T(8,128)(2,1)}) custom-call(bf16[512,768]{1,0:T(8,128)(2,1)} %get-tuple-element.253.refs_0_, bf16[1024,768]{1,0:T(8,128)(2,1)} %get-tuple-element.165.refs_2_.refs_1_, ...), custom_call_target="tpu_custom_call", output_to_operand_aliasing={{0}: (8, {}), {1}: (9, {}), {2}: (10, {})} | custom-call | flops 4000000000 | bytes 15368192 | tf_op jit(solution)/shard_map/attention_backward/pallas_call | solution.py:181
  295.4 6.8 %head_weights_backward.1 = (bf16[4,144,768]{2,1,0:T(8,128)(2,1)}, bf16[4,144,768]{2,1,0:T(8,128)(2,1)}) custom-call(bf16[2,3,128,1024]{3,2,1,0:T(8,128)(2,1)} %copy-done.3, bf16[2,3,128,1024]{3,2,1,0:T(8,128)(2,1)} %collective-permute-done.4.refs_1_, bf16[3,512,768]{2,1,0:T(8,128)(2,1)} %get-tuple-element.265.refs_2_, ...), custom_call_target="tpu_custom_call" | custom-call | flops 4000000000 | bytes 7536640 | tf_op jit(solution)/shard_map/head_weights_backward/pallas_call | solution.py:181
  302.5 5.9 %collective-permute-done.41 = bf16[2,128,1280]{2,1,0:T(8,128)(2,1)S(1)} collective-permute-done((bf16[2,128,1280]{2,1,0:T(8,128)(2,1)}, bf16[2,128,1280]{2,1,0:T(8,128)(2,1)S(1)}, u32[]{:S(2)}, u32[]{:S(2)}) %collective-permute-start.41) | collective-permute-done | bytes 655392 | tf_op jit(solution)/shard_map/ppermute | solution.py:1443
  324.6 7.7 %collective-permute-done.46.refs_1_ = bf16[2,512,256]{2,1,0:T(8,128)(2,1)S(1)} collective-permute-done((bf16[2,512,256]{2,1,0:T(8,128)(2,1)S(1)}, bf16[2,512,256]{2,1,0:T(8,128)(2,1)S(1)}, u32[]{:S(2)}, u32[]{:S(2)}) %collective-permute-start.46) | collective-permute-done | bytes 524320 | tf_op jit(solution)/shard_map/ppermute | solution.py:108
  345.6 4.1 %collective-permute-done.49 = bf16[1,128,1280]{2,1,0:T(8,128)(2,1)S(1)} collective-permute-done((bf16[1,128,1280]{2,1,0:T(8,128)(2,1)S(1)}, bf16[1,128,1280]{2,1,0:T(8,128)(2,1)S(1)}, u32[]{:S(2)}, u32[]{:S(2)}) %collective-permute-start.49) | collective-permute-done | bytes 327712 | tf_op jit(solution)/shard_map/ppermute | solution.py:111
  358.9 5.3 %collective-permute-done.51 = bf16[1,144,768]{2,1,0:T(8,128)(2,1)S(1)} collective-permute-done((bf16[1,144,768]{2,1,0:T(8,128)(2,1)S(1)}, bf16[1,144,768]{2,1,0:T(8,128)(2,1)S(1)}, u32[]{:S(2)}, u32[]{:S(2)}) %collective-permute-start.51) | collective-permute-done | bytes 221216 | tf_op jit(solution)/shard_map/ppermute | solution.py:111
  (227 shorter events, 156.6 us)
Async XLA Ops:
  0.7 13.2 %collective-permute-start.1 = (bf16[1,3,128,1024]{3,2,1,0:T(8,128)(2,1)}, bf16[1,3,128,1024]{3,2,1,0:T(8,128)(2,1)S(1)}, u32[]{:S(2)}, u32[]{:S(2)}) collective-permute-start(bf16[1,3,128,1024]{3,2,1,0:T(8,128)(2,1)} %bitcast.99), channel_id=1, source_target_pairs={{0,1},{1,0},{2,3},{3,2},{4,6},{5,7},{6,4},{7,5},{8,9},{9,8},{10,11... | collective-permute-start | bytes 2359304 | tf_op jit(solution)/shard_map/ppermute | solution.py:111
  17.1 23.6 %collective-permute-start.4 = (bf16[2,3,128,1024]{3,2,1,0:T(8,128)(2,1)S(1)}, bf16[2,3,128,1024]{3,2,1,0:T(8,128)(2,1)}, u32[]{:S(2)}, u32[]{:S(2)}) collective-permute-start(bf16[2,3,128,1024]{3,2,1,0:T(8,128)(2,1)S(1)} %pad_maximum_fusion.refs_0_), channel_id=1, source_target_pairs={{0,2},{1,3},{2,0},{3,1},{4,5},{5,4},{6,7},{7,6},{8,10},{9,11},{10,... | collective-permute-start | bytes 4718600 | tf_op jit(solution)/shard_map/ppermute | solution.py:1232
  40.9 13.6 %collective-permute-start.9 = (bf16[4,144,1024]{2,1,0:T(8,128)(2,1)S(1)}, bf16[4,144,1024]{2,1,0:T(8,128)(2,1)}, u32[]{:S(2)}, u32[]{:S(2)}) collective-permute-start(bf16[4,144,1024]{2,1,0:T(8,128)(2,1)S(1)} %pad_maximum_fusion.1.refs_0_), channel_id=1, source_target_pairs={{0,4},{1,5},{2,6},{3,7},{4,0},{5,1},{6,2},{7,3},{8,12},{9,13},{10,... | collective-permute-start | bytes 3538952 | tf_op jit(solution)/shard_map/ppermute | solution.py:75
  41.7 21.8 %collective-permute-start.10 = (bf16[1,3,128,256]{3,2,1,0:T(8,128)(2,1)S(1)}, bf16[1,3,128,256]{3,2,1,0:T(8,128)(2,1)S(1)}, u32[]{:S(2)}, u32[]{:S(2)}) collective-permute-start(bf16[1,3,128,256]{3,2,1,0:T(8,128)(2,1)S(1)} %bitcast.96), channel_id=1, source_target_pairs={{0,1},{1,0},{2,3},{3,2},{4,6},{5,7},{6,4},{7,5},{8,9},{9,8},{10,11... | collective-permute-start | bytes 589832 | tf_op jit(solution)/shard_map/ppermute | solution.py:1238
  50.6 12.9 %collective-permute-start.8 = (bf16[256,512]{1,0:T(8,128)(2,1)S(1)}, bf16[256,512]{1,0:T(8,128)(2,1)S(1)}, u32[]{:S(2)}, u32[]{:S(2)}) collective-permute-start(bf16[256,512]{1,0:T(8,128)(2,1)S(1)} %collective-permute-done.7), channel_id=1, source_target_pairs={{0,8},{1,9},{2,10},{3,11},{4,12},{5,13},{6,14},{7,15},{8,24},{9,25... | collective-permute-start | bytes 786440 | tf_op jit(solution)/shard_map/ppermute | solution.py:1244
  51.1 13.8 %collective-permute-start.6 = (bf16[512,256]{1,0:T(8,128)(2,1)S(1)}, bf16[512,256]{1,0:T(8,128)(2,1)S(1)}, u32[]{:S(2)}, u32[]{:S(2)}) collective-permute-start(bf16[512,256]{1,0:T(8,128)(2,1)S(1)} %copy-done.34), channel_id=1, source_target_pairs={{0,8},{1,9},{2,10},{3,11},{4,12},{5,13},{6,14},{7,15},{8,24},{9,25... | collective-permute-start | bytes 786440 | tf_op jit(solution)/shard_map/ppermute | solution.py:1244
  65.0 11.6 %collective-permute-start.12 = (bf16[1,2,256,512]{3,2,1,0:T(8,128)(2,1)S(1)}, bf16[1,2,256,512]{3,2,1,0:T(8,128)(2,1)S(1)}, u32[]{:S(2)}, u32[]{:S(2)}) collective-permute-start(bf16[1,2,256,512]{3,2,1,0:T(8,128)(2,1)S(1)} %bitcast.81), channel_id=1, source_target_pairs={{0,1},{1,0},{2,3},{3,2},{4,6},{5,7},{6,4},{7,5},{8,9},{9,8},{10,11... | collective-permute-start | bytes 1572872 | tf_op jit(solution)/shard_map/ppermute | solution.py:1238
  65.4 11.3 %collective-permute-start.11 = (bf16[256,512]{1,0:T(8,128)(2,1)S(1)}, bf16[256,512]{1,0:T(8,128)(2,1)S(1)}, u32[]{:S(2)}, u32[]{:S(2)}) collective-permute-start(bf16[256,512]{1,0:T(8,128)(2,1)S(1)} %collective-permute-done.8), channel_id=1, source_target_pairs={{0,8},{1,9},{2,10},{3,11},{4,12},{5,13},{6,14},{7,15},{8,24},{9,25... | collective-permute-start | bytes 786440 | tf_op jit(solution)/shard_map/ppermute | solution.py:1244
  65.9 12.7 %collective-permute-start.13 = (bf16[2,3,128,256]{3,2,1,0:T(8,128)(2,1)S(1)}, bf16[2,3,128,256]{3,2,1,0:T(8,128)(2,1)}, u32[]{:S(2)}, u32[]{:S(2)}) collective-permute-start(bf16[2,3,128,256]{3,2,1,0:T(8,128)(2,1)S(1)} %constant_dynamic-update-slice_fusion.refs_4_), channel_id=1, source_target_pairs={{0,2},{1,3},{2,0},{3,1},{4,5},{5,4},{6,7},{7,6},{8,10},{9,11},{10,... | collective-permute-start | bytes 1179656 | tf_op jit(solution)/shard_map/ppermute | solution.py:1232
  66.0 12.6 %collective-permute-start.14 = (bf16[512,256]{1,0:T(8,128)(2,1)S(1)}, bf16[512,256]{1,0:T(8,128)(2,1)S(1)}, u32[]{:S(2)}, u32[]{:S(2)}) collective-permute-start(bf16[512,256]{1,0:T(8,128)(2,1)S(1)} %collective-permute-done.6), channel_id=1, source_target_pairs={{0,8},{1,9},{2,10},{3,11},{4,12},{5,13},{6,14},{7,15},{8,24},{9,25... | collective-permute-start | bytes 786440 | tf_op jit(solution)/shard_map/ppermute | solution.py:1244
  78.6 17.7 %collective-permute-start.15 = (bf16[2,2,256,512]{3,2,1,0:T(8,128)(2,1)S(1)}, bf16[2,2,256,512]{3,2,1,0:T(8,128)(2,1)}, u32[]{:S(2)}, u32[]{:S(2)}) collective-permute-start(bf16[2,2,256,512]{3,2,1,0:T(8,128)(2,1)S(1)} %constant_dynamic-update-slice_fusion.2.refs_5_), channel_id=1, source_target_pairs={{0,2},{1,3},{2,0},{3,1},{4,5},{5,4},{6,7},{7,6},{8,10},{9,11},{10,... | collective-permute-start | bytes 3145736 | tf_op jit(solution)/shard_map/ppermute | solution.py:1232
  104.4 12.1 %collective-permute-start.21 = (bf16[2,3,128,256]{3,2,1,0:T(8,128)(2,1)S(1)}, bf16[2,3,128,256]{3,2,1,0:T(8,128)(2,1)S(1)}, u32[]{:S(2)}, u32[]{:S(2)}) collective-permute-start(bf16[2,3,128,256]{3,2,1,0:T(8,128)(2,1)S(1)} %pad_maximum_fusion.6), channel_id=1, source_target_pairs={{0,1},{1,0},{2,3},{3,2},{4,6},{5,7},{6,4},{7,5},{8,9},{9,8},{10,11... | collective-permute-start | bytes 1179656 | tf_op jit(solution)/shard_map/ppermute | solution.py:85
  106.2 18.5 %collective-permute-start.22 = (bf16[2,1,256,512]{3,2,1,0:T(8,128)(2,1)}, bf16[2,1,256,512]{3,2,1,0:T(8,128)(2,1)}, u32[]{:S(2)}, u32[]{:S(2)}) collective-permute-start(bf16[2,1,256,512]{3,2,1,0:T(8,128)(2,1)} %constant_dynamic-update-slice_fusion.4.refs_7_), channel_id=1, source_target_pairs={{0,2},{1,3},{2,0},{3,1},{4,5},{5,4},{6,7},{7,6},{8,10},{9,11},{10,... | collective-permute-start | bytes 1572872 | tf_op jit(solution)/shard_map/ppermute | solution.py:1232
  116.5 12.0 %collective-permute-start.24 = (bf16[1,3,512,256]{3,2,1,0:T(8,128)(2,1)S(1)}, bf16[1,3,512,256]{3,2,1,0:T(8,128)(2,1)S(1)}, u32[]{:S(2)}, u32[]{:S(2)}) collective-permute-start(bf16[1,3,512,256]{3,2,1,0:T(8,128)(2,1)S(1)} %bitcast.79), channel_id=1, source_target_pairs={{0,1},{1,0},{2,3},{3,2},{4,6},{5,7},{6,4},{7,5},{8,9},{9,8},{10,11... | collective-permute-start | bytes 2359304 | tf_op jit(solution)/shard_map/ppermute | solution.py:1238
  128.5 20.5 %collective-permute-start.25 = (bf16[2,3,512,256]{3,2,1,0:T(8,128)(2,1)S(1)}, bf16[2,3,512,256]{3,2,1,0:T(8,128)(2,1)S(1)}, u32[]{:S(2)}, u32[]{:S(2)}) collective-permute-start(bf16[2,3,512,256]{3,2,1,0:T(8,128)(2,1)S(1)} %constant_dynamic-update-slice_fusion.6.refs_2_), channel_id=1, source_target_pairs={{0,2},{1,3},{2,0},{3,1},{4,5},{5,4},{6,7},{7,6},{8,10},{9,11},{10,... | collective-permute-start | bytes 4718600 | tf_op jit(solution)/shard_map/ppermute | solution.py:1232
  177.9 26.2 %collective-permute-start.28 = (bf16[2,4,512,256]{3,2,1,0:T(8,128)(2,1)}, bf16[2,4,512,256]{3,2,1,0:T(8,128)(2,1)S(1)}, u32[]{:S(2)}, u32[]{:S(2)}) collective-permute-start(bf16[2,4,512,256]{3,2,1,0:T(8,128)(2,1)} %down_weights.2), channel_id=1, source_target_pairs={{0,2},{1,3},{2,0},{3,1},{4,5},{5,4},{6,7},{7,6},{8,10},{9,11},{10,... | collective-permute-start | bytes 6291464 | tf_op jit(solution)/shard_map/ppermute | solution.py:1394
  207.2 14.8 %collective-permute-start.30 = (bf16[1,4,512,256]{3,2,1,0:T(8,128)(2,1)S(1)}, bf16[1,4,512,256]{3,2,1,0:T(8,128)(2,1)S(1)}, u32[]{:S(2)}, u32[]{:S(2)}) collective-permute-start(bf16[1,4,512,256]{3,2,1,0:T(8,128)(2,1)S(1)} %get-tuple-element.294), channel_id=1, source_target_pairs={{0,1},{1,0},{2,3},{3,2},{4,6},{5,7},{6,4},{7,5},{8,9},{9,8},{10,11... | collective-permute-start | bytes 3145736 | tf_op jit(solution)/shard_map/ppermute | solution.py:1394
  240.8 26.4 %collective-permute-start.34 = (bf16[2,4,128,1024]{3,2,1,0:T(8,128)(2,1)}, bf16[2,4,128,1024]{3,2,1,0:T(8,128)(2,1)}, u32[]{:S(2)}, u32[]{:S(2)}) collective-permute-start(bf16[2,4,128,1024]{3,2,1,0:T(8,128)(2,1)} %up_weights.2), channel_id=1, source_target_pairs={{0,2},{1,3},{2,0},{3,1},{4,5},{5,4},{6,7},{7,6},{8,10},{9,11},{10,... | collective-permute-start | bytes 6291464 | tf_op jit(solution)/shard_map/ppermute | solution.py:1394
  256.6 14.6 %collective-permute-start.36 = (bf16[2,512,256]{2,1,0:T(8,128)(2,1)}, bf16[2,512,256]{2,1,0:T(8,128)(2,1)S(1)}, u32[]{:S(2)}, u32[]{:S(2)}) collective-permute-start(bf16[2,512,256]{2,1,0:T(8,128)(2,1)} %get-tuple-element.251), channel_id=1, source_target_pairs={{0,8},{1,9},{2,10},{3,11},{4,12},{5,13},{6,14},{7,15},{8,0},{9,1},... | collective-permute-start | bytes 1572872 | tf_op jit(solution)/shard_map/ppermute | solution.py:1443
  257.1 15.6 %collective-permute-start.35 = (bf16[2,4,128,256]{3,2,1,0:T(8,128)(2,1)}, bf16[2,4,128,256]{3,2,1,0:T(8,128)(2,1)}, u32[]{:S(2)}, u32[]{:S(2)}) collective-permute-start(bf16[2,4,128,256]{3,2,1,0:T(8,128)(2,1)} %get-tuple-element.296), channel_id=1, source_target_pairs={{0,2},{1,3},{2,0},{3,1},{4,5},{5,4},{6,7},{7,6},{8,10},{9,11},{10,... | collective-permute-start | bytes 1572872 | tf_op jit(solution)/shard_map/ppermute | solution.py:1394
  270.9 17.8 %collective-permute-start.37 = (bf16[1,4,128,1024]{3,2,1,0:T(8,128)(2,1)}, bf16[1,4,128,1024]{3,2,1,0:T(8,128)(2,1)}, u32[]{:S(2)}, u32[]{:S(2)}) collective-permute-start(bf16[1,4,128,1024]{3,2,1,0:T(8,128)(2,1)} %get-tuple-element.292), channel_id=1, source_target_pairs={{0,1},{1,0},{2,3},{3,2},{4,6},{5,7},{6,4},{7,5},{8,9},{9,8},{10,11... | collective-permute-start | bytes 3145736 | tf_op jit(solution)/shard_map/ppermute | solution.py:1394
  274.7 14.0 %collective-permute-start.38 = (bf16[1,4,128,256]{3,2,1,0:T(8,128)(2,1)S(1)}, bf16[1,4,128,256]{3,2,1,0:T(8,128)(2,1)S(1)}, u32[]{:S(2)}, u32[]{:S(2)}) collective-permute-start(bf16[1,4,128,256]{3,2,1,0:T(8,128)(2,1)S(1)} %get-tuple-element.302), channel_id=1, source_target_pairs={{0,1},{1,0},{2,3},{3,2},{4,6},{5,7},{6,4},{7,5},{8,9},{9,8},{10,11... | collective-permute-start | bytes 786440 | tf_op jit(solution)/shard_map/ppermute | solution.py:1394
  275.1 19.6 %collective-permute-start.40 = (bf16[1,512,256]{2,1,0:T(8,128)(2,1)S(1)}, bf16[1,512,256]{2,1,0:T(8,128)(2,1)S(1)}, u32[]{:S(2)}, u32[]{:S(2)}) collective-permute-start(bf16[1,512,256]{2,1,0:T(8,128)(2,1)S(1)} %get-tuple-element.299), channel_id=1, source_target_pairs={{0,16},{1,17},{2,18},{3,19},{4,20},{5,21},{6,22},{7,23},{8,24},{9,... | collective-permute-start | bytes 786440 | tf_op jit(solution)/shard_map/ppermute | solution.py:1451
  293.1 23.4 %collective-permute-start.39 = (bf16[2,3,128,1024]{3,2,1,0:T(8,128)(2,1)}, bf16[2,3,128,1024]{3,2,1,0:T(8,128)(2,1)S(1)}, u32[]{:S(2)}, u32[]{:S(2)}) collective-permute-start(bf16[2,3,128,1024]{3,2,1,0:T(8,128)(2,1)} %get-tuple-element.263), channel_id=1, source_target_pairs={{0,2},{1,3},{2,0},{3,1},{4,5},{5,4},{6,7},{7,6},{8,10},{9,11},{10,... | collective-permute-start | bytes 4718600 | tf_op jit(solution)/shard_map/ppermute | solution.py:1394
  294.8 13.7 %collective-permute-start.41 = (bf16[2,128,1280]{2,1,0:T(8,128)(2,1)}, bf16[2,128,1280]{2,1,0:T(8,128)(2,1)S(1)}, u32[]{:S(2)}, u32[]{:S(2)}) collective-permute-start(bf16[2,128,1280]{2,1,0:T(8,128)(2,1)} %get-tuple-element.269), channel_id=1, source_target_pairs={{0,8},{1,9},{2,10},{3,11},{4,12},{5,13},{6,14},{7,15},{8,0},{9,1},... | collective-permute-start | bytes 1966088 | tf_op jit(solution)/shard_map/ppermute | solution.py:1443
  302.2 16.1 %collective-permute-start.45 = (bf16[1,512,256]{2,1,0:T(8,128)(2,1)S(1)}, bf16[1,512,256]{2,1,0:T(8,128)(2,1)}, u32[]{:S(2)}, u32[]{:S(2)}) collective-permute-start(bf16[1,512,256]{2,1,0:T(8,128)(2,1)S(1)} %bitcast.90), channel_id=1, source_target_pairs={{0,1},{1,0},{2,3},{3,2},{4,6},{5,7},{6,4},{7,5},{8,9},{9,8},{10,11... | collective-permute-start | bytes 786440 | tf_op jit(solution)/shard_map/ppermute | solution.py:1238
  317.9 19.4 %collective-permute-start.43 = (bf16[1,3,128,1024]{3,2,1,0:T(8,128)(2,1)}, bf16[1,3,128,1024]{3,2,1,0:T(8,128)(2,1)}, u32[]{:S(2)}, u32[]{:S(2)}) collective-permute-start(bf16[1,3,128,1024]{3,2,1,0:T(8,128)(2,1)} %add_convert_fusion.4), channel_id=1, source_target_pairs={{0,1},{1,0},{2,3},{3,2},{4,6},{5,7},{6,4},{7,5},{8,9},{9,8},{10,11... | collective-permute-start | bytes 2359304 | tf_op jit(solution)/shard_map/ppermute | solution.py:1394
  319.2 13.1 %collective-permute-start.46 = (bf16[2,512,256]{2,1,0:T(8,128)(2,1)S(1)}, bf16[2,512,256]{2,1,0:T(8,128)(2,1)S(1)}, u32[]{:S(2)}, u32[]{:S(2)}) collective-permute-start(bf16[2,512,256]{2,1,0:T(8,128)(2,1)S(1)} %constant_dynamic-update-slice_fusion.8.refs_0_), channel_id=1, source_target_pairs={{0,2},{1,3},{2,0},{3,1},{4,5},{5,4},{6,7},{7,6},{8,10},{9,11},{10,... | collective-permute-start | bytes 1572872 | tf_op jit(solution)/shard_map/ppermute | solution.py:108
  320.9 16.4 %collective-permute-start.44 = (bf16[2,144,768]{2,1,0:T(8,128)(2,1)}, bf16[2,144,768]{2,1,0:T(8,128)(2,1)S(1)}, u32[]{:S(2)}, u32[]{:S(2)}) collective-permute-start(bf16[2,144,768]{2,1,0:T(8,128)(2,1)} %get-tuple-element.275), channel_id=1, source_target_pairs={{0,8},{1,9},{2,10},{3,11},{4,12},{5,13},{6,14},{7,15},{8,0},{9,1},... | collective-permute-start | bytes 1327112 | tf_op jit(solution)/shard_map/ppermute | solution.py:1443
  321.5 15.9 %collective-permute-start.47 = (bf16[1,128,1280]{2,1,0:T(8,128)(2,1)}, bf16[1,128,1280]{2,1,0:T(8,128)(2,1)S(1)}, u32[]{:S(2)}, u32[]{:S(2)}) collective-permute-start(bf16[1,128,1280]{2,1,0:T(8,128)(2,1)} %get-tuple-element.297), channel_id=1, source_target_pairs={{0,16},{1,17},{2,18},{3,19},{4,20},{5,21},{6,22},{7,23},{8,24},{9,... | collective-permute-start | bytes 983048 | tf_op jit(solution)/shard_map/ppermute | solution.py:1451
  344.2 11.6 %collective-permute-start.50 = (bf16[1,144,768]{2,1,0:T(8,128)(2,1)S(1)}, bf16[1,144,768]{2,1,0:T(8,128)(2,1)S(1)}, u32[]{:S(2)}, u32[]{:S(2)}) collective-permute-start(bf16[1,144,768]{2,1,0:T(8,128)(2,1)S(1)} %get-tuple-element.303), channel_id=1, source_target_pairs={{0,16},{1,17},{2,18},{3,19},{4,20},{5,21},{6,22},{7,23},{8,24},{9,... | collective-permute-start | bytes 663560 | tf_op jit(solution)/shard_map/ppermute | solution.py:1451
  357.6 10.6 %collective-permute-start.53 = (bf16[2,128,1280]{2,1,0:T(8,128)(2,1)S(1)}, bf16[2,128,1280]{2,1,0:T(8,128)(2,1)S(1)}, u32[]{:S(2)}, u32[]{:S(2)}) collective-permute-start(bf16[2,128,1280]{2,1,0:T(8,128)(2,1)S(1)} %pad_maximum_fusion.3.refs_0_), channel_id=1, source_target_pairs={{0,2},{1,3},{2,0},{3,1},{4,5},{5,4},{6,7},{7,6},{8,10},{9,11},{10,... | collective-permute-start | bytes 1966088 | tf_op jit(solution)/shard_map/ppermute | solution.py:108
  (59 other events, 458.3 us)
